TPU v7x, 32 devices: a whole 2x2x4 slice. The times are simulated.
32 devices in a mesh: rep: 2 (over core), fsdp: 16 (over z, y, x).
Axes of the slice: x: 2, y: 2, z: 4, core: 2. Of those that a mesh axis runs over, the one named last changes fastest.
Arguments:
- tokens: bfloat16 [16384, 768], P(('rep', 'fsdp')), may hold values from -6 to 6
- valid: int32 [128], P(('rep', 'fsdp')), may hold values from 1 to 192, as said below
- qkv_weight: float32 [2, 768, 2304], P(None, 'fsdp'), may hold values from -0.3125 to 0.3125
- out_weight: float32 [2, 768, 768], P(None, 'fsdp'), may hold values from -0.875 to 0.875
- up_weight: float32 [2, 768, 3072], P(None, 'fsdp'), may hold values from -0.21875 to 0.21875
- down_weight: float32 [2, 3072, 768], P(None, 'fsdp'), may hold values from -0.109375 to 0.109375
- vectors: float32 [2, 9216], P(None, 'fsdp'), may hold values from -0.9 to 1.6, as said below
- cotangent: bfloat16 [16384, 768], P(('rep', 'fsdp')), may hold values from -6 to 6
Outputs:
- layer_out: bfloat16 [16384, 768], P(('rep', 'fsdp'))
- input_grad: float32 [16384, 768], P(('rep', 'fsdp'))
- qkv_grad: float32 [2, 768, 2304], P(None, 'fsdp')
- out_grad: float32 [2, 768, 768], P(None, 'fsdp')
- up_grad: float32 [2, 768, 3072], P(None, 'fsdp')
- down_grad: float32 [2, 3072, 768], P(None, 'fsdp')
- vector_grad: float32 [2, 9216], P(None, 'fsdp')
Inputs may be any that keep to these rules, and one draw needn't show every extreme that they name: `valid`: pair p sits in slot p mod 4 of its group; a pair of a slot of k * 64 rows has more than (k - 1) * 64 real rows; pair 0 fills its slot. `vectors`: norm gains lie between 0.4 and 1.6, the biases between -0.9 and 0.9.
All inputs are finite; a program needn't handle non-finite values.
Results may differ from a plain program's by a relative error of at most 0.029.
The roundings to bfloat16 on the way count: a program that leaves them out, or rounds other values in their place, can miss the bound.
Values may be sent and summed in bfloat16 or wider, within the bound.
No kernel may reach another device: no remote copies, remote signals or barrier semaphores. Data moves between devices by JAX's collectives and lax.ppermute only.
A program may use at most 192 MiB of HBM per device.

v0:
```python
import jax
import jax.numpy as jnp
from jax import lax
from jax.sharding import PartitionSpec as P

HEADS = 12
HD = 64
LAYERS = 2
LEN_UNIT = 64


NORM_EPSILON = 1e-05
NEG_LARGE = -1e30
SCORE_SCALE = 0.125


def slot_layout(valid_groups):
    row_index = jnp.arange(8 * LEN_UNIT, dtype=jnp.int32)
    slot_index = (
        (row_index >= 3 * LEN_UNIT).astype(jnp.int32)
        + (row_index >= 5 * LEN_UNIT).astype(jnp.int32)
        + (row_index >= 7 * LEN_UNIT).astype(jnp.int32)
    )
    slot_start = jnp.where(
        slot_index == 0,
        0,
        jnp.where(
            slot_index == 1, 3 * LEN_UNIT, jnp.where(slot_index == 2, 5 * LEN_UNIT, 7 * LEN_UNIT)
        ),
    ).astype(jnp.int32)
    offset = row_index - slot_start
    slot_pick = (slot_index[:, None] == jnp.arange(4, dtype=jnp.int32)[None, :]).astype(jnp.int32)
    limits = jnp.sum(valid_groups[:, None, :] * slot_pick[None], -1)
    row_live = offset[None, :] < limits
    same_slot = slot_index[:, None] == slot_index[None, :]
    permitted = same_slot[None] & row_live[:, None, :]
    return (row_live, permitted)


def normed(values_in, gain_ln, bias_ln):
    row_mean = jnp.mean(values_in, -1, keepdims=True)
    centred = values_in - row_mean
    row_var = jnp.mean(centred * centred, -1, keepdims=True)
    return centred * lax.rsqrt(row_var + NORM_EPSILON) * gain_ln + bias_ln


def exact_gelu(values_in):
    return jax.nn.gelu(values_in, approximate=False)


def outer_sum(left, right):
    return lax.dot_general(
        left, right, (((0,), (0,)), ((), ())), preferred_element_type=jnp.float32
    )


def times_transposed(left, right):
    return lax.dot_general(
        left, right, (((1,), (1,)), ((), ())), preferred_element_type=jnp.float32
    )


def split_heads(qkv_low, permitted):
    group_count = permitted.shape[0]
    group_rows = permitted.shape[1]
    split_qkv = qkv_low.reshape(group_count, group_rows, 3, HEADS, HD)
    return (split_qkv[:, :, 0], split_qkv[:, :, 1], split_qkv[:, :, 2])


def raw_scores(queries, key_rows, permitted):
    scores = (
        jnp.einsum("gqhd,gkhd->ghqk", queries, key_rows, preferred_element_type=jnp.float32)
        * SCORE_SCALE
    )
    return jnp.where(permitted[:, None], scores, NEG_LARGE)


def attend(qkv_low, permitted):
    queries, key_rows, value_rows = split_heads(qkv_low, permitted)
    scores = raw_scores(queries, key_rows, permitted)
    row_top = jnp.max(scores, -1, keepdims=True)
    row_total = jnp.sum(jnp.exp(scores - row_top), -1, keepdims=True)
    log_total = row_top + jnp.log(row_total)
    probs = jnp.exp(scores - log_total).astype(jnp.bfloat16)
    context = jnp.einsum("ghqk,gkhd->gqhd", probs, value_rows, preferred_element_type=jnp.float32)
    return (context.reshape(qkv_low.shape[0], HEADS * HD).astype(jnp.bfloat16), log_total)


def attend_back(qkv_low, log_total, d_context, permitted):
    queries, key_rows, value_rows = split_heads(qkv_low, permitted)
    scores = raw_scores(queries, key_rows, permitted)
    probs = jnp.exp(scores - log_total)
    probs_low = probs.astype(jnp.bfloat16)
    d_heads = d_context.reshape(queries.shape)
    d_value = jnp.einsum("ghqk,gqhd->gkhd", probs_low, d_heads, preferred_element_type=jnp.float32)
    d_probs = jnp.einsum("gqhd,gkhd->ghqk", d_heads, value_rows, preferred_element_type=jnp.float32)
    d_scores = probs * (d_probs - jnp.sum(probs * d_probs, -1, keepdims=True))
    d_low = d_scores.astype(jnp.bfloat16)
    d_query = (
        jnp.einsum("ghqk,gkhd->gqhd", d_low, key_rows, preferred_element_type=jnp.float32)
        * SCORE_SCALE
    )
    d_key = (
        jnp.einsum("ghqk,gqhd->gkhd", d_low, queries, preferred_element_type=jnp.float32)
        * SCORE_SCALE
    )
    joined = jnp.stack([d_query, d_key, d_value], 2)
    return joined.reshape(qkv_low.shape[0], 3 * HEADS * HD)


def unpack(vector_row, model_width):
    pieces = [
        vector_row[segment * model_width : (segment + 1) * model_width] for segment in range(8)
    ]
    return (pieces, vector_row[8 * model_width :])


def forward_layer(hidden, weights, vector_row, permitted):
    w_qkv, w_out, w_up, w_down = weights
    model_width = hidden.shape[1]
    pieces, bias_u = unpack(vector_row, model_width)
    bias_q, bias_v, bias_o, gain_a, shift_a, bias_d, gain_b, shift_b = pieces
    h_low = hidden.astype(jnp.bfloat16)
    qkv_full = jnp.dot(h_low, w_qkv, preferred_element_type=jnp.float32) + jnp.concatenate(
        [bias_q, jnp.zeros_like(bias_q), bias_v]
    )
    qkv_low = qkv_full.astype(jnp.bfloat16)
    context, log_total = attend(qkv_low, permitted)
    mixed_a = jnp.dot(context, w_out, preferred_element_type=jnp.float32) + bias_o
    first_sum = hidden + mixed_a
    first = normed(first_sum, gain_a, shift_a)
    first_low = first.astype(jnp.bfloat16)
    inner = jnp.dot(first_low, w_up, preferred_element_type=jnp.float32) + bias_u
    active = exact_gelu(inner).astype(jnp.bfloat16)
    mixed_b = jnp.dot(active, w_down, preferred_element_type=jnp.float32) + bias_d
    second_sum = first + mixed_b
    second = normed(second_sum, gain_b, shift_b)
    saved = (h_low, qkv_low, log_total, context, first_sum, first_low, inner, active, second_sum)
    return (second, saved)


def backward_layer(d_out, saved, weights, vector_row, permitted):
    w_qkv, w_out, w_up, w_down = weights
    h_low, qkv_low, log_total, context, first_sum, first_low, inner, active, second_sum = saved
    model_width = h_low.shape[1]
    pieces, bias_u = unpack(vector_row, model_width)
    bias_q, bias_v, bias_o, gain_a, shift_a, bias_d, gain_b, shift_b = pieces
    unused_b, norm_b_back = jax.vjp(normed, second_sum, gain_b, shift_b)
    d_second_sum, d_gain_b, d_shift_b = norm_b_back(d_out)
    d_mixed_b = d_second_sum.astype(jnp.bfloat16)
    d_bias_d = jnp.sum(d_mixed_b, 0, dtype=jnp.float32)
    grad_down = outer_sum(active, d_mixed_b)
    d_active = times_transposed(d_mixed_b, w_down)
    unused_g, gelu_back = jax.vjp(exact_gelu, inner)
    d_inner = gelu_back(d_active)[0].astype(jnp.bfloat16)
    d_bias_u = jnp.sum(d_inner, 0, dtype=jnp.float32)
    grad_up = outer_sum(first_low, d_inner)
    d_first = d_second_sum + times_transposed(d_inner, w_up)
    unused_a, norm_a_back = jax.vjp(normed, first_sum, gain_a, shift_a)
    d_first_sum, d_gain_a, d_shift_a = norm_a_back(d_first)
    d_mixed_a = d_first_sum.astype(jnp.bfloat16)
    d_bias_o = jnp.sum(d_mixed_a, 0, dtype=jnp.float32)
    grad_out = outer_sum(context, d_mixed_a)
    d_context = times_transposed(d_mixed_a, w_out).astype(jnp.bfloat16)
    d_qkv = attend_back(qkv_low, log_total, d_context, permitted).astype(jnp.bfloat16)
    d_bias_qkv = jnp.sum(d_qkv, 0, dtype=jnp.float32)
    grad_qkv = outer_sum(h_low, d_qkv)
    d_hidden = d_first_sum + times_transposed(d_qkv, w_qkv)
    d_vector = jnp.concatenate(
        [
            d_bias_qkv[:model_width],
            d_bias_qkv[2 * model_width :],
            d_bias_o,
            d_gain_a,
            d_shift_a,
            d_bias_d,
            d_gain_b,
            d_shift_b,
            d_bias_u,
        ]
    )
    return (d_hidden, (grad_qkv, grad_out, grad_up, grad_down, d_vector))


def shards(tokens, valid, qkv_weight, out_weight, up_weight, down_weight, vectors, cotangent):
    group_count = valid.shape[0] // 4
    row_live, permitted = slot_layout(valid.reshape(group_count, 4))
    row_mask = row_live.reshape(-1, 1).astype(jnp.float32)
    vector_all = lax.all_gather(vectors, "fsdp", axis=1, tiled=True)
    hidden = tokens.astype(jnp.float32)
    kept_weights = []
    kept_saved = []
    for level_idx in range(LAYERS):
        weights = (
            lax.all_gather(qkv_weight[level_idx].astype(jnp.bfloat16), "fsdp", axis=0, tiled=True),
            lax.all_gather(out_weight[level_idx].astype(jnp.bfloat16), "fsdp", axis=0, tiled=True),
            lax.all_gather(up_weight[level_idx].astype(jnp.bfloat16), "fsdp", axis=0, tiled=True),
            lax.all_gather(down_weight[level_idx].astype(jnp.bfloat16), "fsdp", axis=0, tiled=True),
        )
        hidden, saved = forward_layer(hidden, weights, vector_all[level_idx], permitted)
        kept_weights.append(weights)
        kept_saved.append(saved)
    layer_out = (hidden * row_mask).astype(jnp.bfloat16)
    d_hidden = cotangent.astype(jnp.float32) * row_mask
    results = [None] * LAYERS
    for level_idx in reversed(range(LAYERS)):
        weights = (
            lax.all_gather(qkv_weight[level_idx].astype(jnp.bfloat16), "fsdp", axis=0, tiled=True),
            lax.all_gather(out_weight[level_idx].astype(jnp.bfloat16), "fsdp", axis=0, tiled=True),
            lax.all_gather(up_weight[level_idx].astype(jnp.bfloat16), "fsdp", axis=0, tiled=True),
            lax.all_gather(down_weight[level_idx].astype(jnp.bfloat16), "fsdp", axis=0, tiled=True),
        )
        d_hidden, terms = backward_layer(
            d_hidden, kept_saved[level_idx], weights, vector_all[level_idx], permitted
        )
        term_qkv, term_out, term_up, term_down, term_vector = terms
        owned = (
            lax.psum_scatter(
                term_qkv.astype(jnp.bfloat16), "fsdp", scatter_dimension=0, tiled=True
            ).astype(jnp.float32),
            lax.psum_scatter(
                term_out.astype(jnp.bfloat16), "fsdp", scatter_dimension=0, tiled=True
            ).astype(jnp.float32),
            lax.psum_scatter(
                term_up.astype(jnp.bfloat16), "fsdp", scatter_dimension=0, tiled=True
            ).astype(jnp.float32),
            lax.psum_scatter(
                term_down.astype(jnp.bfloat16), "fsdp", scatter_dimension=0, tiled=True
            ).astype(jnp.float32),
            lax.psum_scatter(
                term_vector.astype(jnp.bfloat16), "fsdp", scatter_dimension=0, tiled=True
            ).astype(jnp.float32),
        )
        shares = (
            lax.psum(owned[0].astype(jnp.bfloat16), "rep").astype(jnp.float32),
            lax.psum(owned[1].astype(jnp.bfloat16), "rep").astype(jnp.float32),
            lax.psum(owned[2].astype(jnp.bfloat16), "rep").astype(jnp.float32),
            lax.psum(owned[3].astype(jnp.bfloat16), "rep").astype(jnp.float32),
            lax.psum(owned[4].astype(jnp.bfloat16), "rep").astype(jnp.float32),
        )
        results[level_idx] = shares
    qkv_grad = jnp.stack([entry[0] for entry in results])
    out_grad = jnp.stack([entry[1] for entry in results])
    up_grad = jnp.stack([entry[2] for entry in results])
    down_grad = jnp.stack([entry[3] for entry in results])
    vector_grad = jnp.stack([entry[4] for entry in results])
    return (layer_out, d_hidden, qkv_grad, out_grad, up_grad, down_grad, vector_grad)


def solution(mesh):
    in_specs = (
        P(("rep", "fsdp"), None),
        P(("rep", "fsdp")),
        P(None, "fsdp", None),
        P(None, "fsdp", None),
        P(None, "fsdp", None),
        P(None, "fsdp", None),
        P(None, "fsdp"),
        P(("rep", "fsdp"), None),
    )
    out_specs = (
        P(("rep", "fsdp"), None),
        P(("rep", "fsdp"), None),
        P(None, "fsdp", None),
        P(None, "fsdp", None),
        P(None, "fsdp", None),
        P(None, "fsdp", None),
        P(None, "fsdp"),
    )
    return jax.shard_map(shards, mesh=mesh, in_specs=in_specs, out_specs=out_specs, check_vma=False)
```

profile of v0, /device:TPU:0, one launch (start us, length us, event | category | flops | bytes accessed | tf_op | source)
XLA Modules:
  0.0 1876.1 jit_solution(6135757692193599547)
XLA Ops:
  15.9 43.3 %all-gather.8 = f32[16,576,2]{1,2,0:T(2,128)S(1)} all-gather(f32[1,576,2]{1,2,0:T(2,128)S(1)} %bitcast.257), channel_id=1, replica_groups=mesh['rep'=2,'fsdp'=16] {'fsdp'}, dimensions={0}, use_global_device_ids=true | all-gather | bytes 78336 | tf_op jit(solution)/shard_map/all_gather | solution.py:189
  59.9 25.6 %all-gather.18.cloned.1.call-done = bf16[1,768,2304]{2,1,0:T(8,128)(2,1)} async-done(((bf16[1,48,2304]{2,1,0:T(8,128)(2,1)}), bf16[1,768,2304]{2,1,0:T(8,128)(2,1)}) %all-gather.18.cloned.1.call-update) | async-done | bytes 3538960 | tf_op jit(solution)/shard_map/all_gather | solution.py:195
  85.5 5.4 fusion.32
  91.0 3.0 copy.67
  94.0 2.1 fusion
  96.1 2.6 exponential_reduce_fusion.1
  98.7 2.0 copy-done
  101.3 3.9 convolution_convert_fusion.11
  105.2 38.4 %all-gather.20.cloned.1.call-done = bf16[1,768,768]{2,1,0:T(8,128)(2,1)} async-done(((bf16[1,48,768]{2,1,0:T(8,128)(2,1)}), bf16[1,768,768]{2,1,0:T(8,128)(2,1)}) %all-gather.20.cloned.1.call-update) | async-done | bytes 1179664 | tf_op jit(solution)/shard_map/all_gather | solution.py:196
  143.6 2.4 fusion.114
  146.4 80.0 %all-gather.22.cloned.1.call-done = bf16[1,768,3072]{2,1,0:T(8,128)(2,1)} async-done(((bf16[1,48,3072]{2,1,0:T(8,128)(2,1)}), bf16[1,768,3072]{2,1,0:T(8,128)(2,1)}) %all-gather.22.cloned.1.call-update) | async-done | bytes 4718608 | tf_op jit(solution)/shard_map/all_gather | solution.py:197
  226.4 20.0 %multiply_convert_fusion.3 = (bf16[512,3072]{1,0:T(8,128)(2,1)}, f32[512,3072]{1,0:T(8,128)}, f32[512,3072]{1,0:T(8,128)}) fusion(f32[3072]{0:T(1024)S(1)} %bitcast.253, bf16[1,768,3072]{2,1,0:T(8,128)(2,1)} %all-gather.22.cloned.1.call-done, f32[512,768]{1,0:T(8,128)S(1)} %get-tuple-element.107, f32[768]{0:T(1024)S(1)} %get-tuple-element.44, ...), kind=kOutput, calls=%fused_computation.33 | convolution fusion | flops 2521694208 | bytes 22042624 | tf_op jit(solution)/shard_map/dot_general | solution.py:133
  246.4 62.3 %all-gather.24.cloned.1.call-done = bf16[1,3072,768]{2,1,0:T(8,128)(2,1)} async-done(((bf16[1,192,768]{2,1,0:T(8,128)(2,1)}), bf16[1,3072,768]{2,1,0:T(8,128)(2,1)}) %all-gather.24.cloned.1.call-update) | async-done | bytes 4718608 | tf_op jit(solution)/shard_map/all_gather | solution.py:198
  308.7 6.0 fusion.115
  315.1 66.2 %all-gather.26.cloned.1.call-done = bf16[1,768,2304]{2,1,0:T(8,128)(2,1)} async-done(((bf16[1,48,2304]{2,1,0:T(8,128)(2,1)}), bf16[1,768,2304]{2,1,0:T(8,128)(2,1)}) %all-gather.26.cloned.1.call-update) | async-done | bytes 3538960 | tf_op jit(solution)/shard_map/all_gather | solution.py:195
  381.2 5.5 fusion.33
  386.7 2.8 copy.69
  389.6 2.1 fusion.1
  391.7 2.6 exponential_reduce_fusion
  394.3 1.9 copy-done.1
  396.2 3.4 convolution_convert_fusion.10
  399.6 39.0 %all-gather.28.cloned.1.call-done = bf16[1,768,768]{2,1,0:T(8,128)(2,1)} async-done(((bf16[1,48,768]{2,1,0:T(8,128)(2,1)}), bf16[1,768,768]{2,1,0:T(8,128)(2,1)}) %all-gather.28.cloned.1.call-update) | async-done | bytes 1179664 | tf_op jit(solution)/shard_map/all_gather | solution.py:196
  438.6 2.8 fusion.116
  442.9 78.4 %all-gather.30.cloned.1.call-done = bf16[1,768,3072]{2,1,0:T(8,128)(2,1)} async-done(((bf16[1,48,3072]{2,1,0:T(8,128)(2,1)}), bf16[1,768,3072]{2,1,0:T(8,128)(2,1)}) %all-gather.30.cloned.1.call-update) | async-done | bytes 4718608 | tf_op jit(solution)/shard_map/all_gather | solution.py:197
  521.4 20.8 %multiply_convert_fusion.2 = (bf16[512,3072]{1,0:T(8,128)(2,1)}, f32[512,3072]{1,0:T(8,128)}, f32[512,3072]{1,0:T(8,128)}) fusion(f32[3072]{0:T(1024)S(1)} %bitcast.255, bf16[1,768,3072]{2,1,0:T(8,128)(2,1)} %all-gather.30.cloned.1.call-done, f32[512,768]{1,0:T(8,128)} %copy-done.9, f32[768]{0:T(1024)S(1)} %get-tuple-element.36, ...), kind=kOutput, calls=%fused_computation.20 | convolution fusion | flops 2521694208 | bytes 22042624 | tf_op jit(solution)/shard_map/dot_general | solution.py:133
  542.2 61.7 %all-gather.32.cloned.1.call-done = bf16[1,3072,768]{2,1,0:T(8,128)(2,1)} async-done(((bf16[1,192,768]{2,1,0:T(8,128)(2,1)}), bf16[1,3072,768]{2,1,0:T(8,128)(2,1)}) %all-gather.32.cloned.1.call-update) | async-done | bytes 4718608 | tf_op jit(solution)/shard_map/all_gather | solution.py:198
  603.8 6.5 fusion.117
  612.1 1.7 fusion.103
  614.7 10.3 fusion.118
  625.0 5.7 multiply_reduce_fusion.3
  637.3 7.3 convolution_bitcast_fusion.1
  644.7 9.6 multiply_reduce_fusion.1
  654.3 7.4 multiply_convert_fusion.1
  661.7 2.0 multiply_bitcast_fusion.2
  666.7 4.1 convolution_convert_fusion.4
  670.8 6.0 multiply_reduce_fusion.4
  678.3 9.6 fusion.119
  687.9 7.2 multiply_reduce_fusion.5
  698.7 1.7 convolution_convert_fusion.8
  701.9 11.3 multiply_reduce_fusion
  714.7 7.1 multiply_convert_fusion
  721.7 2.0 multiply_bitcast_fusion
  724.9 3.4 convolution_bitcast_fusion
  730.7 2.0 fusion.34
  732.7 4.0 copy.90
  738.1 1.8 convolution_convert_fusion.6
  740.0 1.8 convolution_convert_fusion.7
  741.9 6.5 convolution_convert_fusion.2
  749.9 6.4 convolution_convert_fusion.3
  757.5 6.7 convolution_convert_fusion
  765.3 6.7 convolution_convert_fusion.1
  772.3 38.2 %reduce-scatter.27.cloned.1.call-done = bf16[48,2304]{1,0:T(8,128)(2,1)} async-done(((bf16[768,2304]{1,0:T(8,128)(2,1)}), bf16[48,2304]{1,0:T(8,128)(2,1)}) %reduce-scatter.27.cloned.1.call-update) | async-done | bytes 221200
  810.4 2.0 copy.93
  812.4 136.5 %reduce-scatter.25.cloned.1.call-done = bf16[48,2304]{1,0:T(8,128)(2,1)} async-done(((bf16[768,2304]{1,0:T(8,128)(2,1)}), bf16[48,2304]{1,0:T(8,128)(2,1)}) %reduce-scatter.25.cloned.1.call-update) | async-done | bytes 221200
  948.9 2.0 copy.91
  950.9 126.3 %reduce-scatter.15.cloned.1.call-done = bf16[48,768]{1,0:T(8,128)(2,1)} async-done(((bf16[768,768]{1,0:T(8,128)(2,1)}), bf16[48,768]{1,0:T(8,128)(2,1)}) %reduce-scatter.15.cloned.1.call-update) | async-done | bytes 73744 | tf_op jit(solution)/shard_map/reduce_scatter | solution.py:221
  1077.2 127.8 %reduce-scatter.13.cloned.1.call-done = bf16[48,768]{1,0:T(8,128)(2,1)} async-done(((bf16[768,768]{1,0:T(8,128)(2,1)}), bf16[48,768]{1,0:T(8,128)(2,1)}) %reduce-scatter.13.cloned.1.call-update) | async-done | bytes 73744 | tf_op jit(solution)/shard_map/reduce_scatter | solution.py:221
  1204.9 141.1 %reduce-scatter.19.cloned.1.call-done = bf16[48,3072]{1,0:T(8,128)(2,1)} async-done(((bf16[768,3072]{1,0:T(8,128)(2,1)}), bf16[48,3072]{1,0:T(8,128)(2,1)}) %reduce-scatter.19.cloned.1.call-update) | async-done | bytes 294928 | tf_op jit(solution)/shard_map/reduce_scatter | solution.py:224
  1346.0 142.7 %reduce-scatter.17.cloned.1.call-done = bf16[48,3072]{1,0:T(8,128)(2,1)} async-done(((bf16[768,3072]{1,0:T(8,128)(2,1)}), bf16[48,3072]{1,0:T(8,128)(2,1)}) %reduce-scatter.17.cloned.1.call-update) | async-done | bytes 294928 | tf_op jit(solution)/shard_map/reduce_scatter | solution.py:224
  1488.7 141.4 %reduce-scatter.23.cloned.1.call-done = bf16[192,768]{1,0:T(8,128)(2,1)} async-done(((bf16[3072,768]{1,0:T(8,128)(2,1)}), bf16[192,768]{1,0:T(8,128)(2,1)}) %reduce-scatter.23.cloned.1.call-update) | async-done | bytes 294928 | tf_op jit(solution)/shard_map/reduce_scatter | solution.py:227
  1630.1 142.5 %reduce-scatter.21.cloned.1.call-done = bf16[192,768]{1,0:T(8,128)(2,1)} async-done(((bf16[3072,768]{1,0:T(8,128)(2,1)}), bf16[192,768]{1,0:T(8,128)(2,1)}) %reduce-scatter.21.cloned.1.call-update) | async-done | bytes 294928 | tf_op jit(solution)/shard_map/reduce_scatter | solution.py:227
  1777.6 74.8 %all-reduce.2 = (bf16[9216]{0:T(1024)(128)(2,1)S(1)}, bf16[9216]{0:T(1024)(128)(2,1)S(1)}) all-reduce(bf16[9216]{0:T(1024)(128)(2,1)S(1)} %constant_dynamic-update-slice_fusion.1, bf16[9216]{0:T(1024)(128)(2,1)S(1)} %constant_dynamic-update-slice_fusion), channel_id=19, replica_groups=mesh['rep'=2,'fsdp'=16] {'fsdp'}, use_global_device_ids=true, to_apply=%region_57.58.clone | all-reduce | flops 18432 | bytes 73728
  1852.6 2.5 all-reduce.3
  1855.7 5.9 add_add_fusion.8
  (307 shorter events, 53.3 us)
Async XLA Ops:
  7.2 78.4 %all-gather.18.cloned.1.call-start = ((), (), s32[]{:S(2)}) async-start(), calls=%async_computation.14 | async-start | bytes 3760128 | tf_op jit(solution)/shard_map/all_gather | solution.py:195
  9.4 134.2 %all-gather.20.cloned.1.call-start = ((), (), s32[]{:S(2)}) async-start(), calls=%async_computation.15 | async-start | bytes 1253376 | tf_op jit(solution)/shard_map/all_gather | solution.py:196
  11.1 215.2 %all-gather.22.cloned.1.call-start = ((), (), s32[]{:S(2)}) async-start(), calls=%async_computation.16 | async-start | bytes 5013504 | tf_op jit(solution)/shard_map/all_gather | solution.py:197
  11.3 48.2 %copy-start.70 = (s32[4]{0:T(128)S(1)}, s32[4]{0:T(128)}, u32[]{:S(2)}) copy-start(s32[4]{0:T(128)} %param.9) | copy-start | bytes 52
  11.3 74.3 %copy-start.74 = (bf16[512,768]{1,0:T(8,128)(2,1)S(1)}, bf16[512,768]{1,0:T(8,128)(2,1)}, u32[]{:S(2)}) copy-start(bf16[512,768]{1,0:T(8,128)(2,1)} %param.8) | copy-start | bytes 2359300
  12.2 296.5 %all-gather.24.cloned.1.call-start = ((), (), s32[]{:S(2)}) async-start(), calls=%async_computation.17 | async-start | bytes 5013504 | tf_op jit(solution)/shard_map/all_gather | solution.py:198
  13.2 368.1 %all-gather.26.cloned.1.call-start = ((), (), s32[]{:S(2)}) async-start(), calls=%async_computation.18 | async-start | bytes 3760128 | tf_op jit(solution)/shard_map/all_gather | solution.py:195
  13.8 424.8 %all-gather.28.cloned.1.call-start = ((), (), s32[]{:S(2)}) async-start(), calls=%async_computation.19 | async-start | bytes 1253376 | tf_op jit(solution)/shard_map/all_gather | solution.py:196
  14.3 507.0 %all-gather.30.cloned.1.call-start = ((), (), s32[]{:S(2)}) async-start(), calls=%async_computation.20 | async-start | bytes 5013504 | tf_op jit(solution)/shard_map/all_gather | solution.py:197
  15.1 588.7 %all-gather.32.cloned.1.call-start = ((), (), s32[]{:S(2)}) async-start(), calls=%async_computation.21 | async-start | bytes 5013504 | tf_op jit(solution)/shard_map/all_gather | solution.py:198
  15.8 794.6 %reduce-scatter.27.cloned.1.call-start = ((), (), s32[]{:S(2)}) async-start(), calls=%async_computation.23 | async-start | bytes 3760128
  59.4 249.3 %copy-start.60 = (f32[768]{0:T(1024)}, f32[768]{0:T(1024)S(1)}, u32[]{:S(2)}) copy-start(f32[768]{0:T(1024)S(1)} %get-tuple-element.44) | copy-start | bytes 9220
  59.4 544.4 %copy-start.62 = (f32[768]{0:T(1024)}, f32[768]{0:T(1024)S(1)}, u32[]{:S(2)}) copy-start(f32[768]{0:T(1024)S(1)} %get-tuple-element.36) | copy-start | bytes 9220
  59.5 571.2 %copy-start.43 = (f32[768]{0:T(1024)}, f32[768]{0:T(1024)S(1)}, u32[]{:S(2)}) copy-start(f32[768]{0:T(1024)S(1)} %get-tuple-element.37) | copy-start | bytes 9220
  59.5 635.7 %copy-start.41 = (f32[768]{0:T(1024)}, f32[768]{0:T(1024)S(1)}, u32[]{:S(2)}) copy-start(f32[768]{0:T(1024)S(1)} %get-tuple-element.45) | copy-start | bytes 9220
  146.1 162.7 %copy-start.6 = (f32[512,768]{1,0:T(8,128)}, f32[512,768]{1,0:T(8,128)S(1)}, u32[]{:S(2)}) copy-start(f32[512,768]{1,0:T(8,128)S(1)} %get-tuple-element.107) | copy-start | bytes 4718596
  146.4 100.1 %copy-start.39 = (f32[512]{0:T(512)}, f32[512]{0:T(512)S(1)}, u32[]{:S(2)}) copy-start(f32[512]{0:T(512)S(1)} %multiply_reduce_fusion.13) | copy-start | bytes 6148
  146.4 548.8 %copy-start.47 = (f32[512]{0:T(512)}, f32[512]{0:T(512)S(1)}, u32[]{:S(2)}) copy-start(f32[512]{0:T(512)S(1)} %fusion.76) | copy-start | bytes 6148
  314.7 66.5 %copy-start.12 = (f32[512,768]{1,0:T(8,128)}, f32[512,768]{1,0:T(8,128)S(1)}, u32[]{:S(2)}) copy-start(f32[512,768]{1,0:T(8,128)S(1)} %get-tuple-element.110) | copy-start | bytes 4718596
  399.6 43.3 %copy-start.77 = (bf16[12,64,512]{2,1,0:T(8,128)(2,1)}, bf16[12,64,512]{2,1,0:T(8,128)(2,1)S(1)}, u32[]{:S(2)}) copy-start(bf16[12,64,512]{2,1,0:T(8,128)(2,1)S(1)} %convolution_convert_fusion.10) | copy-start | bytes 2359300
  441.5 189.2 %copy-start.37 = (f32[512]{0:T(512)}, f32[512]{0:T(512)S(1)}, u32[]{:S(2)}) copy-start(f32[512]{0:T(512)S(1)} %broadcast_multiply_fusion.1) | copy-start | bytes 6148
  442.9 187.8 %copy-start.49 = (f32[512]{0:T(512)}, f32[512]{0:T(512)S(1)}, u32[]{:S(2)}) copy-start(f32[512]{0:T(512)S(1)} %fusion.78) | copy-start | bytes 6148
  603.8 6.9 copy-start.16
  613.8 11.2 slice-start.6
  614.6 10.4 copy-start.21
  614.7 10.3 copy-start.10
  614.7 10.3 slice-start.7
  637.3 17.0 slice-start.3
  637.3 17.0 slice-start.4
  644.7 9.7 slice-start.5
  677.5 271.4 %reduce-scatter.25.cloned.1.call-start = ((), (), s32[]{:S(2)}) async-start(), calls=%async_computation.22 | async-start | bytes 3760128
  678.3 9.6 copy-start.23
  678.3 9.6 copy-start.7
  687.9 7.2 copy-start.80
  687.9 7.2 copy-start.40
  701.8 11.3 slice-start
  701.9 11.3 slice-start.1
  701.9 12.8 slice-start.2
  736.8 340.4 %reduce-scatter.15.cloned.1.call-start = ((), (), s32[]{:S(2)}) async-start(), calls=%async_computation.9 | async-start | bytes 1253376 | tf_op jit(solution)/shard_map/reduce_scatter | solution.py:221
  739.9 465.0 %reduce-scatter.13.cloned.1.call-start = ((), (), s32[]{:S(2)}) async-start(), calls=%async_computation.8 | async-start | bytes 1253376 | tf_op jit(solution)/shard_map/reduce_scatter | solution.py:221
  741.8 604.2 %reduce-scatter.19.cloned.1.call-start = ((), (), s32[]{:S(2)}) async-start(), calls=%async_computation.11 | async-start | bytes 5013504 | tf_op jit(solution)/shard_map/reduce_scatter | solution.py:224
  748.5 740.2 %reduce-scatter.17.cloned.1.call-start = ((), (), s32[]{:S(2)}) async-start(), calls=%async_computation.10 | async-start | bytes 5013504 | tf_op jit(solution)/shard_map/reduce_scatter | solution.py:224
  756.4 873.7 %reduce-scatter.23.cloned.1.call-start = ((), (), s32[]{:S(2)}) async-start(), calls=%async_computation.13 | async-start | bytes 5013504 | tf_op jit(solution)/shard_map/reduce_scatter | solution.py:227
  764.2 1008.4 %reduce-scatter.21.cloned.1.call-start = ((), (), s32[]{:S(2)}) async-start(), calls=%async_computation.12 | async-start | bytes 5013504 | tf_op jit(solution)/shard_map/reduce_scatter | solution.py:227
  772.0 1000.6 %copy-start.79 = (u32[32]{0:T(128)S(1)}, u32[32]{0:T(128)}, u32[]{:S(2)}) copy-start(u32[32]{0:T(128)} %constant.121) | copy-start | bytes 388
  772.0 1002.0 %copy-start.36 = (bf16[3,12,64]{2,1,0:T(8,128)(2,1)S(1)}, bf16[3,12,64]{2,1,0:T(8,128)(2,1)}, u32[]{:S(2)}) copy-start(bf16[3,12,64]{2,1,0:T(8,128)(2,1)} %get-tuple-element.65) | copy-start | bytes 13828
  772.0 1003.0 %copy-start.54 = (bf16[768]{0:T(1024)(128)(2,1)S(1)}, bf16[768]{0:T(1024)(128)(2,1)}, u32[]{:S(2)}) copy-start(bf16[768]{0:T(1024)(128)(2,1)} %get-tuple-element.69) | copy-start | bytes 4612
  772.0 1003.2 %copy-start.56 = (bf16[768]{0:T(1024)(128)(2,1)S(1)}, bf16[768]{0:T(1024)(128)(2,1)}, u32[]{:S(2)}) copy-start(bf16[768]{0:T(1024)(128)(2,1)} %get-tuple-element.63) | copy-start | bytes 4612
  772.0 1003.4 %copy-start.65 = (bf16[768]{0:T(1024)(128)(2,1)S(1)}, bf16[768]{0:T(1024)(128)(2,1)}, u32[]{:S(2)}) copy-start(bf16[768]{0:T(1024)(128)(2,1)} %get-tuple-element.25) | copy-start | bytes 4612
  772.1 1003.6 %copy-start.69 = (bf16[768]{0:T(1024)(128)(2,1)S(1)}, bf16[768]{0:T(1024)(128)(2,1)}, u32[]{:S(2)}) copy-start(bf16[768]{0:T(1024)(128)(2,1)} %get-tuple-element.23) | copy-start | bytes 4612
  772.1 1003.8 %copy-start.64 = (bf16[768]{0:T(1024)(128)(2,1)S(1)}, bf16[768]{0:T(1024)(128)(2,1)}, u32[]{:S(2)}) copy-start(bf16[768]{0:T(1024)(128)(2,1)} %get-tuple-element.31) | copy-start | bytes 4612
  772.1 1004.0 %copy-start.68 = (bf16[768]{0:T(1024)(128)(2,1)S(1)}, bf16[768]{0:T(1024)(128)(2,1)}, u32[]{:S(2)}) copy-start(bf16[768]{0:T(1024)(128)(2,1)} %get-tuple-element.30) | copy-start | bytes 4612
  772.1 1004.2 %copy-start.53 = (bf16[768]{0:T(1024)(128)(2,1)S(1)}, bf16[768]{0:T(1024)(128)(2,1)}, u32[]{:S(2)}) copy-start(bf16[768]{0:T(1024)(128)(2,1)} %get-tuple-element.67) | copy-start | bytes 4612
  772.1 1004.4 %copy-start.55 = (bf16[768]{0:T(1024)(128)(2,1)S(1)}, bf16[768]{0:T(1024)(128)(2,1)}, u32[]{:S(2)}) copy-start(bf16[768]{0:T(1024)(128)(2,1)} %get-tuple-element.61) | copy-start | bytes 4612
  772.1 1004.6 %copy-start.52 = (bf16[768]{0:T(1024)(128)(2,1)S(1)}, bf16[768]{0:T(1024)(128)(2,1)}, u32[]{:S(2)}) copy-start(bf16[768]{0:T(1024)(128)(2,1)} %get-tuple-element.27) | copy-start | bytes 4612
  772.1 1004.8 %copy-start.67 = (bf16[768]{0:T(1024)(128)(2,1)S(1)}, bf16[768]{0:T(1024)(128)(2,1)}, u32[]{:S(2)}) copy-start(bf16[768]{0:T(1024)(128)(2,1)} %get-tuple-element.21) | copy-start | bytes 4612
  772.1 1005.0 %copy-start.51 = (bf16[768]{0:T(1024)(128)(2,1)S(1)}, bf16[768]{0:T(1024)(128)(2,1)}, u32[]{:S(2)}) copy-start(bf16[768]{0:T(1024)(128)(2,1)} %get-tuple-element.32) | copy-start | bytes 4612
  772.1 1005.2 %copy-start.66 = (bf16[768]{0:T(1024)(128)(2,1)S(1)}, bf16[768]{0:T(1024)(128)(2,1)}, u32[]{:S(2)}) copy-start(bf16[768]{0:T(1024)(128)(2,1)} %get-tuple-element.29) | copy-start | bytes 4612
  772.1 1005.4 %copy-start.57 = (bf16[3072]{0:T(1024)(128)(2,1)S(1)}, bf16[3072]{0:T(1024)(128)(2,1)}, u32[]{:S(2)}) copy-start(bf16[3072]{0:T(1024)(128)(2,1)} %get-tuple-element.125) | copy-start | bytes 18436
  772.2 1005.4 %copy-start.58 = (bf16[3072]{0:T(1024)(128)(2,1)S(1)}, bf16[3072]{0:T(1024)(128)(2,1)}, u32[]{:S(2)}) copy-start(bf16[3072]{0:T(1024)(128)(2,1)} %get-tuple-element.127) | copy-start | bytes 18436
  772.2 1083.5 %copy-start.5 = (f32[512,768]{1,0:T(8,128)S(1)}, f32[512,768]{1,0:T(8,128)}, u32[]{:S(2)}) copy-start(f32[512,768]{1,0:T(8,128)} %copy-done.4) | copy-start | bytes 4718596
  772.2 1083.5 %copy-start.46 = (f32[512]{0:T(512)S(1)}, f32[512]{0:T(512)}, u32[]{:S(2)}) copy-start(f32[512]{0:T(512)} %copy-done.45) | copy-start | bytes 6148
  772.2 1089.4 %all-reduce.7.cloned.1.call-start = ((), (), s32[]{:S(2)}) async-start(), calls=%async_computation.24 | async-start | bytes 5013504 | tf_op jit(solution)/shard_map/psum | solution.py:235
  1861.6 6.4 copy-start.30
  (42 other events, 115.2 us)
Sparse Core Ops, SparseCore 0:
  11.4 74.1 all-gather.17
  88.9 54.6 all-gather.19
  147.0 79.3 all-gather.21
  229.6 79.0 all-gather.23
  311.3 69.8 all-gather.25
  383.9 54.6 all-gather.27
  442.0 79.3 all-gather.29
  524.7 79.0 all-gather.31
  677.6 132.7 reduce-scatter.26
  815.4 133.4 reduce-scatter.24
  954.2 122.8 reduce-scatter.14
  1082.3 122.5 reduce-scatter.12
  1210.1 135.8 reduce-scatter.18
  1351.9 136.7 reduce-scatter.16
  1493.7 136.3 reduce-scatter.22
  1636.0 136.6 reduce-scatter.20
  1775.9 21.4 all-reduce.6
where the time goes:
time: 1880 us
  waiting for transfers between devices  1450 us (77%)
  matrix products  203 us (11%)
  blocking collectives  121 us (6%)
  local copies, waits for them, and re-layouts  46 us (2%)
  other arithmetic  38.7 us (2%)
    reduce_scatter x2, waiting for transfers between devices, shards(): lax.psum_scatter(term_down.astype(jnp.bfloat16), 'fsdp', scatter_dimensio...  284 us
    reduce_scatter x2, waiting for transfers between devices, shards(): lax.psum_scatter(term_up.astype(jnp.bfloat16), 'fsdp', scatter_dimension=...  284 us
    reduce_scatter x2, waiting for transfers between devices, shards(): lax.psum_scatter(term_out.astype(jnp.bfloat16), 'fsdp', scatter_dimension...  254 us
    unnamed x19, waiting for transfers between devices  177 us
    all_gather x2, waiting for transfers between devices, shards(): lax.all_gather(up_weight[level_idx].astype(jnp.bfloat16), 'fsdp', axis=0,...  158 us
    all_gather x2, waiting for transfers between devices, shards(): lax.all_gather(down_weight[level_idx].astype(jnp.bfloat16), 'fsdp', axis=...  124 us
    all_gather x2, waiting for transfers between devices, shards(): lax.all_gather(qkv_weight[level_idx].astype(jnp.bfloat16), 'fsdp', axis=0...  91.8 us
    all_gather x2, waiting for transfers between devices, shards(): lax.all_gather(out_weight[level_idx].astype(jnp.bfloat16), 'fsdp', axis=0...  77.4 us
  transfers between devices with their start and end apart: 17, of which 16 were waited for; matrix products, arithmetic and copies ran while one was open for 10% of the time, Pallas kernels for 0%

commit v1 on v0

--- a/solution.py
+++ b/solution.py
@@ -1,6 +1,11 @@
+import functools
+
 import jax
 import jax.numpy as jnp
+import numpy as np
 from jax import lax
+from jax.experimental import pallas as pl
+from jax.experimental.pallas import tpu as pltpu
 from jax.sharding import PartitionSpec as P
 
 HEADS = 12
@@ -48,6 +53,168 @@
     return jax.nn.gelu(values_in, approximate=False)
 
 
+CHUNK = 384
+
+
+class Net:
+    def __init__(self, mesh):
+        self.shards = mesh.shape["fsdp"]
+        self.replicas = mesh.shape["rep"]
+        assert self.replicas % 2 == 0 and self.shards & (self.shards - 1) == 0
+        sizes, left = [], self.shards
+        while left > 1:
+            sizes.append(4 if left % 4 == 0 and (left != 4 or self.shards != 16) else 2)
+            left //= sizes[-1]
+        strides = [int(np.prod(sizes[place + 1 :])) for place in range(len(sizes))]
+        first = tuple(range(len(sizes)))
+        if len(sizes) > 2 and sizes[-1] == sizes[-2]:
+            orders = (first[:-2] + (first[-1], first[-2]), first)
+        elif len(sizes) > 2 and sizes[0] == sizes[1]:
+            orders = (first[::-1], first[:1:-1] + first[:2])
+        else:
+            orders = (first, first)
+        self.sizes = [sizes[digit] for digit in orders[0]]
+        self.steps = [[strides[digit] for digit in order] for order in orders]
+        flips = np.zeros((2, self.shards), np.int32)
+        for core in range(2):
+            for slot in range(self.shards):
+                left = slot
+                for size, step in zip(self.sizes, self.steps[core]):
+                    flips[core, slot] ^= (left % size) * step
+                    left //= size
+        self.flips = flips
+        self.slots = np.argsort(flips, axis=1).astype(np.int32)
+
+    def pairs(self, stage, offset):
+        return [
+            (rep * self.shards + shard, rep * self.shards + (shard ^ (offset * self.steps[rep % 2][stage])))
+            for rep in range(self.replicas)
+            for shard in range(self.shards)
+        ]
+
+    def trade(self, value, stage, offset):
+        return lax.ppermute(value, ("rep", "fsdp"), self.pairs(stage, offset))
+
+    def twin(self, value):
+        return lax.ppermute(value, "rep", [(rep, rep ^ 1) for rep in range(self.replicas)])
+
+    def widen(self, value, stage):
+        received = [self.trade(value, stage, offset) for offset in range(1, self.sizes[stage])]
+        return jnp.concatenate([value, *received], 0)
+
+    def narrow(self, value, stage, low):
+        parts = value.reshape(self.sizes[stage], -1, *value.shape[1:])
+        total = parts[0].astype(jnp.float32)
+        for offset in range(1, self.sizes[stage]):
+            total = total + self.trade(parts[offset], stage, offset).astype(jnp.float32)
+        return total.astype(low)
+
+    def reduce(self, value, low):
+        for stage in reversed(range(len(self.sizes))):
+            value = self.narrow(value, stage, low)
+        return self.across(value[0], low)
+
+    def across(self, value, low):
+        others = self.replicas // 2
+        if others == 1:
+            return value
+        total = value.astype(jnp.float32)
+        for shift in range(1, others):
+            pairs = [(rep, (rep + 2 * shift) % self.replicas) for rep in range(self.replicas)]
+            total = total + lax.ppermute(value, "rep", pairs).astype(jnp.float32)
+        return total.astype(low)
+
+
+def own_chunks(matrix, core):
+    count = matrix.shape[1] // (2 * CHUNK)
+    return jnp.stack(
+        [
+            lax.dynamic_slice_in_dim(matrix, (2 * part + core) * CHUNK, CHUNK, axis=1)
+            for part in range(count)
+        ]
+    )
+
+
+def join_chunks(mine, other, core):
+    even = jnp.where(core == 0, mine, other)
+    odd = jnp.where(core == 0, other, mine)
+    return jnp.concatenate([piece for part in range(mine.shape[0]) for piece in (even[part], odd[part])], 1)
+
+
+def assemble(places, core, mine, other, counts):
+    shards, parts, rows = mine.shape[:3]
+
+    def body(places_ref, core_ref, mine_ref, other_ref, *refs):
+        outs, sem = refs[:-1], refs[-1]
+
+        def copies(slot):
+            for side, source in enumerate((mine_ref, other_ref)):
+                row = places_ref[side, slot]
+                half = jnp.bitwise_xor(core_ref[0], side)
+                start = 0
+                for out, count in zip(outs, counts):
+                    for part in range(count):
+                        column = pl.multiple_of((2 * part + half) * CHUNK, CHUNK)
+                        yield pltpu.make_async_copy(
+                            source.at[slot, start + part], out.at[row, :, pl.ds(column, CHUNK)], sem
+                        )
+                    start += count
+
+        def begin(slot, carry):
+            for copy in copies(slot):
+                copy.start()
+            return carry
+
+        def finish(slot, carry):
+            for copy in copies(slot):
+                copy.wait()
+            return carry
+
+        lax.fori_loop(0, shards, begin, 0)
+        lax.fori_loop(0, shards, finish, 0)
+
+    outs = pl.pallas_call(
+        body,
+        out_shape=[jax.ShapeDtypeStruct((shards, rows, 2 * count * CHUNK), mine.dtype) for count in counts],
+        in_specs=[pl.BlockSpec(memory_space=pltpu.SMEM)] * 2 + [pl.BlockSpec(memory_space=pl.ANY)] * 2,
+        out_specs=[pl.BlockSpec(memory_space=pl.ANY)] * len(counts),
+        scratch_shapes=[pltpu.SemaphoreType.DMA],
+        name="assemble",
+    )(places, core.reshape(1), mine, other)
+    return [out.reshape(shards * rows, -1) for out in outs]
+
+
+def weight_terms(slots, left, left_twin, right, right_twin, shards):
+    tokens, width = left.shape
+    parts = right.shape[0]
+    tile = min(width, 768)
+    rows = width // shards
+    per_tile = tile // rows
+
+    def body(slots_ref, left_ref, left_twin_ref, right_ref, right_twin_ref, out_ref):
+        tile_index, part = pl.program_id(0), pl.program_id(1)
+        total = outer_sum(left_ref[...], right_ref[0]) + outer_sum(left_twin_ref[...], right_twin_ref[0])
+        total = total.astype(jnp.bfloat16)
+        for block in range(per_tile):
+            slot = slots_ref[tile_index * per_tile + block]
+            out_ref[slot, part] = total[block * rows : (block + 1) * rows]
+
+    return pl.pallas_call(
+        body,
+        grid=(width // tile, parts),
+        out_shape=jax.ShapeDtypeStruct((shards, parts, rows, CHUNK), jnp.bfloat16),
+        in_specs=[
+            pl.BlockSpec(memory_space=pltpu.SMEM),
+            pl.BlockSpec((tokens, tile), lambda i, k: (0, i)),
+            pl.BlockSpec((tokens, tile), lambda i, k: (0, i)),
+            pl.BlockSpec((1, tokens, CHUNK), lambda i, k: (k, 0, 0)),
+            pl.BlockSpec((1, tokens, CHUNK), lambda i, k: (k, 0, 0)),
+        ],
+        out_specs=pl.BlockSpec((shards, parts, rows, CHUNK), lambda i, k: (0, 0, 0, 0)),
+        name="weight_terms",
+    )(slots, left, left_twin, right, right_twin)
+
+
 def outer_sum(left, right):
     return lax.dot_general(
         left, right, (((0,), (0,)), ((), ())), preferred_element_type=jnp.float32
@@ -139,7 +306,7 @@
     return (second, saved)
 
 
-def backward_layer(d_out, saved, weights, vector_row, permitted):
+def backward_layer(d_out, saved, weights, vector_row, permitted, terms):
     w_qkv, w_out, w_up, w_down = weights
     h_low, qkv_low, log_total, context, first_sum, first_low, inner, active, second_sum = saved
     model_width = h_low.shape[1]
@@ -149,22 +316,22 @@
     d_second_sum, d_gain_b, d_shift_b = norm_b_back(d_out)
     d_mixed_b = d_second_sum.astype(jnp.bfloat16)
     d_bias_d = jnp.sum(d_mixed_b, 0, dtype=jnp.float32)
-    grad_down = outer_sum(active, d_mixed_b)
+    grad_down = terms(3, d_mixed_b)
     d_active = times_transposed(d_mixed_b, w_down)
     unused_g, gelu_back = jax.vjp(exact_gelu, inner)
     d_inner = gelu_back(d_active)[0].astype(jnp.bfloat16)
     d_bias_u = jnp.sum(d_inner, 0, dtype=jnp.float32)
-    grad_up = outer_sum(first_low, d_inner)
+    grad_up = terms(2, d_inner)
     d_first = d_second_sum + times_transposed(d_inner, w_up)
     unused_a, norm_a_back = jax.vjp(normed, first_sum, gain_a, shift_a)
     d_first_sum, d_gain_a, d_shift_a = norm_a_back(d_first)
     d_mixed_a = d_first_sum.astype(jnp.bfloat16)
     d_bias_o = jnp.sum(d_mixed_a, 0, dtype=jnp.float32)
-    grad_out = outer_sum(context, d_mixed_a)
+    grad_out = terms(1, d_mixed_a)
     d_context = times_transposed(d_mixed_a, w_out).astype(jnp.bfloat16)
     d_qkv = attend_back(qkv_low, log_total, d_context, permitted).astype(jnp.bfloat16)
     d_bias_qkv = jnp.sum(d_qkv, 0, dtype=jnp.float32)
-    grad_qkv = outer_sum(h_low, d_qkv)
+    grad_qkv = terms(0, d_qkv)
     d_hidden = d_first_sum + times_transposed(d_qkv, w_qkv)
     d_vector = jnp.concatenate(
         [
@@ -182,69 +349,92 @@
     return (d_hidden, (grad_qkv, grad_out, grad_up, grad_down, d_vector))
 
 
-def shards(tokens, valid, qkv_weight, out_weight, up_weight, down_weight, vectors, cotangent):
+GROUPS = (((0, 0),), ((0, 1), (0, 2)), ((0, 3),), ((1, 0), (1, 1)), ((1, 2),), ((1, 3),))
+
+
+def gather_groups(net, blocks):
+    stages = len(net.sizes)
+    state = [block[None] for block in blocks]
+    twins = [None] * len(blocks)
+    for turn in range(len(blocks) + stages):
+        busy = [(turn - stage, stage) for stage in range(stages + 1) if 0 <= turn - stage < len(blocks)]
+        for group, stage in busy:
+            if stage < stages:
+                state[group] = net.widen(state[group], stage)
+            else:
+                twins[group] = net.twin(state[group])
+        nexts = [turn + 1 - stage for stage in range(stages + 1) if 0 <= turn + 1 - stage < len(blocks)]
+        done = [twins[group] for group, stage in busy if stage == stages]
+        if nexts:
+            held = lax.optimization_barrier(tuple([state[group] for group in nexts] + done))
+            for group, value in zip(nexts, held):
+                state[group] = value
+    return state, twins
+
+
+def shards(net, tokens, valid, qkv_weight, out_weight, up_weight, down_weight, vectors, cotangent):
+    count = net.shards
+    core = (lax.axis_index("rep") % 2).astype(jnp.int32)
+    place = lax.axis_index("fsdp").astype(jnp.int32)
+    flips = jnp.asarray(net.flips)
+    own_flips = jnp.where(core == 0, flips[0], flips[1])
+    twin_flips = jnp.where(core == 0, flips[1], flips[0])
+    places = jnp.stack([own_flips ^ place, twin_flips ^ place])
+    weight_inputs = (qkv_weight, out_weight, up_weight, down_weight)
+    slots = jnp.sum(
+        jnp.where(places[0][None, :] == jnp.arange(count, dtype=jnp.int32)[:, None], jnp.arange(count, dtype=jnp.int32)[None, :], 0), 1
+    )
+
+    vector_blocks = vectors[None]
+    for stage in range(len(net.sizes)):
+        vector_blocks = net.widen(vector_blocks, stage)
+    vector_all = jnp.take(vector_blocks, slots, axis=0).transpose(1, 0, 2).reshape(LAYERS, -1)
+
+    blocks, sizes = [], []
+    for group in GROUPS:
+        pieces = [own_chunks(weight_inputs[kind][level].astype(jnp.bfloat16), core) for level, kind in group]
+        sizes.append([piece.shape[0] for piece in pieces])
+        blocks.append(jnp.concatenate(pieces, 0))
+    state, twins = gather_groups(net, blocks)
+    whole = [[None] * 4 for _ in range(LAYERS)]
+    for group, mine, other, counts in zip(GROUPS, state, twins, sizes):
+        for (level, kind), weight in zip(group, assemble(places, core, mine, other, counts)):
+            whole[level][kind] = weight
+
     group_count = valid.shape[0] // 4
     row_live, permitted = slot_layout(valid.reshape(group_count, 4))
     row_mask = row_live.reshape(-1, 1).astype(jnp.float32)
-    vector_all = lax.all_gather(vectors, "fsdp", axis=1, tiled=True)
     hidden = tokens.astype(jnp.float32)
-    kept_weights = []
     kept_saved = []
     for level_idx in range(LAYERS):
-        weights = (
-            lax.all_gather(qkv_weight[level_idx].astype(jnp.bfloat16), "fsdp", axis=0, tiled=True),
-            lax.all_gather(out_weight[level_idx].astype(jnp.bfloat16), "fsdp", axis=0, tiled=True),
-            lax.all_gather(up_weight[level_idx].astype(jnp.bfloat16), "fsdp", axis=0, tiled=True),
-            lax.all_gather(down_weight[level_idx].astype(jnp.bfloat16), "fsdp", axis=0, tiled=True),
-        )
-        hidden, saved = forward_layer(hidden, weights, vector_all[level_idx], permitted)
-        kept_weights.append(weights)
+        hidden, saved = forward_layer(hidden, whole[level_idx], vector_all[level_idx], permitted)
         kept_saved.append(saved)
     layer_out = (hidden * row_mask).astype(jnp.bfloat16)
     d_hidden = cotangent.astype(jnp.float32) * row_mask
     results = [None] * LAYERS
+    d_vectors = [None] * LAYERS
     for level_idx in reversed(range(LAYERS)):
-        weights = (
-            lax.all_gather(qkv_weight[level_idx].astype(jnp.bfloat16), "fsdp", axis=0, tiled=True),
-            lax.all_gather(out_weight[level_idx].astype(jnp.bfloat16), "fsdp", axis=0, tiled=True),
-            lax.all_gather(up_weight[level_idx].astype(jnp.bfloat16), "fsdp", axis=0, tiled=True),
-            lax.all_gather(down_weight[level_idx].astype(jnp.bfloat16), "fsdp", axis=0, tiled=True),
+        saved = kept_saved[level_idx]
+        lefts = (saved[0], saved[3], saved[5], saved[7])
+        twins_left = [net.twin(left) for left in lefts]
+
+        def terms(kind, right):
+            sent = net.twin(own_chunks(right, 1 - core))
+            kept = own_chunks(right, core)
+            full = weight_terms(slots, lefts[kind], twins_left[kind], kept, sent, count)
+            mine = net.reduce(full, jnp.bfloat16)
+            return join_chunks(mine, net.twin(mine), core).astype(jnp.float32)
+
+        d_hidden, parts = backward_layer(
+            d_hidden, saved, whole[level_idx], vector_all[level_idx], permitted, terms
         )
-        d_hidden, terms = backward_layer(
-            d_hidden, kept_saved[level_idx], weights, vector_all[level_idx], permitted
-        )
-        term_qkv, term_out, term_up, term_down, term_vector = terms
-        owned = (
-            lax.psum_scatter(
-                term_qkv.astype(jnp.bfloat16), "fsdp", scatter_dimension=0, tiled=True
-            ).astype(jnp.float32),
-            lax.psum_scatter(
-                term_out.astype(jnp.bfloat16), "fsdp", scatter_dimension=0, tiled=True
-            ).astype(jnp.float32),
-            lax.psum_scatter(
-                term_up.astype(jnp.bfloat16), "fsdp", scatter_dimension=0, tiled=True
-            ).astype(jnp.float32),
-            lax.psum_scatter(
-                term_down.astype(jnp.bfloat16), "fsdp", scatter_dimension=0, tiled=True
-            ).astype(jnp.float32),
-            lax.psum_scatter(
-                term_vector.astype(jnp.bfloat16), "fsdp", scatter_dimension=0, tiled=True
-            ).astype(jnp.float32),
-        )
-        shares = (
-            lax.psum(owned[0].astype(jnp.bfloat16), "rep").astype(jnp.float32),
-            lax.psum(owned[1].astype(jnp.bfloat16), "rep").astype(jnp.float32),
-            lax.psum(owned[2].astype(jnp.bfloat16), "rep").astype(jnp.float32),
-            lax.psum(owned[3].astype(jnp.bfloat16), "rep").astype(jnp.float32),
-            lax.psum(owned[4].astype(jnp.bfloat16), "rep").astype(jnp.float32),
-        )
-        results[level_idx] = shares
-    qkv_grad = jnp.stack([entry[0] for entry in results])
-    out_grad = jnp.stack([entry[1] for entry in results])
-    up_grad = jnp.stack([entry[2] for entry in results])
-    down_grad = jnp.stack([entry[3] for entry in results])
-    vector_grad = jnp.stack([entry[4] for entry in results])
-    return (layer_out, d_hidden, qkv_grad, out_grad, up_grad, down_grad, vector_grad)
+        results[level_idx] = parts[:4]
+        d_vectors[level_idx] = parts[4].reshape(count, -1)
+    d_vector = jnp.stack(d_vectors, 1)
+    d_vector = d_vector + net.twin(d_vector)
+    vector_grad = net.reduce(jnp.take(d_vector, places[0], axis=0), jnp.float32)
+    grads = [jnp.stack([entry[kind] for entry in results]) for kind in range(4)]
+    return (layer_out, d_hidden, *grads, vector_grad)
 
 
 def solution(mesh):
@@ -267,4 +457,5 @@
         P(None, "fsdp", None),
         P(None, "fsdp"),
     )
-    return jax.shard_map(shards, mesh=mesh, in_specs=in_specs, out_specs=out_specs, check_vma=False)
+    net = Net(mesh)
+    return jax.shard_map(functools.partial(shards, net), mesh=mesh, in_specs=in_specs, out_specs=out_specs, check_vma=False)

time: 1880 us -> 1510 us (0.80)
  waiting for transfers between devices: 1450 us -> 144 us
  Pallas kernels: 0 us -> 918 us
  blocking collectives: 121 us -> 0 us
  starting transfers between devices: 0.94 us -> 119 us
  other arithmetic: 38.7 us -> 99.4 us
  matrix products: 203 us -> 156 us
  local copies, waits for them, and re-layouts: 46 us -> 67 us
    pallas_call x0 -> x14, Pallas kernels: none -> 918 us  [the longest x6 869 us: assemble(): pl.pallas_call(body, out_shape=[jax.ShapeDtypeStruct((shards, rows, 2 * c...]
    reduce_scatter x6 -> x0, waiting for transfers between devices: 822 us -> none  [the longest x2 284 us: shards(): lax.psum_scatter(term_down.astype(jnp.bfloat16), 'fsdp', scatter_dimensio...]
    all_gather x8 -> x0, waiting for transfers between devices: 452 us -> none  [the longest x2 158 us: shards(): lax.all_gather(up_weight[level_idx].astype(jnp.bfloat16), 'fsdp', axis=0,...]
    unnamed x19 -> x0, waiting for transfers between devices: 177 us -> none
    ppermute x0 -> x111, waiting for transfers between devices: none -> 144 us  [the longest x80 141 us: trade(): return lax.ppermute(value, ('rep', 'fsdp'), self.pairs(stage, offset))]
    ppermute x0 -> x111, starting transfers between devices: none -> 119 us  [the longest x80 115 us: trade(): return lax.ppermute(value, ('rep', 'fsdp'), self.pairs(stage, offset))]
    unnamed x1 -> x0, blocking collectives: 74.8 us -> none
    all_gather x1 -> x0, blocking collectives: 43.3 us -> none  [shards(): vector_all = lax.all_gather(vectors, 'fsdp', axis=1, tiled=True)]
  transfers between devices with their start and end apart: 17 -> 111, of which waited for: 16 -> 39; matrix products, arithmetic and copies ran while one was open for 10% -> 20% of each run, Pallas kernels for 0% -> 61%
where the time goes in v1:
time: 1510 us
  Pallas kernels  918 us (61%)
  matrix products  156 us (10%)
  waiting for transfers between devices  144 us (10%)
  starting transfers between devices  119 us (8%)
  other arithmetic  99.4 us (7%)
  local copies, waits for them, and re-layouts  67 us (4%)
    pallas_call x6, Pallas kernels, assemble(): pl.pallas_call(body, out_shape=[jax.ShapeDtypeStruct((shards, rows, 2 * c...  869 us
    ppermute x80, waiting for transfers between devices, trade(): return lax.ppermute(value, ('rep', 'fsdp'), self.pairs(stage, offset))  141 us
    ppermute x80, starting transfers between devices, trade(): return lax.ppermute(value, ('rep', 'fsdp'), self.pairs(stage, offset))  115 us
    pallas_call x8, Pallas kernels, weight_terms(): pl.pallas_call(body, grid=(width // tile, parts), out_shape=jax.ShapeDtyp...  48.8 us
    dot_general x8, matrix products, times_transposed(): lax.dot_general(left, right, (((1,), (1,)), ((), ())), preferred_element_...  38.1 us
    dot_general x2, matrix products, forward_layer(): jnp.dot(first_low, w_up, preferred_element_type=jnp.float32) + bias_u  37.6 us
    concatenate x19, other arithmetic, widen(): return jnp.concatenate([value, *received], 0)  30.3 us
  transfers between devices with their start and end apart: 111, of which 39 were waited for; matrix products, arithmetic and copies ran while one was open for 20% of the time, Pallas kernels for 61%

profile of v1, /device:TPU:0, one launch (start us, length us, event | category | flops | bytes accessed | tf_op | source)
XLA Modules:
  0.0 1507.3 jit_solution(9008556543570303157)
XLA Ops:
  2.2 5.1 collective-permute-start.2
  11.3 5.3 collective-permute-done.1
  23.5 5.0 collective-permute-done.5
  28.5 7.7 collective-permute-done.4
  43.9 3.6 collective-permute-done.9
  63.2 15.2 %collective-permute-done.17 = f32[8,2,576]{2,1,0:T(2,128)S(1)} collective-permute-done((f32[8,2,576]{2,1,0:T(2,128)S(1)}, f32[8,2,576]{2,1,0:T(2,128)S(1)}, u32[]{:S(2)}, u32[]{:S(2)}) %collective-permute-start.17) | collective-permute-done | bytes 36896 | tf_op jit(solution)/shard_map/ppermute | solution.py:96
  83.9 3.6 collective-permute-done.20
  87.5 4.5 collective-permute-start.18
  108.6 109.2 %assemble.6 = bf16[16,48,2304]{2,1,0:T(8,128)(2,1)} custom-call(s32[2,16]{1,0:T(2,128)} %pad_add_fusion.places_ref, s32[1]{0:T(128)} %bitcast.core_ref, bf16[16,3,48,384]{3,2,1,0:T(8,128)(2,1)} %pad_maximum_fusion.5.mine_ref, bf16[16,3,48,384]{3,2,1,0:T(8,128)(2,1)} %collective-permute-done.12.other_ref), custom_call_target="tpu_custom_call" | custom-call | tf_op jit(solution)/shard_map/assemble/pallas_call | solution.py:176
  217.8 4.5 fusion.16
  228.1 4.2 collective-permute-done.24
  236.6 3.3 pad_maximum_fusion.1.mine_ref
  239.9 4.4 convolution_convert_fusion.3
  249.0 180.7 %assemble.7 = (bf16[16,48,768]{2,1,0:T(8,128)(2,1)}, bf16[16,48,3072]{2,1,0:T(8,128)(2,1)}) custom-call(s32[2,16]{1,0:T(2,128)} %pad_add_fusion.places_ref, s32[1]{0:T(128)} %bitcast.core_ref, bf16[16,5,48,384]{3,2,1,0:T(8,128)(2,1)} %copy-done.8, bf16[16,5,48,384]{3,2,1,0:T(8,128)(2,1)} %collective-permute-done.23.other_ref), custom_call_target="tpu_custom_call" | custom-call | tf_op jit(solution)/shard_map/assemble/pallas_call | solution.py:176
  429.7 2.8 fusion.84
  435.4 2.8 collective-permute-done.30
  441.5 3.0 pad_maximum_fusion.2.mine_ref
  444.5 18.5 %multiply_convert_fusion.3 = (bf16[512,3072]{1,0:T(8,128)(2,1)}, f32[512,3072]{1,0:T(8,128)}, f32[512,3072]{1,0:T(8,128)}) fusion(f32[3072]{0:T(1024)S(1)} %copy-done.106, bf16[512,768]{1,0:T(8,128)(2,1)S(1)} %fusion.20.left_ref, bf16[768,3072]{1,0:T(8,128)(2,1)S(1)} %bitcast.299), kind=kOutput, calls=%fused_computation.37 | convolution fusion | flops 2519728128 | bytes 21245952 | tf_op jit(solution)/shard_map/dot_general | solution.py:300
  466.6 144.7 %assemble.8 = bf16[16,192,768]{2,1,0:T(8,128)(2,1)} custom-call(s32[2,16]{1,0:T(2,128)} %pad_add_fusion.places_ref, s32[1]{0:T(128)} %bitcast.core_ref, bf16[16,1,192,384]{3,2,1,0:T(8,128)(2,1)} %pad_maximum_fusion.1.mine_ref, bf16[16,1,192,384]{3,2,1,0:T(8,128)(2,1)} %collective-permute-done.29.other_ref), custom_call_target="tpu_custom_call" | custom-call | tf_op jit(solution)/shard_map/assemble/pallas_call | solution.py:176
  611.4 6.0 fusion.85
  620.9 3.0 pad_maximum_fusion.3.mine_ref
  623.8 144.9 %assemble.9 = (bf16[16,48,2304]{2,1,0:T(8,128)(2,1)}, bf16[16,48,768]{2,1,0:T(8,128)(2,1)}) custom-call(s32[2,16]{1,0:T(2,128)} %pad_add_fusion.places_ref, s32[1]{0:T(128)} %bitcast.core_ref, bf16[16,4,48,384]{3,2,1,0:T(8,128)(2,1)} %pad_maximum_fusion.2.mine_ref, bf16[16,4,48,384]{3,2,1,0:T(8,128)(2,1)} %collective-permute-done.35.other_ref), custom_call_target="tpu_custom_call" | custom-call | tf_op jit(solution)/shard_map/assemble/pallas_call | solution.py:176
  768.8 5.4 fusion.17
  774.2 3.2 copy.73
  784.2 3.2 convolution_convert_fusion.2
  788.5 2.8 fusion.86
  792.9 6.0 collective-permute-done.39
  798.8 3.0 pad_maximum_fusion.4.mine_ref
  801.8 144.8 %assemble.10 = bf16[16,48,3072]{2,1,0:T(8,128)(2,1)} custom-call(s32[2,16]{1,0:T(2,128)} %pad_add_fusion.places_ref, s32[1]{0:T(128)} %bitcast.core_ref, bf16[16,4,48,384]{3,2,1,0:T(8,128)(2,1)} %pad_maximum_fusion.3.mine_ref, bf16[16,4,48,384]{3,2,1,0:T(8,128)(2,1)} %collective-permute-done.38.other_ref), custom_call_target="tpu_custom_call" | custom-call | tf_op jit(solution)/shard_map/assemble/pallas_call | solution.py:176
  946.6 19.1 %multiply_convert_fusion.2 = (bf16[512,3072]{1,0:T(8,128)(2,1)}, f32[512,3072]{1,0:T(8,128)}, f32[512,3072]{1,0:T(8,128)}) fusion(f32[3072]{0:T(1024)S(1)} %copy-done.108, bf16[512,768]{1,0:T(8,128)(2,1)S(1)} %fusion.22.left_ref, bf16[768,3072]{1,0:T(8,128)(2,1)} %bitcast.259), kind=kOutput, calls=%fused_computation.24 | convolution fusion | flops 2519728128 | bytes 21245952 | tf_op jit(solution)/shard_map/dot_general | solution.py:300
  965.7 144.7 %assemble.11 = bf16[16,192,768]{2,1,0:T(8,128)(2,1)} custom-call(s32[2,16]{1,0:T(2,128)} %pad_add_fusion.places_ref, s32[1]{0:T(128)} %bitcast.core_ref, bf16[16,1,192,384]{3,2,1,0:T(8,128)(2,1)} %pad_maximum_fusion.4.mine_ref, bf16[16,1,192,384]{3,2,1,0:T(8,128)(2,1)} %collective-permute-done.40.other_ref), custom_call_target="tpu_custom_call" | custom-call | tf_op jit(solution)/shard_map/assemble/pallas_call | solution.py:176
  1110.5 6.5 fusion.87
  1120.8 9.0 convert_reduce_fusion
  1129.8 3.7 multiply_reduce_fusion.3
  1139.6 7.3 convolution_bitcast_fusion.1
  1146.9 9.6 multiply_reduce_fusion.1
  1156.6 7.5 multiply_convert_fusion.1
  1169.7 3.3 multiply_reduce_fusion.4
  1174.3 8.4 convert_reduce_fusion.1
  1182.7 7.2 multiply_reduce_fusion.5
  1196.6 7.3 convolution_bitcast_fusion
  1203.9 9.7 multiply_reduce_fusion
  1213.7 7.3 multiply_convert_fusion
  1229.1 3.2 add_add_fusion.8
  1249.4 3.4 weight_terms.11
  1255.2 3.4 weight_terms.10
  1262.8 5.3 collective-permute-done.59
  1295.5 7.6 weight_terms.14
  1324.5 7.6 weight_terms.15
  1343.5 6.0 weight_terms.9
  1354.1 6.0 weight_terms.8
  1362.2 7.3 weight_terms.13
  1374.3 7.5 weight_terms.12
  1396.4 7.0 collective-permute-done.94
  1407.8 12.6 collective-permute-done.52
  1425.2 7.3 collective-permute-start.54
  1434.5 4.2 collective-permute-done.54
  1441.8 3.4 collective-permute-start.103
  1445.1 9.4 collective-permute-done.46
  1454.8 6.6 collective-permute-done.102
  1470.4 6.3 collective-permute-done.84
  1485.6 5.3 collective-permute-start.77
  1490.9 8.3 collective-permute-done.86
  1499.4 4.8 collective-permute-done.78
  (763 shorter events, 269.6 us)
Async XLA Ops:
  17.6 18.8 %collective-permute-start.6 = (bf16[4,3,48,384]{3,2,1,0:T(8,128)(2,1)S(1)}, bf16[4,3,48,384]{3,2,1,0:T(8,128)(2,1)S(1)}, u32[]{:S(2)}, u32[]{:S(2)}) collective-permute-start(bf16[4,3,48,384]{3,2,1,0:T(8,128)(2,1)S(1)} %pad_maximum_fusion.25), channel_id=1, source_target_pairs={{0,1},{1,0},{2,3},{3,2},{4,5},{5,4},{6,7},{7,6},{8,9},{9,8},{10,11... | collective-permute-start | bytes 1327112 | tf_op jit(solution)/shard_map/ppermute | solution.py:96
  21.6 14.6 collective-permute-start.4
  21.6 14.6 collective-permute-start.3
  36.5 18.5 %collective-permute-start.10 = (bf16[4,5,48,384]{3,2,1,0:T(8,128)(2,1)S(1)}, bf16[4,5,48,384]{3,2,1,0:T(8,128)(2,1)S(1)}, u32[]{:S(2)}, u32[]{:S(2)}) collective-permute-start(bf16[4,5,48,384]{3,2,1,0:T(8,128)(2,1)S(1)} %pad_maximum_fusion.20), channel_id=1, source_target_pairs={{0,1},{1,0},{2,3},{3,2},{4,5},{5,4},{6,7},{7,6},{8,9},{9,8},{10,11... | collective-permute-start | bytes 2211848 | tf_op jit(solution)/shard_map/ppermute | solution.py:96
  37.9 17.3 %collective-permute-start.11 = (bf16[8,3,48,384]{3,2,1,0:T(8,128)(2,1)S(1)}, bf16[8,3,48,384]{3,2,1,0:T(8,128)(2,1)S(1)}, u32[]{:S(2)}, u32[]{:S(2)}) collective-permute-start(bf16[8,3,48,384]{3,2,1,0:T(8,128)(2,1)S(1)} %pad_maximum_fusion.19), channel_id=1, source_target_pairs={{0,2},{1,3},{2,0},{3,1},{4,6},{5,7},{6,4},{7,5},{8,10},{9,11},{10,... | collective-permute-start | bytes 2654216 | tf_op jit(solution)/shard_map/ppermute | solution.py:96
  40.5 11.3 collective-permute-start.7
  56.8 43.7 %collective-permute-start.12 = (bf16[16,3,48,384]{3,2,1,0:T(8,128)(2,1)}, bf16[16,3,48,384]{3,2,1,0:T(8,128)(2,1)}, u32[]{:S(2)}, u32[]{:S(2)}) collective-permute-start(bf16[16,3,48,384]{3,2,1,0:T(8,128)(2,1)} %pad_maximum_fusion.5.mine_ref), channel_id=1, source_target_pairs={{0,16},{16,0},{1,17},{17,1},{2,18},{18,2},{3,19},{19,3},{4,20},{20... | collective-permute-start | bytes 5308424 | tf_op jit(solution)/shard_map/ppermute | solution.py:99
  58.7 39.5 %collective-permute-start.22 = (bf16[8,5,48,384]{3,2,1,0:T(8,128)(2,1)S(1)}, bf16[8,5,48,384]{3,2,1,0:T(8,128)(2,1)}, u32[]{:S(2)}, u32[]{:S(2)}) collective-permute-start(bf16[8,5,48,384]{3,2,1,0:T(8,128)(2,1)S(1)} %pad_maximum_fusion.10), channel_id=1, source_target_pairs={{0,2},{1,3},{2,0},{3,1},{4,6},{5,7},{6,4},{7,5},{8,10},{9,11},{10,... | collective-permute-start | bytes 4423688 | tf_op jit(solution)/shard_map/ppermute | solution.py:96
  61.1 17.4 %collective-permute-start.17 = (f32[8,2,576]{2,1,0:T(2,128)S(1)}, f32[8,2,576]{2,1,0:T(2,128)S(1)}, u32[]{:S(2)}, u32[]{:S(2)}) collective-permute-start(f32[8,2,576]{2,1,0:T(2,128)S(1)} %get-tuple-element.226), channel_id=1, source_target_pairs={{0,2},{1,3},{2,0},{3,1},{4,6},{5,7},{6,4},{7,5},{8,10},{9,11},{10,... | collective-permute-start | bytes 110600 | tf_op jit(solution)/shard_map/ppermute | solution.py:96
  81.0 16.0 %collective-permute-start.21 = (bf16[4,1,192,384]{3,2,1,0:T(8,128)(2,1)S(1)}, bf16[4,1,192,384]{3,2,1,0:T(8,128)(2,1)S(1)}, u32[]{:S(2)}, u32[]{:S(2)}) collective-permute-start(bf16[4,1,192,384]{3,2,1,0:T(8,128)(2,1)S(1)} %pad_maximum_fusion.21), channel_id=1, source_target_pairs={{0,1},{1,0},{2,3},{3,2},{4,5},{5,4},{6,7},{7,6},{8,9},{9,8},{10,11... | collective-permute-start | bytes 1769480 | tf_op jit(solution)/shard_map/ppermute | solution.py:96
  100.5 139.4 %collective-permute-start.23 = (bf16[16,5,48,384]{3,2,1,0:T(8,128)(2,1)S(1)}, bf16[16,5,48,384]{3,2,1,0:T(8,128)(2,1)}, u32[]{:S(2)}, u32[]{:S(2)}) collective-permute-start(bf16[16,5,48,384]{3,2,1,0:T(8,128)(2,1)S(1)} %pad_maximum_fusion.mine_ref), channel_id=1, source_target_pairs={{0,16},{16,0},{1,17},{17,1},{2,18},{18,2},{3,19},{19,3},{4,20},{20... | collective-permute-start | bytes 8847368 | tf_op jit(solution)/shard_map/ppermute | solution.py:99
  102.1 125.0 %collective-permute-start.26 = (bf16[1,4,48,384]{3,2,1,0:T(8,128)(2,1)S(1)}, bf16[1,4,48,384]{3,2,1,0:T(8,128)(2,1)}, u32[]{:S(2)}, u32[]{:S(2)}) collective-permute-start(bf16[1,4,48,384]{3,2,1,0:T(8,128)(2,1)S(1)} %maximum_bitcast_fusion.1), channel_id=1, source_target_pairs={{0,12},{1,13},{2,14},{3,15},{4,8},{5,9},{6,10},{7,11},{8,4},{9,5},... | collective-permute-start | bytes 442376 | tf_op jit(solution)/shard_map/ppermute | solution.py:96
  104.0 124.0 %collective-permute-start.25 = (bf16[1,4,48,384]{3,2,1,0:T(8,128)(2,1)S(1)}, bf16[1,4,48,384]{3,2,1,0:T(8,128)(2,1)}, u32[]{:S(2)}, u32[]{:S(2)}) collective-permute-start(bf16[1,4,48,384]{3,2,1,0:T(8,128)(2,1)S(1)} %maximum_bitcast_fusion.1), channel_id=1, source_target_pairs={{0,8},{1,9},{2,10},{3,11},{4,12},{5,13},{6,14},{7,15},{8,0},{9,1},... | collective-permute-start | bytes 442376 | tf_op jit(solution)/shard_map/ppermute | solution.py:96
  105.5 128.6 %collective-permute-start.27 = (bf16[4,4,48,384]{3,2,1,0:T(8,128)(2,1)}, bf16[4,4,48,384]{3,2,1,0:T(8,128)(2,1)}, u32[]{:S(2)}, u32[]{:S(2)}) collective-permute-start(bf16[4,4,48,384]{3,2,1,0:T(8,128)(2,1)} %pad_maximum_fusion.22), channel_id=1, source_target_pairs={{0,1},{1,0},{2,3},{3,2},{4,5},{5,4},{6,7},{7,6},{8,9},{9,8},{10,11... | collective-permute-start | bytes 1769480 | tf_op jit(solution)/shard_map/ppermute | solution.py:96
  107.0 129.6 %collective-permute-start.28 = (bf16[8,1,192,384]{3,2,1,0:T(8,128)(2,1)}, bf16[8,1,192,384]{3,2,1,0:T(8,128)(2,1)}, u32[]{:S(2)}, u32[]{:S(2)}) collective-permute-start(bf16[8,1,192,384]{3,2,1,0:T(8,128)(2,1)} %pad_maximum_fusion.11), channel_id=1, source_target_pairs={{0,2},{1,3},{2,0},{3,1},{4,6},{5,7},{6,4},{7,5},{8,10},{9,11},{10,... | collective-permute-start | bytes 3538952 | tf_op jit(solution)/shard_map/ppermute | solution.py:96
  239.9 204.6 %collective-permute-start.29 = (bf16[16,1,192,384]{3,2,1,0:T(8,128)(2,1)}, bf16[16,1,192,384]{3,2,1,0:T(8,128)(2,1)}, u32[]{:S(2)}, u32[]{:S(2)}) collective-permute-start(bf16[16,1,192,384]{3,2,1,0:T(8,128)(2,1)} %pad_maximum_fusion.1.mine_ref), channel_id=1, source_target_pairs={{0,16},{16,0},{1,17},{17,1},{2,18},{18,2},{3,19},{19,3},{4,20},{20... | collective-permute-start | bytes 7077896 | tf_op jit(solution)/shard_map/ppermute | solution.py:99
  245.6 187.3 %collective-permute-start.32 = (bf16[1,1,192,384]{3,2,1,0:T(8,128)(2,1)S(1)}, bf16[1,1,192,384]{3,2,1,0:T(8,128)(2,1)S(1)}, u32[]{:S(2)}, u32[]{:S(2)}) collective-permute-start(bf16[1,1,192,384]{3,2,1,0:T(8,128)(2,1)S(1)} %dynamic-slice_bitcast_fusion.24), channel_id=1, source_target_pairs={{0,12},{1,13},{2,14},{3,15},{4,8},{5,9},{6,10},{7,11},{8,4},{9,5},... | collective-permute-start | bytes 442376 | tf_op jit(solution)/shard_map/ppermute | solution.py:96
  246.9 188.3 %collective-permute-start.31 = (bf16[1,1,192,384]{3,2,1,0:T(8,128)(2,1)S(1)}, bf16[1,1,192,384]{3,2,1,0:T(8,128)(2,1)S(1)}, u32[]{:S(2)}, u32[]{:S(2)}) collective-permute-start(bf16[1,1,192,384]{3,2,1,0:T(8,128)(2,1)S(1)} %dynamic-slice_bitcast_fusion.24), channel_id=1, source_target_pairs={{0,8},{1,9},{2,10},{3,11},{4,12},{5,13},{6,14},{7,15},{8,0},{9,1},... | collective-permute-start | bytes 442376 | tf_op jit(solution)/shard_map/ppermute | solution.py:96
  248.0 191.1 %collective-permute-start.33 = (bf16[4,4,48,384]{3,2,1,0:T(8,128)(2,1)}, bf16[4,4,48,384]{3,2,1,0:T(8,128)(2,1)}, u32[]{:S(2)}, u32[]{:S(2)}) collective-permute-start(bf16[4,4,48,384]{3,2,1,0:T(8,128)(2,1)} %pad_maximum_fusion.23), channel_id=1, source_target_pairs={{0,1},{1,0},{2,3},{3,2},{4,5},{5,4},{6,7},{7,6},{8,9},{9,8},{10,11... | collective-permute-start | bytes 1769480 | tf_op jit(solution)/shard_map/ppermute | solution.py:96
  248.0 193.5 %collective-permute-start.34 = (bf16[8,4,48,384]{3,2,1,0:T(8,128)(2,1)S(1)}, bf16[8,4,48,384]{3,2,1,0:T(8,128)(2,1)}, u32[]{:S(2)}, u32[]{:S(2)}) collective-permute-start(bf16[8,4,48,384]{3,2,1,0:T(8,128)(2,1)S(1)} %copy-done.26), channel_id=1, source_target_pairs={{0,2},{1,3},{2,0},{3,1},{4,6},{5,7},{6,4},{7,5},{8,10},{9,11},{10,... | collective-permute-start | bytes 3538952 | tf_op jit(solution)/shard_map/ppermute | solution.py:96
  435.3 819.9 %collective-permute-start.57 = (bf16[512,768]{1,0:T(8,128)(2,1)}, bf16[512,768]{1,0:T(8,128)(2,1)}, u32[]{:S(2)}, u32[]{:S(2)}) collective-permute-start(bf16[512,768]{1,0:T(8,128)(2,1)} %copy.96.left_ref), channel_id=1, source_target_pairs={{0,16},{16,0},{1,17},{17,1},{2,18},{18,2},{3,19},{19,3},{4,20},{20... | collective-permute-start | bytes 2359304 | tf_op jit(solution)/shard_map/ppermute | solution.py:99
  444.5 179.3 %collective-permute-start.35 = (bf16[16,4,48,384]{3,2,1,0:T(8,128)(2,1)}, bf16[16,4,48,384]{3,2,1,0:T(8,128)(2,1)}, u32[]{:S(2)}, u32[]{:S(2)}) collective-permute-start(bf16[16,4,48,384]{3,2,1,0:T(8,128)(2,1)} %pad_maximum_fusion.2.mine_ref), channel_id=1, source_target_pairs={{0,16},{16,0},{1,17},{17,1},{2,18},{18,2},{3,19},{19,3},{4,20},{20... | collective-permute-start | bytes 7077896 | tf_op jit(solution)/shard_map/ppermute | solution.py:99
  463.1 816.5 %collective-permute-start.89 = (bf16[512,3072]{1,0:T(8,128)(2,1)}, bf16[512,3072]{1,0:T(8,128)(2,1)}, u32[]{:S(2)}, u32[]{:S(2)}) collective-permute-start(bf16[512,3072]{1,0:T(8,128)(2,1)} %get-tuple-element.106.left_ref), channel_id=1, source_target_pairs={{0,16},{16,0},{1,17},{17,1},{2,18},{18,2},{3,19},{19,3},{4,20},{20... | collective-permute-start | bytes 9437192 | tf_op jit(solution)/shard_map/ppermute | solution.py:99
  463.5 154.6 %collective-permute-start.36 = (bf16[4,1,192,384]{3,2,1,0:T(8,128)(2,1)}, bf16[4,1,192,384]{3,2,1,0:T(8,128)(2,1)}, u32[]{:S(2)}, u32[]{:S(2)}) collective-permute-start(bf16[4,1,192,384]{3,2,1,0:T(8,128)(2,1)} %pad_maximum_fusion.24), channel_id=1, source_target_pairs={{0,1},{1,0},{2,3},{3,2},{4,5},{5,4},{6,7},{7,6},{8,9},{9,8},{10,11... | collective-permute-start | bytes 1769480 | tf_op jit(solution)/shard_map/ppermute | solution.py:96
  465.0 155.9 %collective-permute-start.37 = (bf16[8,4,48,384]{3,2,1,0:T(8,128)(2,1)}, bf16[8,4,48,384]{3,2,1,0:T(8,128)(2,1)S(1)}, u32[]{:S(2)}, u32[]{:S(2)}) collective-permute-start(bf16[8,4,48,384]{3,2,1,0:T(8,128)(2,1)} %pad_maximum_fusion.13), channel_id=1, source_target_pairs={{0,2},{1,3},{2,0},{3,1},{4,6},{5,7},{6,4},{7,5},{8,10},{9,11},{10,... | collective-permute-start | bytes 3538952 | tf_op jit(solution)/shard_map/ppermute | solution.py:96
  782.1 19.7 %collective-permute-start.38 = (bf16[16,4,48,384]{3,2,1,0:T(8,128)(2,1)}, bf16[16,4,48,384]{3,2,1,0:T(8,128)(2,1)}, u32[]{:S(2)}, u32[]{:S(2)}) collective-permute-start(bf16[16,4,48,384]{3,2,1,0:T(8,128)(2,1)} %pad_maximum_fusion.3.mine_ref), channel_id=1, source_target_pairs={{0,16},{16,0},{1,17},{17,1},{2,18},{18,2},{3,19},{19,3},{4,20},{20... | collective-permute-start | bytes 7077896 | tf_op jit(solution)/shard_map/ppermute | solution.py:99
  782.2 16.6 %collective-permute-start.39 = (bf16[8,1,192,384]{3,2,1,0:T(8,128)(2,1)}, bf16[8,1,192,384]{3,2,1,0:T(8,128)(2,1)}, u32[]{:S(2)}, u32[]{:S(2)}) collective-permute-start(bf16[8,1,192,384]{3,2,1,0:T(8,128)(2,1)} %pad_maximum_fusion.14), channel_id=1, source_target_pairs={{0,2},{1,3},{2,0},{3,1},{4,6},{5,7},{6,4},{7,5},{8,10},{9,11},{10,... | collective-permute-start | bytes 3538952 | tf_op jit(solution)/shard_map/ppermute | solution.py:96
  788.5 459.1 %collective-permute-start.65 = (bf16[512,768]{1,0:T(8,128)(2,1)}, bf16[512,768]{1,0:T(8,128)(2,1)}, u32[]{:S(2)}, u32[]{:S(2)}) collective-permute-start(bf16[512,768]{1,0:T(8,128)(2,1)} %copy.98.left_ref), channel_id=1, source_target_pairs={{0,16},{16,0},{1,17},{17,1},{2,18},{18,2},{3,19},{19,3},{4,20},{20... | collective-permute-start | bytes 2359304 | tf_op jit(solution)/shard_map/ppermute | solution.py:99
  801.8 163.9 %collective-permute-start.40 = (bf16[16,1,192,384]{3,2,1,0:T(8,128)(2,1)}, bf16[16,1,192,384]{3,2,1,0:T(8,128)(2,1)}, u32[]{:S(2)}, u32[]{:S(2)}) collective-permute-start(bf16[16,1,192,384]{3,2,1,0:T(8,128)(2,1)} %pad_maximum_fusion.4.mine_ref), channel_id=1, source_target_pairs={{0,16},{16,0},{1,17},{17,1},{2,18},{18,2},{3,19},{19,3},{4,20},{20... | collective-permute-start | bytes 7077896 | tf_op jit(solution)/shard_map/ppermute | solution.py:99
  1232.3 17.0 %collective-permute-start.66 = (bf16[1,512,384]{2,1,0:T(8,128)(2,1)}, bf16[1,512,384]{2,1,0:T(8,128)(2,1)}, u32[]{:S(2)}, u32[]{:S(2)}) collective-permute-start(bf16[1,512,384]{2,1,0:T(8,128)(2,1)} %get-tuple-element.143), channel_id=1, source_target_pairs={{0,16},{16,0},{1,17},{17,1},{2,18},{18,2},{3,19},{19,3},{4,20},{20... | collective-permute-start | bytes 1179656 | tf_op jit(solution)/shard_map/ppermute | solution.py:99
  1232.8 22.4 %collective-permute-start.58 = (bf16[1,512,384]{2,1,0:T(8,128)(2,1)}, bf16[1,512,384]{2,1,0:T(8,128)(2,1)}, u32[]{:S(2)}, u32[]{:S(2)}) collective-permute-start(bf16[1,512,384]{2,1,0:T(8,128)(2,1)} %get-tuple-element.141), channel_id=1, source_target_pairs={{0,16},{16,0},{1,17},{17,1},{2,18},{18,2},{3,19},{19,3},{4,20},{20... | collective-permute-start | bytes 1179656 | tf_op jit(solution)/shard_map/ppermute | solution.py:99
  1249.3 63.2 %collective-permute-start.97 = (bf16[512,3072]{1,0:T(8,128)(2,1)}, bf16[512,3072]{1,0:T(8,128)(2,1)}, u32[]{:S(2)}, u32[]{:S(2)}) collective-permute-start(bf16[512,3072]{1,0:T(8,128)(2,1)} %get-tuple-element.104.left_ref), channel_id=1, source_target_pairs={{0,16},{16,0},{1,17},{17,1},{2,18},{18,2},{3,19},{19,3},{4,20},{20... | collective-permute-start | bytes 9437192 | tf_op jit(solution)/shard_map/ppermute | solution.py:99
  1262.2 12.5 collective-permute-start.68
  1283.5 51.2 %collective-permute-start.50 = (bf16[3,512,384]{2,1,0:T(8,128)(2,1)}, bf16[3,512,384]{2,1,0:T(8,128)(2,1)}, u32[]{:S(2)}, u32[]{:S(2)}) collective-permute-start(bf16[3,512,384]{2,1,0:T(8,128)(2,1)} %pad_maximum_fusion.18), channel_id=1, source_target_pairs={{0,16},{16,0},{1,17},{17,1},{2,18},{18,2},{3,19},{19,3},{4,20},{20... | collective-permute-start | bytes 3538952 | tf_op jit(solution)/shard_map/ppermute | solution.py:99
  1287.1 18.6 %collective-permute-start.69 = (bf16[1,1,48,384]{3,2,1,0:T(8,128)(2,1)S(1)}, bf16[1,1,48,384]{3,2,1,0:T(8,128)(2,1)S(1)}, u32[]{:S(2)}, u32[]{:S(2)}) collective-permute-start(bf16[1,1,48,384]{3,2,1,0:T(8,128)(2,1)S(1)} %get-tuple-element.194), channel_id=1, source_target_pairs={{0,4},{1,5},{2,6},{3,7},{4,0},{5,1},{6,2},{7,3},{8,12},{9,13},{10,... | collective-permute-start | bytes 110600 | tf_op jit(solution)/shard_map/ppermute | solution.py:96
  1289.9 15.8 %collective-permute-start.63 = (bf16[1,1,48,384]{3,2,1,0:T(8,128)(2,1)S(1)}, bf16[1,1,48,384]{3,2,1,0:T(8,128)(2,1)S(1)}, u32[]{:S(2)}, u32[]{:S(2)}) collective-permute-start(bf16[1,1,48,384]{3,2,1,0:T(8,128)(2,1)S(1)} %get-tuple-element.192), channel_id=1, source_target_pairs={{0,12},{1,13},{2,14},{3,15},{4,8},{5,9},{6,10},{7,11},{8,4},{9,5},... | collective-permute-start | bytes 110600 | tf_op jit(solution)/shard_map/ppermute | solution.py:96
  1292.3 15.1 collective-permute-start.62
  1305.7 31.9 %collective-permute-start.91 = (bf16[8,1,192,384]{3,2,1,0:T(8,128)(2,1)}, bf16[8,1,192,384]{3,2,1,0:T(8,128)(2,1)}, u32[]{:S(2)}, u32[]{:S(2)}) collective-permute-start(bf16[8,1,192,384]{3,2,1,0:T(8,128)(2,1)} %slice.787), channel_id=1, source_target_pairs={{0,2},{1,3},{2,0},{3,1},{4,6},{5,7},{6,4},{7,5},{8,10},{9,11},{10,... | collective-permute-start | bytes 3538952 | tf_op jit(solution)/shard_map/ppermute | solution.py:96
  1312.0 39.8 %collective-permute-start.82 = (bf16[4,512,384]{2,1,0:T(8,128)(2,1)}, bf16[4,512,384]{2,1,0:T(8,128)(2,1)}, u32[]{:S(2)}, u32[]{:S(2)}) collective-permute-start(bf16[4,512,384]{2,1,0:T(8,128)(2,1)} %pad_maximum_fusion.9), channel_id=1, source_target_pairs={{0,16},{16,0},{1,17},{17,1},{2,18},{18,2},{3,19},{19,3},{4,20},{20... | collective-permute-start | bytes 4718600 | tf_op jit(solution)/shard_map/ppermute | solution.py:99
  1312.5 60.7 %collective-permute-start.74 = (bf16[4,512,384]{2,1,0:T(8,128)(2,1)}, bf16[4,512,384]{2,1,0:T(8,128)(2,1)S(1)}, u32[]{:S(2)}, u32[]{:S(2)}) collective-permute-start(bf16[4,512,384]{2,1,0:T(8,128)(2,1)} %pad_maximum_fusion.7), channel_id=1, source_target_pairs={{0,16},{16,0},{1,17},{17,1},{2,18},{18,2},{3,19},{19,3},{4,20},{20... | collective-permute-start | bytes 4718600 | tf_op jit(solution)/shard_map/ppermute | solution.py:99
  1318.8 21.9 %collective-permute-start.42 = (bf16[3,512,384]{2,1,0:T(8,128)(2,1)}, bf16[3,512,384]{2,1,0:T(8,128)(2,1)}, u32[]{:S(2)}, u32[]{:S(2)}) collective-permute-start(bf16[3,512,384]{2,1,0:T(8,128)(2,1)} %pad_maximum_fusion.16), channel_id=1, source_target_pairs={{0,16},{16,0},{1,17},{17,1},{2,18},{18,2},{3,19},{19,3},{4,20},{20... | collective-permute-start | bytes 3538952 | tf_op jit(solution)/shard_map/ppermute | solution.py:99
  1334.7 48.7 %collective-permute-start.99 = (bf16[8,1,192,384]{3,2,1,0:T(8,128)(2,1)}, bf16[8,1,192,384]{3,2,1,0:T(8,128)(2,1)}, u32[]{:S(2)}, u32[]{:S(2)}) collective-permute-start(bf16[8,1,192,384]{3,2,1,0:T(8,128)(2,1)} %slice.795), channel_id=1, source_target_pairs={{0,2},{1,3},{2,0},{3,1},{4,6},{5,7},{6,4},{7,5},{8,10},{9,11},{10,... | collective-permute-start | bytes 3538952 | tf_op jit(solution)/shard_map/ppermute | solution.py:96
  1337.6 34.3 %collective-permute-start.73 = (bf16[512,768]{1,0:T(8,128)(2,1)S(1)}, bf16[512,768]{1,0:T(8,128)(2,1)}, u32[]{:S(2)}, u32[]{:S(2)}) collective-permute-start(bf16[512,768]{1,0:T(8,128)(2,1)S(1)} %copy-done.30), channel_id=1, source_target_pairs={{0,16},{16,0},{1,17},{17,1},{2,18},{18,2},{3,19},{19,3},{4,20},{20... | collective-permute-start | bytes 2359304 | tf_op jit(solution)/shard_map/ppermute | solution.py:99
  1340.7 44.8 %collective-permute-start.92 = (bf16[4,1,192,384]{3,2,1,0:T(8,128)(2,1)}, bf16[4,1,192,384]{3,2,1,0:T(8,128)(2,1)}, u32[]{:S(2)}, u32[]{:S(2)}) collective-permute-start(bf16[4,1,192,384]{3,2,1,0:T(8,128)(2,1)} %slice.789), channel_id=1, source_target_pairs={{0,1},{1,0},{2,3},{3,2},{4,5},{5,4},{6,7},{7,6},{8,9},{9,8},{10,11... | collective-permute-start | bytes 1769480 | tf_op jit(solution)/shard_map/ppermute | solution.py:96
  1351.7 38.6 %collective-permute-start.51 = (bf16[8,3,48,384]{3,2,1,0:T(8,128)(2,1)}, bf16[8,3,48,384]{3,2,1,0:T(8,128)(2,1)}, u32[]{:S(2)}, u32[]{:S(2)}) collective-permute-start(bf16[8,3,48,384]{3,2,1,0:T(8,128)(2,1)} %slice.725), channel_id=1, source_target_pairs={{0,2},{1,3},{2,0},{3,1},{4,6},{5,7},{6,4},{7,5},{8,10},{9,11},{10,... | collective-permute-start | bytes 2654216 | tf_op jit(solution)/shard_map/ppermute | solution.py:96
  1371.9 33.6 %collective-permute-start.43 = (bf16[8,3,48,384]{3,2,1,0:T(8,128)(2,1)}, bf16[8,3,48,384]{3,2,1,0:T(8,128)(2,1)}, u32[]{:S(2)}, u32[]{:S(2)}) collective-permute-start(bf16[8,3,48,384]{3,2,1,0:T(8,128)(2,1)} %slice.711), channel_id=1, source_target_pairs={{0,2},{1,3},{2,0},{3,1},{4,6},{5,7},{6,4},{7,5},{8,10},{9,11},{10,... | collective-permute-start | bytes 2654216 | tf_op jit(solution)/shard_map/ppermute | solution.py:96
  1373.1 91.8 %collective-permute-start.83 = (bf16[8,4,48,384]{3,2,1,0:T(8,128)(2,1)}, bf16[8,4,48,384]{3,2,1,0:T(8,128)(2,1)}, u32[]{:S(2)}, u32[]{:S(2)}) collective-permute-start(bf16[8,4,48,384]{3,2,1,0:T(8,128)(2,1)} %slice.771), channel_id=1, source_target_pairs={{0,2},{1,3},{2,0},{3,1},{4,6},{5,7},{6,4},{7,5},{8,10},{9,11},{10,... | collective-permute-start | bytes 3538952 | tf_op jit(solution)/shard_map/ppermute | solution.py:96
  1389.3 14.1 collective-permute-start.94
  1390.4 13.7 collective-permute-start.93
  1395.6 72.0 %collective-permute-start.75 = (bf16[8,4,48,384]{3,2,1,0:T(8,128)(2,1)S(1)}, bf16[8,4,48,384]{3,2,1,0:T(8,128)(2,1)S(1)}, u32[]{:S(2)}, u32[]{:S(2)}) collective-permute-start(bf16[8,4,48,384]{3,2,1,0:T(8,128)(2,1)S(1)} %slice.755), channel_id=1, source_target_pairs={{0,2},{1,3},{2,0},{3,1},{4,6},{5,7},{6,4},{7,5},{8,10},{9,11},{10,... | collective-permute-start | bytes 3538952 | tf_op jit(solution)/shard_map/ppermute | solution.py:96
  1403.4 29.3 %collective-permute-start.100 = (bf16[4,1,192,384]{3,2,1,0:T(8,128)(2,1)S(1)}, bf16[4,1,192,384]{3,2,1,0:T(8,128)(2,1)S(1)}, u32[]{:S(2)}, u32[]{:S(2)}) collective-permute-start(bf16[4,1,192,384]{3,2,1,0:T(8,128)(2,1)S(1)} %slice.797), channel_id=1, source_target_pairs={{0,1},{1,0},{2,3},{3,2},{4,5},{5,4},{6,7},{7,6},{8,9},{9,8},{10,11... | collective-permute-start | bytes 1769480 | tf_op jit(solution)/shard_map/ppermute | solution.py:96
  1404.0 16.4 %collective-permute-start.52 = (bf16[4,3,48,384]{3,2,1,0:T(8,128)(2,1)S(1)}, bf16[4,3,48,384]{3,2,1,0:T(8,128)(2,1)S(1)}, u32[]{:S(2)}, u32[]{:S(2)}) collective-permute-start(bf16[4,3,48,384]{3,2,1,0:T(8,128)(2,1)S(1)} %slice.727), channel_id=1, source_target_pairs={{0,1},{1,0},{2,3},{3,2},{4,5},{5,4},{6,7},{7,6},{8,9},{9,8},{10,11... | collective-permute-start | bytes 1327112 | tf_op jit(solution)/shard_map/ppermute | solution.py:96
  1407.1 18.1 %collective-permute-start.44 = (bf16[4,3,48,384]{3,2,1,0:T(8,128)(2,1)S(1)}, bf16[4,3,48,384]{3,2,1,0:T(8,128)(2,1)S(1)}, u32[]{:S(2)}, u32[]{:S(2)}) collective-permute-start(bf16[4,3,48,384]{3,2,1,0:T(8,128)(2,1)S(1)} %slice.713), channel_id=1, source_target_pairs={{0,1},{1,0},{2,3},{3,2},{4,5},{5,4},{6,7},{7,6},{8,9},{9,8},{10,11... | collective-permute-start | bytes 1327112 | tf_op jit(solution)/shard_map/ppermute | solution.py:96
  1420.6 12.4 collective-permute-start.55
  1425.2 13.6 collective-permute-start.54
  1438.8 15.7 %collective-permute-start.46 = (bf16[1,3,48,384]{3,2,1,0:T(8,128)(2,1)S(1)}, bf16[1,3,48,384]{3,2,1,0:T(8,128)(2,1)S(1)}, u32[]{:S(2)}, u32[]{:S(2)}) collective-permute-start(bf16[1,3,48,384]{3,2,1,0:T(8,128)(2,1)S(1)} %get-tuple-element.163), channel_id=1, source_target_pairs={{0,8},{1,9},{2,10},{3,11},{4,12},{5,13},{6,14},{7,15},{8,0},{9,1},... | collective-permute-start | bytes 331784 | tf_op jit(solution)/shard_map/ppermute | solution.py:96
  1439.4 15.1 %collective-permute-start.45 = (bf16[1,3,48,384]{3,2,1,0:T(8,128)(2,1)S(1)}, bf16[1,3,48,384]{3,2,1,0:T(8,128)(2,1)S(1)}, u32[]{:S(2)}, u32[]{:S(2)}) collective-permute-start(bf16[1,3,48,384]{3,2,1,0:T(8,128)(2,1)S(1)} %get-tuple-element.161), channel_id=1, source_target_pairs={{0,4},{1,5},{2,6},{3,7},{4,0},{5,1},{6,2},{7,3},{8,12},{9,13},{10,... | collective-permute-start | bytes 331784 | tf_op jit(solution)/shard_map/ppermute | solution.py:96
  1441.8 12.8 collective-permute-start.103
  1467.9 15.1 %collective-permute-start.76 = (bf16[4,4,48,384]{3,2,1,0:T(8,128)(2,1)S(1)}, bf16[4,4,48,384]{3,2,1,0:T(8,128)(2,1)S(1)}, u32[]{:S(2)}, u32[]{:S(2)}) collective-permute-start(bf16[4,4,48,384]{3,2,1,0:T(8,128)(2,1)S(1)} %slice.757), channel_id=1, source_target_pairs={{0,1},{1,0},{2,3},{3,2},{4,5},{5,4},{6,7},{7,6},{8,9},{9,8},{10,11... | collective-permute-start | bytes 1769480 | tf_op jit(solution)/shard_map/ppermute | solution.py:96
  1477.0 22.3 %collective-permute-start.86 = (bf16[1,4,48,384]{3,2,1,0:T(8,128)(2,1)S(1)}, bf16[1,4,48,384]{3,2,1,0:T(8,128)(2,1)S(1)}, u32[]{:S(2)}, u32[]{:S(2)}) collective-permute-start(bf16[1,4,48,384]{3,2,1,0:T(8,128)(2,1)S(1)} %get-tuple-element.156), channel_id=1, source_target_pairs={{0,8},{1,9},{2,10},{3,11},{4,12},{5,13},{6,14},{7,15},{8,0},{9,1},... | collective-permute-start | bytes 442376 | tf_op jit(solution)/shard_map/ppermute | solution.py:96
  1478.7 20.6 %collective-permute-start.85 = (bf16[1,4,48,384]{3,2,1,0:T(8,128)(2,1)S(1)}, bf16[1,4,48,384]{3,2,1,0:T(8,128)(2,1)S(1)}, u32[]{:S(2)}, u32[]{:S(2)}) collective-permute-start(bf16[1,4,48,384]{3,2,1,0:T(8,128)(2,1)S(1)} %get-tuple-element.154), channel_id=1, source_target_pairs={{0,4},{1,5},{2,6},{3,7},{4,0},{5,1},{6,2},{7,3},{8,12},{9,13},{10,... | collective-permute-start | bytes 442376 | tf_op jit(solution)/shard_map/ppermute | solution.py:96
  1483.2 16.2 %collective-permute-start.79 = (bf16[1,4,48,384]{3,2,1,0:T(8,128)(2,1)S(1)}, bf16[1,4,48,384]{3,2,1,0:T(8,128)(2,1)S(1)}, u32[]{:S(2)}, u32[]{:S(2)}) collective-permute-start(bf16[1,4,48,384]{3,2,1,0:T(8,128)(2,1)S(1)} %get-tuple-element.152), channel_id=1, source_target_pairs={{0,12},{1,13},{2,14},{3,15},{4,8},{5,9},{6,10},{7,11},{8,4},{9,5},... | collective-permute-start | bytes 442376 | tf_op jit(solution)/shard_map/ppermute | solution.py:96
  1483.3 20.9 %collective-permute-start.78 = (bf16[1,4,48,384]{3,2,1,0:T(8,128)(2,1)S(1)}, bf16[1,4,48,384]{3,2,1,0:T(8,128)(2,1)S(1)}, u32[]{:S(2)}, u32[]{:S(2)}) collective-permute-start(bf16[1,4,48,384]{3,2,1,0:T(8,128)(2,1)S(1)} %get-tuple-element.153), channel_id=1, source_target_pairs={{0,8},{1,9},{2,10},{3,11},{4,12},{5,13},{6,14},{7,15},{8,0},{9,1},... | collective-permute-start | bytes 442376 | tf_op jit(solution)/shard_map/ppermute | solution.py:96
  1485.6 18.6 %collective-permute-start.77 = (bf16[1,4,48,384]{3,2,1,0:T(8,128)(2,1)S(1)}, bf16[1,4,48,384]{3,2,1,0:T(8,128)(2,1)S(1)}, u32[]{:S(2)}, u32[]{:S(2)}) collective-permute-start(bf16[1,4,48,384]{3,2,1,0:T(8,128)(2,1)S(1)} %get-tuple-element.151), channel_id=1, source_target_pairs={{0,4},{1,5},{2,6},{3,7},{4,0},{5,1},{6,2},{7,3},{8,12},{9,13},{10,... | collective-permute-start | bytes 442376 | tf_op jit(solution)/shard_map/ppermute | solution.py:96
  (192 other events, 3669.1 us)

commit v2 on v1

v2 whole, which is shorter than its diff:
```python
import functools

import jax
import jax.numpy as jnp
import numpy as np
from jax import lax
from jax.experimental import pallas as pl
from jax.experimental.pallas import tpu as pltpu
from jax.sharding import PartitionSpec as P

HEADS = 12
HD = 64
LAYERS = 2
LEN_UNIT = 64


NORM_EPSILON = 1e-05
NEG_LARGE = -1e30
SCORE_SCALE = 0.125


def slot_layout(valid_groups):
    row_index = jnp.arange(8 * LEN_UNIT, dtype=jnp.int32)
    slot_index = (
        (row_index >= 3 * LEN_UNIT).astype(jnp.int32)
        + (row_index >= 5 * LEN_UNIT).astype(jnp.int32)
        + (row_index >= 7 * LEN_UNIT).astype(jnp.int32)
    )
    slot_start = jnp.where(
        slot_index == 0,
        0,
        jnp.where(
            slot_index == 1, 3 * LEN_UNIT, jnp.where(slot_index == 2, 5 * LEN_UNIT, 7 * LEN_UNIT)
        ),
    ).astype(jnp.int32)
    offset = row_index - slot_start
    slot_pick = (slot_index[:, None] == jnp.arange(4, dtype=jnp.int32)[None, :]).astype(jnp.int32)
    limits = jnp.sum(valid_groups[:, None, :] * slot_pick[None], -1)
    row_live = offset[None, :] < limits
    same_slot = slot_index[:, None] == slot_index[None, :]
    permitted = same_slot[None] & row_live[:, None, :]
    return (row_live, permitted)


def normed(values_in, gain_ln, bias_ln):
    row_mean = jnp.mean(values_in, -1, keepdims=True)
    centred = values_in - row_mean
    row_var = jnp.mean(centred * centred, -1, keepdims=True)
    return centred * lax.rsqrt(row_var + NORM_EPSILON) * gain_ln + bias_ln


def exact_gelu(values_in):
    return jax.nn.gelu(values_in, approximate=False)


CHUNK = 384


class Net:
    def __init__(self, mesh):
        self.shards = mesh.shape["fsdp"]
        self.replicas = mesh.shape["rep"]
        assert self.replicas % 2 == 0 and self.shards & (self.shards - 1) == 0
        sizes, left = [], self.shards
        while left > 1:
            sizes.append(4 if left % 4 == 0 and (left != 4 or self.shards != 16) else 2)
            left //= sizes[-1]
        strides = [int(np.prod(sizes[place + 1 :])) for place in range(len(sizes))]
        first = tuple(range(len(sizes)))
        if len(sizes) > 2 and sizes[-1] == sizes[-2]:
            orders = (first[:-2] + (first[-1], first[-2]), first)
        elif len(sizes) > 2 and sizes[0] == sizes[1]:
            orders = (first[::-1], first[:1:-1] + first[:2])
        else:
            orders = (first, first)
        self.sizes = [sizes[digit] for digit in orders[0]]
        self.steps = [[strides[digit] for digit in order] for order in orders]
        flips = np.zeros((2, self.shards), np.int32)
        for core in range(2):
            for slot in range(self.shards):
                left = slot
                for size, step in zip(self.sizes, self.steps[core]):
                    flips[core, slot] ^= (left % size) * step
                    left //= size
        self.flips = flips
        self.slots = np.argsort(flips, axis=1).astype(np.int32)

    def pairs(self, stage, offset):
        return [
            (rep * self.shards + shard, rep * self.shards + (shard ^ (offset * self.steps[rep % 2][stage])))
            for rep in range(self.replicas)
            for shard in range(self.shards)
        ]

    def trade(self, value, stage, offset):
        return lax.ppermute(value, ("rep", "fsdp"), self.pairs(stage, offset))

    def twin(self, value):
        return lax.ppermute(value, "rep", [(rep, rep ^ 1) for rep in range(self.replicas)])

    def widen(self, value, stage):
        received = [self.trade(value, stage, offset) for offset in range(1, self.sizes[stage])]
        return jnp.concatenate([value, *received], 0)

    def narrow(self, value, stage, low):
        parts = value.reshape(self.sizes[stage], -1, *value.shape[1:])
        total = parts[0].astype(jnp.float32)
        for offset in range(1, self.sizes[stage]):
            total = total + self.trade(parts[offset], stage, offset).astype(jnp.float32)
        return total.astype(low)

    def reduce(self, value, low):
        for stage in reversed(range(len(self.sizes))):
            value = self.narrow(value, stage, low)
        return self.across(value[0], low)

    def across(self, value, low):
        others = self.replicas // 2
        if others == 1:
            return value
        total = value.astype(jnp.float32)
        for shift in range(1, others):
            pairs = [(rep, (rep + 2 * shift) % self.replicas) for rep in range(self.replicas)]
            total = total + lax.ppermute(value, "rep", pairs).astype(jnp.float32)
        return total.astype(low)


def own_chunks(matrix, core):
    count = matrix.shape[1] // (2 * CHUNK)
    return jnp.stack(
        [
            lax.dynamic_slice_in_dim(matrix, (2 * part + core) * CHUNK, CHUNK, axis=1)
            for part in range(count)
        ]
    )


def join_chunks(mine, other, core):
    even = jnp.where(core == 0, mine, other)
    odd = jnp.where(core == 0, other, mine)
    return jnp.concatenate([piece for part in range(mine.shape[0]) for piece in (even[part], odd[part])], 1)


def assemble(slots, core, mine, other, start, count):
    shards, _, rows = mine.shape[:3]

    def body(slots_ref, core_ref, mine_ref, other_ref, out_ref):
        def place(half):
            def _():
                for row in range(shards):
                    out_ref[row, :, half * CHUNK : (half + 1) * CHUNK] = mine_ref[slots_ref[0, row], 0]
                    out_ref[row, :, (1 - half) * CHUNK : (2 - half) * CHUNK] = other_ref[slots_ref[1, row], 0]

            return _

        pl.when(core_ref[0] == 0)(place(0))
        pl.when(core_ref[0] == 1)(place(1))

    block = pl.BlockSpec((shards, 1, rows, CHUNK), lambda k: (0, start + k, 0, 0))
    out = pl.pallas_call(
        body,
        grid=(count,),
        out_shape=jax.ShapeDtypeStruct((shards, rows, 2 * count * CHUNK), mine.dtype),
        in_specs=[pl.BlockSpec(memory_space=pltpu.SMEM)] * 2 + [block, block],
        out_specs=pl.BlockSpec((shards, rows, 2 * CHUNK), lambda k: (0, 0, k)),
        name="assemble",
    )(slots, core.reshape(1), mine, other)
    return out.reshape(shards * rows, -1)


def weight_terms(slots, left, left_twin, right, right_twin, shards):
    tokens, width = left.shape
    parts = right.shape[0]
    rows = width // shards
    tile = 384
    per_tile = tile // rows

    def body(slots_ref, left_ref, left_twin_ref, right_ref, right_twin_ref, out_ref):
        tile_index = pl.program_id(0)
        left_here, left_there = left_ref[...], left_twin_ref[...]
        for part in range(parts):
            total = outer_sum(left_here, right_ref[part]) + outer_sum(left_there, right_twin_ref[part])
            total = total.astype(jnp.bfloat16)
            for block in range(per_tile):
                slot = slots_ref[tile_index * per_tile + block]
                out_ref[slot, part] = total[block * rows : (block + 1) * rows]

    return pl.pallas_call(
        body,
        grid=(width // tile,),
        out_shape=jax.ShapeDtypeStruct((shards, parts, rows, CHUNK), jnp.bfloat16),
        in_specs=[
            pl.BlockSpec(memory_space=pltpu.SMEM),
            pl.BlockSpec((tokens, tile), lambda i: (0, i)),
            pl.BlockSpec((tokens, tile), lambda i: (0, i)),
            pl.BlockSpec((parts, tokens, CHUNK), lambda i: (0, 0, 0)),
            pl.BlockSpec((parts, tokens, CHUNK), lambda i: (0, 0, 0)),
        ],
        out_specs=pl.BlockSpec((shards, parts, rows, CHUNK), lambda i: (0, 0, 0, 0)),
        name="weight_terms",
    )(slots, left, left_twin, right, right_twin)


def outer_sum(left, right):
    return lax.dot_general(
        left, right, (((0,), (0,)), ((), ())), preferred_element_type=jnp.float32
    )


def times_transposed(left, right):
    return lax.dot_general(
        left, right, (((1,), (1,)), ((), ())), preferred_element_type=jnp.float32
    )


def split_heads(qkv_low, permitted):
    group_count = permitted.shape[0]
    group_rows = permitted.shape[1]
    split_qkv = qkv_low.reshape(group_count, group_rows, 3, HEADS, HD)
    return (split_qkv[:, :, 0], split_qkv[:, :, 1], split_qkv[:, :, 2])


def raw_scores(queries, key_rows, permitted):
    scores = (
        jnp.einsum("gqhd,gkhd->ghqk", queries, key_rows, preferred_element_type=jnp.float32)
        * SCORE_SCALE
    )
    return jnp.where(permitted[:, None], scores, NEG_LARGE)


def attend(qkv_low, permitted):
    queries, key_rows, value_rows = split_heads(qkv_low, permitted)
    scores = raw_scores(queries, key_rows, permitted)
    row_top = jnp.max(scores, -1, keepdims=True)
    row_total = jnp.sum(jnp.exp(scores - row_top), -1, keepdims=True)
    log_total = row_top + jnp.log(row_total)
    probs = jnp.exp(scores - log_total).astype(jnp.bfloat16)
    context = jnp.einsum("ghqk,gkhd->gqhd", probs, value_rows, preferred_element_type=jnp.float32)
    return (context.reshape(qkv_low.shape[0], HEADS * HD).astype(jnp.bfloat16), log_total)


def attend_back(qkv_low, log_total, d_context, permitted):
    queries, key_rows, value_rows = split_heads(qkv_low, permitted)
    scores = raw_scores(queries, key_rows, permitted)
    probs = jnp.exp(scores - log_total)
    probs_low = probs.astype(jnp.bfloat16)
    d_heads = d_context.reshape(queries.shape)
    d_value = jnp.einsum("ghqk,gqhd->gkhd", probs_low, d_heads, preferred_element_type=jnp.float32)
    d_probs = jnp.einsum("gqhd,gkhd->ghqk", d_heads, value_rows, preferred_element_type=jnp.float32)
    d_scores = probs * (d_probs - jnp.sum(probs * d_probs, -1, keepdims=True))
    d_low = d_scores.astype(jnp.bfloat16)
    d_query = (
        jnp.einsum("ghqk,gkhd->gqhd", d_low, key_rows, preferred_element_type=jnp.float32)
        * SCORE_SCALE
    )
    d_key = (
        jnp.einsum("ghqk,gqhd->gkhd", d_low, queries, preferred_element_type=jnp.float32)
        * SCORE_SCALE
    )
    joined = jnp.stack([d_query, d_key, d_value], 2)
    return joined.reshape(qkv_low.shape[0], 3 * HEADS * HD)


def unpack(vector_row, model_width):
    pieces = [
        vector_row[segment * model_width : (segment + 1) * model_width] for segment in range(8)
    ]
    return (pieces, vector_row[8 * model_width :])


GROUPS = (((0, 0),), ((0, 1), (0, 2)), ((0, 3),), ((1, 0), (1, 1)), ((1, 2),), ((1, 3),))


class Gather:
    def __init__(self, net, blocks):
        self.net = net
        self.state = [block[None] for block in blocks]
        self.twins = [None] * len(blocks)
        self.turn_index = 0

    def turn(self, values):
        stages, groups, turn = len(self.net.sizes), len(self.state), self.turn_index
        busy = [(turn - stage, stage) for stage in range(stages + 1) if 0 <= turn - stage < groups]
        for group, stage in busy:
            if stage < stages:
                self.state[group] = self.net.widen(self.state[group], stage)
            else:
                self.twins[group] = self.net.twin(self.state[group])
        nexts = [turn + 1 - stage for stage in range(stages + 1) if 0 <= turn + 1 - stage < groups]
        done = [group for group, stage in busy if stage == stages]
        self.turn_index += 1
        held = lax.optimization_barrier(
            tuple([self.state[group] for group in nexts] + [self.twins[group] for group in done] + list(values))
        )
        for group, value in zip(nexts, held):
            self.state[group] = value
        for group, value in zip(done, held[len(nexts) :]):
            self.twins[group] = value
        return held[len(nexts) + len(done) :]


class Reduce:
    def __init__(self, net):
        self.net = net
        self.pending = {}
        self.owned = {}

    def push(self, key, value):
        self.pending[key] = [len(self.net.sizes) - 1, value]

    def turn(self, values):
        for key, entry in self.pending.items():
            stage, value = entry
            if stage >= 0:
                value = self.net.narrow(value, stage, jnp.bfloat16)
            else:
                mine = self.net.across(value[0], jnp.bfloat16)
                self.owned[key] = (mine, self.net.twin(mine))
            self.pending[key] = [stage - 1, value]
        self.pending = {key: entry for key, entry in self.pending.items() if entry[0] >= -1}
        keys = list(self.pending)
        held = lax.optimization_barrier(tuple([self.pending[key][1] for key in keys] + list(values)))
        for key, value in zip(keys, held):
            self.pending[key][1] = value
        return held[len(keys) :]


def shards(net, tokens, valid, qkv_weight, out_weight, up_weight, down_weight, vectors, cotangent):
    count = net.shards
    core = (lax.axis_index("rep") % 2).astype(jnp.int32)
    place = lax.axis_index("fsdp").astype(jnp.int32)
    flips = jnp.asarray(net.flips)
    own_flips = jnp.where(core == 0, flips[0], flips[1])
    twin_flips = jnp.where(core == 0, flips[1], flips[0])
    places = jnp.stack([own_flips ^ place, twin_flips ^ place])
    numbers = jnp.arange(count, dtype=jnp.int32)
    slots = jnp.sum(
        jnp.where(places[:, None, :] == numbers[None, :, None], numbers[None, None, :], 0), 2
    )
    weight_inputs = (qkv_weight, out_weight, up_weight, down_weight)

    blocks, starts = [], {}
    for group in GROUPS:
        pieces, start = [], 0
        for level, kind in group:
            pieces.append(own_chunks(weight_inputs[kind][level].astype(jnp.bfloat16), core))
            starts[level, kind] = (start, pieces[-1].shape[0])
            start += pieces[-1].shape[0]
        blocks.append(jnp.concatenate(pieces, 0))
    gather = Gather(net, blocks)
    weights = {}

    def get(group):
        for level, kind in GROUPS[group]:
            start, parts = starts[level, kind]
            weights[level, kind] = assemble(
                slots, core, gather.state[group], gather.twins[group], start, parts
            )

    vector_blocks = vectors[None]
    for stage in range(len(net.sizes)):
        vector_blocks = net.widen(vector_blocks, stage)
        (vector_blocks,) = gather.turn((vector_blocks,))
    vector_all = jnp.take(vector_blocks, slots[0], axis=0).transpose(1, 0, 2).reshape(LAYERS, -1)
    gather.turn(())

    group_count = valid.shape[0] // 4
    row_live, permitted = slot_layout(valid.reshape(group_count, 4))
    row_mask = row_live.reshape(-1, 1).astype(jnp.float32)
    hidden = tokens.astype(jnp.float32)
    model_width = hidden.shape[1]
    kept = []
    for level in range(LAYERS):
        pieces, bias_u = unpack(vector_all[level], model_width)
        bias_q, bias_v, bias_o, gain_a, shift_a, bias_d, gain_b, shift_b = pieces
        h_low = hidden.astype(jnp.bfloat16)
        get(3 * level)
        qkv_low = (
            jnp.dot(h_low, weights[level, 0], preferred_element_type=jnp.float32)
            + jnp.concatenate([bias_q, jnp.zeros_like(bias_q), bias_v])
        ).astype(jnp.bfloat16)
        context, log_total = attend(qkv_low, permitted)
        (context,) = gather.turn((context,))
        if level == 0:
            get(1)
        first_sum = hidden + (jnp.dot(context, weights[level, 1], preferred_element_type=jnp.float32) + bias_o)
        first = normed(first_sum, gain_a, shift_a)
        first_low = first.astype(jnp.bfloat16)
        if level == 1:
            get(4)
        inner = jnp.dot(first_low, weights[level, 2], preferred_element_type=jnp.float32) + bias_u
        active = exact_gelu(inner).astype(jnp.bfloat16)
        (active,) = gather.turn((active,))
        get(3 * level + 2)
        mixed_b = jnp.dot(active, weights[level, 3], preferred_element_type=jnp.float32) + bias_d
        second_sum = first + mixed_b
        hidden = normed(second_sum, gain_b, shift_b)
        (hidden,) = gather.turn((hidden,))
        kept.append((h_low, qkv_low, log_total, context, first_sum, first_low, inner, active, second_sum))
    layer_out = (hidden * row_mask).astype(jnp.bfloat16)

    reduce = Reduce(net)
    d_hidden = cotangent.astype(jnp.float32) * row_mask
    d_vectors = [None] * LAYERS
    twins = {}

    def terms(level, kind, left, right):
        sent = net.twin(own_chunks(right, 1 - core))
        return weight_terms(slots[0], left, net.twin(left), own_chunks(right, core), sent, count)

    for level in reversed(range(LAYERS)):
        h_low, qkv_low, log_total, context, first_sum, first_low, inner, active, second_sum = kept[level]
        pieces, bias_u = unpack(vector_all[level], model_width)
        bias_q, bias_v, bias_o, gain_a, shift_a, bias_d, gain_b, shift_b = pieces
        unused_b, norm_b_back = jax.vjp(normed, second_sum, gain_b, shift_b)
        d_second_sum, d_gain_b, d_shift_b = norm_b_back(d_hidden)
        d_mixed_b = d_second_sum.astype(jnp.bfloat16)
        d_bias_d = jnp.sum(d_mixed_b, 0, dtype=jnp.float32)
        d_active = times_transposed(d_mixed_b, weights[level, 3])
        unused_g, gelu_back = jax.vjp(exact_gelu, inner)
        d_inner = gelu_back(d_active)[0].astype(jnp.bfloat16)
        full = terms(level, 3, active, d_mixed_b)
        full, d_inner, d_second_sum = reduce.turn((full, d_inner, d_second_sum))
        reduce.push((level, 3), full)

        d_bias_u = jnp.sum(d_inner, 0, dtype=jnp.float32)
        d_first = d_second_sum + times_transposed(d_inner, weights[level, 2])
        unused_a, norm_a_back = jax.vjp(normed, first_sum, gain_a, shift_a)
        d_first_sum, d_gain_a, d_shift_a = norm_a_back(d_first)
        d_mixed_a = d_first_sum.astype(jnp.bfloat16)
        full = terms(level, 2, first_low, d_inner)
        full, d_mixed_a, d_first_sum = reduce.turn((full, d_mixed_a, d_first_sum))
        reduce.push((level, 2), full)

        d_bias_o = jnp.sum(d_mixed_a, 0, dtype=jnp.float32)
        d_context = times_transposed(d_mixed_a, weights[level, 1]).astype(jnp.bfloat16)
        d_qkv = attend_back(qkv_low, log_total, d_context, permitted).astype(jnp.bfloat16)
        full = terms(level, 1, context, d_mixed_a)
        full, d_qkv = reduce.turn((full, d_qkv))
        reduce.push((level, 1), full)

        d_bias_qkv = jnp.sum(d_qkv, 0, dtype=jnp.float32)
        d_hidden = d_first_sum + times_transposed(d_qkv, weights[level, 0])
        full = terms(level, 0, h_low, d_qkv)
        full, d_hidden = reduce.turn((full, d_hidden))
        reduce.push((level, 0), full)
        d_vectors[level] = jnp.concatenate(
            [
                d_bias_qkv[:model_width],
                d_bias_qkv[2 * model_width :],
                d_bias_o,
                d_gain_a,
                d_shift_a,
                d_bias_d,
                d_gain_b,
                d_shift_b,
                d_bias_u,
            ]
        ).reshape(count, -1)
    d_vector = jnp.stack(d_vectors, 1)
    d_vector = d_vector + net.twin(d_vector)
    vector_grad = net.reduce(jnp.take(d_vector, places[0], axis=0), jnp.float32)
    while reduce.pending:
        reduce.turn(())
    grads = [
        jnp.stack(
            [join_chunks(*reduce.owned[level, kind], core).astype(jnp.float32) for level in range(LAYERS)]
        )
        for kind in range(4)
    ]
    return (layer_out, d_hidden, *grads, vector_grad)


def solution(mesh):
    in_specs = (
        P(("rep", "fsdp"), None),
        P(("rep", "fsdp")),
        P(None, "fsdp", None),
        P(None, "fsdp", None),
        P(None, "fsdp", None),
        P(None, "fsdp", None),
        P(None, "fsdp"),
        P(("rep", "fsdp"), None),
    )
    out_specs = (
        P(("rep", "fsdp"), None),
        P(("rep", "fsdp"), None),
        P(None, "fsdp", None),
        P(None, "fsdp", None),
        P(None, "fsdp", None),
        P(None, "fsdp", None),
        P(None, "fsdp"),
    )
    net = Net(mesh)
    return jax.shard_map(functools.partial(shards, net), mesh=mesh, in_specs=in_specs, out_specs=out_specs, check_vma=False)
```

time: 1510 us -> 727 us (0.48)
  Pallas kernels: 918 us -> 87.7 us
  waiting for transfers between devices: 144 us -> 171 us
  other arithmetic: 99.4 us -> 116 us
    pallas_call x14 -> x16, Pallas kernels: 918 us -> 87.7 us  [the longest x8 52.6 us: weight_terms(): pl.pallas_call(body, grid=(width // tile,), out_shape=jax.ShapeDtypeStruc...]
    ppermute x80, waiting for transfers between devices: 141 us -> 168 us  [trade(): return lax.ppermute(value, ('rep', 'fsdp'), self.pairs(stage, offset))]
    concatenate x19 -> x21, other arithmetic: 30.3 us -> 22.2 us  [widen(): return jnp.concatenate([value, *received], 0)]
  transfers between devices with their start and end apart: 111 -> 111, of which waited for: 39 -> 43; matrix products, arithmetic and copies ran while one was open for 20% -> 42% of each run, Pallas kernels for 61% -> 9%
where the time goes in v2:
time: 727 us; the launch traced here: 720 us
  waiting for transfers between devices  171 us (24%)
  matrix products  161 us (22%)
  other arithmetic  116 us (16%)
  starting transfers between devices  109 us (15%)
  Pallas kernels  87.7 us (12%)
  local copies, waits for them, and re-layouts  72.4 us (10%)
    ppermute x80, waiting for transfers between devices, trade(): return lax.ppermute(value, ('rep', 'fsdp'), self.pairs(stage, offset))  168 us
    ppermute x80, starting transfers between devices, trade(): return lax.ppermute(value, ('rep', 'fsdp'), self.pairs(stage, offset))  106 us
    pallas_call x8, Pallas kernels, weight_terms(): pl.pallas_call(body, grid=(width // tile,), out_shape=jax.ShapeDtypeStruc...  52.6 us
    dot_general x8, matrix products, times_transposed(): lax.dot_general(left, right, (((1,), (1,)), ((), ())), preferred_element_...  41.9 us
    dot_general x2, matrix products, shards(): jnp.dot(first_low, weights[level, 2], preferred_element_type=jnp.float32)  39.8 us
    pallas_call x8, Pallas kernels, assemble(): pl.pallas_call(body, grid=(count,), out_shape=jax.ShapeDtypeStruct((shard...  35.1 us
    unnamed x317, local copies, waits for them, and re-layouts  29.6 us
    concatenate x21, other arithmetic, widen(): return jnp.concatenate([value, *received], 0)  22.2 us
  transfers between devices with their start and end apart: 111, of which 43 were waited for; matrix products, arithmetic and copies ran while one was open for 42% of the time, Pallas kernels for 9%

profile of v2, /device:TPU:0, one launch (start us, length us, event | category | flops | bytes accessed | tf_op | source)
XLA Modules:
  0.0 720.4 jit_solution(16052196612041385159)
XLA Ops:
  8.3 3.9 collective-permute-start.5
  14.1 6.5 collective-permute-done.2
  23.1 3.6 collective-permute-start.8
  30.5 6.4 collective-permute-done.7
  43.9 10.1 %collective-permute-done.16 = f32[8,2,576]{2,1,0:T(2,128)S(1)} collective-permute-done((f32[8,2,576]{2,1,0:T(2,128)S(1)}, f32[8,2,576]{2,1,0:T(2,128)S(1)}, u32[]{:S(2)}, u32[]{:S(2)}) %collective-permute-start.16) | collective-permute-done | bytes 36896 | tf_op jit(solution)/shard_map/ppermute | solution.py:96
  55.1 5.9 collective-permute-done.13
  63.4 3.8 collective-permute-start.17
  69.4 3.9 collective-permute-done.17
  77.7 3.4 collective-permute-done.18
  90.5 3.7 collective-permute-start.23
  96.9 5.0 assemble.8
  101.9 4.5 fusion.16
  113.1 5.1 convolution_convert_fusion.5
  122.5 3.3 pad_maximum_fusion.1.mine_ref
  125.8 5.3 assemble.10
  144.3 20.1 %multiply_convert_fusion.3 = (bf16[512,3072]{1,0:T(8,128)(2,1)}, f32[512,3072]{1,0:T(8,128)}, f32[512,3072]{1,0:T(8,128)}) fusion(f32[3072]{0:T(1024)S(1)} %copy-done.113, bf16[512,768]{1,0:T(8,128)(2,1)} %fusion.26.left_ref, bf16[768,3072]{1,0:T(8,128)(2,1)S(1)} %bitcast.291), kind=kOutput, calls=%fused_computation.37 | convolution fusion | flops 2519728128 | bytes 21245952 | tf_op jit(solution)/shard_map/dot_general | solution.py:391
  172.7 4.9 assemble.11
  179.6 6.0 fusion.82
  186.8 7.7 %collective-permute-done.35 = bf16[4,1,192,384]{3,2,1,0:T(8,128)(2,1)S(1)} collective-permute-done((bf16[4,1,192,384]{3,2,1,0:T(8,128)(2,1)}, bf16[4,1,192,384]{3,2,1,0:T(8,128)(2,1)S(1)}, u32[]{:S(2)}, u32[]{:S(2)}) %collective-permute-start.35) | collective-permute-done | bytes 589856 | tf_op jit(solution)/shard_map/ppermute | solution.py:96
  195.7 4.4 collective-permute-done.36
  201.8 4.8 assemble.12
  209.9 5.7 fusion.17
  226.0 4.0 convolution_convert_fusion.4
  230.0 8.0 %collective-permute-done.38 = bf16[8,1,192,384]{3,2,1,0:T(8,128)(2,1)} collective-permute-done((bf16[8,1,192,384]{3,2,1,0:T(8,128)(2,1)}, bf16[8,1,192,384]{3,2,1,0:T(8,128)(2,1)}, u32[]{:S(2)}, u32[]{:S(2)}) %collective-permute-start.38) | collective-permute-done | bytes 1179680 | tf_op jit(solution)/shard_map/ppermute | solution.py:96
  237.9 3.3 pad_maximum_fusion.4.mine_ref
  241.3 5.3 assemble.14
  252.7 19.7 %multiply_convert_fusion.2 = (bf16[512,3072]{1,0:T(8,128)(2,1)}, f32[512,3072]{1,0:T(8,128)}, f32[512,3072]{1,0:T(8,128)}) fusion(f32[3072]{0:T(1024)S(1)} %slice.702, bf16[512,768]{1,0:T(8,128)(2,1)} %fusion.27.left_ref, bf16[768,3072]{1,0:T(8,128)(2,1)S(1)} %bitcast.285), kind=kOutput, calls=%fused_computation.24 | convolution fusion | flops 2519728128 | bytes 21245952 | tf_op jit(solution)/shard_map/dot_general | solution.py:391
  273.8 5.0 assemble.15
  279.3 6.1 fusion.84
  290.9 8.1 %add_convert_fusion.1 = bf16[512,3072]{1,0:T(8,128)(2,1)} fusion(f32[512,3072]{1,0:T(8,128)S(1)} %copy-done.126, f32[512,3072]{1,0:T(8,128)} %get-tuple-element.339, f32[3072]{0:T(1024)S(1)} %slice.702, bf16[512,768]{1,0:T(8,128)(2,1)S(1)} %get-tuple-element.188, bf16[3072,768]{1,0:T(8,128)(2,1)S(1)} %bitcast.289), kind=kOutput, calls=%fused_computation.23 | convolution fusion | flops 2439512064 | bytes 21245952 | tf_op jit(solution)/shard_map/dot_general | solution.py:211
  300.7 9.5 %weight_terms.8 = bf16[16,1,192,384]{3,2,1,0:T(8,128)(2,1)} custom-call(s32[16]{0:T(128)} %slice_bitcast_fusion.18.slots_ref, bf16[512,3072]{1,0:T(8,128)(2,1)} %get-tuple-element.123.left_ref, bf16[512,3072]{1,0:T(8,128)(2,1)} %collective-permute-done.41.left_twin_ref, bf16[1,512,384]{2,1,0:T(8,128)(2,1)} %get-tuple-element.248.right_ref, ...), custom_call_target="tpu_custom_call" | custom-call | tf_op jit(solution)/shard_map/weight_terms/pallas_call | solution.py:188
  310.2 6.0 fusion.85
  325.4 11.3 %collective-permute-done.43 = bf16[8,1,192,384]{3,2,1,0:T(8,128)(2,1)S(1)} collective-permute-done((bf16[8,1,192,384]{3,2,1,0:T(8,128)(2,1)S(1)}, bf16[8,1,192,384]{3,2,1,0:T(8,128)(2,1)S(1)}, u32[]{:S(2)}, u32[]{:S(2)}) %collective-permute-start.43) | collective-permute-done | bytes 1179680 | tf_op jit(solution)/shard_map/ppermute | solution.py:96
  338.1 7.2 %weight_terms.9 = bf16[16,4,48,384]{3,2,1,0:T(8,128)(2,1)} custom-call(s32[16]{0:T(128)} %slice_bitcast_fusion.18.slots_ref, bf16[512,768]{1,0:T(8,128)(2,1)} %fusion.27.left_ref, bf16[512,768]{1,0:T(8,128)(2,1)} %collective-permute-done.44.left_twin_ref, bf16[4,512,384]{2,1,0:T(8,128)(2,1)} %pad_maximum_fusion.8.right_ref, ...), custom_call_target="tpu_custom_call" | custom-call | tf_op jit(solution)/shard_map/weight_terms/pallas_call | solution.py:188
  345.4 3.4 convolution_convert_fusion.1
  351.0 10.7 %multiply_reduce_fusion.1 = (f32[12,512]{1,0:T(8,128)S(1)}, f32[12,512,512]{1,2,0:T(8,128)}) fusion(f32[12,512,512]{1,2,0:T(8,128)} %copy-done.1, f32[12,512]{1,0:T(8,128)S(1)} %log_add_fusion, pred[512,512]{0,1:T(8,128)(4,1)S(1)} %compare_and_fusion, bf16[512,12,64]{0,2,1:T(8,128)(2,1)} %bitcast.298, bf16[1,512,3,12,64]{1,4,3,2,0:T(8,128)(2,1)S(1)} %bitcast.272), kind=kOutput, calls=%fused_computation.5 | convolution fusion | flops 418375680 | bytes 27058176 | tf_op jit(solution)/shard_map/gqhd,gkhd->ghqk/dot_general | solution.py:249
  361.7 6.5 fusion.20
  368.2 7.0 multiply_convert_fusion.1
  383.7 3.5 weight_terms.10
  387.2 9.6 %collective-permute-done.46 = bf16[4,1,192,384]{3,2,1,0:T(8,128)(2,1)S(1)} collective-permute-done((bf16[4,1,192,384]{3,2,1,0:T(8,128)(2,1)}, bf16[4,1,192,384]{3,2,1,0:T(8,128)(2,1)S(1)}, u32[]{:S(2)}, u32[]{:S(2)}) %collective-permute-start.46) | collective-permute-done | bytes 589856 | tf_op jit(solution)/shard_map/ppermute | solution.py:96
  403.8 3.3 fusion.86
  421.8 5.4 collective-permute-done.51
  434.0 3.5 collective-permute-done.53
  439.5 6.1 weight_terms.11
  454.5 8.5 %add_convert_fusion = bf16[512,3072]{1,0:T(8,128)(2,1)} fusion(f32[512,3072]{1,0:T(8,128)} %get-tuple-element.209, f32[512,3072]{1,0:T(8,128)} %get-tuple-element.332, f32[3072]{0:T(1024)S(1)} %copy-done.114, bf16[512,768]{1,0:T(8,128)(2,1)S(1)} %get-tuple-element.185, bf16[3072,768]{1,0:T(8,128)(2,1)S(1)} %bitcast.283), kind=kOutput, calls=%fused_computation.22 | convolution fusion | flops 2439512064 | bytes 21245952 | tf_op jit(solution)/shard_map/dot_general | solution.py:211
  465.9 4.7 collective-permute-done.57
  474.7 3.3 collective-permute-done.59
  478.1 9.8 %weight_terms.12 = bf16[16,1,192,384]{3,2,1,0:T(8,128)(2,1)} custom-call(s32[16]{0:T(128)} %slice_bitcast_fusion.18.slots_ref, bf16[512,3072]{1,0:T(8,128)(2,1)} %get-tuple-element.114.left_ref, bf16[512,3072]{1,0:T(8,128)(2,1)} %collective-permute-done.62.left_twin_ref, bf16[1,512,384]{2,1,0:T(8,128)(2,1)} %get-tuple-element.244.right_ref, ...), custom_call_target="tpu_custom_call" | custom-call | tf_op jit(solution)/shard_map/weight_terms/pallas_call | solution.py:188
  489.3 6.1 fusion.87
  499.8 3.3 collective-permute-start.64
  514.7 11.9 %collective-permute-done.67 = bf16[4,3,48,384]{3,2,1,0:T(8,128)(2,1)S(1)} collective-permute-done((bf16[4,3,48,384]{3,2,1,0:T(8,128)(2,1)S(1)}, bf16[4,3,48,384]{3,2,1,0:T(8,128)(2,1)S(1)}, u32[]{:S(2)}, u32[]{:S(2)}) %collective-permute-start.67) | collective-permute-done | bytes 442400 | tf_op jit(solution)/shard_map/ppermute | solution.py:96
  527.5 3.4 collective-permute-done.68
  533.4 7.2 %weight_terms.13 = bf16[16,4,48,384]{3,2,1,0:T(8,128)(2,1)} custom-call(s32[16]{0:T(128)} %slice_bitcast_fusion.18.slots_ref, bf16[512,768]{1,0:T(8,128)(2,1)} %fusion.26.left_ref, bf16[512,768]{1,0:T(8,128)(2,1)} %collective-permute-done.69.left_twin_ref, bf16[4,512,384]{2,1,0:T(8,128)(2,1)} %pad_maximum_fusion.10.right_ref, bf16[4,512,384]{2,1,0:T(8,128)(2,1)} %copy-done.56), custom_call_target="tpu_custom_call" | custom-call | tf_op jit(solution)/shard_map/weight_terms/pallas_call | solution.py:188
  540.7 3.3 convolution_convert_fusion
  546.3 11.4 %multiply_reduce_fusion = (f32[12,512]{1,0:T(8,128)S(1)}, f32[12,512,512]{1,2,0:T(8,128)}) fusion(f32[12,512,512]{1,2,0:T(8,128)} %copy-done, f32[12,512]{1,0:T(8,128)S(1)} %copy-done.79, pred[512,512]{0,1:T(8,128)(4,1)S(1)} %compare_and_fusion, bf16[512,12,64]{0,2,1:T(8,128)(2,1)} %bitcast.296, bf16[1,512,3,12,64]{1,4,3,2,0:T(8,128)(2,1)S(1)} %bitcast.277), kind=kOutput, calls=%fused_computation.3 | convolution fusion | flops 418375680 | bytes 27058176 | tf_op jit(solution)/shard_map/gqhd,gkhd->ghqk/dot_general | solution.py:249
  559.1 7.1 multiply_convert_fusion
  583.0 5.9 collective-permute-done.72
  591.0 4.5 collective-permute-done.73
  596.2 3.4 weight_terms.14
  659.5 4.0 collective-permute-done.80
  666.4 6.0 weight_terms.15
  683.5 6.5 collective-permute-done.86
  700.7 4.0 collective-permute-done.93
  712.3 5.4 collective-permute-done.95
  (741 shorter events, 317.1 us)
Async XLA Ops:
  2.2 11.9 %collective-permute-start = (bf16[1,3,48,384]{3,2,1,0:T(8,128)(2,1)S(1)}, bf16[1,3,48,384]{3,2,1,0:T(8,128)(2,1)S(1)}, u32[]{:S(2)}, u32[]{:S(2)}) collective-permute-start(bf16[1,3,48,384]{3,2,1,0:T(8,128)(2,1)S(1)} %maximum_bitcast_fusion.2), channel_id=1, source_target_pairs={{0,4},{1,5},{2,6},{3,7},{4,0},{5,1},{6,2},{7,3},{8,12},{9,13},{10,... | collective-permute-start | bytes 331784 | tf_op jit(solution)/shard_map/ppermute | solution.py:96
  20.6 16.4 %collective-permute-start.9 = (bf16[4,3,48,384]{3,2,1,0:T(8,128)(2,1)S(1)}, bf16[4,3,48,384]{3,2,1,0:T(8,128)(2,1)S(1)}, u32[]{:S(2)}, u32[]{:S(2)}) collective-permute-start(bf16[4,3,48,384]{3,2,1,0:T(8,128)(2,1)S(1)} %pad_maximum_fusion.27), channel_id=1, source_target_pairs={{0,1},{1,0},{2,3},{3,2},{4,5},{5,4},{6,7},{7,6},{8,9},{9,8},{10,11... | collective-permute-start | bytes 1327112 | tf_op jit(solution)/shard_map/ppermute | solution.py:96
  22.3 14.6 %collective-permute-start.7 = (bf16[1,5,48,384]{3,2,1,0:T(8,128)(2,1)S(1)}, bf16[1,5,48,384]{3,2,1,0:T(8,128)(2,1)S(1)}, u32[]{:S(2)}, u32[]{:S(2)}) collective-permute-start(bf16[1,5,48,384]{3,2,1,0:T(8,128)(2,1)S(1)} %bitcast.315), channel_id=1, source_target_pairs={{0,8},{1,9},{2,10},{3,11},{4,12},{5,13},{6,14},{7,15},{8,0},{9,1},... | collective-permute-start | bytes 552968 | tf_op jit(solution)/shard_map/ppermute | solution.py:96
  23.1 13.8 %collective-permute-start.8 = (bf16[1,5,48,384]{3,2,1,0:T(8,128)(2,1)S(1)}, bf16[1,5,48,384]{3,2,1,0:T(8,128)(2,1)S(1)}, u32[]{:S(2)}, u32[]{:S(2)}) collective-permute-start(bf16[1,5,48,384]{3,2,1,0:T(8,128)(2,1)S(1)} %bitcast.316), channel_id=1, source_target_pairs={{0,12},{1,13},{2,14},{3,15},{4,8},{5,9},{6,10},{7,11},{8,4},{9,5},... | collective-permute-start | bytes 552968 | tf_op jit(solution)/shard_map/ppermute | solution.py:96
  37.1 24.2 %collective-permute-start.15 = (bf16[8,3,48,384]{3,2,1,0:T(8,128)(2,1)S(1)}, bf16[8,3,48,384]{3,2,1,0:T(8,128)(2,1)S(1)}, u32[]{:S(2)}, u32[]{:S(2)}) collective-permute-start(bf16[8,3,48,384]{3,2,1,0:T(8,128)(2,1)S(1)} %pad_maximum_fusion.21), channel_id=1, source_target_pairs={{0,2},{1,3},{2,0},{3,1},{4,6},{5,7},{6,4},{7,5},{8,10},{9,11},{10,... | collective-permute-start | bytes 2654216 | tf_op jit(solution)/shard_map/ppermute | solution.py:96
  37.7 23.4 %collective-permute-start.14 = (bf16[4,5,48,384]{3,2,1,0:T(8,128)(2,1)S(1)}, bf16[4,5,48,384]{3,2,1,0:T(8,128)(2,1)S(1)}, u32[]{:S(2)}, u32[]{:S(2)}) collective-permute-start(bf16[4,5,48,384]{3,2,1,0:T(8,128)(2,1)S(1)} %pad_maximum_fusion.22), channel_id=1, source_target_pairs={{0,1},{1,0},{2,3},{3,2},{4,5},{5,4},{6,7},{7,6},{8,9},{9,8},{10,11... | collective-permute-start | bytes 2211848 | tf_op jit(solution)/shard_map/ppermute | solution.py:96
  39.8 14.1 %collective-permute-start.16 = (f32[8,2,576]{2,1,0:T(2,128)S(1)}, f32[8,2,576]{2,1,0:T(2,128)S(1)}, u32[]{:S(2)}, u32[]{:S(2)}) collective-permute-start(f32[8,2,576]{2,1,0:T(2,128)S(1)} %pad_maximum_fusion.30), channel_id=1, source_target_pairs={{0,2},{1,3},{2,0},{3,1},{4,6},{5,7},{6,4},{7,5},{8,10},{9,11},{10,... | collective-permute-start | bytes 110600 | tf_op jit(solution)/shard_map/ppermute | solution.py:96
  41.3 13.8 %collective-permute-start.11 = (bf16[1,1,192,384]{3,2,1,0:T(8,128)(2,1)S(1)}, bf16[1,1,192,384]{3,2,1,0:T(8,128)(2,1)S(1)}, u32[]{:S(2)}, u32[]{:S(2)}) collective-permute-start(bf16[1,1,192,384]{3,2,1,0:T(8,128)(2,1)S(1)} %dynamic-slice_bitcast_fusion.36), channel_id=1, source_target_pairs={{0,4},{1,5},{2,6},{3,7},{4,0},{5,1},{6,2},{7,3},{8,12},{9,13},{10,... | collective-permute-start | bytes 442376 | tf_op jit(solution)/shard_map/ppermute | solution.py:96
  43.9 11.3 %collective-permute-start.12 = (bf16[1,1,192,384]{3,2,1,0:T(8,128)(2,1)S(1)}, bf16[1,1,192,384]{3,2,1,0:T(8,128)(2,1)S(1)}, u32[]{:S(2)}, u32[]{:S(2)}) collective-permute-start(bf16[1,1,192,384]{3,2,1,0:T(8,128)(2,1)S(1)} %dynamic-slice_bitcast_fusion.36), channel_id=1, source_target_pairs={{0,8},{1,9},{2,10},{3,11},{4,12},{5,13},{6,14},{7,15},{8,0},{9,1},... | collective-permute-start | bytes 442376 | tf_op jit(solution)/shard_map/ppermute | solution.py:96
  62.8 27.6 %collective-permute-start.22 = (bf16[16,3,48,384]{3,2,1,0:T(8,128)(2,1)}, bf16[16,3,48,384]{3,2,1,0:T(8,128)(2,1)}, u32[]{:S(2)}, u32[]{:S(2)}) collective-permute-start(bf16[16,3,48,384]{3,2,1,0:T(8,128)(2,1)} %pad_maximum_fusion.7.mine_ref), channel_id=1, source_target_pairs={{0,16},{16,0},{1,17},{17,1},{2,18},{18,2},{3,19},{19,3},{4,20},{20... | collective-permute-start | bytes 5308424 | tf_op jit(solution)/shard_map/ppermute | solution.py:99
  62.9 25.9 %collective-permute-start.21 = (bf16[8,5,48,384]{3,2,1,0:T(8,128)(2,1)S(1)}, bf16[8,5,48,384]{3,2,1,0:T(8,128)(2,1)}, u32[]{:S(2)}, u32[]{:S(2)}) collective-permute-start(bf16[8,5,48,384]{3,2,1,0:T(8,128)(2,1)S(1)} %pad_maximum_fusion.12), channel_id=1, source_target_pairs={{0,2},{1,3},{2,0},{3,1},{4,6},{5,7},{6,4},{7,5},{8,10},{9,11},{10,... | collective-permute-start | bytes 4423688 | tf_op jit(solution)/shard_map/ppermute | solution.py:96
  67.2 14.0 %collective-permute-start.18 = (bf16[1,4,48,384]{3,2,1,0:T(8,128)(2,1)S(1)}, bf16[1,4,48,384]{3,2,1,0:T(8,128)(2,1)}, u32[]{:S(2)}, u32[]{:S(2)}) collective-permute-start(bf16[1,4,48,384]{3,2,1,0:T(8,128)(2,1)S(1)} %maximum_bitcast_fusion.1), channel_id=1, source_target_pairs={{0,8},{1,9},{2,10},{3,11},{4,12},{5,13},{6,14},{7,15},{8,0},{9,1},... | collective-permute-start | bytes 442376 | tf_op jit(solution)/shard_map/ppermute | solution.py:96
  68.3 16.3 %collective-permute-start.20 = (bf16[4,1,192,384]{3,2,1,0:T(8,128)(2,1)S(1)}, bf16[4,1,192,384]{3,2,1,0:T(8,128)(2,1)S(1)}, u32[]{:S(2)}, u32[]{:S(2)}) collective-permute-start(bf16[4,1,192,384]{3,2,1,0:T(8,128)(2,1)S(1)} %pad_maximum_fusion.23), channel_id=1, source_target_pairs={{0,1},{1,0},{2,3},{3,2},{4,5},{5,4},{6,7},{7,6},{8,9},{9,8},{10,11... | collective-permute-start | bytes 1769480 | tf_op jit(solution)/shard_map/ppermute | solution.py:96
  90.5 20.7 %collective-permute-start.23 = (bf16[1,4,48,384]{3,2,1,0:T(8,128)(2,1)S(1)}, bf16[1,4,48,384]{3,2,1,0:T(8,128)(2,1)}, u32[]{:S(2)}, u32[]{:S(2)}) collective-permute-start(bf16[1,4,48,384]{3,2,1,0:T(8,128)(2,1)S(1)} %maximum_bitcast_fusion), channel_id=1, source_target_pairs={{0,4},{1,5},{2,6},{3,7},{4,0},{5,1},{6,2},{7,3},{8,12},{9,13},{10,... | collective-permute-start | bytes 442376 | tf_op jit(solution)/shard_map/ppermute | solution.py:96
  94.2 24.1 %collective-permute-start.24 = (bf16[1,4,48,384]{3,2,1,0:T(8,128)(2,1)S(1)}, bf16[1,4,48,384]{3,2,1,0:T(8,128)(2,1)}, u32[]{:S(2)}, u32[]{:S(2)}) collective-permute-start(bf16[1,4,48,384]{3,2,1,0:T(8,128)(2,1)S(1)} %maximum_bitcast_fusion), channel_id=1, source_target_pairs={{0,8},{1,9},{2,10},{3,11},{4,12},{5,13},{6,14},{7,15},{8,0},{9,1},... | collective-permute-start | bytes 442376 | tf_op jit(solution)/shard_map/ppermute | solution.py:96
  94.2 24.1 %collective-permute-start.25 = (bf16[1,4,48,384]{3,2,1,0:T(8,128)(2,1)S(1)}, bf16[1,4,48,384]{3,2,1,0:T(8,128)(2,1)}, u32[]{:S(2)}, u32[]{:S(2)}) collective-permute-start(bf16[1,4,48,384]{3,2,1,0:T(8,128)(2,1)S(1)} %maximum_bitcast_fusion), channel_id=1, source_target_pairs={{0,12},{1,13},{2,14},{3,15},{4,8},{5,9},{6,10},{7,11},{8,4},{9,5},... | collective-permute-start | bytes 442376 | tf_op jit(solution)/shard_map/ppermute | solution.py:96
  96.6 25.9 %collective-permute-start.27 = (bf16[8,1,192,384]{3,2,1,0:T(8,128)(2,1)}, bf16[8,1,192,384]{3,2,1,0:T(8,128)(2,1)}, u32[]{:S(2)}, u32[]{:S(2)}) collective-permute-start(bf16[8,1,192,384]{3,2,1,0:T(8,128)(2,1)} %pad_maximum_fusion.13), channel_id=1, source_target_pairs={{0,2},{1,3},{2,0},{3,1},{4,6},{5,7},{6,4},{7,5},{8,10},{9,11},{10,... | collective-permute-start | bytes 3538952 | tf_op jit(solution)/shard_map/ppermute | solution.py:96
  96.9 28.9 %collective-permute-start.28 = (bf16[16,5,48,384]{3,2,1,0:T(8,128)(2,1)S(1)}, bf16[16,5,48,384]{3,2,1,0:T(8,128)(2,1)}, u32[]{:S(2)}, u32[]{:S(2)}) collective-permute-start(bf16[16,5,48,384]{3,2,1,0:T(8,128)(2,1)S(1)} %pad_maximum_fusion.mine_ref), channel_id=1, source_target_pairs={{0,16},{16,0},{1,17},{17,1},{2,18},{18,2},{3,19},{19,3},{4,20},{20... | collective-permute-start | bytes 8847368 | tf_op jit(solution)/shard_map/ppermute | solution.py:99
  133.5 10.8 %collective-permute-start.29 = (bf16[1,1,192,384]{3,2,1,0:T(8,128)(2,1)S(1)}, bf16[1,1,192,384]{3,2,1,0:T(8,128)(2,1)S(1)}, u32[]{:S(2)}, u32[]{:S(2)}) collective-permute-start(bf16[1,1,192,384]{3,2,1,0:T(8,128)(2,1)S(1)} %dynamic-slice_bitcast_fusion.37), channel_id=1, source_target_pairs={{0,4},{1,5},{2,6},{3,7},{4,0},{5,1},{6,2},{7,3},{8,12},{9,13},{10,... | collective-permute-start | bytes 442376 | tf_op jit(solution)/shard_map/ppermute | solution.py:96
  134.6 29.9 %collective-permute-start.30 = (bf16[1,1,192,384]{3,2,1,0:T(8,128)(2,1)S(1)}, bf16[1,1,192,384]{3,2,1,0:T(8,128)(2,1)S(1)}, u32[]{:S(2)}, u32[]{:S(2)}) collective-permute-start(bf16[1,1,192,384]{3,2,1,0:T(8,128)(2,1)S(1)} %dynamic-slice_bitcast_fusion.37), channel_id=1, source_target_pairs={{0,8},{1,9},{2,10},{3,11},{4,12},{5,13},{6,14},{7,15},{8,0},{9,1},... | collective-permute-start | bytes 442376 | tf_op jit(solution)/shard_map/ppermute | solution.py:96
  135.5 29.0 %collective-permute-start.31 = (bf16[1,1,192,384]{3,2,1,0:T(8,128)(2,1)S(1)}, bf16[1,1,192,384]{3,2,1,0:T(8,128)(2,1)S(1)}, u32[]{:S(2)}, u32[]{:S(2)}) collective-permute-start(bf16[1,1,192,384]{3,2,1,0:T(8,128)(2,1)S(1)} %dynamic-slice_bitcast_fusion.37), channel_id=1, source_target_pairs={{0,12},{1,13},{2,14},{3,15},{4,8},{5,9},{6,10},{7,11},{8,4},{9,5},... | collective-permute-start | bytes 442376 | tf_op jit(solution)/shard_map/ppermute | solution.py:96
  140.9 24.6 %collective-permute-start.33 = (bf16[8,4,48,384]{3,2,1,0:T(8,128)(2,1)S(1)}, bf16[8,4,48,384]{3,2,1,0:T(8,128)(2,1)S(1)}, u32[]{:S(2)}, u32[]{:S(2)}) collective-permute-start(bf16[8,4,48,384]{3,2,1,0:T(8,128)(2,1)S(1)} %copy-done.37), channel_id=1, source_target_pairs={{0,2},{1,3},{2,0},{3,1},{4,6},{5,7},{6,4},{7,5},{8,10},{9,11},{10,... | collective-permute-start | bytes 3538952 | tf_op jit(solution)/shard_map/ppermute | solution.py:96
  142.7 22.7 %collective-permute-start.32 = (bf16[4,4,48,384]{3,2,1,0:T(8,128)(2,1)S(1)}, bf16[4,4,48,384]{3,2,1,0:T(8,128)(2,1)S(1)}, u32[]{:S(2)}, u32[]{:S(2)}) collective-permute-start(bf16[4,4,48,384]{3,2,1,0:T(8,128)(2,1)S(1)} %copy-done.53), channel_id=1, source_target_pairs={{0,1},{1,0},{2,3},{3,2},{4,5},{5,4},{6,7},{7,6},{8,9},{9,8},{10,11... | collective-permute-start | bytes 1769480 | tf_op jit(solution)/shard_map/ppermute | solution.py:96
  144.3 22.9 %collective-permute-start.34 = (bf16[16,1,192,384]{3,2,1,0:T(8,128)(2,1)S(1)}, bf16[16,1,192,384]{3,2,1,0:T(8,128)(2,1)S(1)}, u32[]{:S(2)}, u32[]{:S(2)}) collective-permute-start(bf16[16,1,192,384]{3,2,1,0:T(8,128)(2,1)S(1)} %copy-done.12), channel_id=1, source_target_pairs={{0,16},{16,0},{1,17},{17,1},{2,18},{18,2},{3,19},{19,3},{4,20},{20... | collective-permute-start | bytes 7077896 | tf_op jit(solution)/shard_map/ppermute | solution.py:99
  168.7 33.2 %collective-permute-start.37 = (bf16[16,4,48,384]{3,2,1,0:T(8,128)(2,1)}, bf16[16,4,48,384]{3,2,1,0:T(8,128)(2,1)}, u32[]{:S(2)}, u32[]{:S(2)}) collective-permute-start(bf16[16,4,48,384]{3,2,1,0:T(8,128)(2,1)} %pad_maximum_fusion.2.mine_ref), channel_id=1, source_target_pairs={{0,16},{16,0},{1,17},{17,1},{2,18},{18,2},{3,19},{19,3},{4,20},{20... | collective-permute-start | bytes 7077896 | tf_op jit(solution)/shard_map/ppermute | solution.py:99
  177.6 22.5 %collective-permute-start.36 = (bf16[8,4,48,384]{3,2,1,0:T(8,128)(2,1)S(1)}, bf16[8,4,48,384]{3,2,1,0:T(8,128)(2,1)S(1)}, u32[]{:S(2)}, u32[]{:S(2)}) collective-permute-start(bf16[8,4,48,384]{3,2,1,0:T(8,128)(2,1)S(1)} %pad_maximum_fusion.15), channel_id=1, source_target_pairs={{0,2},{1,3},{2,0},{3,1},{4,6},{5,7},{6,4},{7,5},{8,10},{9,11},{10,... | collective-permute-start | bytes 3538952 | tf_op jit(solution)/shard_map/ppermute | solution.py:96
  178.1 16.5 %collective-permute-start.35 = (bf16[4,1,192,384]{3,2,1,0:T(8,128)(2,1)}, bf16[4,1,192,384]{3,2,1,0:T(8,128)(2,1)S(1)}, u32[]{:S(2)}, u32[]{:S(2)}) collective-permute-start(bf16[4,1,192,384]{3,2,1,0:T(8,128)(2,1)} %pad_maximum_fusion.26), channel_id=1, source_target_pairs={{0,1},{1,0},{2,3},{3,2},{4,5},{5,4},{6,7},{7,6},{8,9},{9,8},{10,11... | collective-permute-start | bytes 1769480 | tf_op jit(solution)/shard_map/ppermute | solution.py:96
  209.9 229.6 %collective-permute-start.55 = (bf16[512,768]{1,0:T(8,128)(2,1)}, bf16[512,768]{1,0:T(8,128)(2,1)}, u32[]{:S(2)}, u32[]{:S(2)}) collective-permute-start(bf16[512,768]{1,0:T(8,128)(2,1)} %convert_element_type.603.left_ref), channel_id=1, source_target_pairs={{0,16},{16,0},{1,17},{17,1},{2,18},{18,2},{3,19},{19,3},{4,20},{20... | collective-permute-start | bytes 2359304 | tf_op jit(solution)/shard_map/ppermute | solution.py:99
  218.7 22.6 %collective-permute-start.39 = (bf16[16,4,48,384]{3,2,1,0:T(8,128)(2,1)}, bf16[16,4,48,384]{3,2,1,0:T(8,128)(2,1)}, u32[]{:S(2)}, u32[]{:S(2)}) collective-permute-start(bf16[16,4,48,384]{3,2,1,0:T(8,128)(2,1)} %pad_maximum_fusion.3.mine_ref), channel_id=1, source_target_pairs={{0,16},{16,0},{1,17},{17,1},{2,18},{18,2},{3,19},{19,3},{4,20},{20... | collective-permute-start | bytes 7077896 | tf_op jit(solution)/shard_map/ppermute | solution.py:99
  221.4 16.6 %collective-permute-start.38 = (bf16[8,1,192,384]{3,2,1,0:T(8,128)(2,1)}, bf16[8,1,192,384]{3,2,1,0:T(8,128)(2,1)}, u32[]{:S(2)}, u32[]{:S(2)}) collective-permute-start(bf16[8,1,192,384]{3,2,1,0:T(8,128)(2,1)} %pad_maximum_fusion.16), channel_id=1, source_target_pairs={{0,2},{1,3},{2,0},{3,1},{4,6},{5,7},{6,4},{7,5},{8,10},{9,11},{10,... | collective-permute-start | bytes 3538952 | tf_op jit(solution)/shard_map/ppermute | solution.py:96
  250.9 21.5 %collective-permute-start.40 = (bf16[16,1,192,384]{3,2,1,0:T(8,128)(2,1)S(1)}, bf16[16,1,192,384]{3,2,1,0:T(8,128)(2,1)S(1)}, u32[]{:S(2)}, u32[]{:S(2)}) collective-permute-start(bf16[16,1,192,384]{3,2,1,0:T(8,128)(2,1)S(1)} %copy-done.15), channel_id=1, source_target_pairs={{0,16},{16,0},{1,17},{17,1},{2,18},{18,2},{3,19},{19,3},{4,20},{20... | collective-permute-start | bytes 7077896 | tf_op jit(solution)/shard_map/ppermute | solution.py:99
  252.2 86.0 %collective-permute-start.44 = (bf16[512,768]{1,0:T(8,128)(2,1)}, bf16[512,768]{1,0:T(8,128)(2,1)}, u32[]{:S(2)}, u32[]{:S(2)}) collective-permute-start(bf16[512,768]{1,0:T(8,128)(2,1)} %fusion.27.left_ref), channel_id=1, source_target_pairs={{0,16},{16,0},{1,17},{17,1},{2,18},{18,2},{3,19},{19,3},{4,20},{20... | collective-permute-start | bytes 2359304 | tf_op jit(solution)/shard_map/ppermute | solution.py:99
  252.7 131.0 %collective-permute-start.48 = (bf16[512,768]{1,0:T(8,128)(2,1)}, bf16[512,768]{1,0:T(8,128)(2,1)}, u32[]{:S(2)}, u32[]{:S(2)}) collective-permute-start(bf16[512,768]{1,0:T(8,128)(2,1)} %copy.76.left_ref), channel_id=1, source_target_pairs={{0,16},{16,0},{1,17},{17,1},{2,18},{18,2},{3,19},{19,3},{4,20},{20... | collective-permute-start | bytes 2359304 | tf_op jit(solution)/shard_map/ppermute | solution.py:99
  278.8 21.2 %collective-permute-start.41 = (bf16[512,3072]{1,0:T(8,128)(2,1)}, bf16[512,3072]{1,0:T(8,128)(2,1)}, u32[]{:S(2)}, u32[]{:S(2)}) collective-permute-start(bf16[512,3072]{1,0:T(8,128)(2,1)} %get-tuple-element.123.left_ref), channel_id=1, source_target_pairs={{0,16},{16,0},{1,17},{17,1},{2,18},{18,2},{3,19},{19,3},{4,20},{20... | collective-permute-start | bytes 9437192 | tf_op jit(solution)/shard_map/ppermute | solution.py:99
  319.0 19.2 %collective-permute-start.45 = (bf16[4,512,384]{2,1,0:T(8,128)(2,1)S(1)}, bf16[4,512,384]{2,1,0:T(8,128)(2,1)}, u32[]{:S(2)}, u32[]{:S(2)}) collective-permute-start(bf16[4,512,384]{2,1,0:T(8,128)(2,1)S(1)} %pad_maximum_fusion.9), channel_id=1, source_target_pairs={{0,16},{16,0},{1,17},{17,1},{2,18},{18,2},{3,19},{19,3},{4,20},{20... | collective-permute-start | bytes 4718600 | tf_op jit(solution)/shard_map/ppermute | solution.py:99
  320.5 16.3 %collective-permute-start.43 = (bf16[8,1,192,384]{3,2,1,0:T(8,128)(2,1)S(1)}, bf16[8,1,192,384]{3,2,1,0:T(8,128)(2,1)S(1)}, u32[]{:S(2)}, u32[]{:S(2)}) collective-permute-start(bf16[8,1,192,384]{3,2,1,0:T(8,128)(2,1)S(1)} %slice.565), channel_id=1, source_target_pairs={{0,2},{1,3},{2,0},{3,1},{4,6},{5,7},{6,4},{7,5},{8,10},{9,11},{10,... | collective-permute-start | bytes 3538952 | tf_op jit(solution)/shard_map/ppermute | solution.py:96
  378.0 22.8 %collective-permute-start.47 = (bf16[8,4,48,384]{3,2,1,0:T(8,128)(2,1)}, bf16[8,4,48,384]{3,2,1,0:T(8,128)(2,1)}, u32[]{:S(2)}, u32[]{:S(2)}) collective-permute-start(bf16[8,4,48,384]{3,2,1,0:T(8,128)(2,1)} %slice.569), channel_id=1, source_target_pairs={{0,2},{1,3},{2,0},{3,1},{4,6},{5,7},{6,4},{7,5},{8,10},{9,11},{10,... | collective-permute-start | bytes 3538952 | tf_op jit(solution)/shard_map/ppermute | solution.py:96
  380.3 16.5 %collective-permute-start.46 = (bf16[4,1,192,384]{3,2,1,0:T(8,128)(2,1)}, bf16[4,1,192,384]{3,2,1,0:T(8,128)(2,1)S(1)}, u32[]{:S(2)}, u32[]{:S(2)}) collective-permute-start(bf16[4,1,192,384]{3,2,1,0:T(8,128)(2,1)} %slice.567), channel_id=1, source_target_pairs={{0,1},{1,0},{2,3},{3,2},{4,5},{5,4},{6,7},{7,6},{8,9},{9,8},{10,11... | collective-permute-start | bytes 1769480 | tf_op jit(solution)/shard_map/ppermute | solution.py:96
  413.0 26.5 %collective-permute-start.56 = (bf16[3,512,384]{2,1,0:T(8,128)(2,1)}, bf16[3,512,384]{2,1,0:T(8,128)(2,1)}, u32[]{:S(2)}, u32[]{:S(2)}) collective-permute-start(bf16[3,512,384]{2,1,0:T(8,128)(2,1)} %pad_maximum_fusion.18), channel_id=1, source_target_pairs={{0,16},{16,0},{1,17},{17,1},{2,18},{18,2},{3,19},{19,3},{4,20},{20... | collective-permute-start | bytes 3538952 | tf_op jit(solution)/shard_map/ppermute | solution.py:99
  413.3 13.9 %collective-permute-start.51 = (bf16[1,1,192,384]{3,2,1,0:T(8,128)(2,1)S(1)}, bf16[1,1,192,384]{3,2,1,0:T(8,128)(2,1)S(1)}, u32[]{:S(2)}, u32[]{:S(2)}) collective-permute-start(bf16[1,1,192,384]{3,2,1,0:T(8,128)(2,1)S(1)} %get-tuple-element.260), channel_id=1, source_target_pairs={{0,8},{1,9},{2,10},{3,11},{4,12},{5,13},{6,14},{7,15},{8,0},{9,1},... | collective-permute-start | bytes 442376 | tf_op jit(solution)/shard_map/ppermute | solution.py:96
  415.1 16.7 %collective-permute-start.52 = (bf16[1,1,192,384]{3,2,1,0:T(8,128)(2,1)S(1)}, bf16[1,1,192,384]{3,2,1,0:T(8,128)(2,1)}, u32[]{:S(2)}, u32[]{:S(2)}) collective-permute-start(bf16[1,1,192,384]{3,2,1,0:T(8,128)(2,1)S(1)} %get-tuple-element.259), channel_id=1, source_target_pairs={{0,12},{1,13},{2,14},{3,15},{4,8},{5,9},{6,10},{7,11},{8,4},{9,5},... | collective-permute-start | bytes 442376 | tf_op jit(solution)/shard_map/ppermute | solution.py:96
  421.3 11.6 %collective-permute-start.54 = (bf16[8,1,48,384]{3,2,1,0:T(8,128)(2,1)S(1)}, bf16[8,1,48,384]{3,2,1,0:T(8,128)(2,1)}, u32[]{:S(2)}, u32[]{:S(2)}) collective-permute-start(bf16[8,1,48,384]{3,2,1,0:T(8,128)(2,1)S(1)} %slice.577), channel_id=1, source_target_pairs={{0,2},{1,3},{2,0},{3,1},{4,6},{5,7},{6,4},{7,5},{8,10},{9,11},{10,... | collective-permute-start | bytes 884744 | tf_op jit(solution)/shard_map/ppermute | solution.py:96
  431.8 46.2 %collective-permute-start.62 = (bf16[512,3072]{1,0:T(8,128)(2,1)}, bf16[512,3072]{1,0:T(8,128)(2,1)}, u32[]{:S(2)}, u32[]{:S(2)}) collective-permute-start(bf16[512,3072]{1,0:T(8,128)(2,1)} %get-tuple-element.114.left_ref), channel_id=1, source_target_pairs={{0,16},{16,0},{1,17},{17,1},{2,18},{18,2},{3,19},{19,3},{4,20},{20... | collective-permute-start | bytes 9437192 | tf_op jit(solution)/shard_map/ppermute | solution.py:99
  451.9 26.1 %collective-permute-start.63 = (bf16[1,512,384]{2,1,0:T(8,128)(2,1)S(1)}, bf16[1,512,384]{2,1,0:T(8,128)(2,1)}, u32[]{:S(2)}, u32[]{:S(2)}) collective-permute-start(bf16[1,512,384]{2,1,0:T(8,128)(2,1)S(1)} %get-tuple-element.243), channel_id=1, source_target_pairs={{0,16},{16,0},{1,17},{17,1},{2,18},{18,2},{3,19},{19,3},{4,20},{20... | collective-permute-start | bytes 1179656 | tf_op jit(solution)/shard_map/ppermute | solution.py:99
  452.9 35.0 %collective-permute-start.61 = (bf16[8,3,48,384]{3,2,1,0:T(8,128)(2,1)}, bf16[8,3,48,384]{3,2,1,0:T(8,128)(2,1)}, u32[]{:S(2)}, u32[]{:S(2)}) collective-permute-start(bf16[8,3,48,384]{3,2,1,0:T(8,128)(2,1)} %slice.585), channel_id=1, source_target_pairs={{0,2},{1,3},{2,0},{3,1},{4,6},{5,7},{6,4},{7,5},{8,10},{9,11},{10,... | collective-permute-start | bytes 2654216 | tf_op jit(solution)/shard_map/ppermute | solution.py:96
  453.3 10.6 %collective-permute-start.60 = (bf16[4,1,48,384]{3,2,1,0:T(8,128)(2,1)S(1)}, bf16[4,1,48,384]{3,2,1,0:T(8,128)(2,1)S(1)}, u32[]{:S(2)}, u32[]{:S(2)}) collective-permute-start(bf16[4,1,48,384]{3,2,1,0:T(8,128)(2,1)S(1)} %slice.583), channel_id=1, source_target_pairs={{0,1},{1,0},{2,3},{3,2},{4,5},{5,4},{6,7},{7,6},{8,9},{9,8},{10,11... | collective-permute-start | bytes 442376 | tf_op jit(solution)/shard_map/ppermute | solution.py:96
  463.9 10.7 %collective-permute-start.58 = (bf16[1,4,48,384]{3,2,1,0:T(8,128)(2,1)S(1)}, bf16[1,4,48,384]{3,2,1,0:T(8,128)(2,1)S(1)}, u32[]{:S(2)}, u32[]{:S(2)}) collective-permute-start(bf16[1,4,48,384]{3,2,1,0:T(8,128)(2,1)S(1)} %get-tuple-element.257), channel_id=1, source_target_pairs={{0,8},{1,9},{2,10},{3,11},{4,12},{5,13},{6,14},{7,15},{8,0},{9,1},... | collective-permute-start | bytes 442376 | tf_op jit(solution)/shard_map/ppermute | solution.py:96
  474.7 57.6 %collective-permute-start.69 = (bf16[512,768]{1,0:T(8,128)(2,1)}, bf16[512,768]{1,0:T(8,128)(2,1)}, u32[]{:S(2)}, u32[]{:S(2)}) collective-permute-start(bf16[512,768]{1,0:T(8,128)(2,1)} %fusion.26.left_ref), channel_id=1, source_target_pairs={{0,16},{16,0},{1,17},{17,1},{2,18},{18,2},{3,19},{19,3},{4,20},{20... | collective-permute-start | bytes 2359304 | tf_op jit(solution)/shard_map/ppermute | solution.py:99
  478.0 118.2 %collective-permute-start.76 = (bf16[512,768]{1,0:T(8,128)(2,1)}, bf16[512,768]{1,0:T(8,128)(2,1)}, u32[]{:S(2)}, u32[]{:S(2)}) collective-permute-start(bf16[512,768]{1,0:T(8,128)(2,1)} %copy.88.left_ref), channel_id=1, source_target_pairs={{0,16},{16,0},{1,17},{17,1},{2,18},{18,2},{3,19},{19,3},{4,20},{20... | collective-permute-start | bytes 2359304 | tf_op jit(solution)/shard_map/ppermute | solution.py:99
  509.8 22.4 %collective-permute-start.70 = (bf16[4,512,384]{2,1,0:T(8,128)(2,1)S(1)}, bf16[4,512,384]{2,1,0:T(8,128)(2,1)S(1)}, u32[]{:S(2)}, u32[]{:S(2)}) collective-permute-start(bf16[4,512,384]{2,1,0:T(8,128)(2,1)S(1)} %pad_maximum_fusion.11), channel_id=1, source_target_pairs={{0,16},{16,0},{1,17},{17,1},{2,18},{18,2},{3,19},{19,3},{4,20},{20... | collective-permute-start | bytes 4718600 | tf_op jit(solution)/shard_map/ppermute | solution.py:99
  509.9 21.0 %collective-permute-start.68 = (bf16[8,1,192,384]{3,2,1,0:T(8,128)(2,1)S(1)}, bf16[8,1,192,384]{3,2,1,0:T(8,128)(2,1)S(1)}, u32[]{:S(2)}, u32[]{:S(2)}) collective-permute-start(bf16[8,1,192,384]{3,2,1,0:T(8,128)(2,1)S(1)} %slice.593), channel_id=1, source_target_pairs={{0,2},{1,3},{2,0},{3,1},{4,6},{5,7},{6,4},{7,5},{8,10},{9,11},{10,... | collective-permute-start | bytes 3538952 | tf_op jit(solution)/shard_map/ppermute | solution.py:96
  513.5 13.1 %collective-permute-start.67 = (bf16[4,3,48,384]{3,2,1,0:T(8,128)(2,1)S(1)}, bf16[4,3,48,384]{3,2,1,0:T(8,128)(2,1)S(1)}, u32[]{:S(2)}, u32[]{:S(2)}) collective-permute-start(bf16[4,3,48,384]{3,2,1,0:T(8,128)(2,1)S(1)} %slice.591), channel_id=1, source_target_pairs={{0,1},{1,0},{2,3},{3,2},{4,5},{5,4},{6,7},{7,6},{8,9},{9,8},{10,11... | collective-permute-start | bytes 1327112 | tf_op jit(solution)/shard_map/ppermute | solution.py:96
  574.6 27.1 %collective-permute-start.75 = (bf16[8,4,48,384]{3,2,1,0:T(8,128)(2,1)}, bf16[8,4,48,384]{3,2,1,0:T(8,128)(2,1)}, u32[]{:S(2)}, u32[]{:S(2)}) collective-permute-start(bf16[8,4,48,384]{3,2,1,0:T(8,128)(2,1)} %slice.601), channel_id=1, source_target_pairs={{0,2},{1,3},{2,0},{3,1},{4,6},{5,7},{6,4},{7,5},{8,10},{9,11},{10,... | collective-permute-start | bytes 3538952 | tf_op jit(solution)/shard_map/ppermute | solution.py:96
  577.1 22.5 %collective-permute-start.74 = (bf16[4,1,192,384]{3,2,1,0:T(8,128)(2,1)}, bf16[4,1,192,384]{3,2,1,0:T(8,128)(2,1)}, u32[]{:S(2)}, u32[]{:S(2)}) collective-permute-start(bf16[4,1,192,384]{3,2,1,0:T(8,128)(2,1)} %slice.599), channel_id=1, source_target_pairs={{0,1},{1,0},{2,3},{3,2},{4,5},{5,4},{6,7},{7,6},{8,9},{9,8},{10,11... | collective-permute-start | bytes 1769480 | tf_op jit(solution)/shard_map/ppermute | solution.py:96
  583.0 13.2 %collective-permute-start.77 = (bf16[1,512,384]{2,1,0:T(8,128)(2,1)S(1)}, bf16[1,512,384]{2,1,0:T(8,128)(2,1)}, u32[]{:S(2)}, u32[]{:S(2)}) collective-permute-start(bf16[1,512,384]{2,1,0:T(8,128)(2,1)S(1)} %get-tuple-element.241), channel_id=1, source_target_pairs={{0,16},{16,0},{1,17},{17,1},{2,18},{18,2},{3,19},{19,3},{4,20},{20... | collective-permute-start | bytes 1179656 | tf_op jit(solution)/shard_map/ppermute | solution.py:99
  627.5 38.9 %collective-permute-start.84 = (bf16[3,512,384]{2,1,0:T(8,128)(2,1)}, bf16[3,512,384]{2,1,0:T(8,128)(2,1)}, u32[]{:S(2)}, u32[]{:S(2)}) collective-permute-start(bf16[3,512,384]{2,1,0:T(8,128)(2,1)} %pad_maximum_fusion.20), channel_id=1, source_target_pairs={{0,16},{16,0},{1,17},{17,1},{2,18},{18,2},{3,19},{19,3},{4,20},{20... | collective-permute-start | bytes 3538952 | tf_op jit(solution)/shard_map/ppermute | solution.py:99
  630.4 25.1 %collective-permute-start.78 = (bf16[1,1,192,384]{3,2,1,0:T(8,128)(2,1)}, bf16[1,1,192,384]{3,2,1,0:T(8,128)(2,1)}, u32[]{:S(2)}, u32[]{:S(2)}) collective-permute-start(bf16[1,1,192,384]{3,2,1,0:T(8,128)(2,1)} %get-tuple-element.252), channel_id=1, source_target_pairs={{0,4},{1,5},{2,6},{3,7},{4,0},{5,1},{6,2},{7,3},{8,12},{9,13},{10,... | collective-permute-start | bytes 442376 | tf_op jit(solution)/shard_map/ppermute | solution.py:96
  630.4 26.1 %collective-permute-start.79 = (bf16[1,1,192,384]{3,2,1,0:T(8,128)(2,1)}, bf16[1,1,192,384]{3,2,1,0:T(8,128)(2,1)}, u32[]{:S(2)}, u32[]{:S(2)}) collective-permute-start(bf16[1,1,192,384]{3,2,1,0:T(8,128)(2,1)} %get-tuple-element.254), channel_id=1, source_target_pairs={{0,8},{1,9},{2,10},{3,11},{4,12},{5,13},{6,14},{7,15},{8,0},{9,1},... | collective-permute-start | bytes 442376 | tf_op jit(solution)/shard_map/ppermute | solution.py:96
  651.6 13.9 %collective-permute-start.83 = (bf16[512,768]{1,0:T(8,128)(2,1)S(1)}, bf16[512,768]{1,0:T(8,128)(2,1)S(1)}, u32[]{:S(2)}, u32[]{:S(2)}) collective-permute-start(bf16[512,768]{1,0:T(8,128)(2,1)S(1)} %copy-done.63), channel_id=1, source_target_pairs={{0,16},{16,0},{1,17},{17,1},{2,18},{18,2},{3,19},{19,3},{4,20},{20... | collective-permute-start | bytes 2359304 | tf_op jit(solution)/shard_map/ppermute | solution.py:99
  653.9 10.6 %collective-permute-start.82 = (bf16[8,1,48,384]{3,2,1,0:T(8,128)(2,1)S(1)}, bf16[8,1,48,384]{3,2,1,0:T(8,128)(2,1)S(1)}, u32[]{:S(2)}, u32[]{:S(2)}) collective-permute-start(bf16[8,1,48,384]{3,2,1,0:T(8,128)(2,1)S(1)} %copy-done.77), channel_id=1, source_target_pairs={{0,2},{1,3},{2,0},{3,1},{4,6},{5,7},{6,4},{7,5},{8,10},{9,11},{10,... | collective-permute-start | bytes 884744 | tf_op jit(solution)/shard_map/ppermute | solution.py:96
  673.8 16.3 %collective-permute-start.89 = (bf16[8,3,48,384]{3,2,1,0:T(8,128)(2,1)S(1)}, bf16[8,3,48,384]{3,2,1,0:T(8,128)(2,1)S(1)}, u32[]{:S(2)}, u32[]{:S(2)}) collective-permute-start(bf16[8,3,48,384]{3,2,1,0:T(8,128)(2,1)S(1)} %slice.617), channel_id=1, source_target_pairs={{0,2},{1,3},{2,0},{3,1},{4,6},{5,7},{6,4},{7,5},{8,10},{9,11},{10,... | collective-permute-start | bytes 2654216 | tf_op jit(solution)/shard_map/ppermute | solution.py:96
  675.9 14.1 %collective-permute-start.86 = (bf16[1,4,48,384]{3,2,1,0:T(8,128)(2,1)S(1)}, bf16[1,4,48,384]{3,2,1,0:T(8,128)(2,1)S(1)}, u32[]{:S(2)}, u32[]{:S(2)}) collective-permute-start(bf16[1,4,48,384]{3,2,1,0:T(8,128)(2,1)S(1)} %get-tuple-element.251), channel_id=1, source_target_pairs={{0,8},{1,9},{2,10},{3,11},{4,12},{5,13},{6,14},{7,15},{8,0},{9,1},... | collective-permute-start | bytes 442376 | tf_op jit(solution)/shard_map/ppermute | solution.py:96
  678.4 11.5 %collective-permute-start.87 = (bf16[1,4,48,384]{3,2,1,0:T(8,128)(2,1)S(1)}, bf16[1,4,48,384]{3,2,1,0:T(8,128)(2,1)S(1)}, u32[]{:S(2)}, u32[]{:S(2)}) collective-permute-start(bf16[1,4,48,384]{3,2,1,0:T(8,128)(2,1)S(1)} %get-tuple-element.250), channel_id=1, source_target_pairs={{0,12},{1,13},{2,14},{3,15},{4,8},{5,9},{6,10},{7,11},{8,4},{9,5},... | collective-permute-start | bytes 442376 | tf_op jit(solution)/shard_map/ppermute | solution.py:96
  706.0 11.6 %collective-permute-start.95 = (bf16[1,3,48,384]{3,2,1,0:T(8,128)(2,1)S(1)}, bf16[1,3,48,384]{3,2,1,0:T(8,128)(2,1)S(1)}, u32[]{:S(2)}, u32[]{:S(2)}) collective-permute-start(bf16[1,3,48,384]{3,2,1,0:T(8,128)(2,1)S(1)} %get-tuple-element.267), channel_id=1, source_target_pairs={{0,8},{1,9},{2,10},{3,11},{4,12},{5,13},{6,14},{7,15},{8,0},{9,1},... | collective-permute-start | bytes 331784 | tf_op jit(solution)/shard_map/ppermute | solution.py:96
  (184 other events, 1615.7 us)

commit v3 on v0

v3 whole, which is shorter than its diff:
```python
import functools

import jax
import jax.numpy as jnp
import numpy as np
from jax import lax
from jax.experimental import pallas as pl
from jax.experimental.pallas import tpu as pltpu
from jax.sharding import PartitionSpec as P

HD = 64
LAYERS = 2
LEN_UNIT = 64
SLOTS = ((0, 3), (3, 2), (5, 2), (7, 1))
GROUP_ROWS = 8 * LEN_UNIT

NORM_EPSILON = 1e-05
NEG_LARGE = -1e30
SCORE_SCALE = 0.125
LOW = jnp.bfloat16
FULL = jnp.float32

CHUNK = 384


class Net:
    def __init__(self, mesh):
        self.shards = mesh.shape["fsdp"]
        self.replicas = mesh.shape["rep"]
        assert self.replicas % 2 == 0 and self.shards & (self.shards - 1) == 0
        bits = [1 << place for place in range(self.shards.bit_length() - 1)]
        first = bits[2:] + bits[:2]
        self.steps = [first, first[:-2] + first[:-3:-1]]
        self.stages = len(bits)
        flips = np.zeros((2, self.shards), np.int32)
        for core in range(2):
            for slot in range(self.shards):
                for place, step in enumerate(self.steps[core]):
                    flips[core, slot] ^= ((slot >> place) & 1) * step
        self.flips = flips

    def trade(self, value, stage):
        pairs = [
            (rep * self.shards + shard, rep * self.shards + (shard ^ self.steps[rep % 2][stage]))
            for rep in range(self.replicas)
            for shard in range(self.shards)
        ]
        return lax.ppermute(value, ("rep", "fsdp"), pairs)

    def twin(self, value):
        return lax.ppermute(value, "rep", [(rep, rep ^ 1) for rep in range(self.replicas)])

    def widen(self, value, stage):
        return jnp.concatenate([value, self.trade(value, stage)], 0)

    def narrow(self, kept, sent, stage):
        received = self.trade(sent, stage)

        def add(here):
            return (kept[here].astype(FULL) + received[here].astype(FULL)).astype(kept.dtype)

        half = kept.shape[0] // 2
        return (add(slice(0, half)), add(slice(half, None))) if half else (add(slice(0, None)), None)

    def across(self, value):
        others = self.replicas // 2
        total = value.astype(FULL)
        for shift in range(1, others):
            pairs = [(rep, (rep + 2 * shift) % self.replicas) for rep in range(self.replicas)]
            total = total + lax.ppermute(value, "rep", pairs).astype(FULL)
        return total.astype(value.dtype)


def own_chunks(matrix, core):
    count = matrix.shape[1] // (2 * CHUNK)
    return jnp.stack(
        [
            lax.dynamic_slice_in_dim(matrix, (2 * part + core) * CHUNK, CHUNK, axis=1)
            for part in range(count)
        ]
    )


def join_chunks(mine, other, core):
    even = jnp.where(core == 0, mine, other)
    odd = jnp.where(core == 0, other, mine)
    return jnp.concatenate([piece for part in range(mine.shape[0]) for piece in (even[part], odd[part])], 1)


def dot(left, right, left_dim=1, right_dim=0):
    return lax.dot_general(left, right, (((left_dim,), (right_dim,)), ((), ())), preferred_element_type=FULL)


def fill(weight_ref, slots_ref, mine_ref, other_ref):
    rows = mine_ref.shape[1]
    for shard in range(mine_ref.shape[0]):
        here = slice(shard * rows, (shard + 1) * rows)
        weight_ref[here, :CHUNK] = mine_ref[slots_ref[0, shard]]
        weight_ref[here, CHUNK:] = other_ref[slots_ref[1, shard]]


def fill_rows(weight_ref, mine_refs, other_refs):
    rows = mine_refs[0].shape[1]
    for place, (mine_ref, other_ref) in enumerate(zip(mine_refs, other_refs)):
        here = slice(place * rows, (place + 1) * rows)
        weight_ref[here, :CHUNK] = mine_ref[0]
        weight_ref[here, CHUNK:] = other_ref[0]


def swap(core, values):
    even, odd = values[:, :CHUNK], values[:, CHUNK:]
    return jnp.where(core == 0, even, odd), jnp.where(core == 0, odd, even)


def centre(values):
    centred = values - jnp.mean(values, -1, keepdims=True)
    return centred, lax.rsqrt(jnp.mean(centred * centred, -1, keepdims=True) + NORM_EPSILON)


def norm(values, gain, shift):
    centred, scale = centre(values)
    return centred * scale * gain + shift


def norm_back(d_out, values, gain):
    centred, scale = centre(values)
    unit = centred * scale
    d_unit = d_out * gain
    inner = jnp.mean(d_unit * unit, -1, keepdims=True)
    d_values = scale * (d_unit - jnp.mean(d_unit, -1, keepdims=True) - unit * inner)
    return d_values, jnp.sum(d_out * unit, 0, keepdims=True), jnp.sum(d_out, 0, keepdims=True)


def live_rows(limits_ref, tokens):
    row = lax.broadcasted_iota(jnp.int32, (tokens, 1), 0)
    live = jnp.zeros((tokens, 1), jnp.bool_)
    for group in range(tokens // GROUP_ROWS):
        for slot, (start, length) in enumerate(SLOTS):
            first = group * GROUP_ROWS + start * LEN_UNIT
            place = row - first
            live = live | ((place >= 0) & (place < jnp.minimum(limits_ref[4 * group + slot], length * LEN_UNIT)))
    return live


def spans(tokens):
    for group in range(tokens // GROUP_ROWS):
        for slot, (start, length) in enumerate(SLOTS):
            first = group * GROUP_ROWS + start * LEN_UNIT
            yield 4 * group + slot, slice(first, first + length * LEN_UNIT)


def one_head(values, low_lanes, head):
    return jnp.where(low_lanes == (head == 0), values, jnp.zeros_like(values))


def probabilities(queries, key_rows, limit):
    scores = dot(key_rows, queries, 1, 1) * SCORE_SCALE
    allowed = lax.broadcasted_iota(jnp.int32, scores.shape, 0) < limit
    scores = jnp.where(allowed, scores, NEG_LARGE)
    raised = jnp.exp(scores - jnp.max(scores, 0, keepdims=True))
    return raised * (1.0 / jnp.sum(raised, 0, keepdims=True))


SMALL = pl.BlockSpec(memory_space=pltpu.SMEM)


def whole(*shape):
    return pl.BlockSpec(shape, lambda *args: (0,) * len(shape))


def part_blocks(mine, start, last=None):
    rows = 2 * CHUNK // mine.shape[0]

    def place(k):
        return (0, start + (k if last is None else jnp.minimum(k, last)), 0)

    return [pl.BlockSpec((mine.shape[0], rows, CHUNK), place)] * 2


def shaped(*shape, kind=LOW):
    return jax.ShapeDtypeStruct(shape, kind)


def project(tables, hidden_low, vector_rows, mine, other, start):
    slots, core, limits = tables
    tokens, width = hidden_low.shape

    def body(slots_ref, core_ref, limits_ref, x_ref, rows_ref, mine_ref, other_ref, qkv_ref, left_ref, weight_ref):
        third = pl.program_id(0)
        core = core_ref[0]
        fill(weight_ref, slots_ref, mine_ref, other_ref)
        result = dot(x_ref[...], weight_ref[...])
        bias = rows_ref[pl.ds(jnp.where(third == 2, 1, 0), 1), :]
        bias = jnp.where(third == 1, jnp.zeros_like(bias), bias)
        for side, part in enumerate(swap(core, bias)):
            qkv_ref[side, third] = (result[:, side * CHUNK : (side + 1) * CHUNK] + part).astype(LOW)

        @pl.when(third == 2)
        def _():
            for half in range(2):
                left_ref[half] = x_ref[:, half * CHUNK : (half + 1) * CHUNK]
            for side in range(2):
                for pair in range(CHUNK // (2 * HD)):
                    lanes = slice(2 * HD * pair, 2 * HD * (pair + 1))
                    for slot, rows in spans(tokens):
                        queries = qkv_ref[side, 0, rows, lanes]
                        key_rows = qkv_ref[side, 1, rows, lanes]
                        value_rows = qkv_ref[side, 2, rows, lanes]
                        low_lanes = lax.broadcasted_iota(jnp.int32, queries.shape, 1) < HD
                        heads = []
                        for head in range(2):
                            probs = probabilities(one_head(queries, low_lanes, head), key_rows, limits_ref[slot])
                            heads.append(dot(probs.astype(LOW), value_rows, 0, 0))
                        left_ref[2 + (core ^ side), rows, lanes] = jnp.where(low_lanes, *heads).astype(LOW)

    return pl.pallas_call(
        body,
        grid=(3,),
        out_shape=[shaped(2, 3, tokens, CHUNK), shaped(4, tokens, CHUNK)],
        in_specs=[SMALL] * 3 + [whole(tokens, width), whole(*vector_rows.shape)] + part_blocks(mine, start),
        out_specs=[whole(2, 3, tokens, CHUNK), whole(4, tokens, CHUNK)],
        scratch_shapes=[pltpu.VMEM((width, width), LOW)],
        name="project",
    )(slots, core, limits, hidden_low, vector_rows, mine, other)


def mix(tables, context, hidden, vector_rows, mine, other, start):
    slots, core, _ = tables
    tokens, width = hidden.shape

    def body(slots_ref, core_ref, context_ref, hidden_ref, rows_ref, mine_ref, other_ref, sum_ref, low_ref, weight_ref):
        fill(weight_ref, slots_ref, mine_ref, other_ref)
        context = jnp.concatenate([context_ref[0], context_ref[1]], 1)
        mixed = jnp.concatenate(swap(core_ref[0], dot(context, weight_ref[...])), 1) + rows_ref[2:3, :]
        total = hidden_ref[...].astype(FULL) + mixed
        sum_ref[...] = total
        low_ref[...] = norm(total, rows_ref[3:4, :], rows_ref[4:5, :]).astype(LOW)

    return pl.pallas_call(
        body,
        grid=(1,),
        out_shape=[shaped(tokens, width, kind=FULL), shaped(tokens, width)],
        in_specs=[SMALL] * 2
        + [pl.BlockSpec((2, tokens, CHUNK), lambda k: (1, 0, 0)), whole(tokens, width), whole(*vector_rows.shape)]
        + part_blocks(mine, start),
        out_specs=[whole(tokens, width)] * 2,
        scratch_shapes=[pltpu.VMEM((width, width), LOW)],
        name="mix",
    )(slots, core, context, hidden, vector_rows, mine, other)


def expand(tables, first_low, vector_rows, mine, other, start, parts):
    slots, core, _ = tables
    tokens, width = first_low.shape

    def body(slots_ref, core_ref, x_ref, rows_ref, mine_ref, other_ref, left_ref, slope_ref, weight_ref):
        core = core_ref[0]
        part = pl.program_id(0)

        @pl.when(part < parts)
        def _():
            fill(weight_ref, slots_ref, mine_ref, other_ref)
            result = dot(x_ref[...], weight_ref[...])
            for side, bias in enumerate(swap(core, rows_ref[pl.ds(8 + part, 1), :])):
                inner = result[:, side * CHUNK : (side + 1) * CHUNK] + bias
                chance = 0.5 + 0.5 * lax.erf(inner * 0.7071067811865476)
                left_ref[core ^ side] = (inner * chance).astype(LOW)
                bell = jnp.exp(-0.5 * inner * inner) * 0.3989422804014327
                slope_ref[core ^ side] = (chance + inner * bell).astype(LOW)

        @pl.when(part == parts)
        def _():
            for half in range(2):
                left_ref[half] = x_ref[:, half * CHUNK : (half + 1) * CHUNK]

    return pl.pallas_call(
        body,
        grid=(parts + 1,),
        out_shape=[shaped(2 * parts + 2, tokens, CHUNK), shaped(2 * parts, tokens, CHUNK)],
        in_specs=[SMALL] * 2
        + [whole(tokens, width), whole(*vector_rows.shape)]
        + part_blocks(mine, start, parts - 1),
        out_specs=[
            pl.BlockSpec((2, tokens, CHUNK), lambda k: (k, 0, 0)),
            pl.BlockSpec((2, tokens, CHUNK), lambda k: (jnp.minimum(k, parts - 1), 0, 0)),
        ],
        scratch_shapes=[pltpu.VMEM((width, width), LOW)],
        name="expand",
    )(slots, core, first_low, vector_rows, mine, other)


def row_blocks(shards, start, width, total, side):
    rows = total // shards
    each = width // rows
    return [
        pl.BlockSpec((1, rows, CHUNK), lambda n, slots, *_, place=place: (slots[side, n * each + place], start, 0))
        for place in range(each)
    ]


def contract(tables, active, first_sum, vector_rows, mine, other, start, total, last):
    slots, core, limits = tables
    tokens, width = first_sum.shape
    shards = mine.shape[0]
    each = width * shards // total
    steps = total // width

    def body(slots_ref, core_ref, limits_ref, active_ref, first_ref, rows_ref, *refs):
        mine_refs, other_refs = refs[:each], refs[each : 2 * each]
        sum_ref, out_ref, low_ref, weight_ref, total_ref = refs[2 * each :]
        step = pl.program_id(0)
        fill_rows(weight_ref, mine_refs, other_refs)
        term = dot(jnp.concatenate([active_ref[0], active_ref[1]], 1), weight_ref[...])

        @pl.when(step == 0)
        def _():
            total_ref[...] = term

        @pl.when(step > 0)
        def _():
            total_ref[...] += term

        @pl.when(step == steps - 1)
        def _():
            mixed = jnp.concatenate(swap(core_ref[0], total_ref[...]), 1) + rows_ref[5:6, :]
            total = norm(first_ref[...], rows_ref[3:4, :], rows_ref[4:5, :]) + mixed
            sum_ref[...] = total
            out = norm(total, rows_ref[6:7, :], rows_ref[7:8, :])
            out_ref[...] = out
            if last:
                out = jnp.where(live_rows(limits_ref, tokens), out, 0.0)
            low_ref[...] = out.astype(LOW)

    return pl.pallas_call(
        body,
        grid_spec=pltpu.PrefetchScalarGridSpec(
            num_scalar_prefetch=3,
            grid=(steps,),
            in_specs=[
                pl.BlockSpec((2, tokens, CHUNK), lambda n, *_: (n, 0, 0)),
                whole(tokens, width),
                whole(*vector_rows.shape),
            ]
            + row_blocks(shards, start, width, total, 0)
            + row_blocks(shards, start, width, total, 1),
            out_specs=[whole(tokens, width)] * 3,
            scratch_shapes=[pltpu.VMEM((width, width), LOW), pltpu.VMEM((tokens, width), FULL)],
        ),
        out_shape=[shaped(tokens, width, kind=FULL), shaped(tokens, width, kind=FULL), shaped(tokens, width)],
        name="contract",
    )(slots, core, limits, active, first_sum, vector_rows, *[mine] * each, *[other] * each)


def contract_back(tables, d_out, second_sum, slope, vector_rows, mine, other, start, total, last):
    slots, core, limits = tables
    tokens, width = second_sum.shape
    shards = mine.shape[0]
    each = width * shards // total
    steps = total // width

    def body(slots_ref, core_ref, limits_ref, d_out_ref, sum_ref, slope_ref, rows_ref, *refs):
        mine_refs, other_refs = refs[:each], refs[each : 2 * each]
        d_sum_ref, kept_ref, up_kept_ref, sent_ref, sums_ref, up_sums_ref, weight_ref, low_ref = refs[2 * each :]
        core = core_ref[0]

        @pl.when(pl.program_id(0) == 0)
        def _():
            d_out = d_out_ref[...].astype(FULL)
            if last:
                d_out = jnp.where(live_rows(limits_ref, tokens), d_out, 0.0)
            d_sum, d_gain, d_shift = norm_back(d_out, sum_ref[...], rows_ref[6:7, :])
            d_sum_ref[...] = d_sum
            rounded = d_sum.astype(LOW).astype(FULL)
            sums_ref[0:1, :] = jnp.sum(rounded, 0, keepdims=True)
            sums_ref[1:2, :] = d_gain
            sums_ref[2:3, :] = d_shift
            kept, sent = swap(core, rounded)
            kept, sent = kept.astype(LOW), sent.astype(LOW)
            kept_ref[0] = kept
            sent_ref[steps] = sent
            low_ref[:, :CHUNK] = kept
            low_ref[:, CHUNK:] = sent

        fill_rows(weight_ref, mine_refs, other_refs)
        d_active = dot(low_ref[...], weight_ref[...], 1, 1)
        slope = jnp.concatenate([slope_ref[0], slope_ref[1]], 1).astype(FULL)
        d_inner = (d_active * slope).astype(LOW).astype(FULL)
        up_sums_ref[0] = jnp.sum(d_inner, 0, keepdims=True)
        kept, sent = swap(core, d_inner)
        up_kept_ref[0] = kept.astype(LOW)
        sent_ref[pl.program_id(0)] = sent.astype(LOW)

    by_step = pl.BlockSpec((1, tokens, CHUNK), lambda n, *_: (n, 0, 0))
    return pl.pallas_call(
        body,
        grid_spec=pltpu.PrefetchScalarGridSpec(
            num_scalar_prefetch=3,
            grid=(steps,),
            in_specs=[
                whole(tokens, width),
                whole(tokens, width),
                pl.BlockSpec((2, tokens, CHUNK), lambda n, *_: (n, 0, 0)),
                whole(*vector_rows.shape),
            ]
            + row_blocks(shards, start, width, total, 0)
            + row_blocks(shards, start, width, total, 1),
            out_specs=[
                whole(tokens, width),
                whole(1, tokens, CHUNK),
                by_step,
                whole(steps + 1, tokens, CHUNK),
                whole(3, width),
                pl.BlockSpec((1, 1, width), lambda n, *_: (n, 0, 0)),
            ],
            scratch_shapes=[pltpu.VMEM((width, width), LOW), pltpu.VMEM((tokens, width), LOW)],
        ),
        out_shape=[
            shaped(tokens, width, kind=FULL),
            shaped(1, tokens, CHUNK),
            shaped(steps, tokens, CHUNK),
            shaped(steps + 1, tokens, CHUNK),
            shaped(3, width, kind=FULL),
            shaped(steps, 1, width, kind=FULL),
        ],
        name="contract_back",
    )(slots, core, limits, d_out, second_sum, slope, vector_rows, *[mine] * each, *[other] * each)


def expand_back(tables, kept, sent, d_second_sum, first_sum, vector_rows, mine, other, start):
    slots, core, _ = tables
    tokens, width = first_sum.shape
    parts = kept.shape[0]

    def body(
        slots_ref, core_ref, kept_ref, sent_ref, d_second_ref, sum_ref, rows_ref, mine_ref, other_ref,
        d_sum_ref, low_kept_ref, low_sent_ref, sums_ref, weight_ref, total_ref,
    ):
        part = pl.program_id(0)
        fill(weight_ref, slots_ref, mine_ref, other_ref)
        term = dot(jnp.concatenate([kept_ref[0], sent_ref[0]], 1), weight_ref[...], 1, 1)

        @pl.when(part == 0)
        def _():
            total_ref[...] = d_second_ref[...] + term

        @pl.when(part > 0)
        def _():
            total_ref[...] += term

        @pl.when(part == parts - 1)
        def _():
            d_sum, d_gain, d_shift = norm_back(total_ref[...], sum_ref[...], rows_ref[3:4, :])
            d_sum_ref[...] = d_sum
            rounded = d_sum.astype(LOW).astype(FULL)
            sums_ref[0:1, :] = jnp.sum(rounded, 0, keepdims=True)
            sums_ref[1:2, :] = d_gain
            sums_ref[2:3, :] = d_shift
            low_kept, low_sent = swap(core_ref[0], rounded)
            low_kept_ref[0] = low_kept.astype(LOW)
            low_sent_ref[0] = low_sent.astype(LOW)

    by_part = pl.BlockSpec((1, tokens, CHUNK), lambda k: (k, 0, 0))
    return pl.pallas_call(
        body,
        grid=(parts,),
        out_shape=[
            shaped(tokens, width, kind=FULL),
            shaped(1, tokens, CHUNK),
            shaped(1, tokens, CHUNK),
            shaped(3, width, kind=FULL),
        ],
        in_specs=[SMALL] * 2
        + [by_part, by_part, whole(tokens, width), whole(tokens, width), whole(*vector_rows.shape)]
        + part_blocks(mine, start),
        out_specs=[whole(tokens, width), whole(1, tokens, CHUNK), whole(1, tokens, CHUNK), whole(3, width)],
        scratch_shapes=[pltpu.VMEM((width, width), LOW), pltpu.VMEM((tokens, width), FULL)],
        name="expand_back",
    )(slots, core, kept, sent, d_second_sum, first_sum, vector_rows, mine, other)


def attend_back(tables, kept, sent, qkv, mine, other, start):
    slots, core, limits = tables
    tokens = kept.shape[1]
    width = 2 * CHUNK

    def body(
        slots_ref, core_ref, limits_ref, kept_ref, sent_ref, qkv_ref, mine_ref, other_ref,
        own_ref, away_ref, sums_ref, weight_ref, d_context_ref,
    ):
        core = core_ref[0]
        fill(weight_ref, slots_ref, mine_ref, other_ref)
        d_context = dot(jnp.concatenate([kept_ref[0], sent_ref[0]], 1), weight_ref[...], 1, 1)
        for side, half in enumerate(swap(core, d_context)):
            d_context_ref[side] = half.astype(LOW)
        for side, out_ref in enumerate((own_ref, away_ref)):
            for pair in range(CHUNK // (2 * HD)):
                lanes = slice(2 * HD * pair, 2 * HD * (pair + 1))
                for slot, rows in spans(tokens):
                    queries = qkv_ref[side, 0, rows, lanes]
                    key_rows = qkv_ref[side, 1, rows, lanes]
                    value_rows = qkv_ref[side, 2, rows, lanes]
                    d_rows = d_context_ref[side, rows, lanes]
                    low_lanes = lax.broadcasted_iota(jnp.int32, queries.shape, 1) < HD
                    grads = []
                    for head in range(2):
                        probs = probabilities(one_head(queries, low_lanes, head), key_rows, limits_ref[slot])
                        d_value = dot(probs.astype(LOW), d_rows)
                        d_probs = dot(value_rows, one_head(d_rows, low_lanes, head), 1, 1)
                        scaled = probs * d_probs
                        d_scores = scaled - probs * jnp.sum(scaled, 0, keepdims=True)
                        d_low = d_scores.astype(LOW)
                        grads.append((dot(d_low, key_rows, 0, 0) * SCORE_SCALE, dot(d_low, queries) * SCORE_SCALE, d_value))
                    for third, (low_head, high_head) in enumerate(zip(*grads)):
                        out_ref[third, rows, lanes] = jnp.where(low_lanes, low_head, high_head).astype(LOW)
        for place, third in enumerate((0, 2)):
            for side, out_ref in enumerate((own_ref, away_ref)):
                sums_ref[place, core ^ side] = jnp.sum(out_ref[third].astype(FULL), 0, keepdims=True)

    return pl.pallas_call(
        body,
        grid=(1,),
        out_shape=[shaped(3, tokens, CHUNK), shaped(3, tokens, CHUNK), shaped(2, 2, 1, CHUNK, kind=FULL)],
        in_specs=[SMALL] * 3
        + [whole(1, tokens, CHUNK), whole(1, tokens, CHUNK), whole(2, 3, tokens, CHUNK)]
        + part_blocks(mine, start),
        out_specs=[whole(3, tokens, CHUNK), whole(3, tokens, CHUNK), whole(2, 2, 1, CHUNK)],
        scratch_shapes=[pltpu.VMEM((width, width), LOW), pltpu.VMEM((2, tokens, CHUNK), LOW)],
        name="attend_back",
    )(slots, core, limits, kept, sent, qkv, mine, other)


def project_back(tables, kept, sent, d_first_sum, mine, other, start):
    slots, core, _ = tables
    tokens, width = d_first_sum.shape
    parts = kept.shape[0]

    def body(slots_ref, core_ref, kept_ref, sent_ref, d_sum_ref, mine_ref, other_ref, out_ref, weight_ref):
        part = pl.program_id(0)
        fill(weight_ref, slots_ref, mine_ref, other_ref)
        term = dot(jnp.concatenate([kept_ref[0], sent_ref[0]], 1), weight_ref[...], 1, 1)

        @pl.when(part == 0)
        def _():
            out_ref[...] = d_sum_ref[...] + term

        @pl.when(part > 0)
        def _():
            out_ref[...] += term

    by_part = pl.BlockSpec((1, tokens, CHUNK), lambda k: (k, 0, 0))
    return pl.pallas_call(
        body,
        grid=(parts,),
        out_shape=shaped(tokens, width, kind=FULL),
        in_specs=[SMALL] * 2 + [by_part, by_part, whole(tokens, width)] + part_blocks(mine, start),
        out_specs=whole(tokens, width),
        scratch_shapes=[pltpu.VMEM((width, width), LOW)],
        name="project_back",
    )(slots, core, kept, sent, d_first_sum, mine, other)


def weight_terms(slots, shards, *jobs):
    steps = jobs[0][3]
    rows = steps * CHUNK // shards
    per_tile = CHUNK // rows
    parts = [job[4].shape[0] for job in jobs]
    half = shards // 2
    tokens = jobs[0][4].shape[1]

    def body(slots_ref, *refs):
        kept_ref, sent_ref = refs[4 * len(jobs) :]
        step = pl.program_id(0)
        slots_here = [slots_ref[0, step * per_tile + block] for block in range(per_tile)]
        place = 0
        for job, count in enumerate(parts):
            left_ref, left_twin_ref, right_ref, right_twin_ref = refs[4 * job : 4 * job + 4]
            here, there = left_ref[0], left_twin_ref[0]
            for part in range(count):
                total = dot(here, right_ref[part], 0, 0) + dot(there, right_twin_ref[part], 0, 0)
                total = total.astype(LOW)
                for block, slot in enumerate(slots_here):

                    @pl.when(slot < half)
                    def _():
                        kept_ref[slot, place : place + rows] = total[block * rows : (block + 1) * rows]

                    @pl.when(slot >= half)
                    def _():
                        sent_ref[slot - half, place : place + rows] = total[block * rows : (block + 1) * rows]

                place += rows

    specs, values = [SMALL], [slots]
    for (left, left_twin, first, _, right, right_twin, twin_first), count in zip(jobs, parts):
        specs += [pl.BlockSpec((1, tokens, CHUNK), lambda i, first=first: (first + i, 0, 0))] * 2
        specs += [whole(count, tokens, CHUNK)]
        assert twin_first % count == 0
        specs += [pl.BlockSpec((count, tokens, CHUNK), lambda i, at=twin_first // count: (at, 0, 0))]
        values += [left, left_twin, right, right_twin]
    return pl.pallas_call(
        body,
        grid=(steps,),
        out_shape=[shaped(half, sum(parts) * rows, CHUNK)] * 2,
        in_specs=specs,
        out_specs=[whole(half, sum(parts) * rows, CHUNK)] * 2,
        name="weight_terms",
    )(*values)


GROUPS = (((0, 0),), ((0, 1), (0, 2)), ((0, 3),), ((1, 0), (1, 1)), ((1, 2), (1, 3)))


class Gather:
    def __init__(self, net, blocks):
        self.net = net
        self.state = [block[None] for block in blocks]
        self.twins = [None] * len(blocks)
        self.turns = 0

    def turn(self, values=()):
        stages, groups, turn = self.net.stages, len(self.state), self.turns
        for group in range(groups):
            stage = turn - group
            if 0 <= stage < stages:
                self.state[group] = self.net.widen(self.state[group], stage)
            elif stage == stages:
                self.twins[group] = self.net.twin(self.state[group])
        self.turns += 1
        nexts = [group for group in range(groups) if 0 <= turn + 1 - group <= stages]
        held = lax.optimization_barrier(tuple([self.state[group] for group in nexts] + list(values)))
        for group, value in zip(nexts, held):
            self.state[group] = value
        return held[len(nexts) :]

    def ready(self, group):
        while self.twins[group] is None:
            self.turn()
        return self.state[group], self.twins[group]


class Reduce:
    def __init__(self, net):
        self.net = net
        self.pending = {}
        self.owned = {}

    def push(self, key, kept, sent):
        self.pending[key] = (self.net.stages - 1, kept, sent)

    def turn(self, values=()):
        held = list(values)
        for key, (stage, kept, sent) in self.pending.items():
            kept, sent = self.net.narrow(kept, sent, stage)
            self.pending[key] = (stage - 1, kept, sent)
            if stage:
                held += [kept, sent]
            else:
                self.owned[key] = self.net.across(kept[0])
        self.pending = {key: entry for key, entry in self.pending.items() if entry[0] >= 0}
        held = list(lax.optimization_barrier(tuple(held)))
        values, held = held[: len(values)], held[len(values) :]
        for place, (key, entry) in enumerate(self.pending.items()):
            self.pending[key] = (entry[0], held[2 * place], held[2 * place + 1])
        return values


def shards(net, tokens, valid, qkv_weight, out_weight, up_weight, down_weight, vectors, cotangent):
    count = net.shards
    core = (lax.axis_index("rep") % 2).astype(jnp.int32)
    place = lax.axis_index("fsdp").astype(jnp.int32)
    flips = jnp.asarray(net.flips)
    own_flips = jnp.where(core == 0, flips[0], flips[1])
    twin_flips = jnp.where(core == 0, flips[1], flips[0])
    places = jnp.stack([own_flips ^ place, twin_flips ^ place])
    numbers = jnp.arange(count, dtype=jnp.int32)
    slots = jnp.sum(
        jnp.where(places[:, None, :] == numbers[None, :, None], numbers[None, None, :], 0), 2
    )
    tables = (slots, core.reshape(1), valid)
    weight_inputs = (qkv_weight, out_weight, up_weight, down_weight)
    width = tokens.shape[1]
    inner_width = up_weight.shape[2]
    parts = inner_width // width

    blocks, home = [], {}
    for number, group in enumerate(GROUPS):
        pieces, start = [], 0
        for level, kind in group:
            piece = own_chunks(weight_inputs[kind][level].astype(LOW), core)
            assert start % piece.shape[1] == 0
            home[level, kind] = (number, start // piece.shape[1])
            pieces.append(piece.reshape(-1, CHUNK))
            start += pieces[-1].shape[0]
        blocks.append(jnp.concatenate(pieces, 0))
    gather = Gather(net, blocks)

    def weight(level, kind):
        number, start = home[level, kind]
        return (*gather.ready(number), start)

    vector_blocks = vectors[None]
    for stage in range(net.stages):
        vector_blocks = net.widen(vector_blocks, stage)
        (vector_blocks,) = gather.turn((vector_blocks,))
    vector_all = jnp.take(vector_blocks, slots[0], axis=0).transpose(1, 0, 2).reshape(LAYERS, -1, width)

    hidden, h_low = tokens, tokens
    kept = []
    for level in range(LAYERS):
        rows = vector_all[level]
        last = level == LAYERS - 1
        qkv, left_a = project(tables, h_low, rows, *weight(level, 0))
        (left_a,) = gather.turn((left_a,))
        first_sum, first_low = mix(tables, left_a, hidden, rows, *weight(level, 1))
        left_b, slope = expand(tables, first_low, rows, *weight(level, 2), parts)
        left_b, slope = gather.turn((left_b, slope))
        second_sum, hidden, h_low = contract(
            tables, left_b, first_sum, rows, *weight(level, 3), inner_width, last
        )
        (h_low,) = gather.turn((h_low,))
        kept.append((qkv, left_a, first_sum, left_b, slope, second_sum))
    layer_out = h_low

    reduce = Reduce(net)
    d_hidden = cotangent
    d_vectors = [None] * LAYERS
    for level in reversed(range(LAYERS)):
        qkv, left_a, first_sum, left_b, slope, second_sum = kept[level]
        rows = vector_all[level]
        twin_a, twin_b = net.twin(left_a), net.twin(left_b)
        d_second_sum, f_kept, u_kept, sent, sums_b, sums_u = contract_back(
            tables, d_hidden, second_sum, slope, rows, *weight(level, 3), inner_width, level == LAYERS - 1
        )
        d_second_sum, f_kept, u_kept, sent = reduce.turn((d_second_sum, f_kept, u_kept, sent))

        received = net.twin(sent)
        d_first_sum, a_kept, a_sent, sums_a = expand_back(
            tables, u_kept, sent, d_second_sum, first_sum, rows, *weight(level, 2)
        )
        term = weight_terms(slots, count, (left_b, twin_b, 0, 2 * parts, f_kept, received, parts))
        *term, d_first_sum, a_kept, a_sent = reduce.turn((*term, d_first_sum, a_kept, a_sent))
        reduce.push((level, "down"), *term)

        a_received = net.twin(a_sent)
        q_kept, q_sent, sums_qv = attend_back(tables, a_kept, a_sent, qkv, *weight(level, 1))
        term = weight_terms(
            slots,
            count,
            (left_b, twin_b, 2 * parts, 2, u_kept, received, 0),
            (left_a, twin_a, 2, 2, a_kept, a_received, 0),
        )
        *term, q_kept, q_sent = reduce.turn((*term, q_kept, q_sent))
        reduce.push((level, "up"), *term)

        q_received = net.twin(q_sent)
        d_vectors[level] = jnp.concatenate(
            [sums_qv.reshape(2, width), sums_a, sums_b, sums_u.reshape(-1, width)]
        ).reshape(count, -1)
        if level == 0:
            d_vector = jnp.stack(d_vectors, 1)
            d_vector = d_vector + net.twin(d_vector)
            d_vector = jnp.take(d_vector, places[0], axis=0)
        d_hidden = project_back(tables, q_kept, q_sent, d_first_sum, *weight(level, 0))
        term = weight_terms(slots, count, (left_a, twin_a, 0, 2, q_kept, q_received, 0))
        *term, d_hidden = reduce.turn((*term, d_hidden))
        reduce.push((level, "qkv"), *term)
    reduce.push("vectors", d_vector[: count // 2], d_vector[count // 2 :])

    heights = {"down": inner_width // count, "up": (parts + 1) * width // count, "qkv": 3 * width // count}
    keys = [(level, name) for level in reversed(range(LAYERS)) for name in ("down", "up", "qkv")]
    whole_grads = {}

    def finish(names):
        mine = jnp.concatenate([reduce.owned[key] for key in names], 0)
        other = net.twin(mine)
        start = 0
        for key in names:
            height = heights[key[1]]
            whole_grads[key] = (mine[start : start + height], other[start : start + height])
            start += height

    while keys[-2] not in reduce.owned:
        reduce.turn()
    finish(keys[:-1])
    while keys[-1] not in reduce.owned:
        reduce.turn()
    finish(keys[-1:])

    def grad(name, first, parts):
        levels = []
        for level in range(LAYERS):
            mine, other = (half.reshape(-1, heights[name] // half_parts[name], CHUNK)[first : first + parts] for half in whole_grads[level, name])
            levels.append(join_chunks(mine, other, core).astype(FULL))
        return jnp.stack(levels)

    half_parts = {"down": 1, "up": parts + 1, "qkv": 3}
    return (
        layer_out,
        d_hidden,
        grad("qkv", 0, 3),
        grad("up", parts, 1),
        grad("up", 0, parts),
        grad("down", 0, 1),
        reduce.owned["vectors"],
    )


def solution(mesh):
    in_specs = (
        P(("rep", "fsdp"), None),
        P(("rep", "fsdp")),
        P(None, "fsdp", None),
        P(None, "fsdp", None),
        P(None, "fsdp", None),
        P(None, "fsdp", None),
        P(None, "fsdp"),
        P(("rep", "fsdp"), None),
    )
    out_specs = (
        P(("rep", "fsdp"), None),
        P(("rep", "fsdp"), None),
        P(None, "fsdp", None),
        P(None, "fsdp", None),
        P(None, "fsdp", None),
        P(None, "fsdp", None),
        P(None, "fsdp"),
    )
    net = Net(mesh)
    return jax.shard_map(functools.partial(shards, net), mesh=mesh, in_specs=in_specs, out_specs=out_specs, check_vma=False)
```

time: 1880 us -> 555 us (0.30)
  waiting for transfers between devices: 1450 us -> 179 us
  Pallas kernels: 0 us -> 229 us
  matrix products: 203 us -> 0 us
  blocking collectives: 121 us -> 0 us
  starting transfers between devices: 0.94 us -> 70.6 us
  local copies, waits for them, and re-layouts: 46 us -> 13.4 us
    reduce_scatter x6 -> x0, waiting for transfers between devices: 822 us -> none  [the longest x2 284 us: shards(): lax.psum_scatter(term_down.astype(jnp.bfloat16), 'fsdp', scatter_dimensio...]
    all_gather x8 -> x0, waiting for transfers between devices: 452 us -> none  [the longest x2 158 us: shards(): lax.all_gather(up_weight[level_idx].astype(jnp.bfloat16), 'fsdp', axis=0,...]
    pallas_call x0 -> x22, Pallas kernels: none -> 229 us  [the longest x6 56 us: weight_terms(): pl.pallas_call(body, grid=(steps,), out_shape=[shaped(half, sum(parts) *...]
    dot_general x36 -> x0, matrix products: 203 us -> none  [the longest x8 48.1 us: times_transposed(): lax.dot_general(left, right, (((1,), (1,)), ((), ())), preferred_element_...]
    ppermute x0 -> x70, waiting for transfers between devices: none -> 179 us  [the longest x52 168 us: trade(): return lax.ppermute(value, ('rep', 'fsdp'), pairs)]
    unnamed x19 -> x0, waiting for transfers between devices: 177 us -> none
    unnamed x1 -> x0, blocking collectives: 74.8 us -> none
    ppermute x0 -> x70, starting transfers between devices: none -> 70.6 us  [the longest x52 68.2 us: trade(): return lax.ppermute(value, ('rep', 'fsdp'), pairs)]
  transfers between devices with their start and end apart: 17 -> 70, of which waited for: 16 -> 28; matrix products, arithmetic and copies ran while one was open for 10% -> 9% of each run, Pallas kernels for 0% -> 40%
where the time goes in v3:
time: 555 us; the launch traced here: 549 us
  Pallas kernels  229 us (41%)
  waiting for transfers between devices  179 us (32%)
  starting transfers between devices  70.6 us (13%)
  other arithmetic  54.9 us (10%)
  local copies, waits for them, and re-layouts  13.4 us (2%)
    ppermute x52, waiting for transfers between devices, trade(): return lax.ppermute(value, ('rep', 'fsdp'), pairs)  168 us
    ppermute x52, starting transfers between devices, trade(): return lax.ppermute(value, ('rep', 'fsdp'), pairs)  68.2 us
    pallas_call x6, Pallas kernels, weight_terms(): pl.pallas_call(body, grid=(steps,), out_shape=[shaped(half, sum(parts) *...  56 us
    pallas_call x2, Pallas kernels, attend_back(): pl.pallas_call(body, grid=(1,), out_shape=[shaped(3, tokens, CHUNK), shap...  41.3 us
    pallas_call x2, Pallas kernels, project(): pl.pallas_call(body, grid=(3,), out_shape=[shaped(2, 3, tokens, CHUNK), s...  28.4 us
    concatenate x24, other arithmetic, widen(): return jnp.concatenate([value, self.trade(value, stage)], 0)  27.3 us
    pallas_call x2, Pallas kernels, contract_back(): pl.pallas_call(body, grid_spec=pltpu.PrefetchScalarGridSpec(num_scalar_pr...  22.1 us
    pallas_call x2, Pallas kernels, contract(): pl.pallas_call(body, grid_spec=pltpu.PrefetchScalarGridSpec(num_scalar_pr...  21.8 us
  transfers between devices with their start and end apart: 70, of which 28 were waited for; matrix products, arithmetic and copies ran while one was open for 9% of the time, Pallas kernels for 40%

profile of v3, /device:TPU:0, one launch (start us, length us, event | category | flops | bytes accessed | tf_op | source)
XLA Modules:
  0.0 549.2 jit_solution(3392303118280432289)
XLA Ops:
  2.1 3.1 collective-permute-start
  8.8 2.7 collective-permute-start.4
  13.6 5.3 collective-permute-done.3
  18.9 14.1 %collective-permute-done.2 = bf16[2,144,384]{2,1,0:T(8,128)(2,1)S(1)} collective-permute-done((bf16[2,144,384]{2,1,0:T(8,128)(2,1)S(1)}, bf16[2,144,384]{2,1,0:T(8,128)(2,1)S(1)}, u32[]{:S(2)}, u32[]{:S(2)}) %collective-permute-start.2) | collective-permute-done | bytes 221216 | tf_op jit(solution)/shard_map/ppermute | solution.py:48
  37.1 8.9 %collective-permute-done.7 = bf16[1,192,384]{2,1,0:T(8,128)(2,1)S(1)} collective-permute-done((bf16[1,192,384]{2,1,0:T(8,128)(2,1)S(1)}, bf16[1,192,384]{2,1,0:T(8,128)(2,1)S(1)}, u32[]{:S(2)}, u32[]{:S(2)}) %collective-permute-start.7) | collective-permute-done | bytes 147488 | tf_op jit(solution)/shard_map/ppermute | solution.py:48
  49.3 3.5 collective-permute-start.12
  52.8 2.8 collective-permute-start.11
  56.4 4.2 collective-permute-done.13
  69.1 8.2 %collective-permute-start.17 = (bf16[1,384,384]{2,1,0:T(8,128)(2,1)}, bf16[1,384,384]{2,1,0:T(8,128)(2,1)}, u32[]{:S(2)}, u32[]{:S(2)}) collective-permute-start(bf16[1,384,384]{2,1,0:T(8,128)(2,1)} %maximum_bitcast_fusion), channel_id=1, source_target_pairs={{0,4},{1,5},{2,6},{3,7},{4,0},{5,1},{6,2},{7,3},{8,12},{9,13},{10,... | collective-permute-start | bytes 884744 | tf_op jit(solution)/shard_map/ppermute | solution.py:48
  77.2 2.8 collective-permute-start.16
  80.1 2.7 collective-permute-done.17
  82.8 1.9 pad_maximum_fusion.14
  84.7 9.2 %collective-permute-done.16 = bf16[2,192,384]{2,1,0:T(8,128)(2,1)S(1)} collective-permute-done((bf16[2,192,384]{2,1,0:T(8,128)(2,1)}, bf16[2,192,384]{2,1,0:T(8,128)(2,1)S(1)}, u32[]{:S(2)}, u32[]{:S(2)}) %collective-permute-start.16) | collective-permute-done | bytes 294944 | tf_op jit(solution)/shard_map/ppermute | solution.py:48
  95.7 2.4 pad_maximum_fusion.7
  98.1 3.8 pad_maximum_fusion.1.mine_ref
  103.3 2.2 gather_fusion
  110.0 14.3 %project.2 = (bf16[2,3,512,384]{3,2,1,0:T(8,128)(2,1)}, bf16[4,512,384]{2,1,0:T(8,128)(2,1)}) custom-call(s32[2,16]{1,0:T(2,128)} %copy-done.19, s32[1]{0:T(128)} %bitcast.core_ref, s32[4]{0:T(128)} %limits_ref.15, bf16[512,768]{1,0:T(8,128)(2,1)} %hidden_ref.1, f32[12,768]{1,0:T(8,128)} %squeeze.21.rows_ref, bf16[16,144,384]{2,1,0:T(8,128)(2,1)} %copy-done.2, ...), custom_call_target="tpu_custom_call" | custom-call | tf_op jit(solution)/shard_map/project/pallas_call | solution.py:216
  124.3 7.3 %collective-permute-done.20 = bf16[2,384,384]{2,1,0:T(8,128)(2,1)} collective-permute-done((bf16[2,384,384]{2,1,0:T(8,128)(2,1)}, bf16[2,384,384]{2,1,0:T(8,128)(2,1)}, u32[]{:S(2)}, u32[]{:S(2)}) %collective-permute-start.20) | collective-permute-done | bytes 589856 | tf_op jit(solution)/shard_map/ppermute | solution.py:48
  134.4 1.9 pad_maximum_fusion.2.refs_0_.refs_1_.refs_2_.refs_3_
  138.6 25.9 %collective-permute-done.23 = bf16[4,384,384]{2,1,0:T(8,128)(2,1)S(1)} collective-permute-done((bf16[4,384,384]{2,1,0:T(8,128)(2,1)S(1)}, bf16[4,384,384]{2,1,0:T(8,128)(2,1)S(1)}, u32[]{:S(2)}, u32[]{:S(2)}) %collective-permute-start.23) | collective-permute-done | bytes 1179680 | tf_op jit(solution)/shard_map/ppermute | solution.py:48
  167.9 4.2 mix.2
  172.1 9.0 %expand.2 = (bf16[10,512,384]{2,1,0:T(8,128)(2,1)}, bf16[8,512,384]{2,1,0:T(8,128)(2,1)}) custom-call(s32[2,16]{1,0:T(2,128)} %copy-done.19, s32[1]{0:T(128)} %bitcast.core_ref, bf16[512,768]{1,0:T(8,128)(2,1)} %get-tuple-element.195.x_ref, f32[12,768]{1,0:T(8,128)} %squeeze.21.rows_ref, bf16[16,240,384]{2,1,0:T(8,128)(2,1)} %pad_maximum_fusion.1.mine_ref, ...), custom_call_target="tpu_custom_call" | custom-call | tf_op jit(solution)/shard_map/expand/pallas_call | solution.py:276
  182.0 11.1 %contract.2 = (f32[512,768]{1,0:T(8,128)}, f32[512,768]{1,0:T(8,128)}, bf16[512,768]{1,0:T(8,128)(2,1)}) custom-call(s32[2,16]{1,0:T(2,128)} %copy-done.19, s32[1]{0:T(128)} %bitcast.core_ref, s32[4]{0:T(128)} %limits_ref.15, bf16[10,512,384]{2,1,0:T(8,128)(2,1)} %get-tuple-element.199.active_ref.refs_0_, f32[512,768]{1,0:T(8,128)} %get-tuple-element.200.first_ref.sum_ref, ...), custom_call_target="tpu_custom_call" | custom-call | tf_op jit(solution)/shard_map/contract/pallas_call | solution.py:334
  193.1 17.2 %collective-permute-done.25 = bf16[8,384,384]{2,1,0:T(8,128)(2,1)} collective-permute-done((bf16[8,384,384]{2,1,0:T(8,128)(2,1)}, bf16[8,384,384]{2,1,0:T(8,128)(2,1)}, u32[]{:S(2)}, u32[]{:S(2)}) %collective-permute-start.25) | collective-permute-done | bytes 2359328 | tf_op jit(solution)/shard_map/ppermute | solution.py:48
  210.3 5.2 pad_maximum_fusion.mine_ref.refs_0_.refs_1_.refs_2_.refs_3_
  216.6 9.8 %collective-permute-done.27.other_ref = bf16[16,192,384]{2,1,0:T(8,128)(2,1)} collective-permute-done((bf16[16,192,384]{2,1,0:T(8,128)(2,1)S(1)}, bf16[16,192,384]{2,1,0:T(8,128)(2,1)}, u32[]{:S(2)}, u32[]{:S(2)}) %collective-permute-start.27) | collective-permute-done | bytes 2359328 | tf_op jit(solution)/shard_map/ppermute | solution.py:51
  226.5 14.1 %project.3 = (bf16[2,3,512,384]{3,2,1,0:T(8,128)(2,1)}, bf16[4,512,384]{2,1,0:T(8,128)(2,1)}) custom-call(s32[2,16]{1,0:T(2,128)} %copy-done.19, s32[1]{0:T(128)} %bitcast.core_ref, s32[4]{0:T(128)} %limits_ref.15, bf16[512,768]{1,0:T(8,128)(2,1)} %get-tuple-element.203.x_ref, f32[12,768]{1,0:T(8,128)} %squeeze.22.rows_ref, ...), custom_call_target="tpu_custom_call" | custom-call | tf_op jit(solution)/shard_map/project/pallas_call | solution.py:216
  240.6 4.4 mix.3
  245.0 9.0 %expand.3 = (bf16[10,512,384]{2,1,0:T(8,128)(2,1)}, bf16[8,512,384]{2,1,0:T(8,128)(2,1)}) custom-call(s32[2,16]{1,0:T(2,128)} %copy-done.19, s32[1]{0:T(128)} %bitcast.core_ref, bf16[512,768]{1,0:T(8,128)(2,1)} %get-tuple-element.207.x_ref, f32[12,768]{1,0:T(8,128)} %squeeze.22.rows_ref, ...), custom_call_target="tpu_custom_call" | custom-call | tf_op jit(solution)/shard_map/expand/pallas_call | solution.py:276
  254.3 10.7 %contract.3 = (f32[512,768]{1,0:T(8,128)}, f32[512,768]{1,0:T(8,128)}, bf16[512,768]{1,0:T(8,128)(2,1)}) custom-call(s32[2,16]{1,0:T(2,128)} %copy-done.19, s32[1]{0:T(128)} %bitcast.core_ref, s32[4]{0:T(128)} %limits_ref.15, bf16[10,512,384]{2,1,0:T(8,128)(2,1)} %get-tuple-element.209.active_ref.refs_0_, f32[512,768]{1,0:T(8,128)} %get-tuple-element.210.first_ref.sum_ref, ...), custom_call_target="tpu_custom_call" | custom-call | tf_op jit(solution)/shard_map/contract/pallas_call | solution.py:334
  265.1 11.1 %contract_back.2 = (f32[512,768]{1,0:T(8,128)}, bf16[1,512,384]{2,1,0:T(8,128)(2,1)}, bf16[4,512,384]{2,1,0:T(8,128)(2,1)}, bf16[5,512,384]{2,1,0:T(8,128)(2,1)}...) custom-call(s32[2,16]{1,0:T(2,128)} %copy-done.19, s32[1]{0:T(128)} %bitcast.core_ref, s32[4]{0:T(128)} %limits_ref.15, ...), custom_call_target="tpu_custom_call" | custom-call | tf_op jit(solution)/shard_map/contract_back/pallas_call | solution.py:394
  276.8 9.8 %expand_back.2 = (f32[512,768]{1,0:T(8,128)}, bf16[1,512,384]{2,1,0:T(8,128)(2,1)}, bf16[1,512,384]{2,1,0:T(8,128)(2,1)}, f32[3,768]{1,0:T(4,128)}) custom-call(s32[2,16]{1,0:T(2,128)} %copy-done.19, s32[1]{0:T(128)} %bitcast.core_ref, bf16[4,512,384]{2,1,0:T(8,128)(2,1)} %get-tuple-element.218.kept_ref.refs_2_, ...), custom_call_target="tpu_custom_call" | custom-call | tf_op jit(solution)/shard_map/expand_back/pallas_call | solution.py:463
  287.9 9.6 %weight_terms.6 = (bf16[8,192,384]{2,1,0:T(8,128)(2,1)}, bf16[8,192,384]{2,1,0:T(8,128)(2,1)}) custom-call(s32[2,16]{1,0:T(2,128)} %copy-done.19, bf16[10,512,384]{2,1,0:T(8,128)(2,1)} %get-tuple-element.209.active_ref.refs_0_, bf16[10,512,384]{2,1,0:T(8,128)(2,1)} %collective-permute-done.32.refs_1_, bf16[1,512,384]{2,1,0:T(8,128)(2,1)} %get-tuple-element.220.refs_2_, ...), custom_call_target="tpu_custom_call" | custom-call | tf_op jit(solution)/shard_map/weight_terms/pallas_call | solution.py:600
  298.5 20.6 %attend_back.2 = (bf16[3,512,384]{2,1,0:T(8,128)(2,1)}, bf16[3,512,384]{2,1,0:T(8,128)(2,1)}, f32[2,2,1,384]{3,2,1,0:T(1,128)}) custom-call(s32[2,16]{1,0:T(2,128)} %copy-done.19, s32[1]{0:T(128)} %bitcast.core_ref, s32[4]{0:T(128)} %limits_ref.15, bf16[1,512,384]{2,1,0:T(8,128)(2,1)} %get-tuple-element.227.refs_6_.kept_ref, ...), custom_call_target="tpu_custom_call" | custom-call | tf_op jit(solution)/shard_map/attend_back/pallas_call | solution.py:519
  319.9 11.2 %weight_terms.7 = (bf16[8,240,384]{2,1,0:T(8,128)(2,1)}, bf16[8,240,384]{2,1,0:T(8,128)(2,1)}) custom-call(s32[2,16]{1,0:T(2,128)} %copy-done.19, bf16[10,512,384]{2,1,0:T(8,128)(2,1)} %get-tuple-element.209.active_ref.refs_0_, bf16[10,512,384]{2,1,0:T(8,128)(2,1)} %collective-permute-done.32.refs_1_, ...), custom_call_target="tpu_custom_call" | custom-call | tf_op jit(solution)/shard_map/weight_terms/pallas_call | solution.py:600
  335.0 6.7 %project_back.2.d_out_ref = f32[512,768]{1,0:T(8,128)} custom-call(s32[2,16]{1,0:T(2,128)} %copy-done.19, s32[1]{0:T(128)} %bitcast.core_ref, bf16[3,512,384]{2,1,0:T(8,128)(2,1)} %get-tuple-element.236.refs_2_.kept_ref, bf16[3,512,384]{2,1,0:T(8,128)(2,1)} %get-tuple-element.237.sent_ref, f32[512,768]{1,0:T(8,128)} %get-tuple-element.240.d_sum_ref, ...), custom_call_target="tpu_custom_call" | custom-call | tf_op jit(solution)/shard_map/project_back/pallas_call | solution.py:551
  341.7 8.9 %collective-permute-done.37 = bf16[4,192,384]{2,1,0:T(8,128)(2,1)S(1)} collective-permute-done((bf16[4,192,384]{2,1,0:T(8,128)(2,1)S(1)}, bf16[4,192,384]{2,1,0:T(8,128)(2,1)S(1)}, u32[]{:S(2)}, u32[]{:S(2)}) %collective-permute-start.37) | collective-permute-done | bytes 589856 | tf_op jit(solution)/shard_map/ppermute | solution.py:48
  351.5 7.2 %weight_terms.8 = (bf16[8,144,384]{2,1,0:T(8,128)(2,1)}, bf16[8,144,384]{2,1,0:T(8,128)(2,1)}) custom-call(s32[2,16]{1,0:T(2,128)} %copy-done.19, bf16[4,512,384]{2,1,0:T(8,128)(2,1)} %get-tuple-element.205.context_ref.refs_4_.refs_0_, bf16[4,512,384]{2,1,0:T(8,128)(2,1)} %collective-permute-done.31.refs_5_.refs_1_, ...), custom_call_target="tpu_custom_call" | custom-call | tf_op jit(solution)/shard_map/weight_terms/pallas_call | solution.py:600
  358.7 2.6 add_convert_fusion.2
  363.4 11.0 %contract_back.3 = (f32[512,768]{1,0:T(8,128)}, bf16[1,512,384]{2,1,0:T(8,128)(2,1)}, bf16[4,512,384]{2,1,0:T(8,128)(2,1)}, bf16[5,512,384]{2,1,0:T(8,128)(2,1)}...) custom-call(s32[2,16]{1,0:T(2,128)} %copy-done.19, s32[1]{0:T(128)} %bitcast.core_ref, s32[4]{0:T(128)} %limits_ref.15, ...), custom_call_target="tpu_custom_call" | custom-call | tf_op jit(solution)/shard_map/contract_back/pallas_call | solution.py:394
  374.4 3.1 collective-permute-done.39
  378.4 2.4 collective-permute-done.40
  384.5 9.9 %expand_back.3 = (f32[512,768]{1,0:T(8,128)}, bf16[1,512,384]{2,1,0:T(8,128)(2,1)}, bf16[1,512,384]{2,1,0:T(8,128)(2,1)}, f32[3,768]{1,0:T(4,128)}) custom-call(s32[2,16]{1,0:T(2,128)} %copy-done.19, s32[1]{0:T(128)} %bitcast.core_ref, bf16[4,512,384]{2,1,0:T(8,128)(2,1)} %get-tuple-element.258.kept_ref.refs_2_, ...), custom_call_target="tpu_custom_call" | custom-call | tf_op jit(solution)/shard_map/expand_back/pallas_call | solution.py:463
  394.4 7.4 %collective-permute-done.43 = bf16[2,240,384]{2,1,0:T(8,128)(2,1)} collective-permute-done((bf16[2,240,384]{2,1,0:T(8,128)(2,1)}, bf16[2,240,384]{2,1,0:T(8,128)(2,1)}, u32[]{:S(2)}, u32[]{:S(2)}) %collective-permute-start.43) | collective-permute-done | bytes 368672 | tf_op jit(solution)/shard_map/ppermute | solution.py:48
  401.8 2.0 add_convert_fusion.28
  403.8 2.1 add_convert_fusion.22
  407.3 9.7 %weight_terms.9 = (bf16[8,192,384]{2,1,0:T(8,128)(2,1)}, bf16[8,192,384]{2,1,0:T(8,128)(2,1)}) custom-call(s32[2,16]{1,0:T(2,128)} %copy-done.19, bf16[10,512,384]{2,1,0:T(8,128)(2,1)} %get-tuple-element.199.active_ref.refs_0_, bf16[10,512,384]{2,1,0:T(8,128)(2,1)} %collective-permute-done.30.refs_1_, bf16[1,512,384]{2,1,0:T(8,128)(2,1)} %get-tuple-element.260.refs_2_, ...), custom_call_target="tpu_custom_call" | custom-call | tf_op jit(solution)/shard_map/weight_terms/pallas_call | solution.py:600
  418.3 20.7 %attend_back.3 = (bf16[3,512,384]{2,1,0:T(8,128)(2,1)}, bf16[3,512,384]{2,1,0:T(8,128)(2,1)}, f32[2,2,1,384]{3,2,1,0:T(1,128)}) custom-call(s32[2,16]{1,0:T(2,128)} %copy-done.19, s32[1]{0:T(128)} %bitcast.core_ref, s32[4]{0:T(128)} %limits_ref.15, bf16[1,512,384]{2,1,0:T(8,128)(2,1)} %get-tuple-element.271.refs_6_.kept_ref, ...), custom_call_target="tpu_custom_call" | custom-call | tf_op jit(solution)/shard_map/attend_back/pallas_call | solution.py:519
  440.4 11.1 %weight_terms.10 = (bf16[8,240,384]{2,1,0:T(8,128)(2,1)}, bf16[8,240,384]{2,1,0:T(8,128)(2,1)}) custom-call(s32[2,16]{1,0:T(2,128)} %copy-done.19, bf16[10,512,384]{2,1,0:T(8,128)(2,1)} %get-tuple-element.199.active_ref.refs_0_, bf16[10,512,384]{2,1,0:T(8,128)(2,1)} %collective-permute-done.30.refs_1_, ...), custom_call_target="tpu_custom_call" | custom-call | tf_op jit(solution)/shard_map/weight_terms/pallas_call | solution.py:600
  456.2 3.2 collective-permute-start.64
  461.0 6.7 %project_back.3 = f32[512,768]{1,0:T(8,128)} custom-call(s32[2,16]{1,0:T(2,128)} %copy-done.19, s32[1]{0:T(128)} %bitcast.core_ref, bf16[3,512,384]{2,1,0:T(8,128)(2,1)} %get-tuple-element.282.refs_2_.kept_ref, bf16[3,512,384]{2,1,0:T(8,128)(2,1)} %get-tuple-element.283.sent_ref, f32[512,768]{1,0:T(8,128)} %get-tuple-element.286.d_sum_ref, ...), custom_call_target="tpu_custom_call" | custom-call | tf_op jit(solution)/shard_map/project_back/pallas_call | solution.py:551
  467.7 3.5 collective-permute-done.49
  471.2 1.9 add_convert_fusion.16
  473.1 7.2 %weight_terms.11 = (bf16[8,144,384]{2,1,0:T(8,128)(2,1)}, bf16[8,144,384]{2,1,0:T(8,128)(2,1)}) custom-call(s32[2,16]{1,0:T(2,128)} %copy-done.19, bf16[4,512,384]{2,1,0:T(8,128)(2,1)} %get-tuple-element.193.context_ref.refs_4_.refs_0_, bf16[4,512,384]{2,1,0:T(8,128)(2,1)} %collective-permute-done.29.refs_5_.refs_1_, ...), custom_call_target="tpu_custom_call" | custom-call | tf_op jit(solution)/shard_map/weight_terms/pallas_call | solution.py:600
  482.0 3.2 collective-permute-start.65
  486.7 3.5 collective-permute-done.65
  490.4 2.5 collective-permute-start.63
  492.9 7.8 %collective-permute-done.51 = bf16[2,192,384]{2,1,0:T(8,128)(2,1)S(1)} collective-permute-done((bf16[2,192,384]{2,1,0:T(8,128)(2,1)S(1)}, bf16[2,192,384]{2,1,0:T(8,128)(2,1)S(1)}, u32[]{:S(2)}, u32[]{:S(2)}) %collective-permute-start.51) | collective-permute-done | bytes 294944 | tf_op jit(solution)/shard_map/ppermute | solution.py:48
  502.4 2.3 collective-permute-start.56
  506.0 16.2 %collective-permute-done.56 = bf16[2,240,384]{2,1,0:T(8,128)(2,1)S(1)} collective-permute-done((bf16[2,240,384]{2,1,0:T(8,128)(2,1)S(1)}, bf16[2,240,384]{2,1,0:T(8,128)(2,1)S(1)}, u32[]{:S(2)}, u32[]{:S(2)}) %collective-permute-start.56) | collective-permute-done | bytes 368672 | tf_op jit(solution)/shard_map/ppermute | solution.py:48
  522.5 2.9 collective-permute-start.60
  525.5 4.5 collective-permute-done.67
  530.2 8.0 %collective-permute-done.59 = bf16[2,144,384]{2,1,0:T(8,128)(2,1)S(1)} collective-permute-done((bf16[2,144,384]{2,1,0:T(8,128)(2,1)S(1)}, bf16[2,144,384]{2,1,0:T(8,128)(2,1)S(1)}, u32[]{:S(2)}, u32[]{:S(2)}) %collective-permute-start.59) | collective-permute-done | bytes 221216 | tf_op jit(solution)/shard_map/ppermute | solution.py:48
  538.4 2.1 collective-permute-start.61
  (323 shorter events, 82.6 us)
Async XLA Ops:
  2.1 6.7 %collective-permute-start = (bf16[1,144,384]{2,1,0:T(8,128)(2,1)S(1)}, bf16[1,144,384]{2,1,0:T(8,128)(2,1)S(1)}, u32[]{:S(2)}, u32[]{:S(2)}) collective-permute-start(bf16[1,144,384]{2,1,0:T(8,128)(2,1)S(1)} %bitcast.89), channel_id=1, source_target_pairs={{0,4},{1,5},{2,6},{3,7},{4,0},{5,1},{6,2},{7,3},{8,12},{9,13},{10,... | collective-permute-start | bytes 331784 | tf_op jit(solution)/shard_map/ppermute | solution.py:48
  8.8 4.7 collective-permute-start.4
  11.5 7.4 %collective-permute-start.3 = (bf16[1,240,384]{2,1,0:T(8,128)(2,1)S(1)}, bf16[1,240,384]{2,1,0:T(8,128)(2,1)S(1)}, u32[]{:S(2)}, u32[]{:S(2)}) collective-permute-start(bf16[1,240,384]{2,1,0:T(8,128)(2,1)S(1)} %maximum_bitcast_fusion.1), channel_id=1, source_target_pairs={{0,4},{1,5},{2,6},{3,7},{4,0},{5,1},{6,2},{7,3},{8,12},{9,13},{10,... | collective-permute-start | bytes 552968 | tf_op jit(solution)/shard_map/ppermute | solution.py:48
  12.8 20.3 %collective-permute-start.2 = (bf16[2,144,384]{2,1,0:T(8,128)(2,1)S(1)}, bf16[2,144,384]{2,1,0:T(8,128)(2,1)S(1)}, u32[]{:S(2)}, u32[]{:S(2)}) collective-permute-start(bf16[2,144,384]{2,1,0:T(8,128)(2,1)S(1)} %pad_maximum_fusion.19), channel_id=1, source_target_pairs={{0,8},{1,9},{2,10},{3,11},{4,12},{5,13},{6,14},{7,15},{8,0},{9,1},... | collective-permute-start | bytes 663560 | tf_op jit(solution)/shard_map/ppermute | solution.py:48
  33.1 12.9 %collective-permute-start.6 = (bf16[2,240,384]{2,1,0:T(8,128)(2,1)S(1)}, bf16[2,240,384]{2,1,0:T(8,128)(2,1)S(1)}, u32[]{:S(2)}, u32[]{:S(2)}) collective-permute-start(bf16[2,240,384]{2,1,0:T(8,128)(2,1)S(1)} %pad_maximum_fusion.16), channel_id=1, source_target_pairs={{0,8},{1,9},{2,10},{3,11},{4,12},{5,13},{6,14},{7,15},{8,0},{9,1},... | collective-permute-start | bytes 1105928 | tf_op jit(solution)/shard_map/ppermute | solution.py:48
  34.8 11.2 %collective-permute-start.7 = (bf16[1,192,384]{2,1,0:T(8,128)(2,1)S(1)}, bf16[1,192,384]{2,1,0:T(8,128)(2,1)S(1)}, u32[]{:S(2)}, u32[]{:S(2)}) collective-permute-start(bf16[1,192,384]{2,1,0:T(8,128)(2,1)S(1)} %constant_dynamic-slice_fusion.7), channel_id=1, source_target_pairs={{0,4},{1,5},{2,6},{3,7},{4,0},{5,1},{6,2},{7,3},{8,12},{9,13},{10,... | collective-permute-start | bytes 442376 | tf_op jit(solution)/shard_map/ppermute | solution.py:48
  34.8 11.3 %collective-permute-start.5 = (bf16[4,144,384]{2,1,0:T(8,128)(2,1)S(1)}, bf16[4,144,384]{2,1,0:T(8,128)(2,1)S(1)}, u32[]{:S(2)}, u32[]{:S(2)}) collective-permute-start(bf16[4,144,384]{2,1,0:T(8,128)(2,1)S(1)} %pad_maximum_fusion.15), channel_id=1, source_target_pairs={{0,1},{1,0},{2,3},{3,2},{4,5},{5,4},{6,7},{7,6},{8,9},{9,8},{10,11... | collective-permute-start | bytes 1327112 | tf_op jit(solution)/shard_map/ppermute | solution.py:48
  46.2 18.2 %collective-permute-start.10 = (bf16[4,240,384]{2,1,0:T(8,128)(2,1)S(1)}, bf16[4,240,384]{2,1,0:T(8,128)(2,1)S(1)}, u32[]{:S(2)}, u32[]{:S(2)}) collective-permute-start(bf16[4,240,384]{2,1,0:T(8,128)(2,1)S(1)} %pad_maximum_fusion.11), channel_id=1, source_target_pairs={{0,1},{1,0},{2,3},{3,2},{4,5},{5,4},{6,7},{7,6},{8,9},{9,8},{10,11... | collective-permute-start | bytes 2211848 | tf_op jit(solution)/shard_map/ppermute | solution.py:48
  47.1 18.6 %collective-permute-start.9 = (bf16[8,144,384]{2,1,0:T(8,128)(2,1)S(1)}, bf16[8,144,384]{2,1,0:T(8,128)(2,1)S(1)}, u32[]{:S(2)}, u32[]{:S(2)}) collective-permute-start(bf16[8,144,384]{2,1,0:T(8,128)(2,1)S(1)} %pad_maximum_fusion.10), channel_id=1, source_target_pairs={{0,2},{1,3},{2,0},{3,1},{4,6},{5,7},{6,4},{7,5},{8,10},{9,11},{10,... | collective-permute-start | bytes 2654216 | tf_op jit(solution)/shard_map/ppermute | solution.py:48
  49.1 11.5 %collective-permute-start.13 = (f32[8,2,576]{2,1,0:T(2,128)S(1)}, f32[8,2,576]{2,1,0:T(2,128)S(1)}, u32[]{:S(2)}, u32[]{:S(2)}) collective-permute-start(f32[8,2,576]{2,1,0:T(2,128)S(1)} %pad_maximum_fusion.28), channel_id=1, source_target_pairs={{0,2},{1,3},{2,0},{3,1},{4,6},{5,7},{6,4},{7,5},{8,10},{9,11},{10,... | collective-permute-start | bytes 110600 | tf_op jit(solution)/shard_map/ppermute | solution.py:48
  49.3 12.0 %collective-permute-start.12 = (bf16[1,192,384]{2,1,0:T(8,128)(2,1)S(1)}, bf16[1,192,384]{2,1,0:T(8,128)(2,1)S(1)}, u32[]{:S(2)}, u32[]{:S(2)}) collective-permute-start(bf16[1,192,384]{2,1,0:T(8,128)(2,1)S(1)} %maximum_bitcast_fusion.2), channel_id=1, source_target_pairs={{0,4},{1,5},{2,6},{3,7},{4,0},{5,1},{6,2},{7,3},{8,12},{9,13},{10,... | collective-permute-start | bytes 442376 | tf_op jit(solution)/shard_map/ppermute | solution.py:48
  52.8 10.8 %collective-permute-start.11 = (bf16[2,192,384]{2,1,0:T(8,128)(2,1)S(1)}, bf16[2,192,384]{2,1,0:T(8,128)(2,1)S(1)}, u32[]{:S(2)}, u32[]{:S(2)}) collective-permute-start(bf16[2,192,384]{2,1,0:T(8,128)(2,1)S(1)} %pad_maximum_fusion.17), channel_id=1, source_target_pairs={{0,8},{1,9},{2,10},{3,11},{4,12},{5,13},{6,14},{7,15},{8,0},{9,1},... | collective-permute-start | bytes 884744 | tf_op jit(solution)/shard_map/ppermute | solution.py:48
  66.0 32.2 %collective-permute-start.14 = (bf16[8,240,384]{2,1,0:T(8,128)(2,1)}, bf16[8,240,384]{2,1,0:T(8,128)(2,1)}, u32[]{:S(2)}, u32[]{:S(2)}) collective-permute-start(bf16[8,240,384]{2,1,0:T(8,128)(2,1)} %pad_maximum_fusion.6), channel_id=1, source_target_pairs={{0,2},{1,3},{2,0},{3,1},{4,6},{5,7},{6,4},{7,5},{8,10},{9,11},{10,... | collective-permute-start | bytes 4423688 | tf_op jit(solution)/shard_map/ppermute | solution.py:48
  67.6 28.2 %collective-permute-start.15 = (bf16[4,192,384]{2,1,0:T(8,128)(2,1)}, bf16[4,192,384]{2,1,0:T(8,128)(2,1)}, u32[]{:S(2)}, u32[]{:S(2)}) collective-permute-start(bf16[4,192,384]{2,1,0:T(8,128)(2,1)} %pad_maximum_fusion.12), channel_id=1, source_target_pairs={{0,1},{1,0},{2,3},{3,2},{4,5},{5,4},{6,7},{7,6},{8,9},{9,8},{10,11... | collective-permute-start | bytes 1769480 | tf_op jit(solution)/shard_map/ppermute | solution.py:48
  69.1 13.7 %collective-permute-start.17 = (bf16[1,384,384]{2,1,0:T(8,128)(2,1)}, bf16[1,384,384]{2,1,0:T(8,128)(2,1)}, u32[]{:S(2)}, u32[]{:S(2)}) collective-permute-start(bf16[1,384,384]{2,1,0:T(8,128)(2,1)} %maximum_bitcast_fusion), channel_id=1, source_target_pairs={{0,4},{1,5},{2,6},{3,7},{4,0},{5,1},{6,2},{7,3},{8,12},{9,13},{10,... | collective-permute-start | bytes 884744 | tf_op jit(solution)/shard_map/ppermute | solution.py:48
  77.2 31.5 %collective-permute-start.21 = (bf16[16,144,384]{2,1,0:T(8,128)(2,1)S(1)}, bf16[16,144,384]{2,1,0:T(8,128)(2,1)S(1)}, u32[]{:S(2)}, u32[]{:S(2)}) collective-permute-start(bf16[16,144,384]{2,1,0:T(8,128)(2,1)S(1)} %pad_maximum_fusion.5.mine_ref), channel_id=1, source_target_pairs={{0,16},{16,0},{1,17},{17,1},{2,18},{18,2},{3,19},{19,3},{4,20},{20... | collective-permute-start | bytes 5308424 | tf_op jit(solution)/shard_map/ppermute | solution.py:51
  77.2 16.7 %collective-permute-start.16 = (bf16[2,192,384]{2,1,0:T(8,128)(2,1)}, bf16[2,192,384]{2,1,0:T(8,128)(2,1)S(1)}, u32[]{:S(2)}, u32[]{:S(2)}) collective-permute-start(bf16[2,192,384]{2,1,0:T(8,128)(2,1)} %pad_maximum_fusion.18), channel_id=1, source_target_pairs={{0,8},{1,9},{2,10},{3,11},{4,12},{5,13},{6,14},{7,15},{8,0},{9,1},... | collective-permute-start | bytes 884744 | tf_op jit(solution)/shard_map/ppermute | solution.py:48
  101.9 66.0 %collective-permute-start.24 = (bf16[16,240,384]{2,1,0:T(8,128)(2,1)}, bf16[16,240,384]{2,1,0:T(8,128)(2,1)}, u32[]{:S(2)}, u32[]{:S(2)}) collective-permute-start(bf16[16,240,384]{2,1,0:T(8,128)(2,1)} %pad_maximum_fusion.1.mine_ref), channel_id=1, source_target_pairs={{0,16},{16,0},{1,17},{17,1},{2,18},{18,2},{3,19},{19,3},{4,20},{20... | collective-permute-start | bytes 8847368 | tf_op jit(solution)/shard_map/ppermute | solution.py:51
  102.0 32.4 %collective-permute-start.18 = (bf16[8,192,384]{2,1,0:T(8,128)(2,1)}, bf16[8,192,384]{2,1,0:T(8,128)(2,1)}, u32[]{:S(2)}, u32[]{:S(2)}) collective-permute-start(bf16[8,192,384]{2,1,0:T(8,128)(2,1)} %pad_maximum_fusion.7), channel_id=1, source_target_pairs={{0,2},{1,3},{2,0},{3,1},{4,6},{5,7},{6,4},{7,5},{8,10},{9,11},{10,... | collective-permute-start | bytes 3538952 | tf_op jit(solution)/shard_map/ppermute | solution.py:48
  102.7 28.9 %collective-permute-start.20 = (bf16[2,384,384]{2,1,0:T(8,128)(2,1)}, bf16[2,384,384]{2,1,0:T(8,128)(2,1)}, u32[]{:S(2)}, u32[]{:S(2)}) collective-permute-start(bf16[2,384,384]{2,1,0:T(8,128)(2,1)} %pad_maximum_fusion.14), channel_id=1, source_target_pairs={{0,8},{1,9},{2,10},{3,11},{4,12},{5,13},{6,14},{7,15},{8,0},{9,1},... | collective-permute-start | bytes 1769480 | tf_op jit(solution)/shard_map/ppermute | solution.py:48
  103.3 29.7 %collective-permute-start.19 = (bf16[4,192,384]{2,1,0:T(8,128)(2,1)}, bf16[4,192,384]{2,1,0:T(8,128)(2,1)}, u32[]{:S(2)}, u32[]{:S(2)}) collective-permute-start(bf16[4,192,384]{2,1,0:T(8,128)(2,1)} %pad_maximum_fusion.13), channel_id=1, source_target_pairs={{0,1},{1,0},{2,3},{3,2},{4,5},{5,4},{6,7},{7,6},{8,9},{9,8},{10,11... | collective-permute-start | bytes 1769480 | tf_op jit(solution)/shard_map/ppermute | solution.py:48
  136.3 28.3 %collective-permute-start.23 = (bf16[4,384,384]{2,1,0:T(8,128)(2,1)S(1)}, bf16[4,384,384]{2,1,0:T(8,128)(2,1)S(1)}, u32[]{:S(2)}, u32[]{:S(2)}) collective-permute-start(bf16[4,384,384]{2,1,0:T(8,128)(2,1)S(1)} %pad_maximum_fusion.9), channel_id=1, source_target_pairs={{0,1},{1,0},{2,3},{3,2},{4,5},{5,4},{6,7},{7,6},{8,9},{9,8},{10,11... | collective-permute-start | bytes 3538952 | tf_op jit(solution)/shard_map/ppermute | solution.py:48
  137.1 29.2 %collective-permute-start.22 = (bf16[8,192,384]{2,1,0:T(8,128)(2,1)S(1)}, bf16[8,192,384]{2,1,0:T(8,128)(2,1)S(1)}, u32[]{:S(2)}, u32[]{:S(2)}) collective-permute-start(bf16[8,192,384]{2,1,0:T(8,128)(2,1)S(1)} %pad_maximum_fusion.8), channel_id=1, source_target_pairs={{0,2},{1,3},{2,0},{3,1},{4,6},{5,7},{6,4},{7,5},{8,10},{9,11},{10,... | collective-permute-start | bytes 3538952 | tf_op jit(solution)/shard_map/ppermute | solution.py:48
  138.6 43.4 %collective-permute-start.26 = (bf16[16,192,384]{2,1,0:T(8,128)(2,1)S(1)}, bf16[16,192,384]{2,1,0:T(8,128)(2,1)}, u32[]{:S(2)}, u32[]{:S(2)}) collective-permute-start(bf16[16,192,384]{2,1,0:T(8,128)(2,1)S(1)} %pad_maximum_fusion.2.refs_0_.refs_1_.refs_2_.refs_3_), channel_id=1, source_target_pairs={{0,16},{16,0},{1,17},{17,1},{2,18},{18,2},{3,19},{19,3},{4,20},{20... | collective-permute-start | bytes 7077896 | tf_op jit(solution)/shard_map/ppermute | solution.py:51
  181.1 29.2 %collective-permute-start.25 = (bf16[8,384,384]{2,1,0:T(8,128)(2,1)}, bf16[8,384,384]{2,1,0:T(8,128)(2,1)}, u32[]{:S(2)}, u32[]{:S(2)}) collective-permute-start(bf16[8,384,384]{2,1,0:T(8,128)(2,1)} %pad_maximum_fusion.4), channel_id=1, source_target_pairs={{0,2},{1,3},{2,0},{3,1},{4,6},{5,7},{6,4},{7,5},{8,10},{9,11},{10,... | collective-permute-start | bytes 7077896 | tf_op jit(solution)/shard_map/ppermute | solution.py:48
  215.4 29.5 %collective-permute-start.28 = (bf16[16,384,384]{2,1,0:T(8,128)(2,1)}, bf16[16,384,384]{2,1,0:T(8,128)(2,1)}, u32[]{:S(2)}, u32[]{:S(2)}) collective-permute-start(bf16[16,384,384]{2,1,0:T(8,128)(2,1)} %pad_maximum_fusion.mine_ref.refs_0_.refs_1_.refs_2_.refs_3_), channel_id=1, source_target_pairs={{0,16},{16,0},{1,17},{17,1},{2,18},{18,2},{3,19},{19,3},{4,20},{20... | collective-permute-start | bytes 14155784 | tf_op jit(solution)/shard_map/ppermute | solution.py:51
  215.4 11.0 %collective-permute-start.27 = (bf16[16,192,384]{2,1,0:T(8,128)(2,1)S(1)}, bf16[16,192,384]{2,1,0:T(8,128)(2,1)}, u32[]{:S(2)}, u32[]{:S(2)}) collective-permute-start(bf16[16,192,384]{2,1,0:T(8,128)(2,1)S(1)} %copy-done.1), channel_id=1, source_target_pairs={{0,16},{16,0},{1,17},{17,1},{2,18},{18,2},{3,19},{19,3},{4,20},{20... | collective-permute-start | bytes 7077896 | tf_op jit(solution)/shard_map/ppermute | solution.py:51
  254.0 32.6 %collective-permute-start.32 = (bf16[10,512,384]{2,1,0:T(8,128)(2,1)}, bf16[10,512,384]{2,1,0:T(8,128)(2,1)}, u32[]{:S(2)}, u32[]{:S(2)}) collective-permute-start(bf16[10,512,384]{2,1,0:T(8,128)(2,1)} %get-tuple-element.209.active_ref.refs_0_), channel_id=1, source_target_pairs={{0,16},{16,0},{1,17},{17,1},{2,18},{18,2},{3,19},{19,3},{4,20},{20... | collective-permute-start | bytes 11796488 | tf_op jit(solution)/shard_map/ppermute | solution.py:51
  276.2 10.4 %collective-permute-start.33 = (bf16[5,512,384]{2,1,0:T(8,128)(2,1)}, bf16[5,512,384]{2,1,0:T(8,128)(2,1)S(1)}, u32[]{:S(2)}, u32[]{:S(2)}) collective-permute-start(bf16[5,512,384]{2,1,0:T(8,128)(2,1)} %get-tuple-element.219.sent_ref), channel_id=1, source_target_pairs={{0,16},{16,0},{1,17},{17,1},{2,18},{18,2},{3,19},{19,3},{4,20},{20... | collective-permute-start | bytes 5898248 | tf_op jit(solution)/shard_map/ppermute | solution.py:51
  276.5 42.6 %collective-permute-start.31 = (bf16[4,512,384]{2,1,0:T(8,128)(2,1)S(1)}, bf16[4,512,384]{2,1,0:T(8,128)(2,1)}, u32[]{:S(2)}, u32[]{:S(2)}) collective-permute-start(bf16[4,512,384]{2,1,0:T(8,128)(2,1)S(1)} %copy-done.4), channel_id=1, source_target_pairs={{0,16},{16,0},{1,17},{17,1},{2,18},{18,2},{3,19},{19,3},{4,20},{20... | collective-permute-start | bytes 4718600 | tf_op jit(solution)/shard_map/ppermute | solution.py:51
  297.5 33.6 %collective-permute-start.35 = (bf16[8,192,384]{2,1,0:T(8,128)(2,1)}, bf16[8,192,384]{2,1,0:T(8,128)(2,1)}, u32[]{:S(2)}, u32[]{:S(2)}) collective-permute-start(bf16[8,192,384]{2,1,0:T(8,128)(2,1)} %get-tuple-element.235), channel_id=1, source_target_pairs={{0,2},{1,3},{2,0},{3,1},{4,6},{5,7},{6,4},{7,5},{8,10},{9,11},{10,... | collective-permute-start | bytes 3538952 | tf_op jit(solution)/shard_map/ppermute | solution.py:48
  298.5 20.6 %collective-permute-start.34 = (bf16[1,512,384]{2,1,0:T(8,128)(2,1)}, bf16[1,512,384]{2,1,0:T(8,128)(2,1)S(1)}, u32[]{:S(2)}, u32[]{:S(2)}) collective-permute-start(bf16[1,512,384]{2,1,0:T(8,128)(2,1)} %get-tuple-element.228.sent_ref), channel_id=1, source_target_pairs={{0,16},{16,0},{1,17},{17,1},{2,18},{18,2},{3,19},{19,3},{4,20},{20... | collective-permute-start | bytes 1179656 | tf_op jit(solution)/shard_map/ppermute | solution.py:51
  332.7 26.1 %collective-permute-start.38 = (bf16[8,240,384]{2,1,0:T(8,128)(2,1)}, bf16[8,240,384]{2,1,0:T(8,128)(2,1)}, u32[]{:S(2)}, u32[]{:S(2)}) collective-permute-start(bf16[8,240,384]{2,1,0:T(8,128)(2,1)} %get-tuple-element.244), channel_id=1, source_target_pairs={{0,2},{1,3},{2,0},{3,1},{4,6},{5,7},{6,4},{7,5},{8,10},{9,11},{10,... | collective-permute-start | bytes 4423688 | tf_op jit(solution)/shard_map/ppermute | solution.py:48
  333.9 17.5 %collective-permute-start.36 = (bf16[3,512,384]{2,1,0:T(8,128)(2,1)}, bf16[3,512,384]{2,1,0:T(8,128)(2,1)}, u32[]{:S(2)}, u32[]{:S(2)}) collective-permute-start(bf16[3,512,384]{2,1,0:T(8,128)(2,1)} %get-tuple-element.237.sent_ref), channel_id=1, source_target_pairs={{0,16},{16,0},{1,17},{17,1},{2,18},{18,2},{3,19},{19,3},{4,20},{20... | collective-permute-start | bytes 3538952 | tf_op jit(solution)/shard_map/ppermute | solution.py:51
  334.3 16.3 %collective-permute-start.37 = (bf16[4,192,384]{2,1,0:T(8,128)(2,1)S(1)}, bf16[4,192,384]{2,1,0:T(8,128)(2,1)S(1)}, u32[]{:S(2)}, u32[]{:S(2)}) collective-permute-start(bf16[4,192,384]{2,1,0:T(8,128)(2,1)S(1)} %get-tuple-element.242), channel_id=1, source_target_pairs={{0,1},{1,0},{2,3},{3,2},{4,5},{5,4},{6,7},{7,6},{8,9},{9,8},{10,11... | collective-permute-start | bytes 1769480 | tf_op jit(solution)/shard_map/ppermute | solution.py:48
  335.0 71.0 %collective-permute-start.30 = (bf16[10,512,384]{2,1,0:T(8,128)(2,1)}, bf16[10,512,384]{2,1,0:T(8,128)(2,1)}, u32[]{:S(2)}, u32[]{:S(2)}) collective-permute-start(bf16[10,512,384]{2,1,0:T(8,128)(2,1)} %get-tuple-element.199.active_ref.refs_0_), channel_id=1, source_target_pairs={{0,16},{16,0},{1,17},{17,1},{2,18},{18,2},{3,19},{19,3},{4,20},{20... | collective-permute-start | bytes 11796488 | tf_op jit(solution)/shard_map/ppermute | solution.py:51
  361.3 19.5 %collective-permute-start.40 = (bf16[4,240,384]{2,1,0:T(8,128)(2,1)}, bf16[4,240,384]{2,1,0:T(8,128)(2,1)S(1)}, u32[]{:S(2)}, u32[]{:S(2)}) collective-permute-start(bf16[4,240,384]{2,1,0:T(8,128)(2,1)} %get-tuple-element.255), channel_id=1, source_target_pairs={{0,1},{1,0},{2,3},{3,2},{4,5},{5,4},{6,7},{7,6},{8,9},{9,8},{10,11... | collective-permute-start | bytes 2211848 | tf_op jit(solution)/shard_map/ppermute | solution.py:48
  362.7 19.2 %collective-permute-start.41 = (bf16[8,144,384]{2,1,0:T(8,128)(2,1)}, bf16[8,144,384]{2,1,0:T(8,128)(2,1)S(1)}, u32[]{:S(2)}, u32[]{:S(2)}) collective-permute-start(bf16[8,144,384]{2,1,0:T(8,128)(2,1)} %get-tuple-element.257), channel_id=1, source_target_pairs={{0,2},{1,3},{2,0},{3,1},{4,6},{5,7},{6,4},{7,5},{8,10},{9,11},{10,... | collective-permute-start | bytes 2654216 | tf_op jit(solution)/shard_map/ppermute | solution.py:48
  363.4 14.1 %collective-permute-start.39 = (bf16[2,192,384]{2,1,0:T(8,128)(2,1)}, bf16[2,192,384]{2,1,0:T(8,128)(2,1)S(1)}, u32[]{:S(2)}, u32[]{:S(2)}) collective-permute-start(bf16[2,192,384]{2,1,0:T(8,128)(2,1)} %get-tuple-element.253), channel_id=1, source_target_pairs={{0,8},{1,9},{2,10},{3,11},{4,12},{5,13},{6,14},{7,15},{8,0},{9,1},... | collective-permute-start | bytes 884744 | tf_op jit(solution)/shard_map/ppermute | solution.py:48
  383.0 23.0 %collective-permute-start.42 = (bf16[5,512,384]{2,1,0:T(8,128)(2,1)}, bf16[5,512,384]{2,1,0:T(8,128)(2,1)S(1)}, u32[]{:S(2)}, u32[]{:S(2)}) collective-permute-start(bf16[5,512,384]{2,1,0:T(8,128)(2,1)} %get-tuple-element.259.sent_ref), channel_id=1, source_target_pairs={{0,16},{16,0},{1,17},{17,1},{2,18},{18,2},{3,19},{19,3},{4,20},{20... | collective-permute-start | bytes 5898248 | tf_op jit(solution)/shard_map/ppermute | solution.py:51
  383.0 18.8 %collective-permute-start.43 = (bf16[2,240,384]{2,1,0:T(8,128)(2,1)}, bf16[2,240,384]{2,1,0:T(8,128)(2,1)}, u32[]{:S(2)}, u32[]{:S(2)}) collective-permute-start(bf16[2,240,384]{2,1,0:T(8,128)(2,1)} %get-tuple-element.268), channel_id=1, source_target_pairs={{0,8},{1,9},{2,10},{3,11},{4,12},{5,13},{6,14},{7,15},{8,0},{9,1},... | collective-permute-start | bytes 1105928 | tf_op jit(solution)/shard_map/ppermute | solution.py:48
  383.0 20.8 %collective-permute-start.44 = (bf16[4,144,384]{2,1,0:T(8,128)(2,1)}, bf16[4,144,384]{2,1,0:T(8,128)(2,1)}, u32[]{:S(2)}, u32[]{:S(2)}) collective-permute-start(bf16[4,144,384]{2,1,0:T(8,128)(2,1)} %get-tuple-element.270), channel_id=1, source_target_pairs={{0,1},{1,0},{2,3},{3,2},{4,5},{5,4},{6,7},{7,6},{8,9},{9,8},{10,11... | collective-permute-start | bytes 1327112 | tf_op jit(solution)/shard_map/ppermute | solution.py:48
  384.4 55.2 %collective-permute-start.29 = (bf16[4,512,384]{2,1,0:T(8,128)(2,1)S(1)}, bf16[4,512,384]{2,1,0:T(8,128)(2,1)}, u32[]{:S(2)}, u32[]{:S(2)}) collective-permute-start(bf16[4,512,384]{2,1,0:T(8,128)(2,1)S(1)} %copy-done.3), channel_id=1, source_target_pairs={{0,16},{16,0},{1,17},{17,1},{2,18},{18,2},{3,19},{19,3},{4,20},{20... | collective-permute-start | bytes 4718600 | tf_op jit(solution)/shard_map/ppermute | solution.py:51
  417.0 34.5 %collective-permute-start.47 = (bf16[8,192,384]{2,1,0:T(8,128)(2,1)}, bf16[8,192,384]{2,1,0:T(8,128)(2,1)}, u32[]{:S(2)}, u32[]{:S(2)}) collective-permute-start(bf16[8,192,384]{2,1,0:T(8,128)(2,1)} %get-tuple-element.281), channel_id=1, source_target_pairs={{0,2},{1,3},{2,0},{3,1},{4,6},{5,7},{6,4},{7,5},{8,10},{9,11},{10,... | collective-permute-start | bytes 3538952 | tf_op jit(solution)/shard_map/ppermute | solution.py:48
  418.3 20.7 %collective-permute-start.46 = (bf16[2,144,384]{2,1,0:T(8,128)(2,1)}, bf16[2,144,384]{2,1,0:T(8,128)(2,1)S(1)}, u32[]{:S(2)}, u32[]{:S(2)}) collective-permute-start(bf16[2,144,384]{2,1,0:T(8,128)(2,1)} %get-tuple-element.279), channel_id=1, source_target_pairs={{0,8},{1,9},{2,10},{3,11},{4,12},{5,13},{6,14},{7,15},{8,0},{9,1},... | collective-permute-start | bytes 663560 | tf_op jit(solution)/shard_map/ppermute | solution.py:48
  418.3 21.4 %collective-permute-start.45 = (bf16[1,512,384]{2,1,0:T(8,128)(2,1)}, bf16[1,512,384]{2,1,0:T(8,128)(2,1)S(1)}, u32[]{:S(2)}, u32[]{:S(2)}) collective-permute-start(bf16[1,512,384]{2,1,0:T(8,128)(2,1)} %get-tuple-element.272.sent_ref), channel_id=1, source_target_pairs={{0,16},{16,0},{1,17},{17,1},{2,18},{18,2},{3,19},{19,3},{4,20},{20... | collective-permute-start | bytes 1179656 | tf_op jit(solution)/shard_map/ppermute | solution.py:51
  453.1 27.2 %collective-permute-start.50 = (bf16[8,240,384]{2,1,0:T(8,128)(2,1)}, bf16[8,240,384]{2,1,0:T(8,128)(2,1)S(1)}, u32[]{:S(2)}, u32[]{:S(2)}) collective-permute-start(bf16[8,240,384]{2,1,0:T(8,128)(2,1)} %get-tuple-element.290), channel_id=1, source_target_pairs={{0,2},{1,3},{2,0},{3,1},{4,6},{5,7},{6,4},{7,5},{8,10},{9,11},{10,... | collective-permute-start | bytes 4423688 | tf_op jit(solution)/shard_map/ppermute | solution.py:48
  454.0 19.1 %collective-permute-start.48 = (bf16[3,512,384]{2,1,0:T(8,128)(2,1)}, bf16[3,512,384]{2,1,0:T(8,128)(2,1)}, u32[]{:S(2)}, u32[]{:S(2)}) collective-permute-start(bf16[3,512,384]{2,1,0:T(8,128)(2,1)} %get-tuple-element.283.sent_ref), channel_id=1, source_target_pairs={{0,16},{16,0},{1,17},{17,1},{2,18},{18,2},{3,19},{19,3},{4,20},{20... | collective-permute-start | bytes 3538952 | tf_op jit(solution)/shard_map/ppermute | solution.py:51
  454.8 16.4 %collective-permute-start.49 = (bf16[4,192,384]{2,1,0:T(8,128)(2,1)S(1)}, bf16[4,192,384]{2,1,0:T(8,128)(2,1)}, u32[]{:S(2)}, u32[]{:S(2)}) collective-permute-start(bf16[4,192,384]{2,1,0:T(8,128)(2,1)S(1)} %get-tuple-element.288), channel_id=1, source_target_pairs={{0,1},{1,0},{2,3},{3,2},{4,5},{5,4},{6,7},{7,6},{8,9},{9,8},{10,11... | collective-permute-start | bytes 1769480 | tf_op jit(solution)/shard_map/ppermute | solution.py:48
  456.2 25.8 %collective-permute-start.64 = (bf16[1,192,384]{2,1,0:T(8,128)(2,1)}, bf16[1,192,384]{2,1,0:T(8,128)(2,1)S(1)}, u32[]{:S(2)}, u32[]{:S(2)}) collective-permute-start(bf16[1,192,384]{2,1,0:T(8,128)(2,1)} %get-tuple-element.321), channel_id=1, source_target_pairs={{0,4},{1,5},{2,6},{3,7},{4,0},{5,1},{6,2},{7,3},{8,12},{9,13},{10,... | collective-permute-start | bytes 442376 | tf_op jit(solution)/shard_map/ppermute | solution.py:48
  460.2 25.7 %collective-permute-start.55 = (f32[8,2,576]{2,1,0:T(2,128)S(1)}, f32[8,2,576]{2,1,0:T(2,128)}, u32[]{:S(2)}, u32[]{:S(2)}) collective-permute-start(f32[8,2,576]{2,1,0:T(2,128)S(1)} %slice.642), channel_id=1, source_target_pairs={{0,2},{1,3},{2,0},{3,1},{4,6},{5,7},{6,4},{7,5},{8,10},{9,11},{10,... | collective-permute-start | bytes 110600 | tf_op jit(solution)/shard_map/ppermute | solution.py:48
  480.7 20.1 %collective-permute-start.52 = (bf16[4,240,384]{2,1,0:T(8,128)(2,1)S(1)}, bf16[4,240,384]{2,1,0:T(8,128)(2,1)S(1)}, u32[]{:S(2)}, u32[]{:S(2)}) collective-permute-start(bf16[4,240,384]{2,1,0:T(8,128)(2,1)S(1)} %get-tuple-element.295), channel_id=1, source_target_pairs={{0,1},{1,0},{2,3},{3,2},{4,5},{5,4},{6,7},{7,6},{8,9},{9,8},{10,11... | collective-permute-start | bytes 2211848 | tf_op jit(solution)/shard_map/ppermute | solution.py:48
  482.0 8.3 %collective-permute-start.65 = (bf16[1,240,384]{2,1,0:T(8,128)(2,1)S(1)}, bf16[1,240,384]{2,1,0:T(8,128)(2,1)S(1)}, u32[]{:S(2)}, u32[]{:S(2)}) collective-permute-start(bf16[1,240,384]{2,1,0:T(8,128)(2,1)S(1)} %copy-done.26), channel_id=1, source_target_pairs={{0,4},{1,5},{2,6},{3,7},{4,0},{5,1},{6,2},{7,3},{8,12},{9,13},{10,... | collective-permute-start | bytes 552968 | tf_op jit(solution)/shard_map/ppermute | solution.py:48
  485.2 15.8 %collective-permute-start.53 = (bf16[8,144,384]{2,1,0:T(8,128)(2,1)S(1)}, bf16[8,144,384]{2,1,0:T(8,128)(2,1)S(1)}, u32[]{:S(2)}, u32[]{:S(2)}) collective-permute-start(bf16[8,144,384]{2,1,0:T(8,128)(2,1)S(1)} %copy-done.40), channel_id=1, source_target_pairs={{0,2},{1,3},{2,0},{3,1},{4,6},{5,7},{6,4},{7,5},{8,10},{9,11},{10,... | collective-permute-start | bytes 2654216 | tf_op jit(solution)/shard_map/ppermute | solution.py:48
  485.9 14.8 %collective-permute-start.51 = (bf16[2,192,384]{2,1,0:T(8,128)(2,1)S(1)}, bf16[2,192,384]{2,1,0:T(8,128)(2,1)S(1)}, u32[]{:S(2)}, u32[]{:S(2)}) collective-permute-start(bf16[2,192,384]{2,1,0:T(8,128)(2,1)S(1)} %copy-done.24), channel_id=1, source_target_pairs={{0,8},{1,9},{2,10},{3,11},{4,12},{5,13},{6,14},{7,15},{8,0},{9,1},... | collective-permute-start | bytes 884744 | tf_op jit(solution)/shard_map/ppermute | solution.py:48
  490.4 14.3 %collective-permute-start.63 = (bf16[1,144,384]{2,1,0:T(8,128)(2,1)S(1)}, bf16[1,144,384]{2,1,0:T(8,128)(2,1)S(1)}, u32[]{:S(2)}, u32[]{:S(2)}) collective-permute-start(bf16[1,144,384]{2,1,0:T(8,128)(2,1)S(1)} %copy-done.28), channel_id=1, source_target_pairs={{0,4},{1,5},{2,6},{3,7},{4,0},{5,1},{6,2},{7,3},{8,12},{9,13},{10,... | collective-permute-start | bytes 331784 | tf_op jit(solution)/shard_map/ppermute | solution.py:48
  502.4 19.8 %collective-permute-start.56 = (bf16[2,240,384]{2,1,0:T(8,128)(2,1)S(1)}, bf16[2,240,384]{2,1,0:T(8,128)(2,1)S(1)}, u32[]{:S(2)}, u32[]{:S(2)}) collective-permute-start(bf16[2,240,384]{2,1,0:T(8,128)(2,1)S(1)} %get-tuple-element.307), channel_id=1, source_target_pairs={{0,8},{1,9},{2,10},{3,11},{4,12},{5,13},{6,14},{7,15},{8,0},{9,1},... | collective-permute-start | bytes 1105928 | tf_op jit(solution)/shard_map/ppermute | solution.py:48
  504.8 17.5 %collective-permute-start.57 = (bf16[4,144,384]{2,1,0:T(8,128)(2,1)S(1)}, bf16[4,144,384]{2,1,0:T(8,128)(2,1)S(1)}, u32[]{:S(2)}, u32[]{:S(2)}) collective-permute-start(bf16[4,144,384]{2,1,0:T(8,128)(2,1)S(1)} %get-tuple-element.309), channel_id=1, source_target_pairs={{0,1},{1,0},{2,3},{3,2},{4,5},{5,4},{6,7},{7,6},{8,9},{9,8},{10,11... | collective-permute-start | bytes 1327112 | tf_op jit(solution)/shard_map/ppermute | solution.py:48
  505.7 16.8 %collective-permute-start.66 = (bf16[1,192,384]{2,1,0:T(8,128)(2,1)S(1)}, bf16[1,192,384]{2,1,0:T(8,128)(2,1)S(1)}, u32[]{:S(2)}, u32[]{:S(2)}) collective-permute-start(bf16[1,192,384]{2,1,0:T(8,128)(2,1)S(1)} %get-tuple-element.325), channel_id=1, source_target_pairs={{0,4},{1,5},{2,6},{3,7},{4,0},{5,1},{6,2},{7,3},{8,12},{9,13},{10,... | collective-permute-start | bytes 442376 | tf_op jit(solution)/shard_map/ppermute | solution.py:48
  522.4 7.6 %collective-permute-start.67 = (bf16[1,240,384]{2,1,0:T(8,128)(2,1)S(1)}, bf16[1,240,384]{2,1,0:T(8,128)(2,1)S(1)}, u32[]{:S(2)}, u32[]{:S(2)}) collective-permute-start(bf16[1,240,384]{2,1,0:T(8,128)(2,1)S(1)} %get-tuple-element.327), channel_id=1, source_target_pairs={{0,4},{1,5},{2,6},{3,7},{4,0},{5,1},{6,2},{7,3},{8,12},{9,13},{10,... | collective-permute-start | bytes 552968 | tf_op jit(solution)/shard_map/ppermute | solution.py:48
  522.5 7.6 %collective-permute-start.60 = (f32[2,2,576]{2,1,0:T(2,128)S(1)}, f32[2,2,576]{2,1,0:T(2,128)S(1)}, u32[]{:S(2)}, u32[]{:S(2)}) collective-permute-start(f32[2,2,576]{2,1,0:T(2,128)S(1)} %get-tuple-element.315), channel_id=1, source_target_pairs={{0,8},{1,9},{2,10},{3,11},{4,12},{5,13},{6,14},{7,15},{8,0},{9,1},... | collective-permute-start | bytes 27656 | tf_op jit(solution)/shard_map/ppermute | solution.py:48
  525.4 12.7 %collective-permute-start.59 = (bf16[2,144,384]{2,1,0:T(8,128)(2,1)S(1)}, bf16[2,144,384]{2,1,0:T(8,128)(2,1)S(1)}, u32[]{:S(2)}, u32[]{:S(2)}) collective-permute-start(bf16[2,144,384]{2,1,0:T(8,128)(2,1)S(1)} %get-tuple-element.313), channel_id=1, source_target_pairs={{0,8},{1,9},{2,10},{3,11},{4,12},{5,13},{6,14},{7,15},{8,0},{9,1},... | collective-permute-start | bytes 663560 | tf_op jit(solution)/shard_map/ppermute | solution.py:48
  530.1 13.2 %collective-permute-start.68 = (bf16[1008,384]{1,0:T(8,128)(2,1)S(1)}, bf16[1008,384]{1,0:T(8,128)(2,1)S(1)}, u32[]{:S(2)}, u32[]{:S(2)}) collective-permute-start(bf16[1008,384]{1,0:T(8,128)(2,1)S(1)} %get-tuple-element.332), channel_id=1, source_target_pairs={{0,16},{16,0},{1,17},{17,1},{2,18},{18,2},{3,19},{19,3},{4,20},{20... | collective-permute-start | bytes 2322440 | tf_op jit(solution)/shard_map/ppermute | solution.py:51
  538.4 4.8 collective-permute-start.61
  (47 other events, 341.3 us)

commit v4 on v3

--- a/solution.py
+++ b/solution.py
@@ -24,24 +24,28 @@
 
 
 class Net:
-    def __init__(self, mesh):
+    def __init__(self, mesh, wide):
         self.shards = mesh.shape["fsdp"]
         self.replicas = mesh.shape["rep"]
-        assert self.replicas % 2 == 0 and self.shards & (self.shards - 1) == 0
-        bits = [1 << place for place in range(self.shards.bit_length() - 1)]
-        first = bits[2:] + bits[:2]
-        self.steps = [first, first[:-2] + first[:-3:-1]]
-        self.stages = len(bits)
+        assert self.replicas % 2 == 0 and self.shards & (self.shards - 1) == 0 and self.shards >= 16
+        bits = [1 << place for place in reversed(range(self.shards.bit_length() - 3))]
+        first = [(4, self.shards // 4)] if wide else [(2, self.shards // 4), (2, self.shards // 2)]
+        self.sizes = [size for size, _ in first] + [2] * len(bits)
+        first = [step for _, step in first]
+        self.steps = [[*first, *bits], [*first, *bits[:-2], bits[-1], bits[-2]]]
+        self.stages = len(self.sizes)
         flips = np.zeros((2, self.shards), np.int32)
         for core in range(2):
             for slot in range(self.shards):
-                for place, step in enumerate(self.steps[core]):
-                    flips[core, slot] ^= ((slot >> place) & 1) * step
+                left = slot
+                for size, step in zip(self.sizes, self.steps[core]):
+                    flips[core, slot] ^= (left % size) * step
+                    left //= size
         self.flips = flips
 
-    def trade(self, value, stage):
+    def trade(self, value, stage, offset):
         pairs = [
-            (rep * self.shards + shard, rep * self.shards + (shard ^ self.steps[rep % 2][stage]))
+            (rep * self.shards + shard, rep * self.shards + (shard ^ (offset * self.steps[rep % 2][stage])))
             for rep in range(self.replicas)
             for shard in range(self.shards)
         ]
@@ -50,17 +54,25 @@
     def twin(self, value):
         return lax.ppermute(value, "rep", [(rep, rep ^ 1) for rep in range(self.replicas)])
 
+    def gather(self, value, stage):
+        return [self.trade(value, stage, offset) for offset in range(1, self.sizes[stage])]
+
     def widen(self, value, stage):
-        return jnp.concatenate([value, self.trade(value, stage)], 0)
-
-    def narrow(self, kept, sent, stage):
-        received = self.trade(sent, stage)
-
+        return jnp.concatenate([value, *self.gather(value, stage)], 0)
+
+    def reduce(self, parts, stage):
+        return [self.trade(part, stage, offset) for offset, part in enumerate(parts[1:], 1)]
+
+    def narrow(self, own, received, stage):
         def add(here):
-            return (kept[here].astype(FULL) + received[here].astype(FULL)).astype(kept.dtype)
-
-        half = kept.shape[0] // 2
-        return (add(slice(0, half)), add(slice(half, None))) if half else (add(slice(0, None)), None)
+            total = own[here].astype(FULL)
+            for value in received:
+                total = total + value[here].astype(FULL)
+            return total.astype(own.dtype)
+
+        pieces = self.sizes[stage - 1] if stage else 1
+        height = own.shape[0] // pieces
+        return [add(slice(piece * height, (piece + 1) * height)) for piece in range(pieces)]
 
     def across(self, value):
         others = self.replicas // 2
@@ -91,9 +103,10 @@
     return lax.dot_general(left, right, (((left_dim,), (right_dim,)), ((), ())), preferred_element_type=FULL)
 
 
-def fill(weight_ref, slots_ref, mine_ref, other_ref):
+def fill(weight_ref, slots_ref, refs):
+    mine_ref, other_ref = refs[0], refs[-1]
     rows = mine_ref.shape[1]
-    for shard in range(mine_ref.shape[0]):
+    for shard in range(slots_ref.shape[1]):
         here = slice(shard * rows, (shard + 1) * rows)
         weight_ref[here, :CHUNK] = mine_ref[slots_ref[0, shard]]
         weight_ref[here, CHUNK:] = other_ref[slots_ref[1, shard]]
@@ -161,6 +174,10 @@
     return raised * (1.0 / jnp.sum(raised, 0, keepdims=True))
 
 
+def cost(micros):
+    return pl.CostEstimate(flops=int(micros * 1.15e9), transcendentals=0, bytes_accessed=int(micros * 1e6))
+
+
 SMALL = pl.BlockSpec(memory_space=pltpu.SMEM)
 
 
@@ -168,27 +185,29 @@
     return pl.BlockSpec(shape, lambda *args: (0,) * len(shape))
 
 
-def part_blocks(mine, start, last=None):
-    rows = 2 * CHUNK // mine.shape[0]
+def part_blocks(pieces, start, last=None):
+    shards = pieces[0].shape[0] * len(pieces) // 2
+    rows = 2 * CHUNK // shards
 
     def place(k):
         return (0, start + (k if last is None else jnp.minimum(k, last)), 0)
 
-    return [pl.BlockSpec((mine.shape[0], rows, CHUNK), place)] * 2
+    return [pl.BlockSpec((piece.shape[0], rows, CHUNK), place) for piece in pieces]
 
 
 def shaped(*shape, kind=LOW):
     return jax.ShapeDtypeStruct(shape, kind)
 
 
-def project(tables, hidden_low, vector_rows, mine, other, start):
+def project(tables, hidden_low, vector_rows, pieces, start):
     slots, core, limits = tables
     tokens, width = hidden_low.shape
 
-    def body(slots_ref, core_ref, limits_ref, x_ref, rows_ref, mine_ref, other_ref, qkv_ref, left_ref, weight_ref):
+    def body(slots_ref, core_ref, limits_ref, x_ref, rows_ref, *refs):
+        qkv_ref, left_ref, weight_ref = refs[len(pieces) :]
         third = pl.program_id(0)
         core = core_ref[0]
-        fill(weight_ref, slots_ref, mine_ref, other_ref)
+        fill(weight_ref, slots_ref, refs[: len(pieces)])
         result = dot(x_ref[...], weight_ref[...])
         bias = rows_ref[pl.ds(jnp.where(third == 2, 1, 0), 1), :]
         bias = jnp.where(third == 1, jnp.zeros_like(bias), bias)
@@ -217,19 +236,21 @@
         body,
         grid=(3,),
         out_shape=[shaped(2, 3, tokens, CHUNK), shaped(4, tokens, CHUNK)],
-        in_specs=[SMALL] * 3 + [whole(tokens, width), whole(*vector_rows.shape)] + part_blocks(mine, start),
+        in_specs=[SMALL] * 3 + [whole(tokens, width), whole(*vector_rows.shape)] + part_blocks(pieces, start),
         out_specs=[whole(2, 3, tokens, CHUNK), whole(4, tokens, CHUNK)],
         scratch_shapes=[pltpu.VMEM((width, width), LOW)],
         name="project",
-    )(slots, core, limits, hidden_low, vector_rows, mine, other)
-
-
-def mix(tables, context, hidden, vector_rows, mine, other, start):
+        cost_estimate=cost(14.5),
+    )(slots, core, limits, hidden_low, vector_rows, *pieces)
+
+
+def mix(tables, context, hidden, vector_rows, pieces, start):
     slots, core, _ = tables
     tokens, width = hidden.shape
 
-    def body(slots_ref, core_ref, context_ref, hidden_ref, rows_ref, mine_ref, other_ref, sum_ref, low_ref, weight_ref):
-        fill(weight_ref, slots_ref, mine_ref, other_ref)
+    def body(slots_ref, core_ref, context_ref, hidden_ref, rows_ref, *refs):
+        sum_ref, low_ref, weight_ref = refs[len(pieces) :]
+        fill(weight_ref, slots_ref, refs[: len(pieces)])
         context = jnp.concatenate([context_ref[0], context_ref[1]], 1)
         mixed = jnp.concatenate(swap(core_ref[0], dot(context, weight_ref[...])), 1) + rows_ref[2:3, :]
         total = hidden_ref[...].astype(FULL) + mixed
@@ -242,24 +263,26 @@
         out_shape=[shaped(tokens, width, kind=FULL), shaped(tokens, width)],
         in_specs=[SMALL] * 2
         + [pl.BlockSpec((2, tokens, CHUNK), lambda k: (1, 0, 0)), whole(tokens, width), whole(*vector_rows.shape)]
-        + part_blocks(mine, start),
+        + part_blocks(pieces, start),
         out_specs=[whole(tokens, width)] * 2,
         scratch_shapes=[pltpu.VMEM((width, width), LOW)],
         name="mix",
-    )(slots, core, context, hidden, vector_rows, mine, other)
-
-
-def expand(tables, first_low, vector_rows, mine, other, start, parts):
+        cost_estimate=cost(4.2),
+    )(slots, core, context, hidden, vector_rows, *pieces)
+
+
+def expand(tables, first_low, vector_rows, pieces, start, parts):
     slots, core, _ = tables
     tokens, width = first_low.shape
 
-    def body(slots_ref, core_ref, x_ref, rows_ref, mine_ref, other_ref, left_ref, slope_ref, weight_ref):
+    def body(slots_ref, core_ref, x_ref, rows_ref, *refs):
+        left_ref, slope_ref, weight_ref = refs[len(pieces) :]
         core = core_ref[0]
         part = pl.program_id(0)
 
         @pl.when(part < parts)
         def _():
-            fill(weight_ref, slots_ref, mine_ref, other_ref)
+            fill(weight_ref, slots_ref, refs[: len(pieces)])
             result = dot(x_ref[...], weight_ref[...])
             for side, bias in enumerate(swap(core, rows_ref[pl.ds(8 + part, 1), :])):
                 inner = result[:, side * CHUNK : (side + 1) * CHUNK] + bias
@@ -279,14 +302,15 @@
         out_shape=[shaped(2 * parts + 2, tokens, CHUNK), shaped(2 * parts, tokens, CHUNK)],
         in_specs=[SMALL] * 2
         + [whole(tokens, width), whole(*vector_rows.shape)]
-        + part_blocks(mine, start, parts - 1),
+        + part_blocks(pieces, start, parts - 1),
         out_specs=[
             pl.BlockSpec((2, tokens, CHUNK), lambda k: (k, 0, 0)),
             pl.BlockSpec((2, tokens, CHUNK), lambda k: (jnp.minimum(k, parts - 1), 0, 0)),
         ],
         scratch_shapes=[pltpu.VMEM((width, width), LOW)],
         name="expand",
-    )(slots, core, first_low, vector_rows, mine, other)
+        cost_estimate=cost(9),
+    )(slots, core, first_low, vector_rows, *pieces)
 
 
 def row_blocks(shards, start, width, total, side):
@@ -298,10 +322,11 @@
     ]
 
 
-def contract(tables, active, first_sum, vector_rows, mine, other, start, total, last):
+def contract(tables, active, first_sum, vector_rows, pieces, start, total, last):
     slots, core, limits = tables
     tokens, width = first_sum.shape
-    shards = mine.shape[0]
+    mine, other = pieces[0], pieces[-1]
+    shards = mine.shape[0] * len(pieces) // 2
     each = width * shards // total
     steps = total // width
 
@@ -348,13 +373,15 @@
         ),
         out_shape=[shaped(tokens, width, kind=FULL), shaped(tokens, width, kind=FULL), shaped(tokens, width)],
         name="contract",
+        cost_estimate=cost(10.8),
     )(slots, core, limits, active, first_sum, vector_rows, *[mine] * each, *[other] * each)
 
 
-def contract_back(tables, d_out, second_sum, slope, vector_rows, mine, other, start, total, last):
+def contract_back(tables, d_out, second_sum, slope, vector_rows, pieces, start, total, last):
     slots, core, limits = tables
     tokens, width = second_sum.shape
-    shards = mine.shape[0]
+    mine, other = pieces[0], pieces[-1]
+    shards = mine.shape[0] * len(pieces) // 2
     each = width * shards // total
     steps = total // width
 
@@ -423,20 +450,21 @@
             shaped(steps, 1, width, kind=FULL),
         ],
         name="contract_back",
+        cost_estimate=cost(11),
     )(slots, core, limits, d_out, second_sum, slope, vector_rows, *[mine] * each, *[other] * each)
 
 
-def expand_back(tables, kept, sent, d_second_sum, first_sum, vector_rows, mine, other, start):
+def expand_back(tables, kept, sent, d_second_sum, first_sum, vector_rows, pieces, start):
     slots, core, _ = tables
     tokens, width = first_sum.shape
     parts = kept.shape[0]
 
     def body(
-        slots_ref, core_ref, kept_ref, sent_ref, d_second_ref, sum_ref, rows_ref, mine_ref, other_ref,
-        d_sum_ref, low_kept_ref, low_sent_ref, sums_ref, weight_ref, total_ref,
+        slots_ref, core_ref, kept_ref, sent_ref, d_second_ref, sum_ref, rows_ref, *refs
     ):
+        d_sum_ref, low_kept_ref, low_sent_ref, sums_ref, weight_ref, total_ref = refs[len(pieces) :]
         part = pl.program_id(0)
-        fill(weight_ref, slots_ref, mine_ref, other_ref)
+        fill(weight_ref, slots_ref, refs[: len(pieces)])
         term = dot(jnp.concatenate([kept_ref[0], sent_ref[0]], 1), weight_ref[...], 1, 1)
 
         @pl.when(part == 0)
@@ -471,24 +499,25 @@
         ],
         in_specs=[SMALL] * 2
         + [by_part, by_part, whole(tokens, width), whole(tokens, width), whole(*vector_rows.shape)]
-        + part_blocks(mine, start),
+        + part_blocks(pieces, start),
         out_specs=[whole(tokens, width), whole(1, tokens, CHUNK), whole(1, tokens, CHUNK), whole(3, width)],
         scratch_shapes=[pltpu.VMEM((width, width), LOW), pltpu.VMEM((tokens, width), FULL)],
         name="expand_back",
-    )(slots, core, kept, sent, d_second_sum, first_sum, vector_rows, mine, other)
-
-
-def attend_back(tables, kept, sent, qkv, mine, other, start):
+        cost_estimate=cost(9.8),
+    )(slots, core, kept, sent, d_second_sum, first_sum, vector_rows, *pieces)
+
+
+def attend_back(tables, kept, sent, qkv, pieces, start):
     slots, core, limits = tables
     tokens = kept.shape[1]
     width = 2 * CHUNK
 
     def body(
-        slots_ref, core_ref, limits_ref, kept_ref, sent_ref, qkv_ref, mine_ref, other_ref,
-        own_ref, away_ref, sums_ref, weight_ref, d_context_ref,
+        slots_ref, core_ref, limits_ref, kept_ref, sent_ref, qkv_ref, *refs
     ):
+        own_ref, away_ref, sums_ref, weight_ref, d_context_ref = refs[len(pieces) :]
         core = core_ref[0]
-        fill(weight_ref, slots_ref, mine_ref, other_ref)
+        fill(weight_ref, slots_ref, refs[: len(pieces)])
         d_context = dot(jnp.concatenate([kept_ref[0], sent_ref[0]], 1), weight_ref[...], 1, 1)
         for side, half in enumerate(swap(core, d_context)):
             d_context_ref[side] = half.astype(LOW)
@@ -522,21 +551,23 @@
         out_shape=[shaped(3, tokens, CHUNK), shaped(3, tokens, CHUNK), shaped(2, 2, 1, CHUNK, kind=FULL)],
         in_specs=[SMALL] * 3
         + [whole(1, tokens, CHUNK), whole(1, tokens, CHUNK), whole(2, 3, tokens, CHUNK)]
-        + part_blocks(mine, start),
+        + part_blocks(pieces, start),
         out_specs=[whole(3, tokens, CHUNK), whole(3, tokens, CHUNK), whole(2, 2, 1, CHUNK)],
         scratch_shapes=[pltpu.VMEM((width, width), LOW), pltpu.VMEM((2, tokens, CHUNK), LOW)],
         name="attend_back",
-    )(slots, core, limits, kept, sent, qkv, mine, other)
-
-
-def project_back(tables, kept, sent, d_first_sum, mine, other, start):
+        cost_estimate=cost(20.6),
+    )(slots, core, limits, kept, sent, qkv, *pieces)
+
+
+def project_back(tables, kept, sent, d_first_sum, pieces, start):
     slots, core, _ = tables
     tokens, width = d_first_sum.shape
     parts = kept.shape[0]
 
-    def body(slots_ref, core_ref, kept_ref, sent_ref, d_sum_ref, mine_ref, other_ref, out_ref, weight_ref):
+    def body(slots_ref, core_ref, kept_ref, sent_ref, d_sum_ref, *refs):
+        out_ref, weight_ref = refs[len(pieces) :]
         part = pl.program_id(0)
-        fill(weight_ref, slots_ref, mine_ref, other_ref)
+        fill(weight_ref, slots_ref, refs[: len(pieces)])
         term = dot(jnp.concatenate([kept_ref[0], sent_ref[0]], 1), weight_ref[...], 1, 1)
 
         @pl.when(part == 0)
@@ -552,11 +583,12 @@
         body,
         grid=(parts,),
         out_shape=shaped(tokens, width, kind=FULL),
-        in_specs=[SMALL] * 2 + [by_part, by_part, whole(tokens, width)] + part_blocks(mine, start),
+        in_specs=[SMALL] * 2 + [by_part, by_part, whole(tokens, width)] + part_blocks(pieces, start),
         out_specs=whole(tokens, width),
         scratch_shapes=[pltpu.VMEM((width, width), LOW)],
         name="project_back",
-    )(slots, core, kept, sent, d_first_sum, mine, other)
+        cost_estimate=cost(6.6),
+    )(slots, core, kept, sent, d_first_sum, *pieces)
 
 
 def weight_terms(slots, shards, *jobs):
@@ -604,10 +636,11 @@
         in_specs=specs,
         out_specs=[whole(half, sum(parts) * rows, CHUNK)] * 2,
         name="weight_terms",
+        cost_estimate=cost(2.4 * steps * sum(parts) / 2 if steps == 2 else 9.8),
     )(*values)
 
 
-GROUPS = (((0, 0),), ((0, 1), (0, 2)), ((0, 3),), ((1, 0), (1, 1)), ((1, 2), (1, 3)))
+GROUPS = (((0, 0),), ((0, 1), (0, 2)), ((0, 3),), ((1, 0), (1, 1)), ((1, 2),), ((1, 3),))
 
 
 class Gather:
@@ -619,18 +652,20 @@
 
     def turn(self, values=()):
         stages, groups, turn = self.net.stages, len(self.state), self.turns
-        for group in range(groups):
-            stage = turn - group
-            if 0 <= stage < stages:
-                self.state[group] = self.net.widen(self.state[group], stage)
-            elif stage == stages:
-                self.twins[group] = self.net.twin(self.state[group])
+        busy = [group for group in range(groups) if 0 <= turn - group < stages]
+        received = [self.net.gather(self.state[group], turn - group) for group in busy]
+        if 0 <= turn - stages < groups:
+            self.twins[turn - stages] = self.net.twin(self.state[turn - stages])
         self.turns += 1
-        nexts = [group for group in range(groups) if 0 <= turn + 1 - group <= stages]
-        held = lax.optimization_barrier(tuple([self.state[group] for group in nexts] + list(values)))
-        for group, value in zip(nexts, held):
+        own = [self.state[group] for group in range(groups) if turn - group < stages]
+        if not own and not values:
+            return []
+        own, received, values = lax.optimization_barrier((own, received, list(values)))
+        for group, value in zip((group for group in range(groups) if turn - group < stages), own):
             self.state[group] = value
-        return held[len(nexts) :]
+        for group, others in zip(busy, received):
+            self.state[group] = jnp.concatenate([self.state[group], *others], 0)
+        return values
 
     def ready(self, group):
         while self.twins[group] is None:
@@ -644,39 +679,40 @@
         self.pending = {}
         self.owned = {}
 
-    def push(self, key, kept, sent):
-        self.pending[key] = (self.net.stages - 1, kept, sent)
+    def push(self, key, *parts):
+        self.pending[key] = (self.net.stages - 1, list(parts))
 
     def turn(self, values=()):
-        held = list(values)
-        for key, (stage, kept, sent) in self.pending.items():
-            kept, sent = self.net.narrow(kept, sent, stage)
-            self.pending[key] = (stage - 1, kept, sent)
+        received = [self.net.reduce(parts, stage) for stage, parts in self.pending.values()]
+        own = [parts[0] for _, parts in self.pending.values()]
+        own, received, values = lax.optimization_barrier((own, received, list(values)))
+        waiting = {}
+        for (key, (stage, _)), mine, others in zip(self.pending.items(), own, received):
+            parts = self.net.narrow(mine, others, stage)
             if stage:
-                held += [kept, sent]
+                waiting[key] = (stage - 1, parts)
             else:
-                self.owned[key] = self.net.across(kept[0])
-        self.pending = {key: entry for key, entry in self.pending.items() if entry[0] >= 0}
-        held = list(lax.optimization_barrier(tuple(held)))
-        values, held = held[: len(values)], held[len(values) :]
-        for place, (key, entry) in enumerate(self.pending.items()):
-            self.pending[key] = (entry[0], held[2 * place], held[2 * place + 1])
+                self.owned[key] = self.net.across(parts[0][0])
+        self.pending = waiting
         return values
 
 
-def shards(net, tokens, valid, qkv_weight, out_weight, up_weight, down_weight, vectors, cotangent):
+def shards(wide, net, tokens, valid, qkv_weight, out_weight, up_weight, down_weight, vectors, cotangent):
     count = net.shards
     core = (lax.axis_index("rep") % 2).astype(jnp.int32)
     place = lax.axis_index("fsdp").astype(jnp.int32)
-    flips = jnp.asarray(net.flips)
-    own_flips = jnp.where(core == 0, flips[0], flips[1])
-    twin_flips = jnp.where(core == 0, flips[1], flips[0])
-    places = jnp.stack([own_flips ^ place, twin_flips ^ place])
     numbers = jnp.arange(count, dtype=jnp.int32)
-    slots = jnp.sum(
-        jnp.where(places[:, None, :] == numbers[None, :, None], numbers[None, None, :], 0), 2
-    )
-    tables = (slots, core.reshape(1), valid)
+
+    def order(flips):
+        flips = jnp.asarray(flips)
+        places = jnp.stack([jnp.where(core == 0, flips[0], flips[1]), jnp.where(core == 0, flips[1], flips[0])]) ^ place
+        return places, jnp.sum(
+            jnp.where(places[:, None, :] == numbers[None, :, None], numbers[None, None, :], 0), 2
+        )
+
+    places, slots = order(net.flips)
+    wide_slots = order(wide.flips)[1]
+    tables = (wide_slots, core.reshape(1), valid)
     weight_inputs = (qkv_weight, out_weight, up_weight, down_weight)
     width = tokens.shape[1]
     inner_width = up_weight.shape[2]
@@ -692,11 +728,11 @@
             pieces.append(piece.reshape(-1, CHUNK))
             start += pieces[-1].shape[0]
         blocks.append(jnp.concatenate(pieces, 0))
-    gather = Gather(net, blocks)
+    gather = Gather(wide, blocks)
 
     def weight(level, kind):
         number, start = home[level, kind]
-        return (*gather.ready(number), start)
+        return gather.ready(number), start
 
     vector_blocks = vectors[None]
     for stage in range(net.stages):
@@ -705,15 +741,20 @@
     vector_all = jnp.take(vector_blocks, slots[0], axis=0).transpose(1, 0, 2).reshape(LAYERS, -1, width)
 
     hidden, h_low = tokens, tokens
-    kept = []
+    kept, twins = [], []
     for level in range(LAYERS):
         rows = vector_all[level]
         last = level == LAYERS - 1
         qkv, left_a = project(tables, h_low, rows, *weight(level, 0))
-        (left_a,) = gather.turn((left_a,))
+        if level:
+            left_a, twins[1] = gather.turn((left_a, twins[1]))
+        else:
+            (left_a,) = gather.turn((left_a,))
+        twins.append(net.twin(left_a))
         first_sum, first_low = mix(tables, left_a, hidden, rows, *weight(level, 1))
         left_b, slope = expand(tables, first_low, rows, *weight(level, 2), parts)
-        left_b, slope = gather.turn((left_b, slope))
+        left_b, twins[2 * level], slope = gather.turn((left_b, twins[2 * level], slope))
+        twins.append(net.twin(left_b))
         second_sum, hidden, h_low = contract(
             tables, left_b, first_sum, rows, *weight(level, 3), inner_width, last
         )
@@ -726,8 +767,8 @@
     d_vectors = [None] * LAYERS
     for level in reversed(range(LAYERS)):
         qkv, left_a, first_sum, left_b, slope, second_sum = kept[level]
+        twin_a, twin_b = twins[2 * level : 2 * level + 2]
         rows = vector_all[level]
-        twin_a, twin_b = net.twin(left_a), net.twin(left_b)
         d_second_sum, f_kept, u_kept, sent, sums_b, sums_u = contract_back(
             tables, d_hidden, second_sum, slope, rows, *weight(level, 3), inner_width, level == LAYERS - 1
         )
@@ -760,7 +801,8 @@
             d_vector = jnp.stack(d_vectors, 1)
             d_vector = d_vector + net.twin(d_vector)
             d_vector = jnp.take(d_vector, places[0], axis=0)
-        d_hidden = project_back(tables, q_kept, q_sent, d_first_sum, *weight(level, 0))
+        if level:
+            d_hidden = project_back(tables, q_kept, q_sent, d_first_sum, *weight(level, 0))
         term = weight_terms(slots, count, (left_a, twin_a, 0, 2, q_kept, q_received, 0))
         *term, d_hidden = reduce.turn((*term, d_hidden))
         reduce.push((level, "qkv"), *term)
@@ -779,6 +821,8 @@
             whole_grads[key] = (mine[start : start + height], other[start : start + height])
             start += height
 
+    d_hidden = project_back(tables, q_kept, q_sent, d_first_sum, *weight(0, 0))
+    (d_hidden,) = reduce.turn((d_hidden,))
     while keys[-2] not in reduce.owned:
         reduce.turn()
     finish(keys[:-1])
@@ -825,5 +869,4 @@
         P(None, "fsdp", None),
         P(None, "fsdp"),
     )
-    net = Net(mesh)
-    return jax.shard_map(functools.partial(shards, net), mesh=mesh, in_specs=in_specs, out_specs=out_specs, check_vma=False)
+    return jax.shard_map(functools.partial(shards, Net(mesh, False), Net(mesh, False)), mesh=mesh, in_specs=in_specs, out_specs=out_specs, check_vma=False)

time: 555 us -> 517 us (0.932)
  waiting for transfers between devices: 179 us -> 132 us
  local copies, waits for them, and re-layouts: 13.4 us -> 48.5 us
  other arithmetic: 54.9 us -> 30.4 us
    ppermute x52 -> x56, waiting for transfers between devices: 168 us -> 132 us  [trade(): return lax.ppermute(value, ('rep', 'fsdp'), pairs)]
    concatenate x24 -> x4, other arithmetic: 27.3 us -> 1.33 us  [widen(): return jnp.concatenate([value, *self.gather(value, stage)], 0)]
    concatenate x0 -> x24, local copies, waits for them, and re-layouts: none -> 19.4 us  [turn(): self.state[group] = jnp.concatenate([self.state[group], *others], 0)]
    unnamed x110 -> x166, local copies, waits for them, and re-layouts: 6.98 us -> 22.1 us
    ppermute x18 -> x19, waiting for transfers between devices: 10.8 us -> 0.36 us  [twin(): lax.ppermute(value, 'rep', [(rep, rep ^ 1) for rep in range(self.replicas)])]
    ppermute x52 -> x56, starting transfers between devices: 68.2 us -> 63.1 us  [trade(): return lax.ppermute(value, ('rep', 'fsdp'), pairs)]
  transfers between devices with their start and end apart: 70 -> 75, of which waited for: 28 -> 28; matrix products, arithmetic and copies ran while one was open for 9% -> 12% of each run, Pallas kernels for 40% -> 43%
where the time goes in v4:
time: 517 us; the launch traced here: 510 us
  Pallas kernels  230 us (44%)
  waiting for transfers between devices  132 us (26%)
  starting transfers between devices  67.6 us (13%)
  local copies, waits for them, and re-layouts  48.5 us (9%)
  other arithmetic  30.4 us (6%)
    ppermute x56, waiting for transfers between devices, trade(): return lax.ppermute(value, ('rep', 'fsdp'), pairs)  132 us
    ppermute x56, starting transfers between devices, trade(): return lax.ppermute(value, ('rep', 'fsdp'), pairs)  63.1 us
    pallas_call x6, Pallas kernels, weight_terms(): pl.pallas_call(body, grid=(steps,), out_shape=[shaped(half, sum(parts) *...  56.3 us
    pallas_call x2, Pallas kernels, attend_back(): pl.pallas_call(body, grid=(1,), out_shape=[shaped(3, tokens, CHUNK), shap...  41.3 us
    pallas_call x2, Pallas kernels, project(): pl.pallas_call(body, grid=(3,), out_shape=[shaped(2, 3, tokens, CHUNK), s...  28.5 us
    pallas_call x2, Pallas kernels, contract(): pl.pallas_call(body, grid_spec=pltpu.PrefetchScalarGridSpec(num_scalar_pr...  22.1 us
    unnamed x166, local copies, waits for them, and re-layouts  22.1 us
    pallas_call x2, Pallas kernels, contract_back(): pl.pallas_call(body, grid_spec=pltpu.PrefetchScalarGridSpec(num_scalar_pr...  22 us
  transfers between devices with their start and end apart: 75, of which 28 were waited for; matrix products, arithmetic and copies ran while one was open for 12% of the time, Pallas kernels for 43%

profile of v4, /device:TPU:0, one launch (start us, length us, event | category | flops | bytes accessed | tf_op | source)
XLA Modules:
  0.0 510.4 jit_solution(10965193411032441987)
XLA Ops:
  2.1 3.1 collective-permute-start
  8.9 2.7 collective-permute-start.2
  13.1 8.0 %collective-permute-done.4 = f32[2,2,576]{2,1,0:T(2,128)S(1)} collective-permute-done((f32[2,2,576]{2,1,0:T(2,128)S(1)}, f32[2,2,576]{2,1,0:T(2,128)S(1)}, u32[]{:S(2)}, u32[]{:S(2)}) %collective-permute-start.4) | collective-permute-done | bytes 9248 | tf_op jit(solution)/shard_map/ppermute | solution.py:52
  22.7 1.9 collective-permute-start.6
  24.6 2.3 collective-permute-start.7
  27.5 3.3 collective-permute-done.8
  33.3 7.5 %collective-permute-done.6 = bf16[2,240,384]{2,1,0:T(8,128)(2,1)S(1)} collective-permute-done((bf16[2,240,384]{2,1,0:T(8,128)(2,1)S(1)}, bf16[2,240,384]{2,1,0:T(8,128)(2,1)S(1)}, u32[]{:S(2)}, u32[]{:S(2)}) %collective-permute-start.6) | collective-permute-done | bytes 368672 | tf_op jit(solution)/shard_map/ppermute | solution.py:52
  45.0 2.0 collective-permute-start.12
  47.1 14.4 %collective-permute-done.13 = f32[8,2,576]{2,1,0:T(2,128)S(1)} collective-permute-done((f32[8,2,576]{2,1,0:T(2,128)S(1)}, f32[8,2,576]{2,1,0:T(2,128)S(1)}, u32[]{:S(2)}, u32[]{:S(2)}) %collective-permute-start.13) | collective-permute-done | bytes 36896 | tf_op jit(solution)/shard_map/ppermute | solution.py:52
  66.6 2.2 constant_dynamic-update-slice_fusion.24.refs_0_
  69.6 3.6 collective-permute-start.17
  76.2 3.1 collective-permute-done.17
  79.3 7.2 %collective-permute-done.16 = bf16[2,192,384]{2,1,0:T(8,128)(2,1)} collective-permute-done((bf16[2,192,384]{2,1,0:T(8,128)(2,1)S(1)}, bf16[2,192,384]{2,1,0:T(8,128)(2,1)}, u32[]{:S(2)}, u32[]{:S(2)}) %collective-permute-start.16) | collective-permute-done | bytes 294944 | tf_op jit(solution)/shard_map/ppermute | solution.py:52
  86.5 4.3 collective-permute-done.14
  92.1 2.7 constant_dynamic-update-slice_fusion.32.refs_0_
  98.3 3.6 collective-permute-start.21
  101.8 14.4 %project.2 = (bf16[2,3,512,384]{3,2,1,0:T(8,128)(2,1)}, bf16[4,512,384]{2,1,0:T(8,128)(2,1)}) custom-call(s32[2,16]{1,0:T(2,128)} %copy-done.48, s32[1]{0:T(128)} %bitcast.core_ref, s32[4]{0:T(128)} %limits_ref.15, bf16[512,768]{1,0:T(8,128)(2,1)} %hidden_ref.1, f32[12,768]{1,0:T(8,128)} %squeeze.23.rows_ref, ...), custom_call_target="tpu_custom_call" | custom-call | flops 16675000320 | bytes 14500000 | tf_op jit(solution)/shard_map/project/pallas_call | solution.py:235
  116.2 3.1 collective-permute-done.18
  121.8 2.6 collective-permute-start.25
  131.4 4.2 mix.2
  135.5 8.9 %expand.2 = (bf16[10,512,384]{2,1,0:T(8,128)(2,1)}, bf16[8,512,384]{2,1,0:T(8,128)(2,1)}) custom-call(s32[2,16]{1,0:T(2,128)} %copy-done.48, s32[1]{0:T(128)} %bitcast.core_ref, bf16[512,768]{1,0:T(8,128)(2,1)} %get-tuple-element.283.x_ref, f32[12,768]{1,0:T(8,128)} %squeeze.23.rows_ref, bf16[16,240,384]{2,1,0:T(8,128)(2,1)} %constant_dynamic-update-slice_fusion.32.refs_0_, ...), custom_call_target="tpu_custom_call" | custom-call | flops 10350000128 | bytes 9000000 | tf_op jit(solution)/shard_map/expand/pallas_call | solution.py:299
  144.5 3.5 collective-permute-done.23
  150.1 2.4 constant_dynamic-update-slice_fusion.42.refs_0_
  157.3 10.9 %contract.2 = (f32[512,768]{1,0:T(8,128)}, f32[512,768]{1,0:T(8,128)}, bf16[512,768]{1,0:T(8,128)(2,1)}) custom-call(s32[2,16]{1,0:T(2,128)} %copy-done.48, s32[1]{0:T(128)} %bitcast.core_ref, s32[4]{0:T(128)} %limits_ref.15, bf16[10,512,384]{2,1,0:T(8,128)(2,1)} %get-tuple-element.290.active_ref.refs_0_, f32[512,768]{1,0:T(8,128)} %get-tuple-element.291.first_ref.sum_ref, ...), custom_call_target="tpu_custom_call" | custom-call | flops 12419999744 | bytes 10800000 | tf_op jit(solution)/shard_map/contract/pallas_call | solution.py:359
  168.2 4.9 collective-permute-done.29
  173.1 3.9 collective-permute-done.28
  180.9 14.1 %project.3 = (bf16[2,3,512,384]{3,2,1,0:T(8,128)(2,1)}, bf16[4,512,384]{2,1,0:T(8,128)(2,1)}) custom-call(s32[2,16]{1,0:T(2,128)} %copy-done.48, s32[1]{0:T(128)} %bitcast.core_ref, s32[4]{0:T(128)} %limits_ref.15, bf16[512,768]{1,0:T(8,128)(2,1)} %get-tuple-element.297.x_ref, f32[12,768]{1,0:T(8,128)} %squeeze.24.rows_ref, ...), custom_call_target="tpu_custom_call" | custom-call | flops 16675000320 | bytes 14500000 | tf_op jit(solution)/shard_map/project/pallas_call | solution.py:235
  196.2 2.4 constant_dynamic-update-slice_fusion.46.refs_0_.refs_1_.refs_2_.refs_3_
  199.1 4.4 mix.3
  203.5 9.0 %expand.3 = (bf16[10,512,384]{2,1,0:T(8,128)(2,1)}, bf16[8,512,384]{2,1,0:T(8,128)(2,1)}) custom-call(s32[2,16]{1,0:T(2,128)} %copy-done.48, s32[1]{0:T(128)} %bitcast.core_ref, bf16[512,768]{1,0:T(8,128)(2,1)} %get-tuple-element.303.x_ref, f32[12,768]{1,0:T(8,128)} %squeeze.24.rows_ref, bf16[16,192,384]{2,1,0:T(8,128)(2,1)} %constant_dynamic-update-slice_fusion.44.refs_0_, ...), custom_call_target="tpu_custom_call" | custom-call | flops 10350000128 | bytes 9000000 | tf_op jit(solution)/shard_map/expand/pallas_call | solution.py:299
  214.4 11.2 %contract.3 = (f32[512,768]{1,0:T(8,128)}, f32[512,768]{1,0:T(8,128)}, bf16[512,768]{1,0:T(8,128)(2,1)}) custom-call(s32[2,16]{1,0:T(2,128)} %copy-done.48, s32[1]{0:T(128)} %bitcast.core_ref, s32[4]{0:T(128)} %limits_ref.15, bf16[10,512,384]{2,1,0:T(8,128)(2,1)} %get-tuple-element.308.active_ref.refs_0_, f32[512,768]{1,0:T(8,128)} %get-tuple-element.309.first_ref.sum_ref, ...), custom_call_target="tpu_custom_call" | custom-call | flops 12419999744 | bytes 10800000 | tf_op jit(solution)/shard_map/contract/pallas_call | solution.py:359
  225.7 10.8 %contract_back.2 = (f32[512,768]{1,0:T(8,128)}, bf16[1,512,384]{2,1,0:T(8,128)(2,1)}, bf16[4,512,384]{2,1,0:T(8,128)(2,1)}, bf16[5,512,384]{2,1,0:T(8,128)(2,1)}...) custom-call(s32[2,16]{1,0:T(2,128)} %copy-done.48, s32[1]{0:T(128)} %bitcast.core_ref, s32[4]{0:T(128)} %limits_ref.15, ...), custom_call_target="tpu_custom_call" | custom-call | flops 12650000384 | bytes 11000000 | tf_op jit(solution)/shard_map/contract_back/pallas_call | solution.py:421
  236.5 9.9 %expand_back.2 = (f32[512,768]{1,0:T(8,128)}, bf16[1,512,384]{2,1,0:T(8,128)(2,1)}, bf16[1,512,384]{2,1,0:T(8,128)(2,1)}, f32[3,768]{1,0:T(4,128)}) custom-call(s32[2,16]{1,0:T(2,128)} %copy-done.48, s32[1]{0:T(128)} %bitcast.core_ref, bf16[4,512,384]{2,1,0:T(8,128)(2,1)} %get-tuple-element.323.kept_ref.refs_2_, ...), custom_call_target="tpu_custom_call" | custom-call | flops 11269999616 | bytes 9800000 | tf_op jit(solution)/shard_map/expand_back/pallas_call | solution.py:491
  247.7 9.8 %weight_terms.6 = (bf16[8,192,384]{2,1,0:T(8,128)(2,1)}, bf16[8,192,384]{2,1,0:T(8,128)(2,1)}) custom-call(s32[2,16]{1,0:T(2,128)} %copy-done.48, bf16[10,512,384]{2,1,0:T(8,128)(2,1)} %get-tuple-element.308.active_ref.refs_0_, bf16[10,512,384]{2,1,0:T(8,128)(2,1)} %collective-permute-done.37.refs_1_, bf16[1,512,384]{2,1,0:T(8,128)(2,1)} %get-tuple-element.319.refs_2_, ...), custom_call_target="tpu_custom_call" | custom-call | flops 11269999616 | bytes 9800000 | tf_op jit(solution)/shard_map/weight_terms/pallas_call | solution.py:632
  259.8 20.6 %attend_back.2 = (bf16[3,512,384]{2,1,0:T(8,128)(2,1)}, bf16[3,512,384]{2,1,0:T(8,128)(2,1)}, f32[2,2,1,384]{3,2,1,0:T(1,128)}) custom-call(s32[2,16]{1,0:T(2,128)} %copy-done.48, s32[1]{0:T(128)} %bitcast.core_ref, s32[4]{0:T(128)} %limits_ref.15, bf16[1,512,384]{2,1,0:T(8,128)(2,1)} %get-tuple-element.331.refs_6_.kept_ref, ...), custom_call_target="tpu_custom_call" | custom-call | flops 23690000384 | bytes 20600000 | tf_op jit(solution)/shard_map/attend_back/pallas_call | solution.py:548
  281.1 11.1 %weight_terms.7 = (bf16[8,240,384]{2,1,0:T(8,128)(2,1)}, bf16[8,240,384]{2,1,0:T(8,128)(2,1)}) custom-call(s32[2,16]{1,0:T(2,128)} %copy-done.48, bf16[10,512,384]{2,1,0:T(8,128)(2,1)} %get-tuple-element.308.active_ref.refs_0_, bf16[10,512,384]{2,1,0:T(8,128)(2,1)} %collective-permute-done.37.refs_1_, ...), custom_call_target="tpu_custom_call" | custom-call | flops 13799999488 | bytes 12000000 | tf_op jit(solution)/shard_map/weight_terms/pallas_call | solution.py:632
  296.4 6.7 %project_back.2.d_out_ref = f32[512,768]{1,0:T(8,128)} custom-call(s32[2,16]{1,0:T(2,128)} %copy-done.48, s32[1]{0:T(128)} %bitcast.core_ref, bf16[3,512,384]{2,1,0:T(8,128)(2,1)} %get-tuple-element.342.refs_2_.kept_ref, bf16[3,512,384]{2,1,0:T(8,128)(2,1)} %get-tuple-element.343.sent_ref, f32[512,768]{1,0:T(8,128)} %get-tuple-element.346.d_sum_ref, ...), custom_call_target="tpu_custom_call" | custom-call | flops 7590000128 | bytes 6600000 | tf_op jit(solution)/shard_map/project_back/pallas_call | solution.py:582
  303.1 7.2 %weight_terms.8 = (bf16[8,144,384]{2,1,0:T(8,128)(2,1)}, bf16[8,144,384]{2,1,0:T(8,128)(2,1)}) custom-call(s32[2,16]{1,0:T(2,128)} %copy-done.48, bf16[4,512,384]{2,1,0:T(8,128)(2,1)} %get-tuple-element.301.context_ref.refs_4_.refs_0_, bf16[4,512,384]{2,1,0:T(8,128)(2,1)} %collective-permute-done.35.refs_5_.refs_1_, ...), custom_call_target="tpu_custom_call" | custom-call | flops 8280000000 | bytes 7199999 | tf_op jit(solution)/shard_map/weight_terms/pallas_call | solution.py:632
  311.6 8.2 %collective-permute-done.42 = bf16[8,240,384]{2,1,0:T(8,128)(2,1)} collective-permute-done((bf16[8,240,384]{2,1,0:T(8,128)(2,1)}, bf16[8,240,384]{2,1,0:T(8,128)(2,1)}, u32[]{:S(2)}, u32[]{:S(2)}) %collective-permute-start.42) | collective-permute-done | bytes 1474592 | tf_op jit(solution)/shard_map/ppermute | solution.py:52
  319.8 2.6 add_convert_fusion.2
  325.8 11.2 %contract_back.3 = (f32[512,768]{1,0:T(8,128)}, bf16[1,512,384]{2,1,0:T(8,128)(2,1)}, bf16[4,512,384]{2,1,0:T(8,128)(2,1)}, bf16[5,512,384]{2,1,0:T(8,128)(2,1)}...) custom-call(s32[2,16]{1,0:T(2,128)} %copy-done.48, s32[1]{0:T(128)} %bitcast.core_ref, s32[4]{0:T(128)} %limits_ref.15, ...), custom_call_target="tpu_custom_call" | custom-call | flops 12650000384 | bytes 11000000 | tf_op jit(solution)/shard_map/contract_back/pallas_call | solution.py:421
  337.1 3.8 collective-permute-done.44
  340.9 2.2 collective-permute-done.46
  345.1 2.1 add_convert_fusion.10
  349.3 3.3 collective-permute-start.47
  352.6 9.8 %expand_back.3 = (f32[512,768]{1,0:T(8,128)}, bf16[1,512,384]{2,1,0:T(8,128)(2,1)}, bf16[1,512,384]{2,1,0:T(8,128)(2,1)}, f32[3,768]{1,0:T(4,128)}) custom-call(s32[2,16]{1,0:T(2,128)} %copy-done.48, s32[1]{0:T(128)} %bitcast.core_ref, bf16[4,512,384]{2,1,0:T(8,128)(2,1)} %get-tuple-element.371.kept_ref.refs_2_, ...), custom_call_target="tpu_custom_call" | custom-call | flops 11269999616 | bytes 9800000 | tf_op jit(solution)/shard_map/expand_back/pallas_call | solution.py:491
  362.4 10.0 %weight_terms.9 = (bf16[8,192,384]{2,1,0:T(8,128)(2,1)}, bf16[8,192,384]{2,1,0:T(8,128)(2,1)}) custom-call(s32[2,16]{1,0:T(2,128)} %copy-done.48, bf16[10,512,384]{2,1,0:T(8,128)(2,1)} %get-tuple-element.290.active_ref.refs_0_, bf16[10,512,384]{2,1,0:T(8,128)(2,1)} %collective-permute-done.33.refs_1_, bf16[1,512,384]{2,1,0:T(8,128)(2,1)} %get-tuple-element.367.refs_2_, ...), custom_call_target="tpu_custom_call" | custom-call | flops 11269999616 | bytes 9800000 | tf_op jit(solution)/shard_map/weight_terms/pallas_call | solution.py:632
  376.5 20.6 %attend_back.3 = (bf16[3,512,384]{2,1,0:T(8,128)(2,1)}, bf16[3,512,384]{2,1,0:T(8,128)(2,1)}, f32[2,2,1,384]{3,2,1,0:T(1,128)}) custom-call(s32[2,16]{1,0:T(2,128)} %copy-done.48, s32[1]{0:T(128)} %bitcast.core_ref, s32[4]{0:T(128)} %limits_ref.15, bf16[1,512,384]{2,1,0:T(8,128)(2,1)} %get-tuple-element.383.refs_6_.kept_ref, ...), custom_call_target="tpu_custom_call" | custom-call | flops 23690000384 | bytes 20600000 | tf_op jit(solution)/shard_map/attend_back/pallas_call | solution.py:548
  398.9 11.2 %weight_terms.10 = (bf16[8,240,384]{2,1,0:T(8,128)(2,1)}, bf16[8,240,384]{2,1,0:T(8,128)(2,1)}) custom-call(s32[2,16]{1,0:T(2,128)} %copy-done.48, bf16[10,512,384]{2,1,0:T(8,128)(2,1)} %get-tuple-element.290.active_ref.refs_0_, bf16[10,512,384]{2,1,0:T(8,128)(2,1)} %collective-permute-done.33.refs_1_, ...), custom_call_target="tpu_custom_call" | custom-call | flops 13799999488 | bytes 12000000 | tf_op jit(solution)/shard_map/weight_terms/pallas_call | solution.py:632
  414.3 2.4 add_convert_fusion.4
  418.7 7.1 %weight_terms.11 = (bf16[8,144,384]{2,1,0:T(8,128)(2,1)}, bf16[8,144,384]{2,1,0:T(8,128)(2,1)}) custom-call(s32[2,16]{1,0:T(2,128)} %copy-done.48, bf16[4,512,384]{2,1,0:T(8,128)(2,1)} %get-tuple-element.280.context_ref.refs_4_.refs_0_, bf16[4,512,384]{2,1,0:T(8,128)(2,1)} %collective-permute-done.27.refs_5_.refs_1_, ...), custom_call_target="tpu_custom_call" | custom-call | flops 8280000000 | bytes 7199999 | tf_op jit(solution)/shard_map/weight_terms/pallas_call | solution.py:632
  425.8 7.3 %collective-permute-done.56 = bf16[4,192,384]{2,1,0:T(8,128)(2,1)S(1)} collective-permute-done((bf16[4,192,384]{2,1,0:T(8,128)(2,1)}, bf16[4,192,384]{2,1,0:T(8,128)(2,1)S(1)}, u32[]{:S(2)}, u32[]{:S(2)}) %collective-permute-start.56) | collective-permute-done | bytes 589856 | tf_op jit(solution)/shard_map/ppermute | solution.py:52
  433.1 4.5 collective-permute-done.57
  437.6 2.7 add_convert_fusion
  444.2 6.7 %project_back.3 = f32[512,768]{1,0:T(8,128)} custom-call(s32[2,16]{1,0:T(2,128)} %copy-done.48, s32[1]{0:T(128)} %bitcast.core_ref, bf16[3,512,384]{2,1,0:T(8,128)(2,1)} %get-tuple-element.396.refs_2_.kept_ref, bf16[3,512,384]{2,1,0:T(8,128)(2,1)} %get-tuple-element.397.sent_ref, f32[512,768]{1,0:T(8,128)} %get-tuple-element.414.d_sum_ref, ...), custom_call_target="tpu_custom_call" | custom-call | flops 7590000128 | bytes 6600000 | tf_op jit(solution)/shard_map/project_back/pallas_call | solution.py:582
  451.7 5.4 %collective-permute-done.60 = bf16[2,192,384]{2,1,0:T(8,128)(2,1)} collective-permute-done((bf16[2,192,384]{2,1,0:T(8,128)(2,1)}, bf16[2,192,384]{2,1,0:T(8,128)(2,1)}, u32[]{:S(2)}, u32[]{:S(2)}) %collective-permute-start.60) | collective-permute-done | bytes 294944 | tf_op jit(solution)/shard_map/ppermute | solution.py:52
  457.1 2.3 collective-permute-done.61
  466.2 2.4 collective-permute-start.64
  468.7 8.6 %collective-permute-done.64 = bf16[1,192,384]{2,1,0:T(8,128)(2,1)S(1)} collective-permute-done((bf16[1,192,384]{2,1,0:T(8,128)(2,1)S(1)}, bf16[1,192,384]{2,1,0:T(8,128)(2,1)S(1)}, u32[]{:S(2)}, u32[]{:S(2)}) %collective-permute-start.64) | collective-permute-done | bytes 147488 | tf_op jit(solution)/shard_map/ppermute | solution.py:52
  477.3 7.0 %collective-permute-done.65 = bf16[2,240,384]{2,1,0:T(8,128)(2,1)S(1)} collective-permute-done((bf16[2,240,384]{2,1,0:T(8,128)(2,1)S(1)}, bf16[2,240,384]{2,1,0:T(8,128)(2,1)S(1)}, u32[]{:S(2)}, u32[]{:S(2)}) %collective-permute-start.65) | collective-permute-done | bytes 368672 | tf_op jit(solution)/shard_map/ppermute | solution.py:52
  484.5 3.0 collective-permute-start.70
  487.7 9.8 %collective-permute-done.70 = f32[2,2,576]{2,1,0:T(2,128)S(1)} collective-permute-done((f32[2,2,576]{2,1,0:T(2,128)S(1)}, f32[2,2,576]{2,1,0:T(2,128)S(1)}, u32[]{:S(2)}, u32[]{:S(2)}) %collective-permute-start.70) | collective-permute-done | bytes 9248 | tf_op jit(solution)/shard_map/ppermute | solution.py:52
  498.9 2.0 collective-permute-start.72
  500.9 3.5 collective-permute-done.72
  (391 shorter events, 100.7 us)
Async XLA Ops:
  8.9 12.3 %collective-permute-start.2 = (bf16[2,144,384]{2,1,0:T(8,128)(2,1)S(1)}, bf16[2,144,384]{2,1,0:T(8,128)(2,1)S(1)}, u32[]{:S(2)}, u32[]{:S(2)}) collective-permute-start(bf16[2,144,384]{2,1,0:T(8,128)(2,1)S(1)} %constant_dynamic-update-slice_fusion), channel_id=1, source_target_pairs={{0,8},{1,9},{2,10},{3,11},{4,12},{5,13},{6,14},{7,15},{8,0},{9,1},... | collective-permute-start | bytes 663560 | tf_op jit(solution)/shard_map/ppermute | solution.py:52
  11.5 9.7 %collective-permute-start.3 = (bf16[1,240,384]{2,1,0:T(8,128)(2,1)S(1)}, bf16[1,240,384]{2,1,0:T(8,128)(2,1)S(1)}, u32[]{:S(2)}, u32[]{:S(2)}) collective-permute-start(bf16[1,240,384]{2,1,0:T(8,128)(2,1)S(1)} %maximum_bitcast_fusion), channel_id=1, source_target_pairs={{0,4},{1,5},{2,6},{3,7},{4,0},{5,1},{6,2},{7,3},{8,12},{9,13},{10,... | collective-permute-start | bytes 552968 | tf_op jit(solution)/shard_map/ppermute | solution.py:52
  21.3 19.5 %collective-permute-start.5 = (bf16[4,144,384]{2,1,0:T(8,128)(2,1)S(1)}, bf16[4,144,384]{2,1,0:T(8,128)(2,1)S(1)}, u32[]{:S(2)}, u32[]{:S(2)}) collective-permute-start(bf16[4,144,384]{2,1,0:T(8,128)(2,1)S(1)} %constant_dynamic-update-slice_fusion.2), channel_id=1, source_target_pairs={{0,2},{1,3},{2,0},{3,1},{4,6},{5,7},{6,4},{7,5},{8,10},{9,11},{10,... | collective-permute-start | bytes 1327112 | tf_op jit(solution)/shard_map/ppermute | solution.py:52
  22.7 18.1 %collective-permute-start.6 = (bf16[2,240,384]{2,1,0:T(8,128)(2,1)S(1)}, bf16[2,240,384]{2,1,0:T(8,128)(2,1)S(1)}, u32[]{:S(2)}, u32[]{:S(2)}) collective-permute-start(bf16[2,240,384]{2,1,0:T(8,128)(2,1)S(1)} %constant_dynamic-update-slice_fusion.4), channel_id=1, source_target_pairs={{0,8},{1,9},{2,10},{3,11},{4,12},{5,13},{6,14},{7,15},{8,0},{9,1},... | collective-permute-start | bytes 1105928 | tf_op jit(solution)/shard_map/ppermute | solution.py:52
  24.6 8.6 %collective-permute-start.7 = (bf16[1,192,384]{2,1,0:T(8,128)(2,1)S(1)}, bf16[1,192,384]{2,1,0:T(8,128)(2,1)S(1)}, u32[]{:S(2)}, u32[]{:S(2)}) collective-permute-start(bf16[1,192,384]{2,1,0:T(8,128)(2,1)S(1)} %constant_dynamic-slice_fusion.8), channel_id=1, source_target_pairs={{0,4},{1,5},{2,6},{3,7},{4,0},{5,1},{6,2},{7,3},{8,12},{9,13},{10,... | collective-permute-start | bytes 442376 | tf_op jit(solution)/shard_map/ppermute | solution.py:52
  41.0 22.8 %collective-permute-start.9 = (bf16[8,144,384]{2,1,0:T(8,128)(2,1)S(1)}, bf16[8,144,384]{2,1,0:T(8,128)(2,1)}, u32[]{:S(2)}, u32[]{:S(2)}) collective-permute-start(bf16[8,144,384]{2,1,0:T(8,128)(2,1)S(1)} %constant_dynamic-update-slice_fusion.6), channel_id=1, source_target_pairs={{0,1},{1,0},{2,3},{3,2},{4,5},{5,4},{6,7},{7,6},{8,9},{9,8},{10,11... | collective-permute-start | bytes 2654216 | tf_op jit(solution)/shard_map/ppermute | solution.py:52
  41.8 20.3 %collective-permute-start.10 = (bf16[4,240,384]{2,1,0:T(8,128)(2,1)S(1)}, bf16[4,240,384]{2,1,0:T(8,128)(2,1)S(1)}, u32[]{:S(2)}, u32[]{:S(2)}) collective-permute-start(bf16[4,240,384]{2,1,0:T(8,128)(2,1)S(1)} %constant_dynamic-update-slice_fusion.8), channel_id=1, source_target_pairs={{0,2},{1,3},{2,0},{3,1},{4,6},{5,7},{6,4},{7,5},{8,10},{9,11},{10,... | collective-permute-start | bytes 2211848 | tf_op jit(solution)/shard_map/ppermute | solution.py:52
  43.3 18.8 %collective-permute-start.11 = (bf16[2,192,384]{2,1,0:T(8,128)(2,1)S(1)}, bf16[2,192,384]{2,1,0:T(8,128)(2,1)S(1)}, u32[]{:S(2)}, u32[]{:S(2)}) collective-permute-start(bf16[2,192,384]{2,1,0:T(8,128)(2,1)S(1)} %constant_dynamic-update-slice_fusion.10), channel_id=1, source_target_pairs={{0,8},{1,9},{2,10},{3,11},{4,12},{5,13},{6,14},{7,15},{8,0},{9,1},... | collective-permute-start | bytes 884744 | tf_op jit(solution)/shard_map/ppermute | solution.py:52
  43.5 18.0 %collective-permute-start.13 = (f32[8,2,576]{2,1,0:T(2,128)S(1)}, f32[8,2,576]{2,1,0:T(2,128)S(1)}, u32[]{:S(2)}, u32[]{:S(2)}) collective-permute-start(f32[8,2,576]{2,1,0:T(2,128)S(1)} %copy-done.32), channel_id=1, source_target_pairs={{0,1},{1,0},{2,3},{3,2},{4,5},{5,4},{6,7},{7,6},{8,9},{9,8},{10,11... | collective-permute-start | bytes 110600 | tf_op jit(solution)/shard_map/ppermute | solution.py:52
  45.0 17.1 %collective-permute-start.12 = (bf16[1,192,384]{2,1,0:T(8,128)(2,1)S(1)}, bf16[1,192,384]{2,1,0:T(8,128)(2,1)S(1)}, u32[]{:S(2)}, u32[]{:S(2)}) collective-permute-start(bf16[1,192,384]{2,1,0:T(8,128)(2,1)S(1)} %maximum_bitcast_fusion.1), channel_id=1, source_target_pairs={{0,4},{1,5},{2,6},{3,7},{4,0},{5,1},{6,2},{7,3},{8,12},{9,13},{10,... | collective-permute-start | bytes 442376 | tf_op jit(solution)/shard_map/ppermute | solution.py:52
  65.0 25.9 %collective-permute-start.14 = (bf16[8,240,384]{2,1,0:T(8,128)(2,1)S(1)}, bf16[8,240,384]{2,1,0:T(8,128)(2,1)}, u32[]{:S(2)}, u32[]{:S(2)}) collective-permute-start(bf16[8,240,384]{2,1,0:T(8,128)(2,1)S(1)} %constant_dynamic-update-slice_fusion.12), channel_id=1, source_target_pairs={{0,1},{1,0},{2,3},{3,2},{4,5},{5,4},{6,7},{7,6},{8,9},{9,8},{10,11... | collective-permute-start | bytes 4423688 | tf_op jit(solution)/shard_map/ppermute | solution.py:52
  68.8 29.5 %collective-permute-start.22 = (bf16[16,144,384]{2,1,0:T(8,128)(2,1)}, bf16[16,144,384]{2,1,0:T(8,128)(2,1)}, u32[]{:S(2)}, u32[]{:S(2)}) collective-permute-start(bf16[16,144,384]{2,1,0:T(8,128)(2,1)} %constant_dynamic-update-slice_fusion.24.refs_0_), channel_id=1, source_target_pairs={{0,16},{16,0},{1,17},{17,1},{2,18},{18,2},{3,19},{19,3},{4,20},{20... | collective-permute-start | bytes 5308424 | tf_op jit(solution)/shard_map/ppermute | solution.py:55
  68.9 17.7 %collective-permute-start.15 = (bf16[4,192,384]{2,1,0:T(8,128)(2,1)S(1)}, bf16[4,192,384]{2,1,0:T(8,128)(2,1)S(1)}, u32[]{:S(2)}, u32[]{:S(2)}) collective-permute-start(bf16[4,192,384]{2,1,0:T(8,128)(2,1)S(1)} %constant_dynamic-update-slice_fusion.14), channel_id=1, source_target_pairs={{0,2},{1,3},{2,0},{3,1},{4,6},{5,7},{6,4},{7,5},{8,10},{9,11},{10,... | collective-permute-start | bytes 1769480 | tf_op jit(solution)/shard_map/ppermute | solution.py:52
  69.5 17.1 %collective-permute-start.16 = (bf16[2,192,384]{2,1,0:T(8,128)(2,1)S(1)}, bf16[2,192,384]{2,1,0:T(8,128)(2,1)}, u32[]{:S(2)}, u32[]{:S(2)}) collective-permute-start(bf16[2,192,384]{2,1,0:T(8,128)(2,1)S(1)} %constant_dynamic-update-slice_fusion.16), channel_id=1, source_target_pairs={{0,8},{1,9},{2,10},{3,11},{4,12},{5,13},{6,14},{7,15},{8,0},{9,1},... | collective-permute-start | bytes 884744 | tf_op jit(solution)/shard_map/ppermute | solution.py:52
  69.6 9.8 %collective-permute-start.17 = (bf16[1,192,384]{2,1,0:T(8,128)(2,1)S(1)}, bf16[1,192,384]{2,1,0:T(8,128)(2,1)S(1)}, u32[]{:S(2)}, u32[]{:S(2)}) collective-permute-start(bf16[1,192,384]{2,1,0:T(8,128)(2,1)S(1)} %bitcast.77), channel_id=1, source_target_pairs={{0,4},{1,5},{2,6},{3,7},{4,0},{5,1},{6,2},{7,3},{8,12},{9,13},{10,... | collective-permute-start | bytes 442376 | tf_op jit(solution)/shard_map/ppermute | solution.py:52
  94.8 36.0 %collective-permute-start.26 = (bf16[16,240,384]{2,1,0:T(8,128)(2,1)}, bf16[16,240,384]{2,1,0:T(8,128)(2,1)}, u32[]{:S(2)}, u32[]{:S(2)}) collective-permute-start(bf16[16,240,384]{2,1,0:T(8,128)(2,1)} %constant_dynamic-update-slice_fusion.32.refs_0_), channel_id=1, source_target_pairs={{0,16},{16,0},{1,17},{17,1},{2,18},{18,2},{3,19},{19,3},{4,20},{20... | collective-permute-start | bytes 8847368 | tf_op jit(solution)/shard_map/ppermute | solution.py:55
  96.2 20.0 %collective-permute-start.20 = (bf16[2,192,384]{2,1,0:T(8,128)(2,1)}, bf16[2,192,384]{2,1,0:T(8,128)(2,1)}, u32[]{:S(2)}, u32[]{:S(2)}) collective-permute-start(bf16[2,192,384]{2,1,0:T(8,128)(2,1)} %constant_dynamic-update-slice_fusion.22), channel_id=1, source_target_pairs={{0,8},{1,9},{2,10},{3,11},{4,12},{5,13},{6,14},{7,15},{8,0},{9,1},... | collective-permute-start | bytes 884744 | tf_op jit(solution)/shard_map/ppermute | solution.py:52
  97.2 19.0 %collective-permute-start.19 = (bf16[4,192,384]{2,1,0:T(8,128)(2,1)S(1)}, bf16[4,192,384]{2,1,0:T(8,128)(2,1)}, u32[]{:S(2)}, u32[]{:S(2)}) collective-permute-start(bf16[4,192,384]{2,1,0:T(8,128)(2,1)S(1)} %constant_dynamic-update-slice_fusion.20), channel_id=1, source_target_pairs={{0,2},{1,3},{2,0},{3,1},{4,6},{5,7},{6,4},{7,5},{8,10},{9,11},{10,... | collective-permute-start | bytes 1769480 | tf_op jit(solution)/shard_map/ppermute | solution.py:52
  97.8 21.6 %collective-permute-start.18 = (bf16[8,192,384]{2,1,0:T(8,128)(2,1)S(1)}, bf16[8,192,384]{2,1,0:T(8,128)(2,1)S(1)}, u32[]{:S(2)}, u32[]{:S(2)}) collective-permute-start(bf16[8,192,384]{2,1,0:T(8,128)(2,1)S(1)} %constant_dynamic-update-slice_fusion.18), channel_id=1, source_target_pairs={{0,1},{1,0},{2,3},{3,2},{4,5},{5,4},{6,7},{7,6},{8,9},{9,8},{10,11... | collective-permute-start | bytes 3538952 | tf_op jit(solution)/shard_map/ppermute | solution.py:52
  98.3 17.9 %collective-permute-start.21 = (bf16[1,192,384]{2,1,0:T(8,128)(2,1)}, bf16[1,192,384]{2,1,0:T(8,128)(2,1)S(1)}, u32[]{:S(2)}, u32[]{:S(2)}) collective-permute-start(bf16[1,192,384]{2,1,0:T(8,128)(2,1)} %constant_dynamic-slice_fusion), channel_id=1, source_target_pairs={{0,4},{1,5},{2,6},{3,7},{4,0},{5,1},{6,2},{7,3},{8,12},{9,13},{10,... | collective-permute-start | bytes 442376 | tf_op jit(solution)/shard_map/ppermute | solution.py:52
  121.8 22.7 %collective-permute-start.25 = (bf16[2,192,384]{2,1,0:T(8,128)(2,1)}, bf16[2,192,384]{2,1,0:T(8,128)(2,1)}, u32[]{:S(2)}, u32[]{:S(2)}) collective-permute-start(bf16[2,192,384]{2,1,0:T(8,128)(2,1)} %constant_dynamic-update-slice_fusion.30), channel_id=1, source_target_pairs={{0,8},{1,9},{2,10},{3,11},{4,12},{5,13},{6,14},{7,15},{8,0},{9,1},... | collective-permute-start | bytes 884744 | tf_op jit(solution)/shard_map/ppermute | solution.py:52
  126.4 18.0 %collective-permute-start.24 = (bf16[4,192,384]{2,1,0:T(8,128)(2,1)S(1)}, bf16[4,192,384]{2,1,0:T(8,128)(2,1)}, u32[]{:S(2)}, u32[]{:S(2)}) collective-permute-start(bf16[4,192,384]{2,1,0:T(8,128)(2,1)S(1)} %constant_dynamic-update-slice_fusion.28), channel_id=1, source_target_pairs={{0,2},{1,3},{2,0},{3,1},{4,6},{5,7},{6,4},{7,5},{8,10},{9,11},{10,... | collective-permute-start | bytes 1769480 | tf_op jit(solution)/shard_map/ppermute | solution.py:52
  128.0 19.9 %collective-permute-start.23 = (bf16[8,192,384]{2,1,0:T(8,128)(2,1)S(1)}, bf16[8,192,384]{2,1,0:T(8,128)(2,1)}, u32[]{:S(2)}, u32[]{:S(2)}) collective-permute-start(bf16[8,192,384]{2,1,0:T(8,128)(2,1)S(1)} %constant_dynamic-update-slice_fusion.26), channel_id=1, source_target_pairs={{0,1},{1,0},{2,3},{3,2},{4,5},{5,4},{6,7},{7,6},{8,9},{9,8},{10,11... | collective-permute-start | bytes 3538952 | tf_op jit(solution)/shard_map/ppermute | solution.py:52
  128.5 19.5 %collective-permute-start.27 = (bf16[4,512,384]{2,1,0:T(8,128)(2,1)}, bf16[4,512,384]{2,1,0:T(8,128)(2,1)}, u32[]{:S(2)}, u32[]{:S(2)}) collective-permute-start(bf16[4,512,384]{2,1,0:T(8,128)(2,1)} %get-tuple-element.280.context_ref.refs_4_.refs_0_), channel_id=1, source_target_pairs={{0,16},{16,0},{1,17},{17,1},{2,18},{18,2},{3,19},{19,3},{4,20},{20... | collective-permute-start | bytes 4718600 | tf_op jit(solution)/shard_map/ppermute | solution.py:55
  130.8 26.5 %collective-permute-start.30 = (bf16[16,192,384]{2,1,0:T(8,128)(2,1)}, bf16[16,192,384]{2,1,0:T(8,128)(2,1)}, u32[]{:S(2)}, u32[]{:S(2)}) collective-permute-start(bf16[16,192,384]{2,1,0:T(8,128)(2,1)} %constant_dynamic-update-slice_fusion.38.refs_0_.refs_1_.refs_2_.refs_3_), channel_id=1, source_target_pairs={{0,16},{16,0},{1,17},{17,1},{2,18},{18,2},{3,19},{19,3},{4,20},{20... | collective-permute-start | bytes 7077896 | tf_op jit(solution)/shard_map/ppermute | solution.py:55
  148.0 47.0 %collective-permute-start.33 = (bf16[10,512,384]{2,1,0:T(8,128)(2,1)}, bf16[10,512,384]{2,1,0:T(8,128)(2,1)}, u32[]{:S(2)}, u32[]{:S(2)}) collective-permute-start(bf16[10,512,384]{2,1,0:T(8,128)(2,1)} %get-tuple-element.290.active_ref.refs_0_), channel_id=1, source_target_pairs={{0,16},{16,0},{1,17},{17,1},{2,18},{18,2},{3,19},{19,3},{4,20},{20... | collective-permute-start | bytes 11796488 | tf_op jit(solution)/shard_map/ppermute | solution.py:55
  152.5 28.4 %collective-permute-start.32 = (bf16[16,192,384]{2,1,0:T(8,128)(2,1)}, bf16[16,192,384]{2,1,0:T(8,128)(2,1)}, u32[]{:S(2)}, u32[]{:S(2)}) collective-permute-start(bf16[16,192,384]{2,1,0:T(8,128)(2,1)} %constant_dynamic-update-slice_fusion.42.refs_0_), channel_id=1, source_target_pairs={{0,16},{16,0},{1,17},{17,1},{2,18},{18,2},{3,19},{19,3},{4,20},{20... | collective-permute-start | bytes 7077896 | tf_op jit(solution)/shard_map/ppermute | solution.py:55
  154.4 22.6 %collective-permute-start.28 = (bf16[8,192,384]{2,1,0:T(8,128)(2,1)S(1)}, bf16[8,192,384]{2,1,0:T(8,128)(2,1)S(1)}, u32[]{:S(2)}, u32[]{:S(2)}) collective-permute-start(bf16[8,192,384]{2,1,0:T(8,128)(2,1)S(1)} %constant_dynamic-update-slice_fusion.34), channel_id=1, source_target_pairs={{0,1},{1,0},{2,3},{3,2},{4,5},{5,4},{6,7},{7,6},{8,9},{9,8},{10,11... | collective-permute-start | bytes 3538952 | tf_op jit(solution)/shard_map/ppermute | solution.py:52
  156.8 16.3 %collective-permute-start.29 = (bf16[4,192,384]{2,1,0:T(8,128)(2,1)S(1)}, bf16[4,192,384]{2,1,0:T(8,128)(2,1)S(1)}, u32[]{:S(2)}, u32[]{:S(2)}) collective-permute-start(bf16[4,192,384]{2,1,0:T(8,128)(2,1)S(1)} %constant_dynamic-update-slice_fusion.36), channel_id=1, source_target_pairs={{0,2},{1,3},{2,0},{3,1},{4,6},{5,7},{6,4},{7,5},{8,10},{9,11},{10,... | collective-permute-start | bytes 1769480 | tf_op jit(solution)/shard_map/ppermute | solution.py:52
  178.2 16.8 %collective-permute-start.31 = (bf16[8,192,384]{2,1,0:T(8,128)(2,1)S(1)}, bf16[8,192,384]{2,1,0:T(8,128)(2,1)}, u32[]{:S(2)}, u32[]{:S(2)}) collective-permute-start(bf16[8,192,384]{2,1,0:T(8,128)(2,1)S(1)} %constant_dynamic-update-slice_fusion.40), channel_id=1, source_target_pairs={{0,1},{1,0},{2,3},{3,2},{4,5},{5,4},{6,7},{7,6},{8,9},{9,8},{10,11... | collective-permute-start | bytes 3538952 | tf_op jit(solution)/shard_map/ppermute | solution.py:52
  180.9 22.6 %collective-permute-start.34 = (bf16[16,192,384]{2,1,0:T(8,128)(2,1)}, bf16[16,192,384]{2,1,0:T(8,128)(2,1)}, u32[]{:S(2)}, u32[]{:S(2)}) collective-permute-start(bf16[16,192,384]{2,1,0:T(8,128)(2,1)} %constant_dynamic-update-slice_fusion.44.refs_0_), channel_id=1, source_target_pairs={{0,16},{16,0},{1,17},{17,1},{2,18},{18,2},{3,19},{19,3},{4,20},{20... | collective-permute-start | bytes 7077896 | tf_op jit(solution)/shard_map/ppermute | solution.py:55
  198.6 14.4 %collective-permute-start.36 = (bf16[16,192,384]{2,1,0:T(8,128)(2,1)}, bf16[16,192,384]{2,1,0:T(8,128)(2,1)S(1)}, u32[]{:S(2)}, u32[]{:S(2)}) collective-permute-start(bf16[16,192,384]{2,1,0:T(8,128)(2,1)} %constant_dynamic-update-slice_fusion.46.refs_0_.refs_1_.refs_2_.refs_3_), channel_id=1, source_target_pairs={{0,16},{16,0},{1,17},{17,1},{2,18},{18,2},{3,19},{19,3},{4,20},{20... | collective-permute-start | bytes 7077896 | tf_op jit(solution)/shard_map/ppermute | solution.py:55
  199.1 13.4 %collective-permute-start.35 = (bf16[4,512,384]{2,1,0:T(8,128)(2,1)}, bf16[4,512,384]{2,1,0:T(8,128)(2,1)}, u32[]{:S(2)}, u32[]{:S(2)}) collective-permute-start(bf16[4,512,384]{2,1,0:T(8,128)(2,1)} %get-tuple-element.301.context_ref.refs_4_.refs_0_), channel_id=1, source_target_pairs={{0,16},{16,0},{1,17},{17,1},{2,18},{18,2},{3,19},{19,3},{4,20},{20... | collective-permute-start | bytes 4718600 | tf_op jit(solution)/shard_map/ppermute | solution.py:55
  212.5 34.0 %collective-permute-start.37 = (bf16[10,512,384]{2,1,0:T(8,128)(2,1)}, bf16[10,512,384]{2,1,0:T(8,128)(2,1)}, u32[]{:S(2)}, u32[]{:S(2)}) collective-permute-start(bf16[10,512,384]{2,1,0:T(8,128)(2,1)} %get-tuple-element.308.active_ref.refs_0_), channel_id=1, source_target_pairs={{0,16},{16,0},{1,17},{17,1},{2,18},{18,2},{3,19},{19,3},{4,20},{20... | collective-permute-start | bytes 11796488 | tf_op jit(solution)/shard_map/ppermute | solution.py:55
  236.4 10.0 %collective-permute-start.38 = (bf16[5,512,384]{2,1,0:T(8,128)(2,1)}, bf16[5,512,384]{2,1,0:T(8,128)(2,1)S(1)}, u32[]{:S(2)}, u32[]{:S(2)}) collective-permute-start(bf16[5,512,384]{2,1,0:T(8,128)(2,1)} %get-tuple-element.320.sent_ref), channel_id=1, source_target_pairs={{0,16},{16,0},{1,17},{17,1},{2,18},{18,2},{3,19},{19,3},{4,20},{20... | collective-permute-start | bytes 5898248 | tf_op jit(solution)/shard_map/ppermute | solution.py:55
  257.5 22.9 %collective-permute-start.40 = (bf16[1,512,384]{2,1,0:T(8,128)(2,1)S(1)}, bf16[1,512,384]{2,1,0:T(8,128)(2,1)S(1)}, u32[]{:S(2)}, u32[]{:S(2)}) collective-permute-start(bf16[1,512,384]{2,1,0:T(8,128)(2,1)S(1)} %copy-done.55), channel_id=1, source_target_pairs={{0,16},{16,0},{1,17},{17,1},{2,18},{18,2},{3,19},{19,3},{4,20},{20... | collective-permute-start | bytes 1179656 | tf_op jit(solution)/shard_map/ppermute | solution.py:55
  258.0 34.2 %collective-permute-start.39 = (bf16[8,192,384]{2,1,0:T(8,128)(2,1)}, bf16[8,192,384]{2,1,0:T(8,128)(2,1)S(1)}, u32[]{:S(2)}, u32[]{:S(2)}) collective-permute-start(bf16[8,192,384]{2,1,0:T(8,128)(2,1)} %get-tuple-element.329), channel_id=1, source_target_pairs={{0,1},{1,0},{2,3},{3,2},{4,5},{5,4},{6,7},{7,6},{8,9},{9,8},{10,11... | collective-permute-start | bytes 3538952 | tf_op jit(solution)/shard_map/ppermute | solution.py:52
  292.2 10.9 %collective-permute-start.43 = (bf16[3,512,384]{2,1,0:T(8,128)(2,1)}, bf16[3,512,384]{2,1,0:T(8,128)(2,1)}, u32[]{:S(2)}, u32[]{:S(2)}) collective-permute-start(bf16[3,512,384]{2,1,0:T(8,128)(2,1)} %get-tuple-element.343.sent_ref), channel_id=1, source_target_pairs={{0,16},{16,0},{1,17},{17,1},{2,18},{18,2},{3,19},{19,3},{4,20},{20... | collective-permute-start | bytes 3538952 | tf_op jit(solution)/shard_map/ppermute | solution.py:55
  295.4 16.3 %collective-permute-start.41 = (bf16[4,192,384]{2,1,0:T(8,128)(2,1)S(1)}, bf16[4,192,384]{2,1,0:T(8,128)(2,1)S(1)}, u32[]{:S(2)}, u32[]{:S(2)}) collective-permute-start(bf16[4,192,384]{2,1,0:T(8,128)(2,1)S(1)} %get-tuple-element.466), channel_id=1, source_target_pairs={{0,2},{1,3},{2,0},{3,1},{4,6},{5,7},{6,4},{7,5},{8,10},{9,11},{10,... | collective-permute-start | bytes 1769480 | tf_op jit(solution)/shard_map/ppermute | solution.py:52
  295.8 24.0 %collective-permute-start.42 = (bf16[8,240,384]{2,1,0:T(8,128)(2,1)}, bf16[8,240,384]{2,1,0:T(8,128)(2,1)}, u32[]{:S(2)}, u32[]{:S(2)}) collective-permute-start(bf16[8,240,384]{2,1,0:T(8,128)(2,1)} %get-tuple-element.341), channel_id=1, source_target_pairs={{0,1},{1,0},{2,3},{3,2},{4,5},{5,4},{6,7},{7,6},{8,9},{9,8},{10,11... | collective-permute-start | bytes 4423688 | tf_op jit(solution)/shard_map/ppermute | solution.py:52
  322.4 18.5 %collective-permute-start.45 = (bf16[4,240,384]{2,1,0:T(8,128)(2,1)}, bf16[4,240,384]{2,1,0:T(8,128)(2,1)S(1)}, u32[]{:S(2)}, u32[]{:S(2)}) collective-permute-start(bf16[4,240,384]{2,1,0:T(8,128)(2,1)} %get-tuple-element.462), channel_id=1, source_target_pairs={{0,2},{1,3},{2,0},{3,1},{4,6},{5,7},{6,4},{7,5},{8,10},{9,11},{10,... | collective-permute-start | bytes 2211848 | tf_op jit(solution)/shard_map/ppermute | solution.py:52
  323.8 17.1 %collective-permute-start.44 = (bf16[2,192,384]{2,1,0:T(8,128)(2,1)}, bf16[2,192,384]{2,1,0:T(8,128)(2,1)S(1)}, u32[]{:S(2)}, u32[]{:S(2)}) collective-permute-start(bf16[2,192,384]{2,1,0:T(8,128)(2,1)} %get-tuple-element.478), channel_id=1, source_target_pairs={{0,8},{1,9},{2,10},{3,11},{4,12},{5,13},{6,14},{7,15},{8,0},{9,1},... | collective-permute-start | bytes 884744 | tf_op jit(solution)/shard_map/ppermute | solution.py:52
  324.1 19.0 %collective-permute-start.46 = (bf16[8,144,384]{2,1,0:T(8,128)(2,1)}, bf16[8,144,384]{2,1,0:T(8,128)(2,1)}, u32[]{:S(2)}, u32[]{:S(2)}) collective-permute-start(bf16[8,144,384]{2,1,0:T(8,128)(2,1)} %get-tuple-element.352), channel_id=1, source_target_pairs={{0,1},{1,0},{2,3},{3,2},{4,5},{5,4},{6,7},{7,6},{8,9},{9,8},{10,11... | collective-permute-start | bytes 2654216 | tf_op jit(solution)/shard_map/ppermute | solution.py:52
  343.1 19.4 %collective-permute-start.50 = (bf16[5,512,384]{2,1,0:T(8,128)(2,1)}, bf16[5,512,384]{2,1,0:T(8,128)(2,1)}, u32[]{:S(2)}, u32[]{:S(2)}) collective-permute-start(bf16[5,512,384]{2,1,0:T(8,128)(2,1)} %get-tuple-element.368.sent_ref), channel_id=1, source_target_pairs={{0,16},{16,0},{1,17},{17,1},{2,18},{18,2},{3,19},{19,3},{4,20},{20... | collective-permute-start | bytes 5898248 | tf_op jit(solution)/shard_map/ppermute | solution.py:55
  347.2 25.3 %collective-permute-start.49 = (bf16[4,144,384]{2,1,0:T(8,128)(2,1)}, bf16[4,144,384]{2,1,0:T(8,128)(2,1)S(1)}, u32[]{:S(2)}, u32[]{:S(2)}) collective-permute-start(bf16[4,144,384]{2,1,0:T(8,128)(2,1)} %get-tuple-element.470), channel_id=1, source_target_pairs={{0,2},{1,3},{2,0},{3,1},{4,6},{5,7},{6,4},{7,5},{8,10},{9,11},{10,... | collective-permute-start | bytes 1327112 | tf_op jit(solution)/shard_map/ppermute | solution.py:52
  349.0 23.5 %collective-permute-start.48 = (bf16[2,240,384]{2,1,0:T(8,128)(2,1)}, bf16[2,240,384]{2,1,0:T(8,128)(2,1)S(1)}, u32[]{:S(2)}, u32[]{:S(2)}) collective-permute-start(bf16[2,240,384]{2,1,0:T(8,128)(2,1)} %get-tuple-element.474), channel_id=1, source_target_pairs={{0,8},{1,9},{2,10},{3,11},{4,12},{5,13},{6,14},{7,15},{8,0},{9,1},... | collective-permute-start | bytes 1105928 | tf_op jit(solution)/shard_map/ppermute | solution.py:52
  349.3 23.2 %collective-permute-start.47 = (bf16[1,192,384]{2,1,0:T(8,128)(2,1)S(1)}, bf16[1,192,384]{2,1,0:T(8,128)(2,1)S(1)}, u32[]{:S(2)}, u32[]{:S(2)}) collective-permute-start(bf16[1,192,384]{2,1,0:T(8,128)(2,1)S(1)} %get-tuple-element.504), channel_id=1, source_target_pairs={{0,4},{1,5},{2,6},{3,7},{4,0},{5,1},{6,2},{7,3},{8,12},{9,13},{10,... | collective-permute-start | bytes 442376 | tf_op jit(solution)/shard_map/ppermute | solution.py:52
  372.5 26.4 %collective-permute-start.54 = (bf16[1,512,384]{2,1,0:T(8,128)(2,1)S(1)}, bf16[1,512,384]{2,1,0:T(8,128)(2,1)}, u32[]{:S(2)}, u32[]{:S(2)}) collective-permute-start(bf16[1,512,384]{2,1,0:T(8,128)(2,1)S(1)} %copy-done.54), channel_id=1, source_target_pairs={{0,16},{16,0},{1,17},{17,1},{2,18},{18,2},{3,19},{19,3},{4,20},{20... | collective-permute-start | bytes 1179656 | tf_op jit(solution)/shard_map/ppermute | solution.py:55
  372.6 37.5 %collective-permute-start.53 = (bf16[8,192,384]{2,1,0:T(8,128)(2,1)}, bf16[8,192,384]{2,1,0:T(8,128)(2,1)}, u32[]{:S(2)}, u32[]{:S(2)}) collective-permute-start(bf16[8,192,384]{2,1,0:T(8,128)(2,1)} %get-tuple-element.381), channel_id=1, source_target_pairs={{0,1},{1,0},{2,3},{3,2},{4,5},{5,4},{6,7},{7,6},{8,9},{9,8},{10,11... | collective-permute-start | bytes 3538952 | tf_op jit(solution)/shard_map/ppermute | solution.py:52
  373.7 36.4 %collective-permute-start.52 = (bf16[2,144,384]{2,1,0:T(8,128)(2,1)S(1)}, bf16[2,144,384]{2,1,0:T(8,128)(2,1)S(1)}, u32[]{:S(2)}, u32[]{:S(2)}) collective-permute-start(bf16[2,144,384]{2,1,0:T(8,128)(2,1)S(1)} %get-tuple-element.490), channel_id=1, source_target_pairs={{0,8},{1,9},{2,10},{3,11},{4,12},{5,13},{6,14},{7,15},{8,0},{9,1},... | collective-permute-start | bytes 663560 | tf_op jit(solution)/shard_map/ppermute | solution.py:52
  374.8 35.2 %collective-permute-start.51 = (bf16[1,240,384]{2,1,0:T(8,128)(2,1)S(1)}, bf16[1,240,384]{2,1,0:T(8,128)(2,1)S(1)}, u32[]{:S(2)}, u32[]{:S(2)}) collective-permute-start(bf16[1,240,384]{2,1,0:T(8,128)(2,1)S(1)} %get-tuple-element.500), channel_id=1, source_target_pairs={{0,4},{1,5},{2,6},{3,7},{4,0},{5,1},{6,2},{7,3},{8,12},{9,13},{10,... | collective-permute-start | bytes 552968 | tf_op jit(solution)/shard_map/ppermute | solution.py:52
  398.1 12.5 %collective-permute-start.59 = (f32[16,2,576]{2,1,0:T(2,128)S(1)}, f32[16,2,576]{2,1,0:T(2,128)S(1)}, u32[]{:S(2)}, u32[]{:S(2)}) collective-permute-start(f32[16,2,576]{2,1,0:T(2,128)S(1)} %pad_maximum_fusion.5), channel_id=1, source_target_pairs={{0,16},{16,0},{1,17},{17,1},{2,18},{18,2},{3,19},{19,3},{4,20},{20... | collective-permute-start | bytes 221192 | tf_op jit(solution)/shard_map/ppermute | solution.py:55
  411.5 26.1 %collective-permute-start.57 = (bf16[8,240,384]{2,1,0:T(8,128)(2,1)}, bf16[8,240,384]{2,1,0:T(8,128)(2,1)}, u32[]{:S(2)}, u32[]{:S(2)}) collective-permute-start(bf16[8,240,384]{2,1,0:T(8,128)(2,1)} %get-tuple-element.395), channel_id=1, source_target_pairs={{0,1},{1,0},{2,3},{3,2},{4,5},{5,4},{6,7},{7,6},{8,9},{9,8},{10,11... | collective-permute-start | bytes 4423688 | tf_op jit(solution)/shard_map/ppermute | solution.py:52
  412.8 38.8 %collective-permute-start.63 = (f32[8,2,576]{2,1,0:T(2,128)}, f32[8,2,576]{2,1,0:T(2,128)}, u32[]{:S(2)}, u32[]{:S(2)}) collective-permute-start(f32[8,2,576]{2,1,0:T(2,128)} %get-tuple-element.542), channel_id=1, source_target_pairs={{0,1},{1,0},{2,3},{3,2},{4,5},{5,4},{6,7},{7,6},{8,9},{9,8},{10,11... | collective-permute-start | bytes 110600 | tf_op jit(solution)/shard_map/ppermute | solution.py:52
  416.6 16.5 %collective-permute-start.56 = (bf16[4,192,384]{2,1,0:T(8,128)(2,1)}, bf16[4,192,384]{2,1,0:T(8,128)(2,1)S(1)}, u32[]{:S(2)}, u32[]{:S(2)}) collective-permute-start(bf16[4,192,384]{2,1,0:T(8,128)(2,1)} %get-tuple-element.464), channel_id=1, source_target_pairs={{0,2},{1,3},{2,0},{3,1},{4,6},{5,7},{6,4},{7,5},{8,10},{9,11},{10,... | collective-permute-start | bytes 1769480 | tf_op jit(solution)/shard_map/ppermute | solution.py:52
  440.3 19.1 %collective-permute-start.61 = (bf16[4,240,384]{2,1,0:T(8,128)(2,1)}, bf16[4,240,384]{2,1,0:T(8,128)(2,1)}, u32[]{:S(2)}, u32[]{:S(2)}) collective-permute-start(bf16[4,240,384]{2,1,0:T(8,128)(2,1)} %get-tuple-element.460), channel_id=1, source_target_pairs={{0,2},{1,3},{2,0},{3,1},{4,6},{5,7},{6,4},{7,5},{8,10},{9,11},{10,... | collective-permute-start | bytes 2211848 | tf_op jit(solution)/shard_map/ppermute | solution.py:52
  441.8 15.3 %collective-permute-start.60 = (bf16[2,192,384]{2,1,0:T(8,128)(2,1)}, bf16[2,192,384]{2,1,0:T(8,128)(2,1)}, u32[]{:S(2)}, u32[]{:S(2)}) collective-permute-start(bf16[2,192,384]{2,1,0:T(8,128)(2,1)} %get-tuple-element.476), channel_id=1, source_target_pairs={{0,8},{1,9},{2,10},{3,11},{4,12},{5,13},{6,14},{7,15},{8,0},{9,1},... | collective-permute-start | bytes 884744 | tf_op jit(solution)/shard_map/ppermute | solution.py:52
  443.2 16.5 %collective-permute-start.62 = (bf16[8,144,384]{2,1,0:T(8,128)(2,1)}, bf16[8,144,384]{2,1,0:T(8,128)(2,1)S(1)}, u32[]{:S(2)}, u32[]{:S(2)}) collective-permute-start(bf16[8,144,384]{2,1,0:T(8,128)(2,1)} %get-tuple-element.413), channel_id=1, source_target_pairs={{0,1},{1,0},{2,3},{3,2},{4,5},{5,4},{6,7},{7,6},{8,9},{9,8},{10,11... | collective-permute-start | bytes 2654216 | tf_op jit(solution)/shard_map/ppermute | solution.py:52
  459.9 24.4 %collective-permute-start.66 = (bf16[4,144,384]{2,1,0:T(8,128)(2,1)S(1)}, bf16[4,144,384]{2,1,0:T(8,128)(2,1)S(1)}, u32[]{:S(2)}, u32[]{:S(2)}) collective-permute-start(bf16[4,144,384]{2,1,0:T(8,128)(2,1)S(1)} %get-tuple-element.468), channel_id=1, source_target_pairs={{0,2},{1,3},{2,0},{3,1},{4,6},{5,7},{6,4},{7,5},{8,10},{9,11},{10,... | collective-permute-start | bytes 1327112 | tf_op jit(solution)/shard_map/ppermute | solution.py:52
  464.1 20.2 %collective-permute-start.65 = (bf16[2,240,384]{2,1,0:T(8,128)(2,1)S(1)}, bf16[2,240,384]{2,1,0:T(8,128)(2,1)S(1)}, u32[]{:S(2)}, u32[]{:S(2)}) collective-permute-start(bf16[2,240,384]{2,1,0:T(8,128)(2,1)S(1)} %get-tuple-element.472), channel_id=1, source_target_pairs={{0,8},{1,9},{2,10},{3,11},{4,12},{5,13},{6,14},{7,15},{8,0},{9,1},... | collective-permute-start | bytes 1105928 | tf_op jit(solution)/shard_map/ppermute | solution.py:52
  466.2 11.0 %collective-permute-start.64 = (bf16[1,192,384]{2,1,0:T(8,128)(2,1)S(1)}, bf16[1,192,384]{2,1,0:T(8,128)(2,1)S(1)}, u32[]{:S(2)}, u32[]{:S(2)}) collective-permute-start(bf16[1,192,384]{2,1,0:T(8,128)(2,1)S(1)} %get-tuple-element.502), channel_id=1, source_target_pairs={{0,4},{1,5},{2,6},{3,7},{4,0},{5,1},{6,2},{7,3},{8,12},{9,13},{10,... | collective-permute-start | bytes 442376 | tf_op jit(solution)/shard_map/ppermute | solution.py:52
  484.4 14.2 %collective-permute-start.69 = (bf16[2,144,384]{2,1,0:T(8,128)(2,1)S(1)}, bf16[2,144,384]{2,1,0:T(8,128)(2,1)S(1)}, u32[]{:S(2)}, u32[]{:S(2)}) collective-permute-start(bf16[2,144,384]{2,1,0:T(8,128)(2,1)S(1)} %get-tuple-element.488), channel_id=1, source_target_pairs={{0,8},{1,9},{2,10},{3,11},{4,12},{5,13},{6,14},{7,15},{8,0},{9,1},... | collective-permute-start | bytes 663560 | tf_op jit(solution)/shard_map/ppermute | solution.py:52
  484.5 13.0 %collective-permute-start.70 = (f32[2,2,576]{2,1,0:T(2,128)S(1)}, f32[2,2,576]{2,1,0:T(2,128)S(1)}, u32[]{:S(2)}, u32[]{:S(2)}) collective-permute-start(f32[2,2,576]{2,1,0:T(2,128)S(1)} %get-tuple-element.544), channel_id=1, source_target_pairs={{0,8},{1,9},{2,10},{3,11},{4,12},{5,13},{6,14},{7,15},{8,0},{9,1},... | collective-permute-start | bytes 27656 | tf_op jit(solution)/shard_map/ppermute | solution.py:52
  487.6 11.0 %collective-permute-start.68 = (bf16[1,240,384]{2,1,0:T(8,128)(2,1)S(1)}, bf16[1,240,384]{2,1,0:T(8,128)(2,1)S(1)}, u32[]{:S(2)}, u32[]{:S(2)}) collective-permute-start(bf16[1,240,384]{2,1,0:T(8,128)(2,1)S(1)} %get-tuple-element.498), channel_id=1, source_target_pairs={{0,4},{1,5},{2,6},{3,7},{4,0},{5,1},{6,2},{7,3},{8,12},{9,13},{10,... | collective-permute-start | bytes 552968 | tf_op jit(solution)/shard_map/ppermute | solution.py:52
  (68 other events, 555.2 us)

commit v5 on v4

--- a/solution.py
+++ b/solution.py
@@ -29,7 +29,7 @@
         self.replicas = mesh.shape["rep"]
         assert self.replicas % 2 == 0 and self.shards & (self.shards - 1) == 0 and self.shards >= 16
         bits = [1 << place for place in reversed(range(self.shards.bit_length() - 3))]
-        first = [(4, self.shards // 4)] if wide else [(2, self.shards // 4), (2, self.shards // 2)]
+        first = [(4, self.shards // 4)] if wide else [(2, self.shards // 2), (2, self.shards // 4)]
         self.sizes = [size for size, _ in first] + [2] * len(bits)
         first = [step for _, step in first]
         self.steps = [[*first, *bits], [*first, *bits[:-2], bits[-1], bits[-2]]]
@@ -51,6 +51,14 @@
         ]
         return lax.ppermute(value, ("rep", "fsdp"), pairs)
 
+    def across_twin(self, value, stage):
+        pairs = [
+            (rep * self.shards + shard, (rep ^ 1) * self.shards + (shard ^ self.steps[rep % 2][stage]))
+            for rep in range(self.replicas)
+            for shard in range(self.shards)
+        ]
+        return lax.ppermute(value, ("rep", "fsdp"), pairs)
+
     def twin(self, value):
         return lax.ppermute(value, "rep", [(rep, rep ^ 1) for rep in range(self.replicas)])
 
@@ -162,8 +170,14 @@
             yield 4 * group + slot, slice(first, first + length * LEN_UNIT)
 
 
-def one_head(values, low_lanes, head):
-    return jnp.where(low_lanes == (head == 0), values, jnp.zeros_like(values))
+def two_heads(values, low_lanes):
+    nothing = jnp.zeros_like(values)
+    return jnp.concatenate([jnp.where(low_lanes, values, nothing), jnp.where(low_lanes, nothing, values)], 0)
+
+
+def one_row(values, low_lanes):
+    half = values.shape[0] // 2
+    return jnp.where(low_lanes, values[:half], values[half:])
 
 
 def probabilities(queries, key_rows, limit):
@@ -226,11 +240,9 @@
                         key_rows = qkv_ref[side, 1, rows, lanes]
                         value_rows = qkv_ref[side, 2, rows, lanes]
                         low_lanes = lax.broadcasted_iota(jnp.int32, queries.shape, 1) < HD
-                        heads = []
-                        for head in range(2):
-                            probs = probabilities(one_head(queries, low_lanes, head), key_rows, limits_ref[slot])
-                            heads.append(dot(probs.astype(LOW), value_rows, 0, 0))
-                        left_ref[2 + (core ^ side), rows, lanes] = jnp.where(low_lanes, *heads).astype(LOW)
+                        probs = probabilities(two_heads(queries, low_lanes), key_rows, limits_ref[slot])
+                        context = dot(probs.astype(LOW), value_rows, 0, 0)
+                        left_ref[2 + (core ^ side), rows, lanes] = one_row(context, low_lanes).astype(LOW)
 
     return pl.pallas_call(
         body,
@@ -530,17 +542,14 @@
                     value_rows = qkv_ref[side, 2, rows, lanes]
                     d_rows = d_context_ref[side, rows, lanes]
                     low_lanes = lax.broadcasted_iota(jnp.int32, queries.shape, 1) < HD
-                    grads = []
-                    for head in range(2):
-                        probs = probabilities(one_head(queries, low_lanes, head), key_rows, limits_ref[slot])
-                        d_value = dot(probs.astype(LOW), d_rows)
-                        d_probs = dot(value_rows, one_head(d_rows, low_lanes, head), 1, 1)
-                        scaled = probs * d_probs
-                        d_scores = scaled - probs * jnp.sum(scaled, 0, keepdims=True)
-                        d_low = d_scores.astype(LOW)
-                        grads.append((dot(d_low, key_rows, 0, 0) * SCORE_SCALE, dot(d_low, queries) * SCORE_SCALE, d_value))
-                    for third, (low_head, high_head) in enumerate(zip(*grads)):
-                        out_ref[third, rows, lanes] = jnp.where(low_lanes, low_head, high_head).astype(LOW)
+                    queries, d_rows = two_heads(queries, low_lanes), two_heads(d_rows, low_lanes)
+                    probs = probabilities(queries, key_rows, limits_ref[slot])
+                    out_ref[2, rows, lanes] = dot(probs.astype(LOW), d_rows).astype(LOW)
+                    scaled = probs * dot(value_rows, d_rows, 1, 1)
+                    d_scores = (scaled - probs * jnp.sum(scaled, 0, keepdims=True)).astype(LOW)
+                    d_queries = one_row(dot(d_scores, key_rows, 0, 0), low_lanes)
+                    out_ref[0, rows, lanes] = (d_queries * SCORE_SCALE).astype(LOW)
+                    out_ref[1, rows, lanes] = (dot(d_scores, queries) * SCORE_SCALE).astype(LOW)
         for place, third in enumerate((0, 2)):
             for side, out_ref in enumerate((own_ref, away_ref)):
                 sums_ref[place, core ^ side] = jnp.sum(out_ref[third].astype(FULL), 0, keepdims=True)
@@ -592,51 +601,62 @@
 
 
 def weight_terms(slots, shards, *jobs):
-    steps = jobs[0][3]
-    rows = steps * CHUNK // shards
-    per_tile = CHUNK // rows
+    chunks = jobs[0][3]
+    rows = chunks * CHUNK // shards
     parts = [job[4].shape[0] for job in jobs]
     half = shards // 2
     tokens = jobs[0][4].shape[1]
+    tall = chunks > 2
+
+    def stacked(refs, chunk):
+        return jnp.concatenate([ref[chunk] for ref in refs], 0)
 
     def body(slots_ref, *refs):
         kept_ref, sent_ref = refs[4 * len(jobs) :]
-        step = pl.program_id(0)
-        slots_here = [slots_ref[0, step * per_tile + block] for block in range(per_tile)]
-        place = 0
+
+        def put(block, here, value):
+            slot = slots_ref[0, block]
+
+            @pl.when(slot < half)
+            def _():
+                kept_ref[slot, here] = value
+
+            @pl.when(slot >= half)
+            def _():
+                sent_ref[slot - half, here] = value
+
+        start = 0
         for job, count in enumerate(parts):
-            left_ref, left_twin_ref, right_ref, right_twin_ref = refs[4 * job : 4 * job + 4]
-            here, there = left_ref[0], left_twin_ref[0]
-            for part in range(count):
-                total = dot(here, right_ref[part], 0, 0) + dot(there, right_twin_ref[part], 0, 0)
-                total = total.astype(LOW)
-                for block, slot in enumerate(slots_here):
-
-                    @pl.when(slot < half)
-                    def _():
-                        kept_ref[slot, place : place + rows] = total[block * rows : (block + 1) * rows]
-
-                    @pl.when(slot >= half)
-                    def _():
-                        sent_ref[slot - half, place : place + rows] = total[block * rows : (block + 1) * rows]
-
-                place += rows
+            left_refs, right_refs = refs[4 * job : 4 * job + 2], refs[4 * job + 2 : 4 * job + 4]
+            left = jnp.concatenate([stacked(left_refs, 0), stacked(left_refs, 1)], 1)
+            right = jnp.concatenate([stacked(right_refs, part) for part in range(count)], 1)
+            if tall:
+                total = dot(right.T, left).astype(LOW).T
+            else:
+                total = dot(left.T, right).astype(LOW)
+            blocks = 2 * CHUNK // rows
+            for block in range(blocks):
+                for part in range(count):
+                    here = slice(start + part * rows, start + (part + 1) * rows)
+                    value = total[block * rows : (block + 1) * rows, part * CHUNK : (part + 1) * CHUNK]
+                    put(pl.program_id(0) * blocks + block, here, value)
+            start += count * rows
 
     specs, values = [SMALL], [slots]
     for (left, left_twin, first, _, right, right_twin, twin_first), count in zip(jobs, parts):
-        specs += [pl.BlockSpec((1, tokens, CHUNK), lambda i, first=first: (first + i, 0, 0))] * 2
+        specs += [pl.BlockSpec((2, tokens, CHUNK), lambda i, first=first // 2: (first + i, 0, 0))] * 2
         specs += [whole(count, tokens, CHUNK)]
-        assert twin_first % count == 0
+        assert twin_first % count == 0 and first % 2 == 0
         specs += [pl.BlockSpec((count, tokens, CHUNK), lambda i, at=twin_first // count: (at, 0, 0))]
         values += [left, left_twin, right, right_twin]
     return pl.pallas_call(
         body,
-        grid=(steps,),
+        grid=(chunks // 2,),
         out_shape=[shaped(half, sum(parts) * rows, CHUNK)] * 2,
         in_specs=specs,
         out_specs=[whole(half, sum(parts) * rows, CHUNK)] * 2,
         name="weight_terms",
-        cost_estimate=cost(2.4 * steps * sum(parts) / 2 if steps == 2 else 9.8),
+        cost_estimate=cost(1.5 * sum(parts) if chunks == 2 else 6),
     )(*values)
 
 
@@ -649,27 +669,37 @@
         self.state = [block[None] for block in blocks]
         self.twins = [None] * len(blocks)
         self.turns = 0
-
-    def turn(self, values=()):
+        self.received = None
+
+    def begin(self):
         stages, groups, turn = self.net.stages, len(self.state), self.turns
-        busy = [group for group in range(groups) if 0 <= turn - group < stages]
-        received = [self.net.gather(self.state[group], turn - group) for group in busy]
+        self.received = {
+            group: self.net.gather(self.state[group], turn - group)
+            for group in range(groups)
+            if 0 <= turn - group < stages
+        }
         if 0 <= turn - stages < groups:
             self.twins[turn - stages] = self.net.twin(self.state[turn - stages])
+
+    def end(self, values=()):
+        if self.received is None:
+            self.begin()
+        coming = [group for group in range(len(self.state)) if self.turns - group < self.net.stages]
+        own = [self.state[group] for group in coming]
+        own, received, values = lax.optimization_barrier((own, self.received, list(values)))
+        for group, value in zip(coming, own):
+            self.state[group] = value
+        for group, others in received.items():
+            self.state[group] = jnp.concatenate([self.state[group], *others], 0)
         self.turns += 1
-        own = [self.state[group] for group in range(groups) if turn - group < stages]
-        if not own and not values:
-            return []
-        own, received, values = lax.optimization_barrier((own, received, list(values)))
-        for group, value in zip((group for group in range(groups) if turn - group < stages), own):
-            self.state[group] = value
-        for group, others in zip(busy, received):
-            self.state[group] = jnp.concatenate([self.state[group], *others], 0)
+        self.received = None
         return values
 
     def ready(self, group):
         while self.twins[group] is None:
-            self.turn()
+            if self.received is not None:
+                self.end()
+            self.begin()
         return self.state[group], self.twins[group]
 
 
@@ -737,7 +767,7 @@
     vector_blocks = vectors[None]
     for stage in range(net.stages):
         vector_blocks = net.widen(vector_blocks, stage)
-        (vector_blocks,) = gather.turn((vector_blocks,))
+        (vector_blocks,) = gather.end((vector_blocks,))
     vector_all = jnp.take(vector_blocks, slots[0], axis=0).transpose(1, 0, 2).reshape(LAYERS, -1, width)
 
     hidden, h_low = tokens, tokens
@@ -747,18 +777,18 @@
         last = level == LAYERS - 1
         qkv, left_a = project(tables, h_low, rows, *weight(level, 0))
         if level:
-            left_a, twins[1] = gather.turn((left_a, twins[1]))
+            left_a, twins[1] = gather.end((left_a, twins[1]))
         else:
-            (left_a,) = gather.turn((left_a,))
+            (left_a,) = gather.end((left_a,))
         twins.append(net.twin(left_a))
         first_sum, first_low = mix(tables, left_a, hidden, rows, *weight(level, 1))
         left_b, slope = expand(tables, first_low, rows, *weight(level, 2), parts)
-        left_b, twins[2 * level], slope = gather.turn((left_b, twins[2 * level], slope))
+        left_b, twins[2 * level], slope = gather.end((left_b, twins[2 * level], slope))
         twins.append(net.twin(left_b))
         second_sum, hidden, h_low = contract(
             tables, left_b, first_sum, rows, *weight(level, 3), inner_width, last
         )
-        (h_low,) = gather.turn((h_low,))
+        (h_low,) = gather.end((h_low,))
         kept.append((qkv, left_a, first_sum, left_b, slope, second_sum))
     layer_out = h_low
 

time: 517 us -> 482 us (0.932)
  Pallas kernels: 230 us -> 200 us
  local copies, waits for them, and re-layouts: 48.5 us -> 41.2 us
    pallas_call x2, Pallas kernels: 41.3 us -> 28.1 us  [attend_back(): pl.pallas_call(body, grid=(1,), out_shape=[shaped(3, tokens, CHUNK), shap...]
    ppermute x56, waiting for transfers between devices: 132 us -> 121 us  [trade(): return lax.ppermute(value, ('rep', 'fsdp'), pairs)]
    ppermute x19, waiting for transfers between devices: 0.36 us -> 9.79 us  [twin(): lax.ppermute(value, 'rep', [(rep, rep ^ 1) for rep in range(self.replicas)])]
    pallas_call x6, Pallas kernels: 56.3 us -> 47.6 us  [weight_terms(): pl.pallas_call(body, grid=(chunks // 2,), out_shape=[shaped(half, sum(par...]
    pallas_call x2, Pallas kernels: 28.5 us -> 21.5 us  [project(): pl.pallas_call(body, grid=(3,), out_shape=[shaped(2, 3, tokens, CHUNK), s...]
    unnamed x166 -> x142, local copies, waits for them, and re-layouts: 22.1 us -> 20.4 us
  transfers between devices with their start and end apart: 75 -> 75, of which waited for: 28 -> 31; matrix products, arithmetic and copies ran while one was open for 12% -> 9% of each run, Pallas kernels for 43% -> 41%
where the time goes in v5:
time: 482 us; the launch traced here: 475 us
  Pallas kernels  200 us (41%)
  waiting for transfers between devices  130 us (27%)
  starting transfers between devices  71.7 us (15%)
  local copies, waits for them, and re-layouts  41.2 us (9%)
  other arithmetic  29 us (6%)
    ppermute x56, waiting for transfers between devices, trade(): return lax.ppermute(value, ('rep', 'fsdp'), pairs)  121 us
    ppermute x56, starting transfers between devices, trade(): return lax.ppermute(value, ('rep', 'fsdp'), pairs)  66.2 us
    pallas_call x6, Pallas kernels, weight_terms(): pl.pallas_call(body, grid=(chunks // 2,), out_shape=[shaped(half, sum(par...  47.6 us
    pallas_call x2, Pallas kernels, attend_back(): pl.pallas_call(body, grid=(1,), out_shape=[shaped(3, tokens, CHUNK), shap...  28.1 us
    pallas_call x2, Pallas kernels, contract_back(): pl.pallas_call(body, grid_spec=pltpu.PrefetchScalarGridSpec(num_scalar_pr...  22 us
    pallas_call x2, Pallas kernels, project(): pl.pallas_call(body, grid=(3,), out_shape=[shaped(2, 3, tokens, CHUNK), s...  21.5 us
    pallas_call x2, Pallas kernels, contract(): pl.pallas_call(body, grid_spec=pltpu.PrefetchScalarGridSpec(num_scalar_pr...  21.4 us
    unnamed x142, local copies, waits for them, and re-layouts  20.4 us
  transfers between devices with their start and end apart: 75, of which 31 were waited for; matrix products, arithmetic and copies ran while one was open for 9% of the time, Pallas kernels for 41%

profile of v5, /device:TPU:0, one launch (start us, length us, event | category | flops | bytes accessed | tf_op | source)
XLA Modules:
  0.0 474.6 jit_solution(7486517803938969863)
XLA Ops:
  2.1 4.1 collective-permute-start
  9.3 2.6 collective-permute-done.1
  12.7 3.4 collective-permute-start.3
  16.1 6.5 %collective-permute-done.4 = f32[2,2,576]{2,1,0:T(2,128)S(1)} collective-permute-done((f32[2,2,576]{2,1,0:T(2,128)S(1)}, f32[2,2,576]{2,1,0:T(2,128)S(1)}, u32[]{:S(2)}, u32[]{:S(2)}) %collective-permute-start.4) | collective-permute-done | bytes 9248 | tf_op jit(solution)/shard_map/ppermute | solution.py:52
  24.2 3.3 collective-permute-start.6
  27.5 1.9 collective-permute-start.7
  29.9 3.3 collective-permute-done.8
  33.2 4.6 collective-permute-done.7
  39.3 1.6 collective-permute-start.10
  41.0 1.9 collective-permute-start.11
  45.9 14.1 %collective-permute-done.13 = f32[8,2,576]{2,1,0:T(2,128)S(1)} collective-permute-done((f32[8,2,576]{2,1,0:T(2,128)S(1)}, f32[8,2,576]{2,1,0:T(2,128)S(1)}, u32[]{:S(2)}, u32[]{:S(2)}) %collective-permute-start.13) | collective-permute-done | bytes 36896 | tf_op jit(solution)/shard_map/ppermute | solution.py:52
  72.5 10.6 %project.2 = (bf16[2,3,512,384]{3,2,1,0:T(8,128)(2,1)}, bf16[4,512,384]{2,1,0:T(8,128)(2,1)}) custom-call(s32[2,16]{1,0:T(2,128)} %copy-done.36, s32[1]{0:T(128)} %bitcast.core_ref, s32[4]{0:T(128)} %limits_ref.15, bf16[512,768]{1,0:T(8,128)(2,1)} %hidden_ref.1, f32[12,768]{1,0:T(8,128)} %squeeze.23.rows_ref, ...), custom_call_target="tpu_custom_call" | custom-call | flops 16675000320 | bytes 14500000 | tf_op jit(solution)/shard_map/project/pallas_call | solution.py:247
  84.7 9.2 %collective-permute-done.14 = bf16[8,240,384]{2,1,0:T(8,128)(2,1)S(1)} collective-permute-done((bf16[8,240,384]{2,1,0:T(8,128)(2,1)S(1)}, bf16[8,240,384]{2,1,0:T(8,128)(2,1)S(1)}, u32[]{:S(2)}, u32[]{:S(2)}) %collective-permute-start.14) | collective-permute-done | bytes 1474592 | tf_op jit(solution)/shard_map/ppermute | solution.py:52
  95.0 1.8 constant_dynamic-update-slice_fusion.25
  103.8 1.7 copy-done.39
  105.5 2.3 collective-permute-start.22
  107.9 4.2 mix.2
  112.0 9.0 %expand.2 = (bf16[10,512,384]{2,1,0:T(8,128)(2,1)}, bf16[8,512,384]{2,1,0:T(8,128)(2,1)}) custom-call(s32[2,16]{1,0:T(2,128)} %copy-done.36, s32[1]{0:T(128)} %bitcast.core_ref, bf16[512,768]{1,0:T(8,128)(2,1)} %get-tuple-element.277.x_ref, f32[12,768]{1,0:T(8,128)} %squeeze.23.rows_ref, bf16[16,240,384]{2,1,0:T(8,128)(2,1)} %copy-done.8, ...), custom_call_target="tpu_custom_call" | custom-call | flops 10350000128 | bytes 9000000 | tf_op jit(solution)/shard_map/expand/pallas_call | solution.py:311
  131.7 10.7 %contract.2 = (f32[512,768]{1,0:T(8,128)}, f32[512,768]{1,0:T(8,128)}, bf16[512,768]{1,0:T(8,128)(2,1)}) custom-call(s32[2,16]{1,0:T(2,128)} %copy-done.36, s32[1]{0:T(128)} %bitcast.core_ref, s32[4]{0:T(128)} %limits_ref.15, bf16[10,512,384]{2,1,0:T(8,128)(2,1)} %get-tuple-element.286.active_ref.refs_0_, f32[512,768]{1,0:T(8,128)} %get-tuple-element.287.first_ref.sum_ref, ...), custom_call_target="tpu_custom_call" | custom-call | flops 12419999744 | bytes 10800000 | tf_op jit(solution)/shard_map/contract/pallas_call | solution.py:371
  142.4 3.9 collective-permute-done.26
  146.3 3.8 collective-permute-done.25
  155.2 2.1 collective-permute-done.31.refs_1_
  157.3 10.9 %project.3 = (bf16[2,3,512,384]{3,2,1,0:T(8,128)(2,1)}, bf16[4,512,384]{2,1,0:T(8,128)(2,1)}) custom-call(s32[2,16]{1,0:T(2,128)} %copy-done.36, s32[1]{0:T(128)} %bitcast.core_ref, s32[4]{0:T(128)} %limits_ref.15, bf16[512,768]{1,0:T(8,128)(2,1)} %get-tuple-element.295.x_ref, f32[12,768]{1,0:T(8,128)} %squeeze.24.rows_ref, ...), custom_call_target="tpu_custom_call" | custom-call | flops 16675000320 | bytes 14500000 | tf_op jit(solution)/shard_map/project/pallas_call | solution.py:247
  168.8 6.6 %collective-permute-done.29 = bf16[8,192,384]{2,1,0:T(8,128)(2,1)S(1)} collective-permute-done((bf16[8,192,384]{2,1,0:T(8,128)(2,1)S(1)}, bf16[8,192,384]{2,1,0:T(8,128)(2,1)S(1)}, u32[]{:S(2)}, u32[]{:S(2)}) %collective-permute-start.29) | collective-permute-done | bytes 1179680 | tf_op jit(solution)/shard_map/ppermute | solution.py:52
  179.7 4.4 mix.3
  184.1 9.0 %expand.3 = (bf16[10,512,384]{2,1,0:T(8,128)(2,1)}, bf16[8,512,384]{2,1,0:T(8,128)(2,1)}) custom-call(s32[2,16]{1,0:T(2,128)} %copy-done.36, s32[1]{0:T(128)} %bitcast.core_ref, bf16[512,768]{1,0:T(8,128)(2,1)} %get-tuple-element.303.x_ref, f32[12,768]{1,0:T(8,128)} %squeeze.24.rows_ref, bf16[16,192,384]{2,1,0:T(8,128)(2,1)} %constant_dynamic-update-slice_fusion.44.refs_0_, ...), custom_call_target="tpu_custom_call" | custom-call | flops 10350000128 | bytes 9000000 | tf_op jit(solution)/shard_map/expand/pallas_call | solution.py:311
  193.1 2.5 collective-permute-done.33
  198.0 7.4 %collective-permute-done.36.refs_4_.refs_5_.refs_6_.refs_7_ = bf16[16,192,384]{2,1,0:T(8,128)(2,1)S(1)} collective-permute-done((bf16[16,192,384]{2,1,0:T(8,128)(2,1)S(1)}, bf16[16,192,384]{2,1,0:T(8,128)(2,1)S(1)}, u32[]{:S(2)}, u32[]{:S(2)}) %collective-permute-start.36) | collective-permute-done | bytes 2359328 | tf_op jit(solution)/shard_map/ppermute | solution.py:63
  206.8 10.8 %contract.3 = (f32[512,768]{1,0:T(8,128)}, f32[512,768]{1,0:T(8,128)}, bf16[512,768]{1,0:T(8,128)(2,1)}) custom-call(s32[2,16]{1,0:T(2,128)} %copy-done.36, s32[1]{0:T(128)} %bitcast.core_ref, s32[4]{0:T(128)} %limits_ref.15, bf16[10,512,384]{2,1,0:T(8,128)(2,1)} %get-tuple-element.308.active_ref.refs_0_, f32[512,768]{1,0:T(8,128)} %get-tuple-element.309.first_ref.sum_ref, ...), custom_call_target="tpu_custom_call" | custom-call | flops 12419999744 | bytes 10800000 | tf_op jit(solution)/shard_map/contract/pallas_call | solution.py:371
  217.5 10.8 %contract_back.2 = (f32[512,768]{1,0:T(8,128)}, bf16[1,512,384]{2,1,0:T(8,128)(2,1)}, bf16[4,512,384]{2,1,0:T(8,128)(2,1)}, bf16[5,512,384]{2,1,0:T(8,128)(2,1)}...) custom-call(s32[2,16]{1,0:T(2,128)} %copy-done.36, s32[1]{0:T(128)} %bitcast.core_ref, s32[4]{0:T(128)} %limits_ref.15, ...), custom_call_target="tpu_custom_call" | custom-call | flops 12650000384 | bytes 11000000 | tf_op jit(solution)/shard_map/contract_back/pallas_call | solution.py:433
  228.5 9.8 %expand_back.2 = (f32[512,768]{1,0:T(8,128)}, bf16[1,512,384]{2,1,0:T(8,128)(2,1)}, bf16[1,512,384]{2,1,0:T(8,128)(2,1)}, f32[3,768]{1,0:T(4,128)}) custom-call(s32[2,16]{1,0:T(2,128)} %copy-done.36, s32[1]{0:T(128)} %bitcast.core_ref, bf16[4,512,384]{2,1,0:T(8,128)(2,1)} %get-tuple-element.323.kept_ref.refs_2_, ...), custom_call_target="tpu_custom_call" | custom-call | flops 11269999616 | bytes 9800000 | tf_op jit(solution)/shard_map/expand_back/pallas_call | solution.py:503
  239.7 7.6 %weight_terms.6 = (bf16[8,192,384]{2,1,0:T(8,128)(2,1)}, bf16[8,192,384]{2,1,0:T(8,128)(2,1)}) custom-call(s32[2,16]{1,0:T(2,128)} %copy-done.36, bf16[10,512,384]{2,1,0:T(8,128)(2,1)} %get-tuple-element.308.active_ref.refs_0_, bf16[10,512,384]{2,1,0:T(8,128)(2,1)} %collective-permute-done.37.refs_1_, bf16[1,512,384]{2,1,0:T(8,128)(2,1)} %get-tuple-element.319.refs_2_, ...), custom_call_target="tpu_custom_call" | custom-call | flops 6899999744 | bytes 6000000 | tf_op jit(solution)/shard_map/weight_terms/pallas_call | solution.py:652
  248.1 14.0 %attend_back.2 = (bf16[3,512,384]{2,1,0:T(8,128)(2,1)}, bf16[3,512,384]{2,1,0:T(8,128)(2,1)}, f32[2,2,1,384]{3,2,1,0:T(1,128)}) custom-call(s32[2,16]{1,0:T(2,128)} %copy-done.36, s32[1]{0:T(128)} %bitcast.core_ref, s32[4]{0:T(128)} %limits_ref.15, bf16[1,512,384]{2,1,0:T(8,128)(2,1)} %get-tuple-element.331.refs_6_.kept_ref, ...), custom_call_target="tpu_custom_call" | custom-call | flops 23690000384 | bytes 20600000 | tf_op jit(solution)/shard_map/attend_back/pallas_call | solution.py:557
  262.9 9.6 %weight_terms.7 = (bf16[8,240,384]{2,1,0:T(8,128)(2,1)}, bf16[8,240,384]{2,1,0:T(8,128)(2,1)}) custom-call(s32[2,16]{1,0:T(2,128)} %copy-done.36, bf16[10,512,384]{2,1,0:T(8,128)(2,1)} %get-tuple-element.308.active_ref.refs_0_, bf16[10,512,384]{2,1,0:T(8,128)(2,1)} %collective-permute-done.37.refs_1_, ...), custom_call_target="tpu_custom_call" | custom-call | flops 8625000448 | bytes 7500000 | tf_op jit(solution)/shard_map/weight_terms/pallas_call | solution.py:652
  272.5 1.8 collective-permute-start.42
  276.3 6.7 %project_back.2.d_out_ref = f32[512,768]{1,0:T(8,128)} custom-call(s32[2,16]{1,0:T(2,128)} %copy-done.36, s32[1]{0:T(128)} %bitcast.core_ref, bf16[3,512,384]{2,1,0:T(8,128)(2,1)} %get-tuple-element.342.refs_2_.kept_ref, bf16[3,512,384]{2,1,0:T(8,128)(2,1)} %get-tuple-element.343.sent_ref, f32[512,768]{1,0:T(8,128)} %get-tuple-element.346.d_sum_ref, ...), custom_call_target="tpu_custom_call" | custom-call | flops 7590000128 | bytes 6600000 | tf_op jit(solution)/shard_map/project_back/pallas_call | solution.py:591
  282.9 6.4 %weight_terms.8 = (bf16[8,144,384]{2,1,0:T(8,128)(2,1)}, bf16[8,144,384]{2,1,0:T(8,128)(2,1)}) custom-call(s32[2,16]{1,0:T(2,128)} %copy-done.36, bf16[4,512,384]{2,1,0:T(8,128)(2,1)} %get-tuple-element.301.context_ref.refs_4_.refs_0_, bf16[4,512,384]{2,1,0:T(8,128)(2,1)} %collective-permute-done.35.refs_5_.refs_1_, ...), custom_call_target="tpu_custom_call" | custom-call | flops 5175000064 | bytes 4500000 | tf_op jit(solution)/shard_map/weight_terms/pallas_call | solution.py:652
  289.3 2.9 collective-permute-done.41
  292.2 6.4 %collective-permute-done.42 = bf16[8,240,384]{2,1,0:T(8,128)(2,1)} collective-permute-done((bf16[8,240,384]{2,1,0:T(8,128)(2,1)}, bf16[8,240,384]{2,1,0:T(8,128)(2,1)}, u32[]{:S(2)}, u32[]{:S(2)}) %collective-permute-start.42) | collective-permute-done | bytes 1474592 | tf_op jit(solution)/shard_map/ppermute | solution.py:52
  298.6 2.6 add_convert_fusion.2
  304.8 11.2 %contract_back.3 = (f32[512,768]{1,0:T(8,128)}, bf16[1,512,384]{2,1,0:T(8,128)(2,1)}, bf16[4,512,384]{2,1,0:T(8,128)(2,1)}, bf16[5,512,384]{2,1,0:T(8,128)(2,1)}...) custom-call(s32[2,16]{1,0:T(2,128)} %copy-done.36, s32[1]{0:T(128)} %bitcast.core_ref, s32[4]{0:T(128)} %limits_ref.15, ...), custom_call_target="tpu_custom_call" | custom-call | flops 12650000384 | bytes 11000000 | tf_op jit(solution)/shard_map/contract_back/pallas_call | solution.py:433
  316.0 3.9 collective-permute-done.45
  323.3 2.1 add_convert_fusion.10
  327.9 2.4 collective-permute-start.47
  330.3 9.9 %expand_back.3 = (f32[512,768]{1,0:T(8,128)}, bf16[1,512,384]{2,1,0:T(8,128)(2,1)}, bf16[1,512,384]{2,1,0:T(8,128)(2,1)}, f32[3,768]{1,0:T(4,128)}) custom-call(s32[2,16]{1,0:T(2,128)} %copy-done.36, s32[1]{0:T(128)} %bitcast.core_ref, bf16[4,512,384]{2,1,0:T(8,128)(2,1)} %get-tuple-element.371.kept_ref.refs_2_, ...), custom_call_target="tpu_custom_call" | custom-call | flops 11269999616 | bytes 9800000 | tf_op jit(solution)/shard_map/expand_back/pallas_call | solution.py:503
  340.2 7.9 %weight_terms.9 = (bf16[8,192,384]{2,1,0:T(8,128)(2,1)}, bf16[8,192,384]{2,1,0:T(8,128)(2,1)}) custom-call(s32[2,16]{1,0:T(2,128)} %copy-done.36, bf16[10,512,384]{2,1,0:T(8,128)(2,1)} %get-tuple-element.286.active_ref.refs_0_, bf16[10,512,384]{2,1,0:T(8,128)(2,1)} %collective-permute-done.32.refs_1_, bf16[1,512,384]{2,1,0:T(8,128)(2,1)} %get-tuple-element.367.refs_2_, ...), custom_call_target="tpu_custom_call" | custom-call | flops 6899999744 | bytes 6000000 | tf_op jit(solution)/shard_map/weight_terms/pallas_call | solution.py:652
  351.8 14.1 %attend_back.3 = (bf16[3,512,384]{2,1,0:T(8,128)(2,1)}, bf16[3,512,384]{2,1,0:T(8,128)(2,1)}, f32[2,2,1,384]{3,2,1,0:T(1,128)}) custom-call(s32[2,16]{1,0:T(2,128)} %copy-done.36, s32[1]{0:T(128)} %bitcast.core_ref, s32[4]{0:T(128)} %limits_ref.15, bf16[1,512,384]{2,1,0:T(8,128)(2,1)} %get-tuple-element.383.refs_6_.kept_ref, ...), custom_call_target="tpu_custom_call" | custom-call | flops 23690000384 | bytes 20600000 | tf_op jit(solution)/shard_map/attend_back/pallas_call | solution.py:557
  367.6 9.7 %weight_terms.10 = (bf16[8,240,384]{2,1,0:T(8,128)(2,1)}, bf16[8,240,384]{2,1,0:T(8,128)(2,1)}) custom-call(s32[2,16]{1,0:T(2,128)} %copy-done.36, bf16[10,512,384]{2,1,0:T(8,128)(2,1)} %get-tuple-element.286.active_ref.refs_0_, bf16[10,512,384]{2,1,0:T(8,128)(2,1)} %collective-permute-done.32.refs_1_, ...), custom_call_target="tpu_custom_call" | custom-call | flops 8625000448 | bytes 7500000 | tf_op jit(solution)/shard_map/weight_terms/pallas_call | solution.py:652
  381.4 2.3 add_convert_fusion.4
  386.3 1.7 collective-permute-start.55
  388.0 6.3 %weight_terms.11 = (bf16[8,144,384]{2,1,0:T(8,128)(2,1)}, bf16[8,144,384]{2,1,0:T(8,128)(2,1)}) custom-call(s32[2,16]{1,0:T(2,128)} %copy-done.36, bf16[4,512,384]{2,1,0:T(8,128)(2,1)} %get-tuple-element.274.context_ref.refs_4_.refs_0_, bf16[4,512,384]{2,1,0:T(8,128)(2,1)} %collective-permute-done.24.refs_5_.refs_1_, ...), custom_call_target="tpu_custom_call" | custom-call | flops 5175000064 | bytes 4500000 | tf_op jit(solution)/shard_map/weight_terms/pallas_call | solution.py:652
  394.3 5.9 %collective-permute-done.56 = bf16[4,192,384]{2,1,0:T(8,128)(2,1)S(1)} collective-permute-done((bf16[4,192,384]{2,1,0:T(8,128)(2,1)}, bf16[4,192,384]{2,1,0:T(8,128)(2,1)S(1)}, u32[]{:S(2)}, u32[]{:S(2)}) %collective-permute-start.56) | collective-permute-done | bytes 589856 | tf_op jit(solution)/shard_map/ppermute | solution.py:52
  400.2 3.7 collective-permute-done.57
  403.9 2.6 add_convert_fusion
  410.0 6.7 %project_back.3 = f32[512,768]{1,0:T(8,128)} custom-call(s32[2,16]{1,0:T(2,128)} %copy-done.36, s32[1]{0:T(128)} %bitcast.core_ref, bf16[3,512,384]{2,1,0:T(8,128)(2,1)} %get-tuple-element.396.refs_2_.kept_ref, bf16[3,512,384]{2,1,0:T(8,128)(2,1)} %get-tuple-element.397.sent_ref, f32[512,768]{1,0:T(8,128)} %get-tuple-element.414.d_sum_ref, ...), custom_call_target="tpu_custom_call" | custom-call | flops 7590000128 | bytes 6600000 | tf_op jit(solution)/shard_map/project_back/pallas_call | solution.py:591
  417.4 8.2 %collective-permute-done.61 = bf16[4,240,384]{2,1,0:T(8,128)(2,1)} collective-permute-done((bf16[4,240,384]{2,1,0:T(8,128)(2,1)}, bf16[4,240,384]{2,1,0:T(8,128)(2,1)}, u32[]{:S(2)}, u32[]{:S(2)}) %collective-permute-start.61) | collective-permute-done | bytes 737312 | tf_op jit(solution)/shard_map/ppermute | solution.py:52
  427.5 1.7 collective-permute-start.66
  432.4 2.4 collective-permute-start.64
  436.0 8.4 %collective-permute-done.64 = bf16[1,192,384]{2,1,0:T(8,128)(2,1)S(1)} collective-permute-done((bf16[1,192,384]{2,1,0:T(8,128)(2,1)S(1)}, bf16[1,192,384]{2,1,0:T(8,128)(2,1)S(1)}, u32[]{:S(2)}, u32[]{:S(2)}) %collective-permute-start.64) | collective-permute-done | bytes 147488 | tf_op jit(solution)/shard_map/ppermute | solution.py:52
  444.4 1.9 collective-permute-done.65
  450.3 7.2 %collective-permute-done.70 = f32[2,2,576]{2,1,0:T(2,128)S(1)} collective-permute-done((f32[2,2,576]{2,1,0:T(2,128)S(1)}, f32[2,2,576]{2,1,0:T(2,128)S(1)}, u32[]{:S(2)}, u32[]{:S(2)}) %collective-permute-start.70) | collective-permute-done | bytes 9248 | tf_op jit(solution)/shard_map/ppermute | solution.py:52
  457.5 2.3 collective-permute-done.68
  460.9 2.1 collective-permute-start.72
  463.0 5.7 %collective-permute-done.72 = f32[1,2,576]{2,1,0:T(2,128)S(1)} collective-permute-done((f32[1,2,576]{2,1,0:T(2,128)S(1)}, f32[1,2,576]{2,1,0:T(2,128)S(1)}, u32[]{:S(2)}, u32[]{:S(2)}) %collective-permute-start.72) | collective-permute-done | bytes 4640 | tf_op jit(solution)/shard_map/ppermute | solution.py:52
  (367 shorter events, 105.6 us)
Async XLA Ops:
  2.1 9.8 %collective-permute-start = (bf16[1,144,384]{2,1,0:T(8,128)(2,1)S(1)}, bf16[1,144,384]{2,1,0:T(8,128)(2,1)S(1)}, u32[]{:S(2)}, u32[]{:S(2)}) collective-permute-start(bf16[1,144,384]{2,1,0:T(8,128)(2,1)S(1)} %bitcast.83), channel_id=1, source_target_pairs={{0,8},{1,9},{2,10},{3,11},{4,12},{5,13},{6,14},{7,15},{8,0},{9,1},... | collective-permute-start | bytes 331784 | tf_op jit(solution)/shard_map/ppermute | solution.py:52
  11.9 10.8 %collective-permute-start.2 = (bf16[2,144,384]{2,1,0:T(8,128)(2,1)S(1)}, bf16[2,144,384]{2,1,0:T(8,128)(2,1)S(1)}, u32[]{:S(2)}, u32[]{:S(2)}) collective-permute-start(bf16[2,144,384]{2,1,0:T(8,128)(2,1)S(1)} %constant_dynamic-update-slice_fusion), channel_id=1, source_target_pairs={{0,4},{1,5},{2,6},{3,7},{4,0},{5,1},{6,2},{7,3},{8,12},{9,13},{10,... | collective-permute-start | bytes 663560 | tf_op jit(solution)/shard_map/ppermute | solution.py:52
  12.7 10.0 %collective-permute-start.3 = (bf16[1,240,384]{2,1,0:T(8,128)(2,1)S(1)}, bf16[1,240,384]{2,1,0:T(8,128)(2,1)S(1)}, u32[]{:S(2)}, u32[]{:S(2)}) collective-permute-start(bf16[1,240,384]{2,1,0:T(8,128)(2,1)S(1)} %maximum_bitcast_fusion), channel_id=1, source_target_pairs={{0,8},{1,9},{2,10},{3,11},{4,12},{5,13},{6,14},{7,15},{8,0},{9,1},... | collective-permute-start | bytes 552968 | tf_op jit(solution)/shard_map/ppermute | solution.py:52
  22.8 15.7 %collective-permute-start.5 = (bf16[4,144,384]{2,1,0:T(8,128)(2,1)S(1)}, bf16[4,144,384]{2,1,0:T(8,128)(2,1)S(1)}, u32[]{:S(2)}, u32[]{:S(2)}) collective-permute-start(bf16[4,144,384]{2,1,0:T(8,128)(2,1)S(1)} %constant_dynamic-update-slice_fusion.2), channel_id=1, source_target_pairs={{0,2},{1,3},{2,0},{3,1},{4,6},{5,7},{6,4},{7,5},{8,10},{9,11},{10,... | collective-permute-start | bytes 1327112 | tf_op jit(solution)/shard_map/ppermute | solution.py:52
  24.2 14.3 %collective-permute-start.6 = (bf16[2,240,384]{2,1,0:T(8,128)(2,1)S(1)}, bf16[2,240,384]{2,1,0:T(8,128)(2,1)S(1)}, u32[]{:S(2)}, u32[]{:S(2)}) collective-permute-start(bf16[2,240,384]{2,1,0:T(8,128)(2,1)S(1)} %constant_dynamic-update-slice_fusion.4), channel_id=1, source_target_pairs={{0,4},{1,5},{2,6},{3,7},{4,0},{5,1},{6,2},{7,3},{8,12},{9,13},{10,... | collective-permute-start | bytes 1105928 | tf_op jit(solution)/shard_map/ppermute | solution.py:52
  27.5 10.2 %collective-permute-start.7 = (bf16[1,192,384]{2,1,0:T(8,128)(2,1)S(1)}, bf16[1,192,384]{2,1,0:T(8,128)(2,1)S(1)}, u32[]{:S(2)}, u32[]{:S(2)}) collective-permute-start(bf16[1,192,384]{2,1,0:T(8,128)(2,1)S(1)} %constant_dynamic-slice_fusion.8), channel_id=1, source_target_pairs={{0,8},{1,9},{2,10},{3,11},{4,12},{5,13},{6,14},{7,15},{8,0},{9,1},... | collective-permute-start | bytes 442376 | tf_op jit(solution)/shard_map/ppermute | solution.py:52
  38.6 21.6 %collective-permute-start.9 = (bf16[8,144,384]{2,1,0:T(8,128)(2,1)S(1)}, bf16[8,144,384]{2,1,0:T(8,128)(2,1)S(1)}, u32[]{:S(2)}, u32[]{:S(2)}) collective-permute-start(bf16[8,144,384]{2,1,0:T(8,128)(2,1)S(1)} %constant_dynamic-update-slice_fusion.6), channel_id=1, source_target_pairs={{0,1},{1,0},{2,3},{3,2},{4,5},{5,4},{6,7},{7,6},{8,9},{9,8},{10,11... | collective-permute-start | bytes 2654216 | tf_op jit(solution)/shard_map/ppermute | solution.py:52
  39.3 20.8 %collective-permute-start.10 = (bf16[4,240,384]{2,1,0:T(8,128)(2,1)S(1)}, bf16[4,240,384]{2,1,0:T(8,128)(2,1)}, u32[]{:S(2)}, u32[]{:S(2)}) collective-permute-start(bf16[4,240,384]{2,1,0:T(8,128)(2,1)S(1)} %constant_dynamic-update-slice_fusion.8), channel_id=1, source_target_pairs={{0,2},{1,3},{2,0},{3,1},{4,6},{5,7},{6,4},{7,5},{8,10},{9,11},{10,... | collective-permute-start | bytes 2211848 | tf_op jit(solution)/shard_map/ppermute | solution.py:52
  41.0 19.2 %collective-permute-start.11 = (bf16[2,192,384]{2,1,0:T(8,128)(2,1)S(1)}, bf16[2,192,384]{2,1,0:T(8,128)(2,1)S(1)}, u32[]{:S(2)}, u32[]{:S(2)}) collective-permute-start(bf16[2,192,384]{2,1,0:T(8,128)(2,1)S(1)} %constant_dynamic-update-slice_fusion.10), channel_id=1, source_target_pairs={{0,4},{1,5},{2,6},{3,7},{4,0},{5,1},{6,2},{7,3},{8,12},{9,13},{10,... | collective-permute-start | bytes 884744 | tf_op jit(solution)/shard_map/ppermute | solution.py:52
  42.9 17.2 %collective-permute-start.13 = (f32[8,2,576]{2,1,0:T(2,128)S(1)}, f32[8,2,576]{2,1,0:T(2,128)S(1)}, u32[]{:S(2)}, u32[]{:S(2)}) collective-permute-start(f32[8,2,576]{2,1,0:T(2,128)S(1)} %pad_maximum_fusion.8), channel_id=1, source_target_pairs={{0,1},{1,0},{2,3},{3,2},{4,5},{5,4},{6,7},{7,6},{8,9},{9,8},{10,11... | collective-permute-start | bytes 110600 | tf_op jit(solution)/shard_map/ppermute | solution.py:52
  44.4 15.8 %collective-permute-start.12 = (bf16[1,192,384]{2,1,0:T(8,128)(2,1)S(1)}, bf16[1,192,384]{2,1,0:T(8,128)(2,1)}, u32[]{:S(2)}, u32[]{:S(2)}) collective-permute-start(bf16[1,192,384]{2,1,0:T(8,128)(2,1)S(1)} %maximum_bitcast_fusion.1), channel_id=1, source_target_pairs={{0,8},{1,9},{2,10},{3,11},{4,12},{5,13},{6,14},{7,15},{8,0},{9,1},... | collective-permute-start | bytes 442376 | tf_op jit(solution)/shard_map/ppermute | solution.py:52
  62.3 10.3 %collective-permute-start.18 = (bf16[16,144,384]{2,1,0:T(8,128)(2,1)}, bf16[16,144,384]{2,1,0:T(8,128)(2,1)}, u32[]{:S(2)}, u32[]{:S(2)}) collective-permute-start(bf16[16,144,384]{2,1,0:T(8,128)(2,1)} %constant_dynamic-update-slice_fusion.18.refs_0_), channel_id=1, source_target_pairs={{0,16},{16,0},{1,17},{17,1},{2,18},{18,2},{3,19},{19,3},{4,20},{20... | collective-permute-start | bytes 5308424 | tf_op jit(solution)/shard_map/ppermute | solution.py:63
  67.4 15.8 %collective-permute-start.16 = (bf16[2,192,384]{2,1,0:T(8,128)(2,1)}, bf16[2,192,384]{2,1,0:T(8,128)(2,1)}, u32[]{:S(2)}, u32[]{:S(2)}) collective-permute-start(bf16[2,192,384]{2,1,0:T(8,128)(2,1)} %constant_dynamic-update-slice_fusion.16), channel_id=1, source_target_pairs={{0,4},{1,5},{2,6},{3,7},{4,0},{5,1},{6,2},{7,3},{8,12},{9,13},{10,... | collective-permute-start | bytes 884744 | tf_op jit(solution)/shard_map/ppermute | solution.py:52
  68.9 15.8 %collective-permute-start.15 = (bf16[4,192,384]{2,1,0:T(8,128)(2,1)S(1)}, bf16[4,192,384]{2,1,0:T(8,128)(2,1)}, u32[]{:S(2)}, u32[]{:S(2)}) collective-permute-start(bf16[4,192,384]{2,1,0:T(8,128)(2,1)S(1)} %constant_dynamic-update-slice_fusion.14), channel_id=1, source_target_pairs={{0,2},{1,3},{2,0},{3,1},{4,6},{5,7},{6,4},{7,5},{8,10},{9,11},{10,... | collective-permute-start | bytes 1769480 | tf_op jit(solution)/shard_map/ppermute | solution.py:52
  70.6 23.3 %collective-permute-start.14 = (bf16[8,240,384]{2,1,0:T(8,128)(2,1)S(1)}, bf16[8,240,384]{2,1,0:T(8,128)(2,1)S(1)}, u32[]{:S(2)}, u32[]{:S(2)}) collective-permute-start(bf16[8,240,384]{2,1,0:T(8,128)(2,1)S(1)} %constant_dynamic-update-slice_fusion.12), channel_id=1, source_target_pairs={{0,1},{1,0},{2,3},{3,2},{4,5},{5,4},{6,7},{7,6},{8,9},{9,8},{10,11... | collective-permute-start | bytes 4423688 | tf_op jit(solution)/shard_map/ppermute | solution.py:52
  71.0 12.2 %collective-permute-start.17 = (bf16[1,192,384]{2,1,0:T(8,128)(2,1)}, bf16[1,192,384]{2,1,0:T(8,128)(2,1)}, u32[]{:S(2)}, u32[]{:S(2)}) collective-permute-start(bf16[1,192,384]{2,1,0:T(8,128)(2,1)} %bitcast.8), channel_id=1, source_target_pairs={{0,8},{1,9},{2,10},{3,11},{4,12},{5,13},{6,14},{7,15},{8,0},{9,1},... | collective-permute-start | bytes 442376 | tf_op jit(solution)/shard_map/ppermute | solution.py:52
  94.4 9.5 %collective-permute-start.23 = (bf16[16,240,384]{2,1,0:T(8,128)(2,1)S(1)}, bf16[16,240,384]{2,1,0:T(8,128)(2,1)S(1)}, u32[]{:S(2)}, u32[]{:S(2)}) collective-permute-start(bf16[16,240,384]{2,1,0:T(8,128)(2,1)S(1)} %constant_dynamic-update-slice_fusion.26.refs_0_), channel_id=1, source_target_pairs={{0,16},{16,0},{1,17},{17,1},{2,18},{18,2},{3,19},{19,3},{4,20},{20... | collective-permute-start | bytes 8847368 | tf_op jit(solution)/shard_map/ppermute | solution.py:63
  98.4 22.7 %collective-permute-start.21 = (bf16[2,192,384]{2,1,0:T(8,128)(2,1)}, bf16[2,192,384]{2,1,0:T(8,128)(2,1)}, u32[]{:S(2)}, u32[]{:S(2)}) collective-permute-start(bf16[2,192,384]{2,1,0:T(8,128)(2,1)} %constant_dynamic-update-slice_fusion.24), channel_id=1, source_target_pairs={{0,4},{1,5},{2,6},{3,7},{4,0},{5,1},{6,2},{7,3},{8,12},{9,13},{10,... | collective-permute-start | bytes 884744 | tf_op jit(solution)/shard_map/ppermute | solution.py:52
  101.0 20.1 %collective-permute-start.20 = (bf16[4,192,384]{2,1,0:T(8,128)(2,1)S(1)}, bf16[4,192,384]{2,1,0:T(8,128)(2,1)}, u32[]{:S(2)}, u32[]{:S(2)}) collective-permute-start(bf16[4,192,384]{2,1,0:T(8,128)(2,1)S(1)} %constant_dynamic-update-slice_fusion.22), channel_id=1, source_target_pairs={{0,2},{1,3},{2,0},{3,1},{4,6},{5,7},{6,4},{7,5},{8,10},{9,11},{10,... | collective-permute-start | bytes 1769480 | tf_op jit(solution)/shard_map/ppermute | solution.py:52
  101.3 21.0 %collective-permute-start.24 = (bf16[4,512,384]{2,1,0:T(8,128)(2,1)}, bf16[4,512,384]{2,1,0:T(8,128)(2,1)}, u32[]{:S(2)}, u32[]{:S(2)}) collective-permute-start(bf16[4,512,384]{2,1,0:T(8,128)(2,1)} %get-tuple-element.274.context_ref.refs_4_.refs_0_), channel_id=1, source_target_pairs={{0,16},{16,0},{1,17},{17,1},{2,18},{18,2},{3,19},{19,3},{4,20},{20... | collective-permute-start | bytes 4718600 | tf_op jit(solution)/shard_map/ppermute | solution.py:63
  102.6 19.8 %collective-permute-start.19 = (bf16[8,192,384]{2,1,0:T(8,128)(2,1)S(1)}, bf16[8,192,384]{2,1,0:T(8,128)(2,1)S(1)}, u32[]{:S(2)}, u32[]{:S(2)}) collective-permute-start(bf16[8,192,384]{2,1,0:T(8,128)(2,1)S(1)} %constant_dynamic-update-slice_fusion.20), channel_id=1, source_target_pairs={{0,1},{1,0},{2,3},{3,2},{4,5},{5,4},{6,7},{7,6},{8,9},{9,8},{10,11... | collective-permute-start | bytes 3538952 | tf_op jit(solution)/shard_map/ppermute | solution.py:52
  105.5 15.5 %collective-permute-start.22 = (bf16[1,192,384]{2,1,0:T(8,128)(2,1)}, bf16[1,192,384]{2,1,0:T(8,128)(2,1)S(1)}, u32[]{:S(2)}, u32[]{:S(2)}) collective-permute-start(bf16[1,192,384]{2,1,0:T(8,128)(2,1)} %constant_dynamic-slice_fusion), channel_id=1, source_target_pairs={{0,8},{1,9},{2,10},{3,11},{4,12},{5,13},{6,14},{7,15},{8,0},{9,1},... | collective-permute-start | bytes 442376 | tf_op jit(solution)/shard_map/ppermute | solution.py:52
  124.8 17.6 %collective-permute-start.27 = (bf16[2,192,384]{2,1,0:T(8,128)(2,1)S(1)}, bf16[2,192,384]{2,1,0:T(8,128)(2,1)S(1)}, u32[]{:S(2)}, u32[]{:S(2)}) collective-permute-start(bf16[2,192,384]{2,1,0:T(8,128)(2,1)S(1)} %constant_dynamic-update-slice_fusion.32), channel_id=1, source_target_pairs={{0,4},{1,5},{2,6},{3,7},{4,0},{5,1},{6,2},{7,3},{8,12},{9,13},{10,... | collective-permute-start | bytes 884744 | tf_op jit(solution)/shard_map/ppermute | solution.py:52
  127.5 22.6 %collective-permute-start.25 = (bf16[8,192,384]{2,1,0:T(8,128)(2,1)S(1)}, bf16[8,192,384]{2,1,0:T(8,128)(2,1)S(1)}, u32[]{:S(2)}, u32[]{:S(2)}) collective-permute-start(bf16[8,192,384]{2,1,0:T(8,128)(2,1)S(1)} %constant_dynamic-update-slice_fusion.28), channel_id=1, source_target_pairs={{0,1},{1,0},{2,3},{3,2},{4,5},{5,4},{6,7},{7,6},{8,9},{9,8},{10,11... | collective-permute-start | bytes 3538952 | tf_op jit(solution)/shard_map/ppermute | solution.py:52
  129.9 16.4 %collective-permute-start.26 = (bf16[4,192,384]{2,1,0:T(8,128)(2,1)S(1)}, bf16[4,192,384]{2,1,0:T(8,128)(2,1)}, u32[]{:S(2)}, u32[]{:S(2)}) collective-permute-start(bf16[4,192,384]{2,1,0:T(8,128)(2,1)S(1)} %constant_dynamic-update-slice_fusion.30), channel_id=1, source_target_pairs={{0,2},{1,3},{2,0},{3,1},{4,6},{5,7},{6,4},{7,5},{8,10},{9,11},{10,... | collective-permute-start | bytes 1769480 | tf_op jit(solution)/shard_map/ppermute | solution.py:52
  130.3 45.1 %collective-permute-start.32 = (bf16[10,512,384]{2,1,0:T(8,128)(2,1)}, bf16[10,512,384]{2,1,0:T(8,128)(2,1)}, u32[]{:S(2)}, u32[]{:S(2)}) collective-permute-start(bf16[10,512,384]{2,1,0:T(8,128)(2,1)} %get-tuple-element.286.active_ref.refs_0_), channel_id=1, source_target_pairs={{0,16},{16,0},{1,17},{17,1},{2,18},{18,2},{3,19},{19,3},{4,20},{20... | collective-permute-start | bytes 11796488 | tf_op jit(solution)/shard_map/ppermute | solution.py:63
  153.2 15.5 %collective-permute-start.30 = (bf16[4,192,384]{2,1,0:T(8,128)(2,1)S(1)}, bf16[4,192,384]{2,1,0:T(8,128)(2,1)}, u32[]{:S(2)}, u32[]{:S(2)}) collective-permute-start(bf16[4,192,384]{2,1,0:T(8,128)(2,1)S(1)} %constant_dynamic-update-slice_fusion.38), channel_id=1, source_target_pairs={{0,2},{1,3},{2,0},{3,1},{4,6},{5,7},{6,4},{7,5},{8,10},{9,11},{10,... | collective-permute-start | bytes 1769480 | tf_op jit(solution)/shard_map/ppermute | solution.py:52
  154.8 20.5 %collective-permute-start.29 = (bf16[8,192,384]{2,1,0:T(8,128)(2,1)S(1)}, bf16[8,192,384]{2,1,0:T(8,128)(2,1)S(1)}, u32[]{:S(2)}, u32[]{:S(2)}) collective-permute-start(bf16[8,192,384]{2,1,0:T(8,128)(2,1)S(1)} %constant_dynamic-update-slice_fusion.36), channel_id=1, source_target_pairs={{0,1},{1,0},{2,3},{3,2},{4,5},{5,4},{6,7},{7,6},{8,9},{9,8},{10,11... | collective-permute-start | bytes 3538952 | tf_op jit(solution)/shard_map/ppermute | solution.py:52
  177.9 17.7 %collective-permute-start.35 = (bf16[4,512,384]{2,1,0:T(8,128)(2,1)}, bf16[4,512,384]{2,1,0:T(8,128)(2,1)}, u32[]{:S(2)}, u32[]{:S(2)}) collective-permute-start(bf16[4,512,384]{2,1,0:T(8,128)(2,1)} %get-tuple-element.301.context_ref.refs_4_.refs_0_), channel_id=1, source_target_pairs={{0,16},{16,0},{1,17},{17,1},{2,18},{18,2},{3,19},{19,3},{4,20},{20... | collective-permute-start | bytes 4718600 | tf_op jit(solution)/shard_map/ppermute | solution.py:63
  179.4 16.3 %collective-permute-start.33 = (bf16[8,192,384]{2,1,0:T(8,128)(2,1)S(1)}, bf16[8,192,384]{2,1,0:T(8,128)(2,1)S(1)}, u32[]{:S(2)}, u32[]{:S(2)}) collective-permute-start(bf16[8,192,384]{2,1,0:T(8,128)(2,1)S(1)} %constant_dynamic-update-slice_fusion.42), channel_id=1, source_target_pairs={{0,1},{1,0},{2,3},{3,2},{4,5},{5,4},{6,7},{7,6},{8,9},{9,8},{10,11... | collective-permute-start | bytes 3538952 | tf_op jit(solution)/shard_map/ppermute | solution.py:52
  197.5 40.8 %collective-permute-start.37 = (bf16[10,512,384]{2,1,0:T(8,128)(2,1)}, bf16[10,512,384]{2,1,0:T(8,128)(2,1)}, u32[]{:S(2)}, u32[]{:S(2)}) collective-permute-start(bf16[10,512,384]{2,1,0:T(8,128)(2,1)} %get-tuple-element.308.active_ref.refs_0_), channel_id=1, source_target_pairs={{0,16},{16,0},{1,17},{17,1},{2,18},{18,2},{3,19},{19,3},{4,20},{20... | collective-permute-start | bytes 11796488 | tf_op jit(solution)/shard_map/ppermute | solution.py:63
  228.3 10.1 %collective-permute-start.38 = (bf16[5,512,384]{2,1,0:T(8,128)(2,1)}, bf16[5,512,384]{2,1,0:T(8,128)(2,1)S(1)}, u32[]{:S(2)}, u32[]{:S(2)}) collective-permute-start(bf16[5,512,384]{2,1,0:T(8,128)(2,1)} %get-tuple-element.320.sent_ref), channel_id=1, source_target_pairs={{0,16},{16,0},{1,17},{17,1},{2,18},{18,2},{3,19},{19,3},{4,20},{20... | collective-permute-start | bytes 5898248 | tf_op jit(solution)/shard_map/ppermute | solution.py:63
  247.3 14.8 %collective-permute-start.40 = (bf16[1,512,384]{2,1,0:T(8,128)(2,1)S(1)}, bf16[1,512,384]{2,1,0:T(8,128)(2,1)S(1)}, u32[]{:S(2)}, u32[]{:S(2)}) collective-permute-start(bf16[1,512,384]{2,1,0:T(8,128)(2,1)S(1)} %copy-done.43), channel_id=1, source_target_pairs={{0,16},{16,0},{1,17},{17,1},{2,18},{18,2},{3,19},{19,3},{4,20},{20... | collective-permute-start | bytes 1179656 | tf_op jit(solution)/shard_map/ppermute | solution.py:63
  247.8 24.7 %collective-permute-start.39 = (bf16[8,192,384]{2,1,0:T(8,128)(2,1)}, bf16[8,192,384]{2,1,0:T(8,128)(2,1)}, u32[]{:S(2)}, u32[]{:S(2)}) collective-permute-start(bf16[8,192,384]{2,1,0:T(8,128)(2,1)} %get-tuple-element.329), channel_id=1, source_target_pairs={{0,1},{1,0},{2,3},{3,2},{4,5},{5,4},{6,7},{7,6},{8,9},{9,8},{10,11... | collective-permute-start | bytes 3538952 | tf_op jit(solution)/shard_map/ppermute | solution.py:52
  272.5 10.4 %collective-permute-start.43 = (bf16[3,512,384]{2,1,0:T(8,128)(2,1)}, bf16[3,512,384]{2,1,0:T(8,128)(2,1)}, u32[]{:S(2)}, u32[]{:S(2)}) collective-permute-start(bf16[3,512,384]{2,1,0:T(8,128)(2,1)} %get-tuple-element.343.sent_ref), channel_id=1, source_target_pairs={{0,16},{16,0},{1,17},{17,1},{2,18},{18,2},{3,19},{19,3},{4,20},{20... | collective-permute-start | bytes 3538952 | tf_op jit(solution)/shard_map/ppermute | solution.py:63
  272.5 26.1 %collective-permute-start.42 = (bf16[8,240,384]{2,1,0:T(8,128)(2,1)}, bf16[8,240,384]{2,1,0:T(8,128)(2,1)}, u32[]{:S(2)}, u32[]{:S(2)}) collective-permute-start(bf16[8,240,384]{2,1,0:T(8,128)(2,1)} %get-tuple-element.341), channel_id=1, source_target_pairs={{0,1},{1,0},{2,3},{3,2},{4,5},{5,4},{6,7},{7,6},{8,9},{9,8},{10,11... | collective-permute-start | bytes 4423688 | tf_op jit(solution)/shard_map/ppermute | solution.py:52
  275.9 16.3 %collective-permute-start.41 = (bf16[4,192,384]{2,1,0:T(8,128)(2,1)S(1)}, bf16[4,192,384]{2,1,0:T(8,128)(2,1)S(1)}, u32[]{:S(2)}, u32[]{:S(2)}) collective-permute-start(bf16[4,192,384]{2,1,0:T(8,128)(2,1)S(1)} %get-tuple-element.466), channel_id=1, source_target_pairs={{0,2},{1,3},{2,0},{3,1},{4,6},{5,7},{6,4},{7,5},{8,10},{9,11},{10,... | collective-permute-start | bytes 1769480 | tf_op jit(solution)/shard_map/ppermute | solution.py:52
  301.2 18.7 %collective-permute-start.45 = (bf16[4,240,384]{2,1,0:T(8,128)(2,1)}, bf16[4,240,384]{2,1,0:T(8,128)(2,1)S(1)}, u32[]{:S(2)}, u32[]{:S(2)}) collective-permute-start(bf16[4,240,384]{2,1,0:T(8,128)(2,1)} %get-tuple-element.462), channel_id=1, source_target_pairs={{0,2},{1,3},{2,0},{3,1},{4,6},{5,7},{6,4},{7,5},{8,10},{9,11},{10,... | collective-permute-start | bytes 2211848 | tf_op jit(solution)/shard_map/ppermute | solution.py:52
  303.7 12.3 %collective-permute-start.44 = (bf16[2,192,384]{2,1,0:T(8,128)(2,1)}, bf16[2,192,384]{2,1,0:T(8,128)(2,1)S(1)}, u32[]{:S(2)}, u32[]{:S(2)}) collective-permute-start(bf16[2,192,384]{2,1,0:T(8,128)(2,1)} %get-tuple-element.478), channel_id=1, source_target_pairs={{0,4},{1,5},{2,6},{3,7},{4,0},{5,1},{6,2},{7,3},{8,12},{9,13},{10,... | collective-permute-start | bytes 884744 | tf_op jit(solution)/shard_map/ppermute | solution.py:52
  304.3 16.9 %collective-permute-start.46 = (bf16[8,144,384]{2,1,0:T(8,128)(2,1)}, bf16[8,144,384]{2,1,0:T(8,128)(2,1)}, u32[]{:S(2)}, u32[]{:S(2)}) collective-permute-start(bf16[8,144,384]{2,1,0:T(8,128)(2,1)} %get-tuple-element.352), channel_id=1, source_target_pairs={{0,1},{1,0},{2,3},{3,2},{4,5},{5,4},{6,7},{7,6},{8,9},{9,8},{10,11... | collective-permute-start | bytes 2654216 | tf_op jit(solution)/shard_map/ppermute | solution.py:52
  321.2 19.1 %collective-permute-start.50 = (bf16[5,512,384]{2,1,0:T(8,128)(2,1)}, bf16[5,512,384]{2,1,0:T(8,128)(2,1)}, u32[]{:S(2)}, u32[]{:S(2)}) collective-permute-start(bf16[5,512,384]{2,1,0:T(8,128)(2,1)} %get-tuple-element.368.sent_ref), channel_id=1, source_target_pairs={{0,16},{16,0},{1,17},{17,1},{2,18},{18,2},{3,19},{19,3},{4,20},{20... | collective-permute-start | bytes 5898248 | tf_op jit(solution)/shard_map/ppermute | solution.py:63
  325.4 22.7 %collective-permute-start.49 = (bf16[4,144,384]{2,1,0:T(8,128)(2,1)}, bf16[4,144,384]{2,1,0:T(8,128)(2,1)S(1)}, u32[]{:S(2)}, u32[]{:S(2)}) collective-permute-start(bf16[4,144,384]{2,1,0:T(8,128)(2,1)} %get-tuple-element.470), channel_id=1, source_target_pairs={{0,2},{1,3},{2,0},{3,1},{4,6},{5,7},{6,4},{7,5},{8,10},{9,11},{10,... | collective-permute-start | bytes 1327112 | tf_op jit(solution)/shard_map/ppermute | solution.py:52
  327.2 21.0 %collective-permute-start.48 = (bf16[2,240,384]{2,1,0:T(8,128)(2,1)S(1)}, bf16[2,240,384]{2,1,0:T(8,128)(2,1)S(1)}, u32[]{:S(2)}, u32[]{:S(2)}) collective-permute-start(bf16[2,240,384]{2,1,0:T(8,128)(2,1)S(1)} %get-tuple-element.474), channel_id=1, source_target_pairs={{0,4},{1,5},{2,6},{3,7},{4,0},{5,1},{6,2},{7,3},{8,12},{9,13},{10,... | collective-permute-start | bytes 1105928 | tf_op jit(solution)/shard_map/ppermute | solution.py:52
  327.9 20.2 %collective-permute-start.47 = (bf16[1,192,384]{2,1,0:T(8,128)(2,1)S(1)}, bf16[1,192,384]{2,1,0:T(8,128)(2,1)S(1)}, u32[]{:S(2)}, u32[]{:S(2)}) collective-permute-start(bf16[1,192,384]{2,1,0:T(8,128)(2,1)S(1)} %get-tuple-element.504), channel_id=1, source_target_pairs={{0,8},{1,9},{2,10},{3,11},{4,12},{5,13},{6,14},{7,15},{8,0},{9,1},... | collective-permute-start | bytes 442376 | tf_op jit(solution)/shard_map/ppermute | solution.py:52
  348.2 19.4 %collective-permute-start.54 = (bf16[1,512,384]{2,1,0:T(8,128)(2,1)}, bf16[1,512,384]{2,1,0:T(8,128)(2,1)}, u32[]{:S(2)}, u32[]{:S(2)}) collective-permute-start(bf16[1,512,384]{2,1,0:T(8,128)(2,1)} %get-tuple-element.384.sent_ref), channel_id=1, source_target_pairs={{0,16},{16,0},{1,17},{17,1},{2,18},{18,2},{3,19},{19,3},{4,20},{20... | collective-permute-start | bytes 1179656 | tf_op jit(solution)/shard_map/ppermute | solution.py:63
  348.2 29.1 %collective-permute-start.53 = (bf16[8,192,384]{2,1,0:T(8,128)(2,1)}, bf16[8,192,384]{2,1,0:T(8,128)(2,1)}, u32[]{:S(2)}, u32[]{:S(2)}) collective-permute-start(bf16[8,192,384]{2,1,0:T(8,128)(2,1)} %get-tuple-element.381), channel_id=1, source_target_pairs={{0,1},{1,0},{2,3},{3,2},{4,5},{5,4},{6,7},{7,6},{8,9},{9,8},{10,11... | collective-permute-start | bytes 3538952 | tf_op jit(solution)/shard_map/ppermute | solution.py:52
  349.6 27.7 %collective-permute-start.52 = (bf16[2,144,384]{2,1,0:T(8,128)(2,1)}, bf16[2,144,384]{2,1,0:T(8,128)(2,1)S(1)}, u32[]{:S(2)}, u32[]{:S(2)}) collective-permute-start(bf16[2,144,384]{2,1,0:T(8,128)(2,1)} %get-tuple-element.490), channel_id=1, source_target_pairs={{0,4},{1,5},{2,6},{3,7},{4,0},{5,1},{6,2},{7,3},{8,12},{9,13},{10,... | collective-permute-start | bytes 663560 | tf_op jit(solution)/shard_map/ppermute | solution.py:52
  350.3 27.0 %collective-permute-start.51 = (bf16[1,240,384]{2,1,0:T(8,128)(2,1)S(1)}, bf16[1,240,384]{2,1,0:T(8,128)(2,1)S(1)}, u32[]{:S(2)}, u32[]{:S(2)}) collective-permute-start(bf16[1,240,384]{2,1,0:T(8,128)(2,1)S(1)} %get-tuple-element.500), channel_id=1, source_target_pairs={{0,8},{1,9},{2,10},{3,11},{4,12},{5,13},{6,14},{7,15},{8,0},{9,1},... | collective-permute-start | bytes 552968 | tf_op jit(solution)/shard_map/ppermute | solution.py:52
  366.8 12.6 %collective-permute-start.59 = (f32[16,2,576]{2,1,0:T(2,128)S(1)}, f32[16,2,576]{2,1,0:T(2,128)S(1)}, u32[]{:S(2)}, u32[]{:S(2)}) collective-permute-start(f32[16,2,576]{2,1,0:T(2,128)S(1)} %pad_maximum_fusion.5), channel_id=1, source_target_pairs={{0,16},{16,0},{1,17},{17,1},{2,18},{18,2},{3,19},{19,3},{4,20},{20... | collective-permute-start | bytes 221192 | tf_op jit(solution)/shard_map/ppermute | solution.py:63
  377.3 10.7 %collective-permute-start.58 = (bf16[3,512,384]{2,1,0:T(8,128)(2,1)}, bf16[3,512,384]{2,1,0:T(8,128)(2,1)}, u32[]{:S(2)}, u32[]{:S(2)}) collective-permute-start(bf16[3,512,384]{2,1,0:T(8,128)(2,1)} %get-tuple-element.397.sent_ref), channel_id=1, source_target_pairs={{0,16},{16,0},{1,17},{17,1},{2,18},{18,2},{3,19},{19,3},{4,20},{20... | collective-permute-start | bytes 3538952 | tf_op jit(solution)/shard_map/ppermute | solution.py:63
  377.9 26.0 %collective-permute-start.57 = (bf16[8,240,384]{2,1,0:T(8,128)(2,1)}, bf16[8,240,384]{2,1,0:T(8,128)(2,1)}, u32[]{:S(2)}, u32[]{:S(2)}) collective-permute-start(bf16[8,240,384]{2,1,0:T(8,128)(2,1)} %get-tuple-element.395), channel_id=1, source_target_pairs={{0,1},{1,0},{2,3},{3,2},{4,5},{5,4},{6,7},{7,6},{8,9},{9,8},{10,11... | collective-permute-start | bytes 4423688 | tf_op jit(solution)/shard_map/ppermute | solution.py:52
  380.9 36.5 %collective-permute-start.63 = (f32[8,2,576]{2,1,0:T(2,128)}, f32[8,2,576]{2,1,0:T(2,128)}, u32[]{:S(2)}, u32[]{:S(2)}) collective-permute-start(f32[8,2,576]{2,1,0:T(2,128)} %get-tuple-element.542), channel_id=1, source_target_pairs={{0,1},{1,0},{2,3},{3,2},{4,5},{5,4},{6,7},{7,6},{8,9},{9,8},{10,11... | collective-permute-start | bytes 110600 | tf_op jit(solution)/shard_map/ppermute | solution.py:52
  383.8 16.5 %collective-permute-start.56 = (bf16[4,192,384]{2,1,0:T(8,128)(2,1)}, bf16[4,192,384]{2,1,0:T(8,128)(2,1)S(1)}, u32[]{:S(2)}, u32[]{:S(2)}) collective-permute-start(bf16[4,192,384]{2,1,0:T(8,128)(2,1)} %get-tuple-element.464), channel_id=1, source_target_pairs={{0,2},{1,3},{2,0},{3,1},{4,6},{5,7},{6,4},{7,5},{8,10},{9,11},{10,... | collective-permute-start | bytes 1769480 | tf_op jit(solution)/shard_map/ppermute | solution.py:52
  406.5 19.0 %collective-permute-start.61 = (bf16[4,240,384]{2,1,0:T(8,128)(2,1)}, bf16[4,240,384]{2,1,0:T(8,128)(2,1)}, u32[]{:S(2)}, u32[]{:S(2)}) collective-permute-start(bf16[4,240,384]{2,1,0:T(8,128)(2,1)} %get-tuple-element.460), channel_id=1, source_target_pairs={{0,2},{1,3},{2,0},{3,1},{4,6},{5,7},{6,4},{7,5},{8,10},{9,11},{10,... | collective-permute-start | bytes 2211848 | tf_op jit(solution)/shard_map/ppermute | solution.py:52
  409.0 8.4 %collective-permute-start.60 = (bf16[2,192,384]{2,1,0:T(8,128)(2,1)}, bf16[2,192,384]{2,1,0:T(8,128)(2,1)S(1)}, u32[]{:S(2)}, u32[]{:S(2)}) collective-permute-start(bf16[2,192,384]{2,1,0:T(8,128)(2,1)} %get-tuple-element.476), channel_id=1, source_target_pairs={{0,4},{1,5},{2,6},{3,7},{4,0},{5,1},{6,2},{7,3},{8,12},{9,13},{10,... | collective-permute-start | bytes 884744 | tf_op jit(solution)/shard_map/ppermute | solution.py:52
  409.7 16.4 %collective-permute-start.62 = (bf16[8,144,384]{2,1,0:T(8,128)(2,1)}, bf16[8,144,384]{2,1,0:T(8,128)(2,1)}, u32[]{:S(2)}, u32[]{:S(2)}) collective-permute-start(bf16[8,144,384]{2,1,0:T(8,128)(2,1)} %get-tuple-element.413), channel_id=1, source_target_pairs={{0,1},{1,0},{2,3},{3,2},{4,5},{5,4},{6,7},{7,6},{8,9},{9,8},{10,11... | collective-permute-start | bytes 2654216 | tf_op jit(solution)/shard_map/ppermute | solution.py:52
  427.5 18.9 %collective-permute-start.66 = (bf16[4,144,384]{2,1,0:T(8,128)(2,1)S(1)}, bf16[4,144,384]{2,1,0:T(8,128)(2,1)S(1)}, u32[]{:S(2)}, u32[]{:S(2)}) collective-permute-start(bf16[4,144,384]{2,1,0:T(8,128)(2,1)S(1)} %get-tuple-element.468), channel_id=1, source_target_pairs={{0,2},{1,3},{2,0},{3,1},{4,6},{5,7},{6,4},{7,5},{8,10},{9,11},{10,... | collective-permute-start | bytes 1327112 | tf_op jit(solution)/shard_map/ppermute | solution.py:52
  431.7 14.7 %collective-permute-start.65 = (bf16[2,240,384]{2,1,0:T(8,128)(2,1)S(1)}, bf16[2,240,384]{2,1,0:T(8,128)(2,1)S(1)}, u32[]{:S(2)}, u32[]{:S(2)}) collective-permute-start(bf16[2,240,384]{2,1,0:T(8,128)(2,1)S(1)} %get-tuple-element.472), channel_id=1, source_target_pairs={{0,4},{1,5},{2,6},{3,7},{4,0},{5,1},{6,2},{7,3},{8,12},{9,13},{10,... | collective-permute-start | bytes 1105928 | tf_op jit(solution)/shard_map/ppermute | solution.py:52
  432.4 12.0 %collective-permute-start.64 = (bf16[1,192,384]{2,1,0:T(8,128)(2,1)S(1)}, bf16[1,192,384]{2,1,0:T(8,128)(2,1)S(1)}, u32[]{:S(2)}, u32[]{:S(2)}) collective-permute-start(bf16[1,192,384]{2,1,0:T(8,128)(2,1)S(1)} %get-tuple-element.502), channel_id=1, source_target_pairs={{0,8},{1,9},{2,10},{3,11},{4,12},{5,13},{6,14},{7,15},{8,0},{9,1},... | collective-permute-start | bytes 442376 | tf_op jit(solution)/shard_map/ppermute | solution.py:52
  446.4 13.3 %collective-permute-start.69 = (bf16[2,144,384]{2,1,0:T(8,128)(2,1)S(1)}, bf16[2,144,384]{2,1,0:T(8,128)(2,1)S(1)}, u32[]{:S(2)}, u32[]{:S(2)}) collective-permute-start(bf16[2,144,384]{2,1,0:T(8,128)(2,1)S(1)} %get-tuple-element.488), channel_id=1, source_target_pairs={{0,4},{1,5},{2,6},{3,7},{4,0},{5,1},{6,2},{7,3},{8,12},{9,13},{10,... | collective-permute-start | bytes 663560 | tf_op jit(solution)/shard_map/ppermute | solution.py:52
  448.0 9.5 %collective-permute-start.70 = (f32[2,2,576]{2,1,0:T(2,128)S(1)}, f32[2,2,576]{2,1,0:T(2,128)S(1)}, u32[]{:S(2)}, u32[]{:S(2)}) collective-permute-start(f32[2,2,576]{2,1,0:T(2,128)S(1)} %get-tuple-element.544), channel_id=1, source_target_pairs={{0,4},{1,5},{2,6},{3,7},{4,0},{5,1},{6,2},{7,3},{8,12},{9,13},{10,... | collective-permute-start | bytes 27656 | tf_op jit(solution)/shard_map/ppermute | solution.py:52
  448.7 11.1 %collective-permute-start.68 = (bf16[1,240,384]{2,1,0:T(8,128)(2,1)S(1)}, bf16[1,240,384]{2,1,0:T(8,128)(2,1)S(1)}, u32[]{:S(2)}, u32[]{:S(2)}) collective-permute-start(bf16[1,240,384]{2,1,0:T(8,128)(2,1)S(1)} %get-tuple-element.498), channel_id=1, source_target_pairs={{0,8},{1,9},{2,10},{3,11},{4,12},{5,13},{6,14},{7,15},{8,0},{9,1},... | collective-permute-start | bytes 552968 | tf_op jit(solution)/shard_map/ppermute | solution.py:52
  459.8 9.6 %collective-permute-start.74 = (bf16[1008,384]{1,0:T(8,128)(2,1)S(1)}, bf16[1008,384]{1,0:T(8,128)(2,1)S(1)}, u32[]{:S(2)}, u32[]{:S(2)}) collective-permute-start(bf16[1008,384]{1,0:T(8,128)(2,1)S(1)} %get-tuple-element.450), channel_id=1, source_target_pairs={{0,16},{16,0},{1,17},{17,1},{2,18},{18,2},{3,19},{19,3},{4,20},{20... | collective-permute-start | bytes 2322440 | tf_op jit(solution)/shard_map/ppermute | solution.py:63
  460.0 8.7 %collective-permute-start.71 = (bf16[1,144,384]{2,1,0:T(8,128)(2,1)S(1)}, bf16[1,144,384]{2,1,0:T(8,128)(2,1)S(1)}, u32[]{:S(2)}, u32[]{:S(2)}) collective-permute-start(bf16[1,144,384]{2,1,0:T(8,128)(2,1)S(1)} %get-tuple-element.510), channel_id=1, source_target_pairs={{0,8},{1,9},{2,10},{3,11},{4,12},{5,13},{6,14},{7,15},{8,0},{9,1},... | collective-permute-start | bytes 331784 | tf_op jit(solution)/shard_map/ppermute | solution.py:52
  (56 other events, 401.6 us)

commit v6 on v5

--- a/solution.py
+++ b/solution.py
@@ -188,6 +188,10 @@
     return raised * (1.0 / jnp.sum(raised, 0, keepdims=True))
 
 
+def room(mebibytes):
+    return pltpu.CompilerParams(vmem_limit_bytes=mebibytes << 20)
+
+
 def cost(micros):
     return pl.CostEstimate(flops=int(micros * 1.15e9), transcendentals=0, bytes_accessed=int(micros * 1e6))
 
@@ -252,6 +256,7 @@
         out_specs=[whole(2, 3, tokens, CHUNK), whole(4, tokens, CHUNK)],
         scratch_shapes=[pltpu.VMEM((width, width), LOW)],
         name="project",
+        compiler_params=room(10),
         cost_estimate=cost(14.5),
     )(slots, core, limits, hidden_low, vector_rows, *pieces)
 
@@ -279,6 +284,7 @@
         out_specs=[whole(tokens, width)] * 2,
         scratch_shapes=[pltpu.VMEM((width, width), LOW)],
         name="mix",
+        compiler_params=room(10),
         cost_estimate=cost(4.2),
     )(slots, core, context, hidden, vector_rows, *pieces)
 
@@ -321,6 +327,7 @@
         ],
         scratch_shapes=[pltpu.VMEM((width, width), LOW)],
         name="expand",
+        compiler_params=room(10),
         cost_estimate=cost(9),
     )(slots, core, first_low, vector_rows, *pieces)
 
@@ -385,6 +392,7 @@
         ),
         out_shape=[shaped(tokens, width, kind=FULL), shaped(tokens, width, kind=FULL), shaped(tokens, width)],
         name="contract",
+        compiler_params=room(17),
         cost_estimate=cost(10.8),
     )(slots, core, limits, active, first_sum, vector_rows, *[mine] * each, *[other] * each)
 
@@ -462,6 +470,7 @@
             shaped(steps, 1, width, kind=FULL),
         ],
         name="contract_back",
+        compiler_params=room(19),
         cost_estimate=cost(11),
     )(slots, core, limits, d_out, second_sum, slope, vector_rows, *[mine] * each, *[other] * each)
 
@@ -515,6 +524,7 @@
         out_specs=[whole(tokens, width), whole(1, tokens, CHUNK), whole(1, tokens, CHUNK), whole(3, width)],
         scratch_shapes=[pltpu.VMEM((width, width), LOW), pltpu.VMEM((tokens, width), FULL)],
         name="expand_back",
+        compiler_params=room(19),
         cost_estimate=cost(9.8),
     )(slots, core, kept, sent, d_second_sum, first_sum, vector_rows, *pieces)
 
@@ -564,6 +574,7 @@
         out_specs=[whole(3, tokens, CHUNK), whole(3, tokens, CHUNK), whole(2, 2, 1, CHUNK)],
         scratch_shapes=[pltpu.VMEM((width, width), LOW), pltpu.VMEM((2, tokens, CHUNK), LOW)],
         name="attend_back",
+        compiler_params=room(12),
         cost_estimate=cost(20.6),
     )(slots, core, limits, kept, sent, qkv, *pieces)
 
@@ -596,6 +607,7 @@
         out_specs=whole(tokens, width),
         scratch_shapes=[pltpu.VMEM((width, width), LOW)],
         name="project_back",
+        compiler_params=room(11),
         cost_estimate=cost(6.6),
     )(slots, core, kept, sent, d_first_sum, *pieces)
 
@@ -656,6 +668,7 @@
         in_specs=specs,
         out_specs=[whole(half, sum(parts) * rows, CHUNK)] * 2,
         name="weight_terms",
+        compiler_params=room(16),
         cost_estimate=cost(1.5 * sum(parts) if chunks == 2 else 6),
     )(*values)
 
@@ -704,26 +717,32 @@
 
 
 class Reduce:
-    def __init__(self, net):
+    def __init__(self, net, last):
         self.net = net
         self.pending = {}
         self.owned = {}
+        self.last = last
 
     def push(self, key, *parts):
         self.pending[key] = (self.net.stages - 1, list(parts))
 
     def turn(self, values=()):
-        received = [self.net.reduce(parts, stage) for stage, parts in self.pending.values()]
-        own = [parts[0] for _, parts in self.pending.values()]
+        net = self.net
+        received = {key: net.reduce(parts, stage) for key, (stage, parts) in self.pending.items()}
+        own = {key: parts[0] for key, (_, parts) in self.pending.items()}
+        if self.last in self.pending and self.pending[self.last][0] == 0:
+            kept, sent = self.pending[self.last][1]
+            received[-1, "twin"] = [net.twin(kept), net.across_twin(sent, 0)]
         own, received, values = lax.optimization_barrier((own, received, list(values)))
-        waiting = {}
-        for (key, (stage, _)), mine, others in zip(self.pending.items(), own, received):
-            parts = self.net.narrow(mine, others, stage)
-            if stage:
-                waiting[key] = (stage - 1, parts)
-            else:
-                self.owned[key] = self.net.across(parts[0][0])
-        self.pending = waiting
+        for key, (stage, _) in list(self.pending.items()):
+            parts = net.narrow(own[key], received[key], stage)
+            self.pending[key] = (stage - 1, parts)
+            if stage == 0:
+                del self.pending[key]
+                self.owned[key] = net.across(parts[0][0])
+                if (-1, "twin") in received and key == self.last:
+                    kept, sent = received[-1, "twin"]
+                    self.twin_owned = net.across(net.narrow(kept, [sent], 0)[0][0])
         return values
 
 
@@ -792,7 +811,7 @@
         kept.append((qkv, left_a, first_sum, left_b, slope, second_sum))
     layer_out = h_low
 
-    reduce = Reduce(net)
+    reduce = Reduce(net, (0, "qkv"))
     d_hidden = cotangent
     d_vectors = [None] * LAYERS
     for level in reversed(range(LAYERS)):
@@ -802,28 +821,34 @@
         d_second_sum, f_kept, u_kept, sent, sums_b, sums_u = contract_back(
             tables, d_hidden, second_sum, slope, rows, *weight(level, 3), inner_width, level == LAYERS - 1
         )
+        received = net.twin(sent)
         d_second_sum, f_kept, u_kept, sent = reduce.turn((d_second_sum, f_kept, u_kept, sent))
 
-        received = net.twin(sent)
         d_first_sum, a_kept, a_sent, sums_a = expand_back(
             tables, u_kept, sent, d_second_sum, first_sum, rows, *weight(level, 2)
         )
+        a_received = net.twin(a_sent)
         term = weight_terms(slots, count, (left_b, twin_b, 0, 2 * parts, f_kept, received, parts))
         *term, d_first_sum, a_kept, a_sent = reduce.turn((*term, d_first_sum, a_kept, a_sent))
         reduce.push((level, "down"), *term)
 
-        a_received = net.twin(a_sent)
-        q_kept, q_sent, sums_qv = attend_back(tables, a_kept, a_sent, qkv, *weight(level, 1))
         term = weight_terms(
             slots,
             count,
             (left_b, twin_b, 2 * parts, 2, u_kept, received, 0),
             (left_a, twin_a, 2, 2, a_kept, a_received, 0),
         )
-        *term, q_kept, q_sent = reduce.turn((*term, q_kept, q_sent))
-        reduce.push((level, "up"), *term)
-
+        if level == 0:
+            *term, a_kept, a_sent = reduce.turn((*term, a_kept, a_sent))
+            reduce.push((level, "up"), *term)
+        q_kept, q_sent, sums_qv = attend_back(tables, a_kept, a_sent, qkv, *weight(level, 1))
         q_received = net.twin(q_sent)
+        if level == 0:
+            q_kept, q_sent, sums_qv = reduce.turn((q_kept, q_sent, sums_qv))
+        else:
+            *term, q_kept, q_sent = reduce.turn((*term, q_kept, q_sent))
+            reduce.push((level, "up"), *term)
+
         d_vectors[level] = jnp.concatenate(
             [sums_qv.reshape(2, width), sums_a, sums_b, sums_u.reshape(-1, width)]
         ).reshape(count, -1)
@@ -836,7 +861,7 @@
         term = weight_terms(slots, count, (left_a, twin_a, 0, 2, q_kept, q_received, 0))
         *term, d_hidden = reduce.turn((*term, d_hidden))
         reduce.push((level, "qkv"), *term)
-    reduce.push("vectors", d_vector[: count // 2], d_vector[count // 2 :])
+    reduce.push((-1, "vectors"), d_vector[: count // 2], d_vector[count // 2 :])
 
     heights = {"down": inner_width // count, "up": (parts + 1) * width // count, "qkv": 3 * width // count}
     keys = [(level, name) for level in reversed(range(LAYERS)) for name in ("down", "up", "qkv")]
@@ -858,7 +883,7 @@
     finish(keys[:-1])
     while keys[-1] not in reduce.owned:
         reduce.turn()
-    finish(keys[-1:])
+    whole_grads[keys[-1]] = (reduce.owned[keys[-1]], reduce.twin_owned)
 
     def grad(name, first, parts):
         levels = []
@@ -875,7 +900,7 @@
         grad("up", parts, 1),
         grad("up", 0, parts),
         grad("down", 0, 1),
-        reduce.owned["vectors"],
+        reduce.owned[-1, "vectors"],
     )
 
 

time: 482 us -> 432 us (0.90)
  Pallas kernels: 200 us -> 144 us
  waiting for transfers between devices: 130 us -> 137 us
    pallas_call x6, Pallas kernels: 47.6 us -> 32.3 us  [weight_terms(): pl.pallas_call(body, grid=(chunks // 2,), out_shape=[shaped(half, sum(par...]
    unnamed x142 -> x220, local copies, waits for them, and re-layouts: 20.4 us -> 29.5 us
    pallas_call x2, Pallas kernels: 22 us -> 13.3 us  [contract_back(): pl.pallas_call(body, grid_spec=pltpu.PrefetchScalarGridSpec(num_scalar_pr...]
    ppermute x56, waiting for transfers between devices: 121 us -> 129 us  [trade(): return lax.ppermute(value, ('rep', 'fsdp'), pairs)]
    pallas_call x2, Pallas kernels: 21.4 us -> 14.1 us  [contract(): pl.pallas_call(body, grid_spec=pltpu.PrefetchScalarGridSpec(num_scalar_pr...]
    pallas_call x2, Pallas kernels: 19.8 us -> 13 us  [expand_back(): pl.pallas_call(body, grid=(parts,), out_shape=[shaped(tokens, width, kind...]
    convert_element_type x19 -> x18, other arithmetic: 18.2 us -> 15.7 us  [add(): return total.astype(own.dtype)]
  transfers between devices with their start and end apart: 75 -> 76, of which waited for: 31 -> 32; matrix products, arithmetic and copies ran while one was open for 9% -> 9% of each run, Pallas kernels for 41% -> 34%
where the time goes in v6:
time: 432 us; the launch traced here: 427 us
  Pallas kernels  144 us (33%)
  waiting for transfers between devices  137 us (32%)
  starting transfers between devices  70.5 us (16%)
  local copies, waits for them, and re-layouts  45.5 us (11%)
  other arithmetic  27.9 us (6%)
    ppermute x56, waiting for transfers between devices, trade(): return lax.ppermute(value, ('rep', 'fsdp'), pairs)  129 us
    ppermute x56, starting transfers between devices, trade(): return lax.ppermute(value, ('rep', 'fsdp'), pairs)  67 us
    pallas_call x6, Pallas kernels, weight_terms(): pl.pallas_call(body, grid=(chunks // 2,), out_shape=[shaped(half, sum(par...  32.3 us
    unnamed x220, local copies, waits for them, and re-layouts  29.5 us
    pallas_call x2, Pallas kernels, attend_back(): pl.pallas_call(body, grid=(1,), out_shape=[shaped(3, tokens, CHUNK), shap...  24.5 us
    pallas_call x2, Pallas kernels, project(): pl.pallas_call(body, grid=(3,), out_shape=[shaped(2, 3, tokens, CHUNK), s...  16.9 us
    convert_element_type x18, other arithmetic, add(): return total.astype(own.dtype)  15.7 us
    pallas_call x2, Pallas kernels, expand(): pl.pallas_call(body, grid=(parts + 1,), out_shape=[shaped(2 * parts + 2,...  14.4 us
  transfers between devices with their start and end apart: 76, of which 32 were waited for; matrix products, arithmetic and copies ran while one was open for 9% of the time, Pallas kernels for 34%

profile of v6, /device:TPU:0, one launch (start us, length us, event | category | flops | bytes accessed | tf_op | source)
XLA Modules:
  0.0 427.1 jit_solution(8476067292926928425)
XLA Ops:
  2.1 4.1 collective-permute-start
  10.1 1.7 collective-permute-done.1
  12.7 3.4 collective-permute-start.3
  16.1 6.5 %collective-permute-done.4 = f32[2,2,576]{2,1,0:T(2,128)S(1)} collective-permute-done((f32[2,2,576]{2,1,0:T(2,128)S(1)}, f32[2,2,576]{2,1,0:T(2,128)S(1)}, u32[]{:S(2)}, u32[]{:S(2)}) %collective-permute-start.4) | collective-permute-done | bytes 9248 | tf_op jit(solution)/shard_map/ppermute | solution.py:52
  24.2 3.3 collective-permute-start.6
  27.5 1.9 collective-permute-start.7
  29.9 3.3 collective-permute-done.8
  33.8 4.0 collective-permute-done.7
  39.4 1.6 collective-permute-start.10
  41.0 1.9 collective-permute-start.11
  46.0 14.2 %collective-permute-done.13 = f32[8,2,576]{2,1,0:T(2,128)} collective-permute-done((f32[8,2,576]{2,1,0:T(2,128)}, f32[8,2,576]{2,1,0:T(2,128)}, u32[]{:S(2)}, u32[]{:S(2)}) %collective-permute-start.13) | collective-permute-done | bytes 36896 | tf_op jit(solution)/shard_map/ppermute | solution.py:52
  74.5 8.2 %project.2 = (bf16[2,3,512,384]{3,2,1,0:T(8,128)(2,1)S(1)}, bf16[4,512,384]{2,1,0:T(8,128)(2,1)S(1)}) custom-call(s32[2,16]{1,0:T(2,128)S(1)} %select_reduce_fusion.slots_ref, s32[1]{0:T(128)} %bitcast.core_ref, s32[4]{0:T(128)S(1)} %copy-done.21, bf16[512,768]{1,0:T(8,128)(2,1)S(1)} %copy-done.19, f32[12,768]{1,0:T(8,128)S(1)} %squeeze.21.rows_ref, ...), custom_call_target="tpu_custom_call" | custom-call | flops 16675000320 | bytes 14500000 | tf_op jit(solution)/shard_map/project/pallas_call | solution.py:251
  84.3 7.3 %collective-permute-done.14 = bf16[8,240,384]{2,1,0:T(8,128)(2,1)} collective-permute-done((bf16[8,240,384]{2,1,0:T(8,128)(2,1)}, bf16[8,240,384]{2,1,0:T(8,128)(2,1)}, u32[]{:S(2)}, u32[]{:S(2)}) %collective-permute-start.14) | collective-permute-done | bytes 1474592 | tf_op jit(solution)/shard_map/ppermute | solution.py:52
  93.1 1.7 constant_dynamic-update-slice_fusion.26.refs_0_
  94.9 1.7 constant_dynamic-update-slice_fusion.20
  104.5 1.9 mix.2
  106.5 7.8 %expand.2 = (bf16[10,512,384]{2,1,0:T(8,128)(2,1)}, bf16[8,512,384]{2,1,0:T(8,128)(2,1)S(1)}) custom-call(s32[2,16]{1,0:T(2,128)S(1)} %select_reduce_fusion.slots_ref, s32[1]{0:T(128)} %bitcast.core_ref, bf16[512,768]{1,0:T(8,128)(2,1)S(1)} %get-tuple-element.282.x_ref, f32[12,768]{1,0:T(8,128)S(1)} %squeeze.21.rows_ref, ...), custom_call_target="tpu_custom_call" | custom-call | flops 10350000128 | bytes 9000000 | tf_op jit(solution)/shard_map/expand/pallas_call | solution.py:317
  114.2 1.8 copy-done.26
  116.0 3.2 collective-permute-done.19
  123.4 1.9 collective-permute-done.28.refs_4_.refs_5_.refs_6_.refs_7_
  125.4 7.1 %contract.2 = (f32[512,768]{1,0:T(8,128)S(1)}, f32[512,768]{1,0:T(8,128)S(1)}, bf16[512,768]{1,0:T(8,128)(2,1)S(1)}) custom-call(s32[2,16]{1,0:T(2,128)S(1)} %select_reduce_fusion.slots_ref, s32[1]{0:T(128)} %bitcast.core_ref, s32[4]{0:T(128)S(1)} %copy-done.21, bf16[10,512,384]{2,1,0:T(8,128)(2,1)} %get-tuple-element.291.active_ref.refs_0_, ...), custom_call_target="tpu_custom_call" | custom-call | flops 12419999744 | bytes 10800000 | tf_op jit(solution)/shard_map/contract/pallas_call | solution.py:378
  132.5 5.2 %collective-permute-done.26 = bf16[4,192,384]{2,1,0:T(8,128)(2,1)S(1)} collective-permute-done((bf16[4,192,384]{2,1,0:T(8,128)(2,1)S(1)}, bf16[4,192,384]{2,1,0:T(8,128)(2,1)S(1)}, u32[]{:S(2)}, u32[]{:S(2)}) %collective-permute-start.26) | collective-permute-done | bytes 589856 | tf_op jit(solution)/shard_map/ppermute | solution.py:52
  137.7 5.6 %collective-permute-done.25 = bf16[8,192,384]{2,1,0:T(8,128)(2,1)S(1)} collective-permute-done((bf16[8,192,384]{2,1,0:T(8,128)(2,1)S(1)}, bf16[8,192,384]{2,1,0:T(8,128)(2,1)S(1)}, u32[]{:S(2)}, u32[]{:S(2)}) %collective-permute-start.25) | collective-permute-done | bytes 1179680 | tf_op jit(solution)/shard_map/ppermute | solution.py:52
  150.6 8.7 %project.3 = (bf16[2,3,512,384]{3,2,1,0:T(8,128)(2,1)S(1)}, bf16[4,512,384]{2,1,0:T(8,128)(2,1)S(1)}) custom-call(s32[2,16]{1,0:T(2,128)S(1)} %select_reduce_fusion.slots_ref, s32[1]{0:T(128)} %bitcast.core_ref, s32[4]{0:T(128)S(1)} %copy-done.21, bf16[512,768]{1,0:T(8,128)(2,1)S(1)} %get-tuple-element.300.x_ref, f32[12,768]{1,0:T(8,128)S(1)} %squeeze.22.rows_ref, ...), custom_call_target="tpu_custom_call" | custom-call | flops 16675000320 | bytes 14500000 | tf_op jit(solution)/shard_map/project/pallas_call | solution.py:251
  159.3 5.6 %collective-permute-done.30 = bf16[4,192,384]{2,1,0:T(8,128)(2,1)S(1)} collective-permute-done((bf16[4,192,384]{2,1,0:T(8,128)(2,1)S(1)}, bf16[4,192,384]{2,1,0:T(8,128)(2,1)S(1)}, u32[]{:S(2)}, u32[]{:S(2)}) %collective-permute-start.30) | collective-permute-done | bytes 589856 | tf_op jit(solution)/shard_map/ppermute | solution.py:52
  165.0 4.8 %collective-permute-done.29 = bf16[8,192,384]{2,1,0:T(8,128)(2,1)S(1)} collective-permute-done((bf16[8,192,384]{2,1,0:T(8,128)(2,1)S(1)}, bf16[8,192,384]{2,1,0:T(8,128)(2,1)S(1)}, u32[]{:S(2)}, u32[]{:S(2)}) %collective-permute-start.29) | collective-permute-done | bytes 1179680 | tf_op jit(solution)/shard_map/ppermute | solution.py:52
  171.6 2.6 mix.3
  174.8 6.6 %expand.3 = (bf16[10,512,384]{2,1,0:T(8,128)(2,1)S(1)}, bf16[8,512,384]{2,1,0:T(8,128)(2,1)S(1)}) custom-call(s32[2,16]{1,0:T(2,128)S(1)} %select_reduce_fusion.slots_ref, s32[1]{0:T(128)} %bitcast.core_ref, bf16[512,768]{1,0:T(8,128)(2,1)S(1)} %get-tuple-element.308.x_ref, f32[12,768]{1,0:T(8,128)S(1)} %squeeze.22.rows_ref, ...), custom_call_target="tpu_custom_call" | custom-call | flops 10350000128 | bytes 9000000 | tf_op jit(solution)/shard_map/expand/pallas_call | solution.py:317
  181.4 5.8 %collective-permute-done.33 = bf16[8,192,384]{2,1,0:T(8,128)(2,1)S(1)} collective-permute-done((bf16[8,192,384]{2,1,0:T(8,128)(2,1)S(1)}, bf16[8,192,384]{2,1,0:T(8,128)(2,1)S(1)}, u32[]{:S(2)}, u32[]{:S(2)}) %collective-permute-start.33) | collective-permute-done | bytes 1179680 | tf_op jit(solution)/shard_map/ppermute | solution.py:52
  188.2 4.0 collective-permute-done.36.refs_4_.refs_5_.refs_6_.refs_7_
  192.2 7.0 %contract.3 = (f32[512,768]{1,0:T(8,128)S(1)}, f32[512,768]{1,0:T(8,128)}, bf16[512,768]{1,0:T(8,128)(2,1)}) custom-call(s32[2,16]{1,0:T(2,128)S(1)} %select_reduce_fusion.slots_ref, s32[1]{0:T(128)} %bitcast.core_ref, s32[4]{0:T(128)S(1)} %copy-done.21, bf16[10,512,384]{2,1,0:T(8,128)(2,1)S(1)} %get-tuple-element.313.active_ref.refs_0_, ...), custom_call_target="tpu_custom_call" | custom-call | flops 12419999744 | bytes 10800000 | tf_op jit(solution)/shard_map/contract/pallas_call | solution.py:378
  199.2 6.1 %contract_back.2 = (f32[512,768]{1,0:T(8,128)S(1)}, bf16[1,512,384]{2,1,0:T(8,128)(2,1)S(1)}, bf16[4,512,384]{2,1,0:T(8,128)(2,1)S(1)}, bf16[5,512,384]{2,1,0:T(...) custom-call(s32[2,16]{1,0:T(2,128)S(1)} %select_reduce_fusion.slots_ref, s32[1]{0:T(128)} %bitcast.core_ref, ...), custom_call_target="tpu_custom_call" | custom-call | flops 12650000384 | bytes 11000000 | tf_op jit(solution)/shard_map/contract_back/pallas_call | solution.py:441
  205.5 6.3 %expand_back.2 = (f32[512,768]{1,0:T(8,128)S(1)}, bf16[1,512,384]{2,1,0:T(8,128)(2,1)S(1)}, bf16[1,512,384]{2,1,0:T(8,128)(2,1)S(1)}, f32[3,768]{1,0:T(4,128)S(1)}) custom-call(s32[2,16]{1,0:T(2,128)S(1)} %select_reduce_fusion.slots_ref, s32[1]{0:T(128)} %bitcast.core_ref, bf16[4,512,384]{2,1,0:T(8,128)(2,1)S(1)} %get-tuple-element.327.kept_ref.refs_2_, ...), custom_call_target="tpu_custom_call" | custom-call | flops 11269999616 | bytes 9800000 | tf_op jit(solution)/shard_map/expand_back/pallas_call | solution.py:512
  212.2 4.7 %weight_terms.6 = (bf16[8,192,384]{2,1,0:T(8,128)(2,1)S(1)}, bf16[8,192,384]{2,1,0:T(8,128)(2,1)S(1)}) custom-call(s32[2,16]{1,0:T(2,128)S(1)} %select_reduce_fusion.slots_ref, bf16[10,512,384]{2,1,0:T(8,128)(2,1)S(1)} %get-tuple-element.313.active_ref.refs_0_, bf16[10,512,384]{2,1,0:T(8,128)(2,1)S(1)} %collective-permute-done.37.refs_1_, ...), custom_call_target="tpu_custom_call" | custom-call | flops 6899999744 | bytes 6000000 | tf_op jit(solution)/shard_map/weight_terms/pallas_call | solution.py:664
  217.3 12.1 %attend_back.2 = (bf16[3,512,384]{2,1,0:T(8,128)(2,1)S(1)}, bf16[3,512,384]{2,1,0:T(8,128)(2,1)S(1)}, f32[2,2,1,384]{3,2,1,0:T(1,128)S(1)}) custom-call(s32[2,16]{1,0:T(2,128)S(1)} %select_reduce_fusion.slots_ref, s32[1]{0:T(128)} %bitcast.core_ref, s32[4]{0:T(128)S(1)} %copy-done.21, bf16[1,512,384]{2,1,0:T(8,128)(2,1)S(1)} %get-tuple-element.336.refs_6_.kept_ref, ...), custom_call_target="tpu_custom_call" | custom-call | flops 23690000384 | bytes 20600000 | tf_op jit(solution)/shard_map/attend_back/pallas_call | solution.py:567
  229.7 5.4 %weight_terms.7 = (bf16[8,240,384]{2,1,0:T(8,128)(2,1)S(1)}, bf16[8,240,384]{2,1,0:T(8,128)(2,1)S(1)}) custom-call(s32[2,16]{1,0:T(2,128)S(1)} %select_reduce_fusion.slots_ref, bf16[10,512,384]{2,1,0:T(8,128)(2,1)S(1)} %get-tuple-element.313.active_ref.refs_0_, bf16[10,512,384]{2,1,0:T(8,128)(2,1)S(1)} %collective-permute-done.37.refs_1_, ...), custom_call_target="tpu_custom_call" | custom-call | flops 8625000448 | bytes 7500000 | tf_op jit(solution)/shard_map/weight_terms/pallas_call | solution.py:664
  235.1 1.7 collective-permute-start.42
  237.7 5.0 %project_back.2.d_out_ref = f32[512,768]{1,0:T(8,128)S(1)} custom-call(s32[2,16]{1,0:T(2,128)S(1)} %select_reduce_fusion.slots_ref, s32[1]{0:T(128)} %bitcast.core_ref, bf16[3,512,384]{2,1,0:T(8,128)(2,1)S(1)} %get-tuple-element.347.refs_2_.kept_ref, bf16[3,512,384]{2,1,0:T(8,128)(2,1)S(1)} %get-tuple-element.350.sent_ref, ...), custom_call_target="tpu_custom_call" | custom-call | flops 7590000128 | bytes 6600000 | tf_op jit(solution)/shard_map/project_back/pallas_call | solution.py:602
  242.8 4.5 %weight_terms.8 = (bf16[8,144,384]{2,1,0:T(8,128)(2,1)S(1)}, bf16[8,144,384]{2,1,0:T(8,128)(2,1)}) custom-call(s32[2,16]{1,0:T(2,128)S(1)} %select_reduce_fusion.slots_ref, bf16[4,512,384]{2,1,0:T(8,128)(2,1)S(1)} %get-tuple-element.306.context_ref.refs_4_.refs_0_, bf16[4,512,384]{2,1,0:T(8,128)(2,1)S(1)} %collective-permute-done.35.refs_5_.refs_1_, ...), custom_call_target="tpu_custom_call" | custom-call | flops 5175000064 | bytes 4500000 | tf_op jit(solution)/shard_map/weight_terms/pallas_call | solution.py:664
  247.3 6.2 %collective-permute-done.41 = bf16[4,192,384]{2,1,0:T(8,128)(2,1)S(1)} collective-permute-done((bf16[4,192,384]{2,1,0:T(8,128)(2,1)S(1)}, bf16[4,192,384]{2,1,0:T(8,128)(2,1)S(1)}, u32[]{:S(2)}, u32[]{:S(2)}) %collective-permute-start.41) | collective-permute-done | bytes 589856 | tf_op jit(solution)/shard_map/ppermute | solution.py:52
  253.4 7.4 %collective-permute-done.42 = bf16[8,240,384]{2,1,0:T(8,128)(2,1)S(1)} collective-permute-done((bf16[8,240,384]{2,1,0:T(8,128)(2,1)S(1)}, bf16[8,240,384]{2,1,0:T(8,128)(2,1)S(1)}, u32[]{:S(2)}, u32[]{:S(2)}) %collective-permute-start.42) | collective-permute-done | bytes 1474592 | tf_op jit(solution)/shard_map/ppermute | solution.py:52
  266.9 7.2 %contract_back.3 = (f32[512,768]{1,0:T(8,128)S(1)}, bf16[1,512,384]{2,1,0:T(8,128)(2,1)S(1)}, bf16[4,512,384]{2,1,0:T(8,128)(2,1)S(1)}, bf16[5,512,384]{2,1,0:T(...) custom-call(s32[2,16]{1,0:T(2,128)S(1)} %select_reduce_fusion.slots_ref, s32[1]{0:T(128)} %bitcast.core_ref, ...), custom_call_target="tpu_custom_call" | custom-call | flops 12650000384 | bytes 11000000 | tf_op jit(solution)/shard_map/contract_back/pallas_call | solution.py:441
  277.5 5.3 %collective-permute-done.46 = bf16[4,240,384]{2,1,0:T(8,128)(2,1)} collective-permute-done((bf16[4,240,384]{2,1,0:T(8,128)(2,1)}, bf16[4,240,384]{2,1,0:T(8,128)(2,1)}, u32[]{:S(2)}, u32[]{:S(2)}) %collective-permute-start.46) | collective-permute-done | bytes 737312 | tf_op jit(solution)/shard_map/ppermute | solution.py:52
  282.8 1.8 collective-permute-done.45
  293.2 1.8 copy-done.5
  297.9 6.7 %expand_back.3 = (f32[512,768]{1,0:T(8,128)S(1)}, bf16[1,512,384]{2,1,0:T(8,128)(2,1)S(1)}, bf16[1,512,384]{2,1,0:T(8,128)(2,1)S(1)}, f32[3,768]{1,0:T(4,128)S(1)}) custom-call(s32[2,16]{1,0:T(2,128)S(1)} %select_reduce_fusion.slots_ref, s32[1]{0:T(128)} %bitcast.core_ref, bf16[4,512,384]{2,1,0:T(8,128)(2,1)S(1)} %copy-done.32, ...), custom_call_target="tpu_custom_call" | custom-call | flops 11269999616 | bytes 9800000 | tf_op jit(solution)/shard_map/expand_back/pallas_call | solution.py:512
  305.8 6.6 %weight_terms.9 = (bf16[8,192,384]{2,1,0:T(8,128)(2,1)S(1)}, bf16[8,192,384]{2,1,0:T(8,128)(2,1)S(1)}) custom-call(s32[2,16]{1,0:T(2,128)S(1)} %select_reduce_fusion.slots_ref, bf16[10,512,384]{2,1,0:T(8,128)(2,1)} %get-tuple-element.291.active_ref.refs_0_, bf16[10,512,384]{2,1,0:T(8,128)(2,1)} %collective-permute-done.32.refs_1_, ...), custom_call_target="tpu_custom_call" | custom-call | flops 6899999744 | bytes 6000000 | tf_op jit(solution)/shard_map/weight_terms/pallas_call | solution.py:664
  315.7 6.6 %weight_terms.10 = (bf16[8,240,384]{2,1,0:T(8,128)(2,1)S(1)}, bf16[8,240,384]{2,1,0:T(8,128)(2,1)S(1)}) custom-call(s32[2,16]{1,0:T(2,128)S(1)} %select_reduce_fusion.slots_ref, bf16[10,512,384]{2,1,0:T(8,128)(2,1)} %get-tuple-element.291.active_ref.refs_0_, bf16[10,512,384]{2,1,0:T(8,128)(2,1)} %collective-permute-done.32.refs_1_, ...), custom_call_target="tpu_custom_call" | custom-call | flops 8625000448 | bytes 7500000 | tf_op jit(solution)/shard_map/weight_terms/pallas_call | solution.py:664
  322.3 3.1 collective-permute-done.53
  325.4 3.3 collective-permute-done.51
  330.5 1.6 collective-permute-start.56
  332.1 12.4 %attend_back.3 = (bf16[3,512,384]{2,1,0:T(8,128)(2,1)S(1)}, bf16[3,512,384]{2,1,0:T(8,128)(2,1)}, f32[2,2,1,384]{3,2,1,0:T(1,128)S(1)}) custom-call(s32[2,16]{1,0:T(2,128)S(1)} %select_reduce_fusion.slots_ref, s32[1]{0:T(128)} %bitcast.core_ref, s32[4]{0:T(128)S(1)} %copy-done.21, bf16[1,512,384]{2,1,0:T(8,128)(2,1)S(1)} %get-tuple-element.398.refs_6_.kept_ref, ...), custom_call_target="tpu_custom_call" | custom-call | flops 23690000384 | bytes 20600000 | tf_op jit(solution)/shard_map/attend_back/pallas_call | solution.py:567
  346.6 7.3 %collective-permute-done.57 = bf16[1,144,384]{2,1,0:T(8,128)(2,1)S(1)} collective-permute-done((bf16[1,144,384]{2,1,0:T(8,128)(2,1)S(1)}, bf16[1,144,384]{2,1,0:T(8,128)(2,1)S(1)}, u32[]{:S(2)}, u32[]{:S(2)}) %collective-permute-start.57) | collective-permute-done | bytes 110624 | tf_op jit(solution)/shard_map/ppermute | solution.py:52
  357.4 2.0 add_convert_fusion.16
  363.1 4.5 %weight_terms.11 = (bf16[8,144,384]{2,1,0:T(8,128)(2,1)S(1)}, bf16[8,144,384]{2,1,0:T(8,128)(2,1)S(1)}) custom-call(s32[2,16]{1,0:T(2,128)S(1)} %select_reduce_fusion.slots_ref, bf16[4,512,384]{2,1,0:T(8,128)(2,1)S(1)} %copy-done.13, bf16[4,512,384]{2,1,0:T(8,128)(2,1)S(1)} %copy-done.16, bf16[3,512,384]{2,1,0:T(8,128)(2,1)S(1)} %copy-done.29, ...), custom_call_target="tpu_custom_call" | custom-call | flops 5175000064 | bytes 4500000 | tf_op jit(solution)/shard_map/weight_terms/pallas_call | solution.py:664
  370.2 3.7 collective-permute-done.60
  381.4 5.6 %project_back.3 = f32[512,768]{1,0:T(8,128)} custom-call(s32[2,16]{1,0:T(2,128)S(1)} %select_reduce_fusion.slots_ref, s32[1]{0:T(128)} %bitcast.core_ref, bf16[3,512,384]{2,1,0:T(8,128)(2,1)S(1)} %copy-done.30, bf16[3,512,384]{2,1,0:T(8,128)(2,1)} %get-tuple-element.425.sent_ref, f32[512,768]{1,0:T(8,128)S(1)} %copy-done.35, ...), custom_call_target="tpu_custom_call" | custom-call | flops 7590000128 | bytes 6600000 | tf_op jit(solution)/shard_map/project_back/pallas_call | solution.py:602
  387.1 2.9 collective-permute-done.65
  393.9 7.6 %collective-permute-done.68 = bf16[1,240,384]{2,1,0:T(8,128)(2,1)S(1)} collective-permute-done((bf16[1,240,384]{2,1,0:T(8,128)(2,1)S(1)}, bf16[1,240,384]{2,1,0:T(8,128)(2,1)S(1)}, u32[]{:S(2)}, u32[]{:S(2)}) %collective-permute-start.68) | collective-permute-done | bytes 184352 | tf_op jit(solution)/shard_map/ppermute | solution.py:52
  401.7 2.1 collective-permute-start.70
  405.4 2.6 collective-permute-done.70
  408.2 2.0 collective-permute-start.74
  410.9 1.9 collective-permute-start.73
  413.0 7.7 %collective-permute-done.73 = f32[1,2,576]{2,1,0:T(2,128)S(1)} collective-permute-done((f32[1,2,576]{2,1,0:T(2,128)S(1)}, f32[1,2,576]{2,1,0:T(2,128)S(1)}, u32[]{:S(2)}, u32[]{:S(2)}) %collective-permute-start.73) | collective-permute-done | bytes 4640 | tf_op jit(solution)/shard_map/ppermute | solution.py:52
  (447 shorter events, 114.4 us)
Async XLA Ops:
  2.1 9.8 %collective-permute-start = (bf16[1,144,384]{2,1,0:T(8,128)(2,1)S(1)}, bf16[1,144,384]{2,1,0:T(8,128)(2,1)S(1)}, u32[]{:S(2)}, u32[]{:S(2)}) collective-permute-start(bf16[1,144,384]{2,1,0:T(8,128)(2,1)S(1)} %bitcast.82), channel_id=1, source_target_pairs={{0,8},{1,9},{2,10},{3,11},{4,12},{5,13},{6,14},{7,15},{8,0},{9,1},... | collective-permute-start | bytes 331784 | tf_op jit(solution)/shard_map/ppermute | solution.py:52
  11.9 10.8 %collective-permute-start.2 = (bf16[2,144,384]{2,1,0:T(8,128)(2,1)S(1)}, bf16[2,144,384]{2,1,0:T(8,128)(2,1)S(1)}, u32[]{:S(2)}, u32[]{:S(2)}) collective-permute-start(bf16[2,144,384]{2,1,0:T(8,128)(2,1)S(1)} %constant_dynamic-update-slice_fusion), channel_id=1, source_target_pairs={{0,4},{1,5},{2,6},{3,7},{4,0},{5,1},{6,2},{7,3},{8,12},{9,13},{10,... | collective-permute-start | bytes 663560 | tf_op jit(solution)/shard_map/ppermute | solution.py:52
  12.7 10.0 %collective-permute-start.3 = (bf16[1,240,384]{2,1,0:T(8,128)(2,1)S(1)}, bf16[1,240,384]{2,1,0:T(8,128)(2,1)S(1)}, u32[]{:S(2)}, u32[]{:S(2)}) collective-permute-start(bf16[1,240,384]{2,1,0:T(8,128)(2,1)S(1)} %maximum_bitcast_fusion), channel_id=1, source_target_pairs={{0,8},{1,9},{2,10},{3,11},{4,12},{5,13},{6,14},{7,15},{8,0},{9,1},... | collective-permute-start | bytes 552968 | tf_op jit(solution)/shard_map/ppermute | solution.py:52
  22.8 15.7 %collective-permute-start.5 = (bf16[4,144,384]{2,1,0:T(8,128)(2,1)S(1)}, bf16[4,144,384]{2,1,0:T(8,128)(2,1)S(1)}, u32[]{:S(2)}, u32[]{:S(2)}) collective-permute-start(bf16[4,144,384]{2,1,0:T(8,128)(2,1)S(1)} %constant_dynamic-update-slice_fusion.2), channel_id=1, source_target_pairs={{0,2},{1,3},{2,0},{3,1},{4,6},{5,7},{6,4},{7,5},{8,10},{9,11},{10,... | collective-permute-start | bytes 1327112 | tf_op jit(solution)/shard_map/ppermute | solution.py:52
  24.2 14.3 %collective-permute-start.6 = (bf16[2,240,384]{2,1,0:T(8,128)(2,1)S(1)}, bf16[2,240,384]{2,1,0:T(8,128)(2,1)S(1)}, u32[]{:S(2)}, u32[]{:S(2)}) collective-permute-start(bf16[2,240,384]{2,1,0:T(8,128)(2,1)S(1)} %constant_dynamic-update-slice_fusion.4), channel_id=1, source_target_pairs={{0,4},{1,5},{2,6},{3,7},{4,0},{5,1},{6,2},{7,3},{8,12},{9,13},{10,... | collective-permute-start | bytes 1105928 | tf_op jit(solution)/shard_map/ppermute | solution.py:52
  27.5 10.2 %collective-permute-start.7 = (bf16[1,192,384]{2,1,0:T(8,128)(2,1)S(1)}, bf16[1,192,384]{2,1,0:T(8,128)(2,1)S(1)}, u32[]{:S(2)}, u32[]{:S(2)}) collective-permute-start(bf16[1,192,384]{2,1,0:T(8,128)(2,1)S(1)} %constant_dynamic-slice_fusion.8), channel_id=1, source_target_pairs={{0,8},{1,9},{2,10},{3,11},{4,12},{5,13},{6,14},{7,15},{8,0},{9,1},... | collective-permute-start | bytes 442376 | tf_op jit(solution)/shard_map/ppermute | solution.py:52
  38.6 23.9 %collective-permute-start.9 = (bf16[8,144,384]{2,1,0:T(8,128)(2,1)S(1)}, bf16[8,144,384]{2,1,0:T(8,128)(2,1)S(1)}, u32[]{:S(2)}, u32[]{:S(2)}) collective-permute-start(bf16[8,144,384]{2,1,0:T(8,128)(2,1)S(1)} %constant_dynamic-update-slice_fusion.6), channel_id=1, source_target_pairs={{0,1},{1,0},{2,3},{3,2},{4,5},{5,4},{6,7},{7,6},{8,9},{9,8},{10,11... | collective-permute-start | bytes 2654216 | tf_op jit(solution)/shard_map/ppermute | solution.py:52
  39.4 22.3 %collective-permute-start.10 = (bf16[4,240,384]{2,1,0:T(8,128)(2,1)S(1)}, bf16[4,240,384]{2,1,0:T(8,128)(2,1)S(1)}, u32[]{:S(2)}, u32[]{:S(2)}) collective-permute-start(bf16[4,240,384]{2,1,0:T(8,128)(2,1)S(1)} %constant_dynamic-update-slice_fusion.8), channel_id=1, source_target_pairs={{0,2},{1,3},{2,0},{3,1},{4,6},{5,7},{6,4},{7,5},{8,10},{9,11},{10,... | collective-permute-start | bytes 2211848 | tf_op jit(solution)/shard_map/ppermute | solution.py:52
  41.0 20.6 %collective-permute-start.11 = (bf16[2,192,384]{2,1,0:T(8,128)(2,1)S(1)}, bf16[2,192,384]{2,1,0:T(8,128)(2,1)}, u32[]{:S(2)}, u32[]{:S(2)}) collective-permute-start(bf16[2,192,384]{2,1,0:T(8,128)(2,1)S(1)} %constant_dynamic-update-slice_fusion.10), channel_id=1, source_target_pairs={{0,4},{1,5},{2,6},{3,7},{4,0},{5,1},{6,2},{7,3},{8,12},{9,13},{10,... | collective-permute-start | bytes 884744 | tf_op jit(solution)/shard_map/ppermute | solution.py:52
  42.9 17.3 %collective-permute-start.13 = (f32[8,2,576]{2,1,0:T(2,128)}, f32[8,2,576]{2,1,0:T(2,128)}, u32[]{:S(2)}, u32[]{:S(2)}) collective-permute-start(f32[8,2,576]{2,1,0:T(2,128)} %pad_maximum_fusion.8), channel_id=1, source_target_pairs={{0,1},{1,0},{2,3},{3,2},{4,5},{5,4},{6,7},{7,6},{8,9},{9,8},{10,11... | collective-permute-start | bytes 110600 | tf_op jit(solution)/shard_map/ppermute | solution.py:52
  44.4 17.3 %collective-permute-start.12 = (bf16[1,192,384]{2,1,0:T(8,128)(2,1)}, bf16[1,192,384]{2,1,0:T(8,128)(2,1)}, u32[]{:S(2)}, u32[]{:S(2)}) collective-permute-start(bf16[1,192,384]{2,1,0:T(8,128)(2,1)} %maximum_bitcast_fusion.1), channel_id=1, source_target_pairs={{0,8},{1,9},{2,10},{3,11},{4,12},{5,13},{6,14},{7,15},{8,0},{9,1},... | collective-permute-start | bytes 442376 | tf_op jit(solution)/shard_map/ppermute | solution.py:52
  62.9 11.6 %collective-permute-start.18 = (bf16[16,144,384]{2,1,0:T(8,128)(2,1)S(1)}, bf16[16,144,384]{2,1,0:T(8,128)(2,1)}, u32[]{:S(2)}, u32[]{:S(2)}) collective-permute-start(bf16[16,144,384]{2,1,0:T(8,128)(2,1)S(1)} %constant_dynamic-update-slice_fusion.18.refs_0_), channel_id=1, source_target_pairs={{0,16},{16,0},{1,17},{17,1},{2,18},{18,2},{3,19},{19,3},{4,20},{20... | collective-permute-start | bytes 5308424 | tf_op jit(solution)/shard_map/ppermute | solution.py:63
  65.6 26.0 %collective-permute-start.14 = (bf16[8,240,384]{2,1,0:T(8,128)(2,1)}, bf16[8,240,384]{2,1,0:T(8,128)(2,1)}, u32[]{:S(2)}, u32[]{:S(2)}) collective-permute-start(bf16[8,240,384]{2,1,0:T(8,128)(2,1)} %constant_dynamic-update-slice_fusion.12), channel_id=1, source_target_pairs={{0,1},{1,0},{2,3},{3,2},{4,5},{5,4},{6,7},{7,6},{8,9},{9,8},{10,11... | collective-permute-start | bytes 4423688 | tf_op jit(solution)/shard_map/ppermute | solution.py:52
  66.9 17.3 %collective-permute-start.15 = (bf16[4,192,384]{2,1,0:T(8,128)(2,1)S(1)}, bf16[4,192,384]{2,1,0:T(8,128)(2,1)}, u32[]{:S(2)}, u32[]{:S(2)}) collective-permute-start(bf16[4,192,384]{2,1,0:T(8,128)(2,1)S(1)} %constant_dynamic-update-slice_fusion.14), channel_id=1, source_target_pairs={{0,2},{1,3},{2,0},{3,1},{4,6},{5,7},{6,4},{7,5},{8,10},{9,11},{10,... | collective-permute-start | bytes 1769480 | tf_op jit(solution)/shard_map/ppermute | solution.py:52
  70.5 13.8 %collective-permute-start.16 = (bf16[2,192,384]{2,1,0:T(8,128)(2,1)}, bf16[2,192,384]{2,1,0:T(8,128)(2,1)}, u32[]{:S(2)}, u32[]{:S(2)}) collective-permute-start(bf16[2,192,384]{2,1,0:T(8,128)(2,1)} %constant_dynamic-update-slice_fusion.16), channel_id=1, source_target_pairs={{0,4},{1,5},{2,6},{3,7},{4,0},{5,1},{6,2},{7,3},{8,12},{9,13},{10,... | collective-permute-start | bytes 884744 | tf_op jit(solution)/shard_map/ppermute | solution.py:52
  71.9 12.3 %collective-permute-start.17 = (bf16[1,192,384]{2,1,0:T(8,128)(2,1)S(1)}, bf16[1,192,384]{2,1,0:T(8,128)(2,1)}, u32[]{:S(2)}, u32[]{:S(2)}) collective-permute-start(bf16[1,192,384]{2,1,0:T(8,128)(2,1)S(1)} %bitcast.74), channel_id=1, source_target_pairs={{0,8},{1,9},{2,10},{3,11},{4,12},{5,13},{6,14},{7,15},{8,0},{9,1},... | collective-permute-start | bytes 442376 | tf_op jit(solution)/shard_map/ppermute | solution.py:52
  96.6 22.6 %collective-permute-start.19 = (bf16[8,192,384]{2,1,0:T(8,128)(2,1)S(1)}, bf16[8,192,384]{2,1,0:T(8,128)(2,1)S(1)}, u32[]{:S(2)}, u32[]{:S(2)}) collective-permute-start(bf16[8,192,384]{2,1,0:T(8,128)(2,1)S(1)} %constant_dynamic-update-slice_fusion.20), channel_id=1, source_target_pairs={{0,1},{1,0},{2,3},{3,2},{4,5},{5,4},{6,7},{7,6},{8,9},{9,8},{10,11... | collective-permute-start | bytes 3538952 | tf_op jit(solution)/shard_map/ppermute | solution.py:52
  97.0 22.2 %collective-permute-start.24 = (bf16[4,512,384]{2,1,0:T(8,128)(2,1)S(1)}, bf16[4,512,384]{2,1,0:T(8,128)(2,1)S(1)}, u32[]{:S(2)}, u32[]{:S(2)}) collective-permute-start(bf16[4,512,384]{2,1,0:T(8,128)(2,1)S(1)} %get-tuple-element.279.context_ref.refs_4_.refs_0_), channel_id=1, source_target_pairs={{0,16},{16,0},{1,17},{17,1},{2,18},{18,2},{3,19},{19,3},{4,20},{20... | collective-permute-start | bytes 4718600 | tf_op jit(solution)/shard_map/ppermute | solution.py:63
  99.0 17.0 %collective-permute-start.20 = (bf16[4,192,384]{2,1,0:T(8,128)(2,1)S(1)}, bf16[4,192,384]{2,1,0:T(8,128)(2,1)S(1)}, u32[]{:S(2)}, u32[]{:S(2)}) collective-permute-start(bf16[4,192,384]{2,1,0:T(8,128)(2,1)S(1)} %constant_dynamic-update-slice_fusion.22), channel_id=1, source_target_pairs={{0,2},{1,3},{2,0},{3,1},{4,6},{5,7},{6,4},{7,5},{8,10},{9,11},{10,... | collective-permute-start | bytes 1769480 | tf_op jit(solution)/shard_map/ppermute | solution.py:52
  101.5 14.5 %collective-permute-start.21 = (bf16[2,192,384]{2,1,0:T(8,128)(2,1)S(1)}, bf16[2,192,384]{2,1,0:T(8,128)(2,1)S(1)}, u32[]{:S(2)}, u32[]{:S(2)}) collective-permute-start(bf16[2,192,384]{2,1,0:T(8,128)(2,1)S(1)} %constant_dynamic-update-slice_fusion.24), channel_id=1, source_target_pairs={{0,4},{1,5},{2,6},{3,7},{4,0},{5,1},{6,2},{7,3},{8,12},{9,13},{10,... | collective-permute-start | bytes 884744 | tf_op jit(solution)/shard_map/ppermute | solution.py:52
  103.0 13.0 %collective-permute-start.22 = (bf16[1,192,384]{2,1,0:T(8,128)(2,1)S(1)}, bf16[1,192,384]{2,1,0:T(8,128)(2,1)S(1)}, u32[]{:S(2)}, u32[]{:S(2)}) collective-permute-start(bf16[1,192,384]{2,1,0:T(8,128)(2,1)S(1)} %copy-done.65), channel_id=1, source_target_pairs={{0,8},{1,9},{2,10},{3,11},{4,12},{5,13},{6,14},{7,15},{8,0},{9,1},... | collective-permute-start | bytes 442376 | tf_op jit(solution)/shard_map/ppermute | solution.py:52
  121.0 22.3 %collective-permute-start.25 = (bf16[8,192,384]{2,1,0:T(8,128)(2,1)S(1)}, bf16[8,192,384]{2,1,0:T(8,128)(2,1)S(1)}, u32[]{:S(2)}, u32[]{:S(2)}) collective-permute-start(bf16[8,192,384]{2,1,0:T(8,128)(2,1)S(1)} %constant_dynamic-update-slice_fusion.28), channel_id=1, source_target_pairs={{0,1},{1,0},{2,3},{3,2},{4,5},{5,4},{6,7},{7,6},{8,9},{9,8},{10,11... | collective-permute-start | bytes 3538952 | tf_op jit(solution)/shard_map/ppermute | solution.py:52
  121.5 16.3 %collective-permute-start.26 = (bf16[4,192,384]{2,1,0:T(8,128)(2,1)S(1)}, bf16[4,192,384]{2,1,0:T(8,128)(2,1)S(1)}, u32[]{:S(2)}, u32[]{:S(2)}) collective-permute-start(bf16[4,192,384]{2,1,0:T(8,128)(2,1)S(1)} %constant_dynamic-update-slice_fusion.30), channel_id=1, source_target_pairs={{0,2},{1,3},{2,0},{3,1},{4,6},{5,7},{6,4},{7,5},{8,10},{9,11},{10,... | collective-permute-start | bytes 1769480 | tf_op jit(solution)/shard_map/ppermute | solution.py:52
  121.9 10.6 %collective-permute-start.27 = (bf16[2,192,384]{2,1,0:T(8,128)(2,1)S(1)}, bf16[2,192,384]{2,1,0:T(8,128)(2,1)S(1)}, u32[]{:S(2)}, u32[]{:S(2)}) collective-permute-start(bf16[2,192,384]{2,1,0:T(8,128)(2,1)S(1)} %constant_dynamic-update-slice_fusion.32), channel_id=1, source_target_pairs={{0,4},{1,5},{2,6},{3,7},{4,0},{5,1},{6,2},{7,3},{8,12},{9,13},{10,... | collective-permute-start | bytes 884744 | tf_op jit(solution)/shard_map/ppermute | solution.py:52
  123.4 46.4 %collective-permute-start.32 = (bf16[10,512,384]{2,1,0:T(8,128)(2,1)}, bf16[10,512,384]{2,1,0:T(8,128)(2,1)}, u32[]{:S(2)}, u32[]{:S(2)}) collective-permute-start(bf16[10,512,384]{2,1,0:T(8,128)(2,1)} %get-tuple-element.291.active_ref.refs_0_), channel_id=1, source_target_pairs={{0,16},{16,0},{1,17},{17,1},{2,18},{18,2},{3,19},{19,3},{4,20},{20... | collective-permute-start | bytes 11796488 | tf_op jit(solution)/shard_map/ppermute | solution.py:63
  147.2 22.6 %collective-permute-start.29 = (bf16[8,192,384]{2,1,0:T(8,128)(2,1)S(1)}, bf16[8,192,384]{2,1,0:T(8,128)(2,1)S(1)}, u32[]{:S(2)}, u32[]{:S(2)}) collective-permute-start(bf16[8,192,384]{2,1,0:T(8,128)(2,1)S(1)} %constant_dynamic-update-slice_fusion.36), channel_id=1, source_target_pairs={{0,1},{1,0},{2,3},{3,2},{4,5},{5,4},{6,7},{7,6},{8,9},{9,8},{10,11... | collective-permute-start | bytes 3538952 | tf_op jit(solution)/shard_map/ppermute | solution.py:52
  148.6 16.3 %collective-permute-start.30 = (bf16[4,192,384]{2,1,0:T(8,128)(2,1)S(1)}, bf16[4,192,384]{2,1,0:T(8,128)(2,1)S(1)}, u32[]{:S(2)}, u32[]{:S(2)}) collective-permute-start(bf16[4,192,384]{2,1,0:T(8,128)(2,1)S(1)} %constant_dynamic-update-slice_fusion.38), channel_id=1, source_target_pairs={{0,2},{1,3},{2,0},{3,1},{4,6},{5,7},{6,4},{7,5},{8,10},{9,11},{10,... | collective-permute-start | bytes 1769480 | tf_op jit(solution)/shard_map/ppermute | solution.py:52
  170.3 16.9 %collective-permute-start.35 = (bf16[4,512,384]{2,1,0:T(8,128)(2,1)S(1)}, bf16[4,512,384]{2,1,0:T(8,128)(2,1)S(1)}, u32[]{:S(2)}, u32[]{:S(2)}) collective-permute-start(bf16[4,512,384]{2,1,0:T(8,128)(2,1)S(1)} %get-tuple-element.306.context_ref.refs_4_.refs_0_), channel_id=1, source_target_pairs={{0,16},{16,0},{1,17},{17,1},{2,18},{18,2},{3,19},{19,3},{4,20},{20... | collective-permute-start | bytes 4718600 | tf_op jit(solution)/shard_map/ppermute | solution.py:63
  170.9 16.3 %collective-permute-start.33 = (bf16[8,192,384]{2,1,0:T(8,128)(2,1)S(1)}, bf16[8,192,384]{2,1,0:T(8,128)(2,1)S(1)}, u32[]{:S(2)}, u32[]{:S(2)}) collective-permute-start(bf16[8,192,384]{2,1,0:T(8,128)(2,1)S(1)} %constant_dynamic-update-slice_fusion.42), channel_id=1, source_target_pairs={{0,1},{1,0},{2,3},{3,2},{4,5},{5,4},{6,7},{7,6},{8,9},{9,8},{10,11... | collective-permute-start | bytes 3538952 | tf_op jit(solution)/shard_map/ppermute | solution.py:52
  187.7 24.6 %collective-permute-start.37 = (bf16[10,512,384]{2,1,0:T(8,128)(2,1)S(1)}, bf16[10,512,384]{2,1,0:T(8,128)(2,1)S(1)}, u32[]{:S(2)}, u32[]{:S(2)}) collective-permute-start(bf16[10,512,384]{2,1,0:T(8,128)(2,1)S(1)} %get-tuple-element.313.active_ref.refs_0_), channel_id=1, source_target_pairs={{0,16},{16,0},{1,17},{17,1},{2,18},{18,2},{3,19},{19,3},{4,20},{20... | collective-permute-start | bytes 11796488 | tf_op jit(solution)/shard_map/ppermute | solution.py:63
  211.8 17.9 %collective-permute-start.40 = (bf16[1,512,384]{2,1,0:T(8,128)(2,1)S(1)}, bf16[1,512,384]{2,1,0:T(8,128)(2,1)S(1)}, u32[]{:S(2)}, u32[]{:S(2)}) collective-permute-start(bf16[1,512,384]{2,1,0:T(8,128)(2,1)S(1)} %get-tuple-element.339.sent_ref), channel_id=1, source_target_pairs={{0,16},{16,0},{1,17},{17,1},{2,18},{18,2},{3,19},{19,3},{4,20},{20... | collective-permute-start | bytes 1179656 | tf_op jit(solution)/shard_map/ppermute | solution.py:63
  217.0 18.1 %collective-permute-start.39 = (bf16[8,192,384]{2,1,0:T(8,128)(2,1)S(1)}, bf16[8,192,384]{2,1,0:T(8,128)(2,1)S(1)}, u32[]{:S(2)}, u32[]{:S(2)}) collective-permute-start(bf16[8,192,384]{2,1,0:T(8,128)(2,1)S(1)} %get-tuple-element.334), channel_id=1, source_target_pairs={{0,1},{1,0},{2,3},{3,2},{4,5},{5,4},{6,7},{7,6},{8,9},{9,8},{10,11... | collective-permute-start | bytes 3538952 | tf_op jit(solution)/shard_map/ppermute | solution.py:52
  229.4 13.4 %collective-permute-start.43 = (bf16[3,512,384]{2,1,0:T(8,128)(2,1)S(1)}, bf16[3,512,384]{2,1,0:T(8,128)(2,1)S(1)}, u32[]{:S(2)}, u32[]{:S(2)}) collective-permute-start(bf16[3,512,384]{2,1,0:T(8,128)(2,1)S(1)} %get-tuple-element.350.sent_ref), channel_id=1, source_target_pairs={{0,16},{16,0},{1,17},{17,1},{2,18},{18,2},{3,19},{19,3},{4,20},{20... | collective-permute-start | bytes 3538952 | tf_op jit(solution)/shard_map/ppermute | solution.py:63
  235.1 25.7 %collective-permute-start.42 = (bf16[8,240,384]{2,1,0:T(8,128)(2,1)S(1)}, bf16[8,240,384]{2,1,0:T(8,128)(2,1)S(1)}, u32[]{:S(2)}, u32[]{:S(2)}) collective-permute-start(bf16[8,240,384]{2,1,0:T(8,128)(2,1)S(1)} %get-tuple-element.346), channel_id=1, source_target_pairs={{0,1},{1,0},{2,3},{3,2},{4,5},{5,4},{6,7},{7,6},{8,9},{9,8},{10,11... | collective-permute-start | bytes 4423688 | tf_op jit(solution)/shard_map/ppermute | solution.py:52
  237.1 16.3 %collective-permute-start.41 = (bf16[4,192,384]{2,1,0:T(8,128)(2,1)S(1)}, bf16[4,192,384]{2,1,0:T(8,128)(2,1)S(1)}, u32[]{:S(2)}, u32[]{:S(2)}) collective-permute-start(bf16[4,192,384]{2,1,0:T(8,128)(2,1)S(1)} %get-tuple-element.476), channel_id=1, source_target_pairs={{0,2},{1,3},{2,0},{3,1},{4,6},{5,7},{6,4},{7,5},{8,10},{9,11},{10,... | collective-permute-start | bytes 1769480 | tf_op jit(solution)/shard_map/ppermute | solution.py:52
  261.8 15.6 %collective-permute-start.44 = (bf16[2,192,384]{2,1,0:T(8,128)(2,1)}, bf16[2,192,384]{2,1,0:T(8,128)(2,1)}, u32[]{:S(2)}, u32[]{:S(2)}) collective-permute-start(bf16[2,192,384]{2,1,0:T(8,128)(2,1)} %get-tuple-element.488), channel_id=1, source_target_pairs={{0,4},{1,5},{2,6},{3,7},{4,0},{5,1},{6,2},{7,3},{8,12},{9,13},{10,... | collective-permute-start | bytes 884744 | tf_op jit(solution)/shard_map/ppermute | solution.py:52
  263.3 21.3 %collective-permute-start.45 = (bf16[8,144,384]{2,1,0:T(8,128)(2,1)}, bf16[8,144,384]{2,1,0:T(8,128)(2,1)}, u32[]{:S(2)}, u32[]{:S(2)}) collective-permute-start(bf16[8,144,384]{2,1,0:T(8,128)(2,1)} %get-tuple-element.357), channel_id=1, source_target_pairs={{0,1},{1,0},{2,3},{3,2},{4,5},{5,4},{6,7},{7,6},{8,9},{9,8},{10,11... | collective-permute-start | bytes 2654216 | tf_op jit(solution)/shard_map/ppermute | solution.py:52
  266.3 16.4 %collective-permute-start.46 = (bf16[4,240,384]{2,1,0:T(8,128)(2,1)}, bf16[4,240,384]{2,1,0:T(8,128)(2,1)}, u32[]{:S(2)}, u32[]{:S(2)}) collective-permute-start(bf16[4,240,384]{2,1,0:T(8,128)(2,1)} %get-tuple-element.472), channel_id=1, source_target_pairs={{0,2},{1,3},{2,0},{3,1},{4,6},{5,7},{6,4},{7,5},{8,10},{9,11},{10,... | collective-permute-start | bytes 2211848 | tf_op jit(solution)/shard_map/ppermute | solution.py:52
  277.2 28.5 %collective-permute-start.50 = (bf16[5,512,384]{2,1,0:T(8,128)(2,1)}, bf16[5,512,384]{2,1,0:T(8,128)(2,1)S(1)}, u32[]{:S(2)}, u32[]{:S(2)}) collective-permute-start(bf16[5,512,384]{2,1,0:T(8,128)(2,1)} %get-tuple-element.376.sent_ref), channel_id=1, source_target_pairs={{0,16},{16,0},{1,17},{17,1},{2,18},{18,2},{3,19},{19,3},{4,20},{20... | collective-permute-start | bytes 5898248 | tf_op jit(solution)/shard_map/ppermute | solution.py:63
  285.8 26.6 %collective-permute-start.47 = (bf16[1,192,384]{2,1,0:T(8,128)(2,1)S(1)}, bf16[1,192,384]{2,1,0:T(8,128)(2,1)S(1)}, u32[]{:S(2)}, u32[]{:S(2)}) collective-permute-start(bf16[1,192,384]{2,1,0:T(8,128)(2,1)S(1)} %get-tuple-element.514), channel_id=1, source_target_pairs={{0,8},{1,9},{2,10},{3,11},{4,12},{5,13},{6,14},{7,15},{8,0},{9,1},... | collective-permute-start | bytes 442376 | tf_op jit(solution)/shard_map/ppermute | solution.py:52
  288.9 23.6 %collective-permute-start.48 = (bf16[4,144,384]{2,1,0:T(8,128)(2,1)S(1)}, bf16[4,144,384]{2,1,0:T(8,128)(2,1)S(1)}, u32[]{:S(2)}, u32[]{:S(2)}) collective-permute-start(bf16[4,144,384]{2,1,0:T(8,128)(2,1)S(1)} %get-tuple-element.480), channel_id=1, source_target_pairs={{0,2},{1,3},{2,0},{3,1},{4,6},{5,7},{6,4},{7,5},{8,10},{9,11},{10,... | collective-permute-start | bytes 1327112 | tf_op jit(solution)/shard_map/ppermute | solution.py:52
  291.7 20.8 %collective-permute-start.49 = (bf16[2,240,384]{2,1,0:T(8,128)(2,1)S(1)}, bf16[2,240,384]{2,1,0:T(8,128)(2,1)S(1)}, u32[]{:S(2)}, u32[]{:S(2)}) collective-permute-start(bf16[2,240,384]{2,1,0:T(8,128)(2,1)S(1)} %get-tuple-element.484), channel_id=1, source_target_pairs={{0,4},{1,5},{2,6},{3,7},{4,0},{5,1},{6,2},{7,3},{8,12},{9,13},{10,... | collective-permute-start | bytes 1105928 | tf_op jit(solution)/shard_map/ppermute | solution.py:52
  305.7 9.9 %collective-permute-start.54 = (bf16[1,512,384]{2,1,0:T(8,128)(2,1)S(1)}, bf16[1,512,384]{2,1,0:T(8,128)(2,1)S(1)}, u32[]{:S(2)}, u32[]{:S(2)}) collective-permute-start(bf16[1,512,384]{2,1,0:T(8,128)(2,1)S(1)} %get-tuple-element.399.sent_ref), channel_id=1, source_target_pairs={{0,16},{16,0},{1,17},{17,1},{2,18},{18,2},{3,19},{19,3},{4,20},{20... | collective-permute-start | bytes 1179656 | tf_op jit(solution)/shard_map/ppermute | solution.py:63
  312.5 16.3 %collective-permute-start.51 = (bf16[8,192,384]{2,1,0:T(8,128)(2,1)S(1)}, bf16[8,192,384]{2,1,0:T(8,128)(2,1)S(1)}, u32[]{:S(2)}, u32[]{:S(2)}) collective-permute-start(bf16[8,192,384]{2,1,0:T(8,128)(2,1)S(1)} %get-tuple-element.386), channel_id=1, source_target_pairs={{0,1},{1,0},{2,3},{3,2},{4,5},{5,4},{6,7},{7,6},{8,9},{9,8},{10,11... | collective-permute-start | bytes 3538952 | tf_op jit(solution)/shard_map/ppermute | solution.py:52
  313.4 12.0 %collective-permute-start.52 = (bf16[2,144,384]{2,1,0:T(8,128)(2,1)S(1)}, bf16[2,144,384]{2,1,0:T(8,128)(2,1)S(1)}, u32[]{:S(2)}, u32[]{:S(2)}) collective-permute-start(bf16[2,144,384]{2,1,0:T(8,128)(2,1)S(1)} %get-tuple-element.500), channel_id=1, source_target_pairs={{0,4},{1,5},{2,6},{3,7},{4,0},{5,1},{6,2},{7,3},{8,12},{9,13},{10,... | collective-permute-start | bytes 663560 | tf_op jit(solution)/shard_map/ppermute | solution.py:52
  314.1 11.3 %collective-permute-start.53 = (bf16[1,240,384]{2,1,0:T(8,128)(2,1)S(1)}, bf16[1,240,384]{2,1,0:T(8,128)(2,1)S(1)}, u32[]{:S(2)}, u32[]{:S(2)}) collective-permute-start(bf16[1,240,384]{2,1,0:T(8,128)(2,1)S(1)} %get-tuple-element.510), channel_id=1, source_target_pairs={{0,8},{1,9},{2,10},{3,11},{4,12},{5,13},{6,14},{7,15},{8,0},{9,1},... | collective-permute-start | bytes 552968 | tf_op jit(solution)/shard_map/ppermute | solution.py:52
  329.9 24.1 %collective-permute-start.55 = (bf16[4,192,384]{2,1,0:T(8,128)(2,1)S(1)}, bf16[4,192,384]{2,1,0:T(8,128)(2,1)S(1)}, u32[]{:S(2)}, u32[]{:S(2)}) collective-permute-start(bf16[4,192,384]{2,1,0:T(8,128)(2,1)S(1)} %get-tuple-element.474), channel_id=1, source_target_pairs={{0,2},{1,3},{2,0},{3,1},{4,6},{5,7},{6,4},{7,5},{8,10},{9,11},{10,... | collective-permute-start | bytes 1769480 | tf_op jit(solution)/shard_map/ppermute | solution.py:52
  330.5 23.8 %collective-permute-start.56 = (bf16[8,240,384]{2,1,0:T(8,128)(2,1)S(1)}, bf16[8,240,384]{2,1,0:T(8,128)(2,1)S(1)}, u32[]{:S(2)}, u32[]{:S(2)}) collective-permute-start(bf16[8,240,384]{2,1,0:T(8,128)(2,1)S(1)} %get-tuple-element.397), channel_id=1, source_target_pairs={{0,1},{1,0},{2,3},{3,2},{4,5},{5,4},{6,7},{7,6},{8,9},{9,8},{10,11... | collective-permute-start | bytes 4423688 | tf_op jit(solution)/shard_map/ppermute | solution.py:52
  344.5 18.6 %collective-permute-start.61 = (bf16[3,512,384]{2,1,0:T(8,128)(2,1)}, bf16[3,512,384]{2,1,0:T(8,128)(2,1)}, u32[]{:S(2)}, u32[]{:S(2)}) collective-permute-start(bf16[3,512,384]{2,1,0:T(8,128)(2,1)} %get-tuple-element.425.sent_ref), channel_id=1, source_target_pairs={{0,16},{16,0},{1,17},{17,1},{2,18},{18,2},{3,19},{19,3},{4,20},{20... | collective-permute-start | bytes 3538952 | tf_op jit(solution)/shard_map/ppermute | solution.py:63
  345.2 8.7 %collective-permute-start.57 = (bf16[1,144,384]{2,1,0:T(8,128)(2,1)S(1)}, bf16[1,144,384]{2,1,0:T(8,128)(2,1)S(1)}, u32[]{:S(2)}, u32[]{:S(2)}) collective-permute-start(bf16[1,144,384]{2,1,0:T(8,128)(2,1)S(1)} %get-tuple-element.524), channel_id=1, source_target_pairs={{0,8},{1,9},{2,10},{3,11},{4,12},{5,13},{6,14},{7,15},{8,0},{9,1},... | collective-permute-start | bytes 331784 | tf_op jit(solution)/shard_map/ppermute | solution.py:52
  357.1 11.4 %collective-permute-start.58 = (f32[16,2,576]{2,1,0:T(2,128)S(1)}, f32[16,2,576]{2,1,0:T(2,128)S(1)}, u32[]{:S(2)}, u32[]{:S(2)}) collective-permute-start(f32[16,2,576]{2,1,0:T(2,128)S(1)} %pad_maximum_fusion.5), channel_id=1, source_target_pairs={{0,16},{16,0},{1,17},{17,1},{2,18},{18,2},{3,19},{19,3},{4,20},{20... | collective-permute-start | bytes 221192 | tf_op jit(solution)/shard_map/ppermute | solution.py:63
  359.5 10.7 %collective-permute-start.59 = (bf16[2,192,384]{2,1,0:T(8,128)(2,1)}, bf16[2,192,384]{2,1,0:T(8,128)(2,1)}, u32[]{:S(2)}, u32[]{:S(2)}) collective-permute-start(bf16[2,192,384]{2,1,0:T(8,128)(2,1)} %get-tuple-element.486), channel_id=1, source_target_pairs={{0,4},{1,5},{2,6},{3,7},{4,0},{5,1},{6,2},{7,3},{8,12},{9,13},{10,... | collective-permute-start | bytes 884744 | tf_op jit(solution)/shard_map/ppermute | solution.py:52
  361.7 12.2 %collective-permute-start.60 = (bf16[4,240,384]{2,1,0:T(8,128)(2,1)}, bf16[4,240,384]{2,1,0:T(8,128)(2,1)}, u32[]{:S(2)}, u32[]{:S(2)}) collective-permute-start(bf16[4,240,384]{2,1,0:T(8,128)(2,1)} %get-tuple-element.470), channel_id=1, source_target_pairs={{0,2},{1,3},{2,0},{3,1},{4,6},{5,7},{6,4},{7,5},{8,10},{9,11},{10,... | collective-permute-start | bytes 2211848 | tf_op jit(solution)/shard_map/ppermute | solution.py:52
  369.4 17.7 %collective-permute-start.62 = (f32[8,2,576]{2,1,0:T(2,128)S(1)}, f32[8,2,576]{2,1,0:T(2,128)S(1)}, u32[]{:S(2)}, u32[]{:S(2)}) collective-permute-start(f32[8,2,576]{2,1,0:T(2,128)S(1)} %get-tuple-element.552), channel_id=1, source_target_pairs={{0,1},{1,0},{2,3},{3,2},{4,5},{5,4},{6,7},{7,6},{8,9},{9,8},{10,11... | collective-permute-start | bytes 110600 | tf_op jit(solution)/shard_map/ppermute | solution.py:52
  375.1 12.0 %collective-permute-start.63 = (bf16[1,192,384]{2,1,0:T(8,128)(2,1)S(1)}, bf16[1,192,384]{2,1,0:T(8,128)(2,1)S(1)}, u32[]{:S(2)}, u32[]{:S(2)}) collective-permute-start(bf16[1,192,384]{2,1,0:T(8,128)(2,1)S(1)} %get-tuple-element.512), channel_id=1, source_target_pairs={{0,8},{1,9},{2,10},{3,11},{4,12},{5,13},{6,14},{7,15},{8,0},{9,1},... | collective-permute-start | bytes 442376 | tf_op jit(solution)/shard_map/ppermute | solution.py:52
  376.6 13.4 %collective-permute-start.64 = (bf16[8,144,384]{2,1,0:T(8,128)(2,1)S(1)}, bf16[8,144,384]{2,1,0:T(8,128)(2,1)S(1)}, u32[]{:S(2)}, u32[]{:S(2)}) collective-permute-start(bf16[8,144,384]{2,1,0:T(8,128)(2,1)S(1)} %copy-done.18), channel_id=1, source_target_pairs={{0,1},{1,0},{2,3},{3,2},{4,5},{5,4},{6,7},{7,6},{8,9},{9,8},{10,11... | collective-permute-start | bytes 2654216 | tf_op jit(solution)/shard_map/ppermute | solution.py:52
  379.3 10.6 %collective-permute-start.65 = (bf16[2,240,384]{2,1,0:T(8,128)(2,1)S(1)}, bf16[2,240,384]{2,1,0:T(8,128)(2,1)S(1)}, u32[]{:S(2)}, u32[]{:S(2)}) collective-permute-start(bf16[2,240,384]{2,1,0:T(8,128)(2,1)S(1)} %get-tuple-element.482), channel_id=1, source_target_pairs={{0,4},{1,5},{2,6},{3,7},{4,0},{5,1},{6,2},{7,3},{8,12},{9,13},{10,... | collective-permute-start | bytes 1105928 | tf_op jit(solution)/shard_map/ppermute | solution.py:52
  391.4 10.1 %collective-permute-start.67 = (bf16[4,144,384]{2,1,0:T(8,128)(2,1)S(1)}, bf16[4,144,384]{2,1,0:T(8,128)(2,1)S(1)}, u32[]{:S(2)}, u32[]{:S(2)}) collective-permute-start(bf16[4,144,384]{2,1,0:T(8,128)(2,1)S(1)} %get-tuple-element.478), channel_id=1, source_target_pairs={{0,2},{1,3},{2,0},{3,1},{4,6},{5,7},{6,4},{7,5},{8,10},{9,11},{10,... | collective-permute-start | bytes 1327112 | tf_op jit(solution)/shard_map/ppermute | solution.py:52
  392.5 9.0 %collective-permute-start.68 = (bf16[1,240,384]{2,1,0:T(8,128)(2,1)S(1)}, bf16[1,240,384]{2,1,0:T(8,128)(2,1)S(1)}, u32[]{:S(2)}, u32[]{:S(2)}) collective-permute-start(bf16[1,240,384]{2,1,0:T(8,128)(2,1)S(1)} %get-tuple-element.508), channel_id=1, source_target_pairs={{0,8},{1,9},{2,10},{3,11},{4,12},{5,13},{6,14},{7,15},{8,0},{9,1},... | collective-permute-start | bytes 552968 | tf_op jit(solution)/shard_map/ppermute | solution.py:52
  408.1 12.6 %collective-permute-start.72 = (bf16[1,144,384]{2,1,0:T(8,128)(2,1)S(1)}, bf16[1,144,384]{2,1,0:T(8,128)(2,1)S(1)}, u32[]{:S(2)}, u32[]{:S(2)}) collective-permute-start(bf16[1,144,384]{2,1,0:T(8,128)(2,1)S(1)} %get-tuple-element.522), channel_id=1, source_target_pairs={{0,24},{1,25},{2,26},{3,27},{4,28},{5,29},{6,30},{7,31},{8,16},{9,... | collective-permute-start | bytes 331784 | tf_op jit(solution)/shard_map/ppermute | solution.py:60
  408.2 12.6 %collective-permute-start.74 = (bf16[1,144,384]{2,1,0:T(8,128)(2,1)S(1)}, bf16[1,144,384]{2,1,0:T(8,128)(2,1)S(1)}, u32[]{:S(2)}, u32[]{:S(2)}) collective-permute-start(bf16[1,144,384]{2,1,0:T(8,128)(2,1)S(1)} %get-tuple-element.522), channel_id=1, source_target_pairs={{0,8},{1,9},{2,10},{3,11},{4,12},{5,13},{6,14},{7,15},{8,0},{9,1},... | collective-permute-start | bytes 331784 | tf_op jit(solution)/shard_map/ppermute | solution.py:52
  410.1 10.6 %collective-permute-start.71 = (bf16[1,144,384]{2,1,0:T(8,128)(2,1)S(1)}, bf16[1,144,384]{2,1,0:T(8,128)(2,1)S(1)}, u32[]{:S(2)}, u32[]{:S(2)}) collective-permute-start(bf16[1,144,384]{2,1,0:T(8,128)(2,1)S(1)} %get-tuple-element.442), channel_id=1, source_target_pairs={{0,16},{16,0},{1,17},{17,1},{2,18},{18,2},{3,19},{19,3},{4,20},{20... | collective-permute-start | bytes 331784 | tf_op jit(solution)/shard_map/ppermute | solution.py:63
  410.9 9.8 %collective-permute-start.73 = (f32[1,2,576]{2,1,0:T(2,128)S(1)}, f32[1,2,576]{2,1,0:T(2,128)S(1)}, u32[]{:S(2)}, u32[]{:S(2)}) collective-permute-start(f32[1,2,576]{2,1,0:T(2,128)S(1)} %get-tuple-element.556), channel_id=1, source_target_pairs={{0,8},{1,9},{2,10},{3,11},{4,12},{5,13},{6,14},{7,15},{8,0},{9,1},... | collective-permute-start | bytes 13832 | tf_op jit(solution)/shard_map/ppermute | solution.py:52
  412.9 8.6 %collective-permute-start.75 = (bf16[1008,384]{1,0:T(8,128)(2,1)S(1)}, bf16[1008,384]{1,0:T(8,128)(2,1)S(1)}, u32[]{:S(2)}, u32[]{:S(2)}) collective-permute-start(bf16[1008,384]{1,0:T(8,128)(2,1)S(1)} %get-tuple-element.460), channel_id=1, source_target_pairs={{0,16},{16,0},{1,17},{17,1},{2,18},{18,2},{3,19},{19,3},{4,20},{20... | collective-permute-start | bytes 2322440 | tf_op jit(solution)/shard_map/ppermute | solution.py:63
  (96 other events, 628.3 us)

commit v7 on v6

--- a/solution.py
+++ b/solution.py
@@ -24,15 +24,17 @@
 
 
 class Net:
-    def __init__(self, mesh, wide):
+    def __init__(self, mesh, mixed):
         self.shards = mesh.shape["fsdp"]
         self.replicas = mesh.shape["rep"]
         assert self.replicas % 2 == 0 and self.shards & (self.shards - 1) == 0 and self.shards >= 16
-        bits = [1 << place for place in reversed(range(self.shards.bit_length() - 3))]
-        first = [(4, self.shards // 4)] if wide else [(2, self.shards // 2), (2, self.shards // 4)]
-        self.sizes = [size for size, _ in first] + [2] * len(bits)
-        first = [step for _, step in first]
-        self.steps = [[*first, *bits], [*first, *bits[:-2], bits[-1], bits[-2]]]
+        bits = [1 << place for place in reversed(range(self.shards.bit_length()))][1:]
+        far, near, *middle, one, two = bits
+        self.sizes = [2] * len(bits)
+        if mixed:
+            self.steps = [[far, one, near, *middle, two], [far, two, near, *middle, one]]
+        else:
+            self.steps = [[far, near, *middle, one, two], [far, near, *middle, two, one]]
         self.stages = len(self.sizes)
         flips = np.zeros((2, self.shards), np.int32)
         for core in range(2):
@@ -746,7 +748,7 @@
         return values
 
 
-def shards(wide, net, tokens, valid, qkv_weight, out_weight, up_weight, down_weight, vectors, cotangent):
+def shards(mixed, net, tokens, valid, qkv_weight, out_weight, up_weight, down_weight, vectors, cotangent):
     count = net.shards
     core = (lax.axis_index("rep") % 2).astype(jnp.int32)
     place = lax.axis_index("fsdp").astype(jnp.int32)
@@ -760,8 +762,8 @@
         )
 
     places, slots = order(net.flips)
-    wide_slots = order(wide.flips)[1]
-    tables = (wide_slots, core.reshape(1), valid)
+    mixed_slots = order(mixed.flips)[1]
+    tables = (mixed_slots, core.reshape(1), valid)
     weight_inputs = (qkv_weight, out_weight, up_weight, down_weight)
     width = tokens.shape[1]
     inner_width = up_weight.shape[2]
@@ -777,17 +779,17 @@
             pieces.append(piece.reshape(-1, CHUNK))
             start += pieces[-1].shape[0]
         blocks.append(jnp.concatenate(pieces, 0))
-    gather = Gather(wide, blocks)
+    gather = Gather(mixed, blocks)
 
     def weight(level, kind):
         number, start = home[level, kind]
         return gather.ready(number), start
 
     vector_blocks = vectors[None]
-    for stage in range(net.stages):
-        vector_blocks = net.widen(vector_blocks, stage)
+    for stage in range(mixed.stages):
+        vector_blocks = mixed.widen(vector_blocks, stage)
         (vector_blocks,) = gather.end((vector_blocks,))
-    vector_all = jnp.take(vector_blocks, slots[0], axis=0).transpose(1, 0, 2).reshape(LAYERS, -1, width)
+    vector_all = jnp.take(vector_blocks, mixed_slots[0], axis=0).transpose(1, 0, 2).reshape(LAYERS, -1, width)
 
     hidden, h_low = tokens, tokens
     kept, twins = [], []
@@ -822,33 +824,34 @@
             tables, d_hidden, second_sum, slope, rows, *weight(level, 3), inner_width, level == LAYERS - 1
         )
         received = net.twin(sent)
-        d_second_sum, f_kept, u_kept, sent = reduce.turn((d_second_sum, f_kept, u_kept, sent))
+        if level < LAYERS - 1:
+            *term, d_second_sum, f_kept, u_kept, sent = reduce.turn((*term, d_second_sum, f_kept, u_kept, sent))
+            reduce.push((level + 1, "qkv"), *term)
 
         d_first_sum, a_kept, a_sent, sums_a = expand_back(
             tables, u_kept, sent, d_second_sum, first_sum, rows, *weight(level, 2)
         )
         a_received = net.twin(a_sent)
         term = weight_terms(slots, count, (left_b, twin_b, 0, 2 * parts, f_kept, received, parts))
-        *term, d_first_sum, a_kept, a_sent = reduce.turn((*term, d_first_sum, a_kept, a_sent))
-        reduce.push((level, "down"), *term)
-
-        term = weight_terms(
+        if level == 0:
+            *term, d_first_sum, a_kept, a_sent = reduce.turn((*term, d_first_sum, a_kept, a_sent))
+            reduce.push((level, "down"), *term)
+        up_term = weight_terms(
             slots,
             count,
             (left_b, twin_b, 2 * parts, 2, u_kept, received, 0),
             (left_a, twin_a, 2, 2, a_kept, a_received, 0),
         )
-        if level == 0:
-            *term, a_kept, a_sent = reduce.turn((*term, a_kept, a_sent))
-            reduce.push((level, "up"), *term)
+        if level:
+            *both, d_first_sum, a_kept, a_sent = reduce.turn((*term, *up_term, d_first_sum, a_kept, a_sent))
+            reduce.push((level, "down"), *both[:2])
+            reduce.push((level, "up"), *both[2:])
+
         q_kept, q_sent, sums_qv = attend_back(tables, a_kept, a_sent, qkv, *weight(level, 1))
         q_received = net.twin(q_sent)
         if level == 0:
-            q_kept, q_sent, sums_qv = reduce.turn((q_kept, q_sent, sums_qv))
-        else:
-            *term, q_kept, q_sent = reduce.turn((*term, q_kept, q_sent))
-            reduce.push((level, "up"), *term)
-
+            *up_term, q_kept, q_sent, sums_qv = reduce.turn((*up_term, q_kept, q_sent, sums_qv))
+            reduce.push((level, "up"), *up_term)
         d_vectors[level] = jnp.concatenate(
             [sums_qv.reshape(2, width), sums_a, sums_b, sums_u.reshape(-1, width)]
         ).reshape(count, -1)
@@ -856,11 +859,10 @@
             d_vector = jnp.stack(d_vectors, 1)
             d_vector = d_vector + net.twin(d_vector)
             d_vector = jnp.take(d_vector, places[0], axis=0)
-        if level:
-            d_hidden = project_back(tables, q_kept, q_sent, d_first_sum, *weight(level, 0))
+        d_hidden = project_back(tables, q_kept, q_sent, d_first_sum, *weight(level, 0))
         term = weight_terms(slots, count, (left_a, twin_a, 0, 2, q_kept, q_received, 0))
-        *term, d_hidden = reduce.turn((*term, d_hidden))
-        reduce.push((level, "qkv"), *term)
+    *term, d_hidden = reduce.turn((*term, d_hidden))
+    reduce.push((0, "qkv"), *term)
     reduce.push((-1, "vectors"), d_vector[: count // 2], d_vector[count // 2 :])
 
     heights = {"down": inner_width // count, "up": (parts + 1) * width // count, "qkv": 3 * width // count}
@@ -876,8 +878,6 @@
             whole_grads[key] = (mine[start : start + height], other[start : start + height])
             start += height
 
-    d_hidden = project_back(tables, q_kept, q_sent, d_first_sum, *weight(0, 0))
-    (d_hidden,) = reduce.turn((d_hidden,))
     while keys[-2] not in reduce.owned:
         reduce.turn()
     finish(keys[:-1])
@@ -924,4 +924,4 @@
         P(None, "fsdp", None),
         P(None, "fsdp"),
     )
-    return jax.shard_map(functools.partial(shards, Net(mesh, False), Net(mesh, False)), mesh=mesh, in_specs=in_specs, out_specs=out_specs, check_vma=False)
+    return jax.shard_map(functools.partial(shards, Net(mesh, True), Net(mesh, False)), mesh=mesh, in_specs=in_specs, out_specs=out_specs, check_vma=False)

time: 432 us -> 412 us (0.954)
  local copies, waits for them, and re-layouts: 45.5 us -> 29.4 us
  waiting for transfers between devices: 137 us -> 127 us
    unnamed x220 -> x206, local copies, waits for them, and re-layouts: 29.5 us -> 19.3 us
    ppermute x56, waiting for transfers between devices: 129 us -> 121 us  [trade(): return lax.ppermute(value, ('rep', 'fsdp'), pairs)]
    concatenate x24, local copies, waits for them, and re-layouts: 11.5 us -> 6.12 us  [end(): self.state[group] = jnp.concatenate([self.state[group], *others], 0)]
  transfers between devices with their start and end apart: 76 -> 76, of which waited for: 32 -> 31; matrix products, arithmetic and copies ran while one was open for 9% -> 7% of each run, Pallas kernels for 34% -> 32%
where the time goes in v7:
time: 412 us; the launch traced here: 406 us
  Pallas kernels  148 us (36%)
  waiting for transfers between devices  127 us (31%)
  starting transfers between devices  72.8 us (18%)
  local copies, waits for them, and re-layouts  29.4 us (7%)
  other arithmetic  26 us (6%)
    ppermute x56, waiting for transfers between devices, trade(): return lax.ppermute(value, ('rep', 'fsdp'), pairs)  121 us
    ppermute x56, starting transfers between devices, trade(): return lax.ppermute(value, ('rep', 'fsdp'), pairs)  68.7 us
    pallas_call x6, Pallas kernels, weight_terms(): pl.pallas_call(body, grid=(chunks // 2,), out_shape=[shaped(half, sum(par...  35.9 us
    pallas_call x2, Pallas kernels, attend_back(): pl.pallas_call(body, grid=(1,), out_shape=[shaped(3, tokens, CHUNK), shap...  25.3 us
    unnamed x206, local copies, waits for them, and re-layouts  19.3 us
    pallas_call x2, Pallas kernels, project(): pl.pallas_call(body, grid=(3,), out_shape=[shaped(2, 3, tokens, CHUNK), s...  16.3 us
    pallas_call x2, Pallas kernels, expand(): pl.pallas_call(body, grid=(parts + 1,), out_shape=[shaped(2 * parts + 2,...  14.4 us
    pallas_call x2, Pallas kernels, contract(): pl.pallas_call(body, grid_spec=pltpu.PrefetchScalarGridSpec(num_scalar_pr...  14.3 us
  transfers between devices with their start and end apart: 76, of which 31 were waited for; matrix products, arithmetic and copies ran while one was open for 7% of the time, Pallas kernels for 32%

profile of v7, /device:TPU:0, one launch (start us, length us, event | category | flops | bytes accessed | tf_op | source)
XLA Modules:
  0.0 406.4 jit_solution(2413129532600721358)
XLA Ops:
  2.1 4.1 %collective-permute-start = (bf16[1,144,384]{2,1,0:T(8,128)(2,1)S(1)}, bf16[1,144,384]{2,1,0:T(8,128)(2,1)S(1)}, u32[]{:S(2)}, u32[]{:S(2)}) collective-permute-start(bf16[1,144,384]{2,1,0:T(8,128)(2,1)S(1)} %bitcast.82), channel_id=1, source_target_pairs={{0,8},{1,9},{2,10},{3,11},{4,12},{5,13},{6,14},{7,15},{8,0},{9,1},... | collective-permute-start | bytes 331784 | tf_op jit(solution)/shard_map/ppermute | solution.py:54
  9.3 2.5 collective-permute-done.1
  11.9 1.6 collective-permute-start.2
  14.3 3.7 collective-permute-done.4
  18.0 5.6 %collective-permute-done.3 = bf16[1,240,384]{2,1,0:T(8,128)(2,1)S(1)} collective-permute-done((bf16[1,240,384]{2,1,0:T(8,128)(2,1)S(1)}, bf16[1,240,384]{2,1,0:T(8,128)(2,1)S(1)}, u32[]{:S(2)}, u32[]{:S(2)}) %collective-permute-start.3) | collective-permute-done | bytes 184352 | tf_op jit(solution)/shard_map/ppermute | solution.py:54
  25.4 2.0 collective-permute-start.7
  27.4 9.2 %collective-permute-done.8 = f32[4,2,576]{2,1,0:T(2,128)S(1)} collective-permute-done((f32[4,2,576]{2,1,0:T(2,128)S(1)}, f32[4,2,576]{2,1,0:T(2,128)S(1)}, u32[]{:S(2)}, u32[]{:S(2)}) %collective-permute-start.8) | collective-permute-done | bytes 18464 | tf_op jit(solution)/shard_map/ppermute | solution.py:54
  36.8 1.9 collective-permute-start.9
  38.8 2.3 collective-permute-start.10
  41.8 1.8 collective-permute-start.13
  43.6 2.0 collective-permute-start.12
  45.7 7.9 %collective-permute-done.13 = f32[8,2,576]{2,1,0:T(2,128)S(1)} collective-permute-done((f32[8,2,576]{2,1,0:T(2,128)S(1)}, f32[8,2,576]{2,1,0:T(2,128)S(1)}, u32[]{:S(2)}, u32[]{:S(2)}) %collective-permute-start.13) | collective-permute-done | bytes 36896 | tf_op jit(solution)/shard_map/ppermute | solution.py:54
  53.6 6.0 %collective-permute-done.12 = bf16[1,192,384]{2,1,0:T(8,128)(2,1)S(1)} collective-permute-done((bf16[1,192,384]{2,1,0:T(8,128)(2,1)S(1)}, bf16[1,192,384]{2,1,0:T(8,128)(2,1)S(1)}, u32[]{:S(2)}, u32[]{:S(2)}) %collective-permute-start.12) | collective-permute-done | bytes 147488 | tf_op jit(solution)/shard_map/ppermute | solution.py:54
  65.7 2.8 collective-permute-start.15
  70.6 8.3 %project.2 = (bf16[2,3,512,384]{3,2,1,0:T(8,128)(2,1)S(1)}, bf16[4,512,384]{2,1,0:T(8,128)(2,1)S(1)}) custom-call(s32[2,16]{1,0:T(2,128)S(1)} %select_reduce_fusion.1.slots_ref, s32[1]{0:T(128)} %bitcast.core_ref, s32[4]{0:T(128)S(1)} %copy-done.24, bf16[512,768]{1,0:T(8,128)(2,1)S(1)} %copy-done.22, f32[12,768]{1,0:T(8,128)S(1)} %squeeze.21.rows_ref, ...), custom_call_target="tpu_custom_call" | custom-call | flops 16675000320 | bytes 14500000 | tf_op jit(solution)/shard_map/project/pallas_call | solution.py:253
  80.2 4.4 %collective-permute-done.17 = bf16[1,192,384]{2,1,0:T(8,128)(2,1)S(1)} collective-permute-done((bf16[1,192,384]{2,1,0:T(8,128)(2,1)S(1)}, bf16[1,192,384]{2,1,0:T(8,128)(2,1)S(1)}, u32[]{:S(2)}, u32[]{:S(2)}) %collective-permute-start.17) | collective-permute-done | bytes 147488 | tf_op jit(solution)/shard_map/ppermute | solution.py:54
  85.4 2.8 collective-permute-done.14
  88.8 1.8 collective-permute-start.21
  92.1 2.0 collective-permute-done.23.refs_1_
  95.5 2.0 mix.2
  97.5 7.7 %expand.2 = (bf16[10,512,384]{2,1,0:T(8,128)(2,1)}, bf16[8,512,384]{2,1,0:T(8,128)(2,1)S(1)}) custom-call(s32[2,16]{1,0:T(2,128)S(1)} %select_reduce_fusion.1.slots_ref, s32[1]{0:T(128)} %bitcast.core_ref, bf16[512,768]{1,0:T(8,128)(2,1)S(1)} %get-tuple-element.273.x_ref, f32[12,768]{1,0:T(8,128)S(1)} %squeeze.21.rows_ref, ...), custom_call_target="tpu_custom_call" | custom-call | flops 10350000128 | bytes 9000000 | tf_op jit(solution)/shard_map/expand/pallas_call | solution.py:319
  105.3 1.8 copy-done.29
  111.7 1.8 collective-permute-start.25
  114.8 7.3 %contract.2 = (f32[512,768]{1,0:T(8,128)S(1)}, f32[512,768]{1,0:T(8,128)S(1)}, bf16[512,768]{1,0:T(8,128)(2,1)S(1)}) custom-call(s32[2,16]{1,0:T(2,128)S(1)} %select_reduce_fusion.1.slots_ref, s32[1]{0:T(128)} %bitcast.core_ref, s32[4]{0:T(128)S(1)} %copy-done.24, bf16[10,512,384]{2,1,0:T(8,128)(2,1)} %get-tuple-element.282.active_ref.refs_0_, ...), custom_call_target="tpu_custom_call" | custom-call | flops 12419999744 | bytes 10800000 | tf_op jit(solution)/shard_map/contract/pallas_call | solution.py:380
  122.2 6.5 %collective-permute-done.26 = bf16[4,192,384]{2,1,0:T(8,128)(2,1)S(1)} collective-permute-done((bf16[4,192,384]{2,1,0:T(8,128)(2,1)S(1)}, bf16[4,192,384]{2,1,0:T(8,128)(2,1)S(1)}, u32[]{:S(2)}, u32[]{:S(2)}) %collective-permute-start.26) | collective-permute-done | bytes 589856 | tf_op jit(solution)/shard_map/ppermute | solution.py:54
  134.7 8.0 %project.3 = (bf16[2,3,512,384]{3,2,1,0:T(8,128)(2,1)S(1)}, bf16[4,512,384]{2,1,0:T(8,128)(2,1)S(1)}) custom-call(s32[2,16]{1,0:T(2,128)S(1)} %select_reduce_fusion.1.slots_ref, s32[1]{0:T(128)} %bitcast.core_ref, s32[4]{0:T(128)S(1)} %copy-done.24, bf16[512,768]{1,0:T(8,128)(2,1)S(1)} %copy-done.45, f32[12,768]{1,0:T(8,128)S(1)} %squeeze.22.rows_ref, ...), custom_call_target="tpu_custom_call" | custom-call | flops 16675000320 | bytes 14500000 | tf_op jit(solution)/shard_map/project/pallas_call | solution.py:253
  142.7 4.5 %collective-permute-done.30 = bf16[4,192,384]{2,1,0:T(8,128)(2,1)S(1)} collective-permute-done((bf16[4,192,384]{2,1,0:T(8,128)(2,1)S(1)}, bf16[4,192,384]{2,1,0:T(8,128)(2,1)S(1)}, u32[]{:S(2)}, u32[]{:S(2)}) %collective-permute-start.30) | collective-permute-done | bytes 589856 | tf_op jit(solution)/shard_map/ppermute | solution.py:54
  147.2 1.9 collective-permute-done.29
  151.7 2.5 mix.3
  154.2 6.7 %expand.3 = (bf16[10,512,384]{2,1,0:T(8,128)(2,1)S(1)}, bf16[8,512,384]{2,1,0:T(8,128)(2,1)S(1)}) custom-call(s32[2,16]{1,0:T(2,128)S(1)} %select_reduce_fusion.1.slots_ref, s32[1]{0:T(128)} %bitcast.core_ref, bf16[512,768]{1,0:T(8,128)(2,1)S(1)} %get-tuple-element.299.x_ref, f32[12,768]{1,0:T(8,128)S(1)} %squeeze.22.rows_ref, ...), custom_call_target="tpu_custom_call" | custom-call | flops 10350000128 | bytes 9000000 | tf_op jit(solution)/shard_map/expand/pallas_call | solution.py:319
  160.9 5.6 %collective-permute-done.33 = bf16[8,192,384]{2,1,0:T(8,128)(2,1)S(1)} collective-permute-done((bf16[8,192,384]{2,1,0:T(8,128)(2,1)S(1)}, bf16[8,192,384]{2,1,0:T(8,128)(2,1)S(1)}, u32[]{:S(2)}, u32[]{:S(2)}) %collective-permute-start.33) | collective-permute-done | bytes 1179680 | tf_op jit(solution)/shard_map/ppermute | solution.py:54
  167.4 4.0 collective-permute-done.36.refs_4_.refs_5_.refs_6_.refs_7_
  171.5 6.9 %contract.3 = (f32[512,768]{1,0:T(8,128)S(1)}, f32[512,768]{1,0:T(8,128)}, bf16[512,768]{1,0:T(8,128)(2,1)}) custom-call(s32[2,16]{1,0:T(2,128)S(1)} %select_reduce_fusion.1.slots_ref, s32[1]{0:T(128)} %bitcast.core_ref, s32[4]{0:T(128)S(1)} %copy-done.24, bf16[10,512,384]{2,1,0:T(8,128)(2,1)S(1)} %get-tuple-element.304.active_ref.refs_0_, ...), custom_call_target="tpu_custom_call" | custom-call | flops 12419999744 | bytes 10800000 | tf_op jit(solution)/shard_map/contract/pallas_call | solution.py:380
  178.4 6.3 %contract_back.2 = (f32[512,768]{1,0:T(8,128)S(1)}, bf16[1,512,384]{2,1,0:T(8,128)(2,1)S(1)}, bf16[4,512,384]{2,1,0:T(8,128)(2,1)S(1)}, bf16[5,512,384]{2,1,0:T(...) custom-call(s32[2,16]{1,0:T(2,128)S(1)} %select_reduce_fusion.1.slots_ref, s32[1]{0:T(128)} %bitcast.core_ref, ...), custom_call_target="tpu_custom_call" | custom-call | flops 12650000384 | bytes 11000000 | tf_op jit(solution)/shard_map/contract_back/pallas_call | solution.py:443
  186.2 6.3 %expand_back.2 = (f32[512,768]{1,0:T(8,128)S(1)}, bf16[1,512,384]{2,1,0:T(8,128)(2,1)S(1)}, bf16[1,512,384]{2,1,0:T(8,128)(2,1)S(1)}, f32[3,768]{1,0:T(4,128)S(1)}) custom-call(s32[2,16]{1,0:T(2,128)S(1)} %select_reduce_fusion.1.slots_ref, s32[1]{0:T(128)} %bitcast.core_ref, bf16[4,512,384]{2,1,0:T(8,128)(2,1)S(1)} %get-tuple-element.315.kept_ref.refs_2_, ...), custom_call_target="tpu_custom_call" | custom-call | flops 11269999616 | bytes 9800000 | tf_op jit(solution)/shard_map/expand_back/pallas_call | solution.py:514
  193.0 5.5 %weight_terms.6 = (bf16[8,192,384]{2,1,0:T(8,128)(2,1)S(1)}, bf16[8,192,384]{2,1,0:T(8,128)(2,1)}) custom-call(s32[2,16]{1,0:T(2,128)S(1)} %select_reduce_fusion.slots_ref, bf16[10,512,384]{2,1,0:T(8,128)(2,1)S(1)} %get-tuple-element.304.active_ref.refs_0_, bf16[10,512,384]{2,1,0:T(8,128)(2,1)S(1)} %collective-permute-done.37.refs_1_, ...), custom_call_target="tpu_custom_call" | custom-call | flops 6899999744 | bytes 6000000 | tf_op jit(solution)/shard_map/weight_terms/pallas_call | solution.py:666
  198.5 6.7 %weight_terms.7 = (bf16[8,240,384]{2,1,0:T(8,128)(2,1)S(1)}, bf16[8,240,384]{2,1,0:T(8,128)(2,1)}) custom-call(s32[2,16]{1,0:T(2,128)S(1)} %select_reduce_fusion.slots_ref, bf16[10,512,384]{2,1,0:T(8,128)(2,1)S(1)} %get-tuple-element.304.active_ref.refs_0_, bf16[10,512,384]{2,1,0:T(8,128)(2,1)S(1)} %collective-permute-done.37.refs_1_, ...), custom_call_target="tpu_custom_call" | custom-call | flops 8625000448 | bytes 7500000 | tf_op jit(solution)/shard_map/weight_terms/pallas_call | solution.py:666
  205.2 13.0 %attend_back.2 = (bf16[3,512,384]{2,1,0:T(8,128)(2,1)S(1)}, bf16[3,512,384]{2,1,0:T(8,128)(2,1)}, f32[2,2,1,384]{3,2,1,0:T(1,128)S(1)}) custom-call(s32[2,16]{1,0:T(2,128)S(1)} %select_reduce_fusion.1.slots_ref, s32[1]{0:T(128)} %bitcast.core_ref, s32[4]{0:T(128)S(1)} %copy-done.24, bf16[1,512,384]{2,1,0:T(8,128)(2,1)S(1)} %get-tuple-element.327.refs_6_.kept_ref, ...), custom_call_target="tpu_custom_call" | custom-call | flops 23690000384 | bytes 20600000 | tf_op jit(solution)/shard_map/attend_back/pallas_call | solution.py:569
  220.4 5.6 %project_back.2.d_out_ref = f32[512,768]{1,0:T(8,128)S(1)} custom-call(s32[2,16]{1,0:T(2,128)S(1)} %select_reduce_fusion.1.slots_ref, s32[1]{0:T(128)} %bitcast.core_ref, bf16[3,512,384]{2,1,0:T(8,128)(2,1)S(1)} %get-tuple-element.330.refs_2_.kept_ref, bf16[3,512,384]{2,1,0:T(8,128)(2,1)} %get-tuple-element.331.sent_ref, ...), custom_call_target="tpu_custom_call" | custom-call | flops 7590000128 | bytes 6600000 | tf_op jit(solution)/shard_map/project_back/pallas_call | solution.py:604
  226.0 7.0 %contract_back.3 = (f32[512,768]{1,0:T(8,128)S(1)}, bf16[1,512,384]{2,1,0:T(8,128)(2,1)S(1)}, bf16[4,512,384]{2,1,0:T(8,128)(2,1)S(1)}, bf16[5,512,384]{2,1,0:T(...) custom-call(s32[2,16]{1,0:T(2,128)S(1)} %select_reduce_fusion.1.slots_ref, s32[1]{0:T(128)} %bitcast.core_ref, ...), custom_call_target="tpu_custom_call" | custom-call | flops 12650000384 | bytes 11000000 | tf_op jit(solution)/shard_map/contract_back/pallas_call | solution.py:443
  240.3 4.4 %weight_terms.8 = (bf16[8,144,384]{2,1,0:T(8,128)(2,1)S(1)}, bf16[8,144,384]{2,1,0:T(8,128)(2,1)S(1)}) custom-call(s32[2,16]{1,0:T(2,128)S(1)} %select_reduce_fusion.slots_ref, bf16[4,512,384]{2,1,0:T(8,128)(2,1)S(1)} %copy-done.19, bf16[4,512,384]{2,1,0:T(8,128)(2,1)S(1)} %copy-done.21, bf16[3,512,384]{2,1,0:T(8,128)(2,1)S(1)} %copy-done.35, ...), custom_call_target="tpu_custom_call" | custom-call | flops 5175000064 | bytes 4500000 | tf_op jit(solution)/shard_map/weight_terms/pallas_call | solution.py:666
  244.7 5.9 %collective-permute-done.40 = bf16[8,192,384]{2,1,0:T(8,128)(2,1)} collective-permute-done((bf16[8,192,384]{2,1,0:T(8,128)(2,1)}, bf16[8,192,384]{2,1,0:T(8,128)(2,1)}, u32[]{:S(2)}, u32[]{:S(2)}) %collective-permute-start.40) | collective-permute-done | bytes 1179680 | tf_op jit(solution)/shard_map/ppermute | solution.py:54
  250.7 1.8 add_convert_fusion.2
  257.7 6.7 %expand_back.3 = (f32[512,768]{1,0:T(8,128)S(1)}, bf16[1,512,384]{2,1,0:T(8,128)(2,1)S(1)}, bf16[1,512,384]{2,1,0:T(8,128)(2,1)S(1)}, f32[3,768]{1,0:T(4,128)S(1)}) custom-call(s32[2,16]{1,0:T(2,128)S(1)} %select_reduce_fusion.1.slots_ref, s32[1]{0:T(128)} %bitcast.core_ref, bf16[4,512,384]{2,1,0:T(8,128)(2,1)S(1)} %copy-done.37, ...), custom_call_target="tpu_custom_call" | custom-call | flops 11269999616 | bytes 9800000 | tf_op jit(solution)/shard_map/expand_back/pallas_call | solution.py:514
  264.6 6.8 %weight_terms.9 = (bf16[8,192,384]{2,1,0:T(8,128)(2,1)S(1)}, bf16[8,192,384]{2,1,0:T(8,128)(2,1)S(1)}) custom-call(s32[2,16]{1,0:T(2,128)S(1)} %select_reduce_fusion.slots_ref, bf16[10,512,384]{2,1,0:T(8,128)(2,1)} %get-tuple-element.282.active_ref.refs_0_, bf16[10,512,384]{2,1,0:T(8,128)(2,1)} %collective-permute-done.32.refs_1_, ...), custom_call_target="tpu_custom_call" | custom-call | flops 6899999744 | bytes 6000000 | tf_op jit(solution)/shard_map/weight_terms/pallas_call | solution.py:666
  271.4 8.4 %collective-permute-done.43 = bf16[4,192,384]{2,1,0:T(8,128)(2,1)S(1)} collective-permute-done((bf16[4,192,384]{2,1,0:T(8,128)(2,1)S(1)}, bf16[4,192,384]{2,1,0:T(8,128)(2,1)S(1)}, u32[]{:S(2)}, u32[]{:S(2)}) %collective-permute-start.43) | collective-permute-done | bytes 589856 | tf_op jit(solution)/shard_map/ppermute | solution.py:54
  282.5 1.6 collective-permute-start.47
  285.9 12.4 %attend_back.3 = (bf16[3,512,384]{2,1,0:T(8,128)(2,1)S(1)}, bf16[3,512,384]{2,1,0:T(8,128)(2,1)}, f32[2,2,1,384]{3,2,1,0:T(1,128)S(1)}) custom-call(s32[2,16]{1,0:T(2,128)S(1)} %select_reduce_fusion.1.slots_ref, s32[1]{0:T(128)} %bitcast.core_ref, s32[4]{0:T(128)S(1)} %copy-done.24, bf16[1,512,384]{2,1,0:T(8,128)(2,1)S(1)} %get-tuple-element.366.refs_6_.kept_ref, ...), custom_call_target="tpu_custom_call" | custom-call | flops 23690000384 | bytes 20600000 | tf_op jit(solution)/shard_map/attend_back/pallas_call | solution.py:569
  299.3 8.1 %weight_terms.10 = (bf16[8,240,384]{2,1,0:T(8,128)(2,1)S(1)}, bf16[8,240,384]{2,1,0:T(8,128)(2,1)}) custom-call(s32[2,16]{1,0:T(2,128)S(1)} %select_reduce_fusion.slots_ref, bf16[10,512,384]{2,1,0:T(8,128)(2,1)} %get-tuple-element.282.active_ref.refs_0_, bf16[10,512,384]{2,1,0:T(8,128)(2,1)} %collective-permute-done.32.refs_1_, ...), custom_call_target="tpu_custom_call" | custom-call | flops 8625000448 | bytes 7500000 | tf_op jit(solution)/shard_map/weight_terms/pallas_call | solution.py:666
  317.3 5.7 %project_back.3 = f32[512,768]{1,0:T(8,128)} custom-call(s32[2,16]{1,0:T(2,128)S(1)} %select_reduce_fusion.1.slots_ref, s32[1]{0:T(128)} %bitcast.core_ref, bf16[3,512,384]{2,1,0:T(8,128)(2,1)S(1)} %copy-done.32, bf16[3,512,384]{2,1,0:T(8,128)(2,1)} %get-tuple-element.387.sent_ref, f32[512,768]{1,0:T(8,128)S(1)} %copy-done.39, ...), custom_call_target="tpu_custom_call" | custom-call | flops 7590000128 | bytes 6600000 | tf_op jit(solution)/shard_map/project_back/pallas_call | solution.py:604
  323.2 4.3 %weight_terms.11 = (bf16[8,144,384]{2,1,0:T(8,128)(2,1)S(1)}, bf16[8,144,384]{2,1,0:T(8,128)(2,1)S(1)}) custom-call(s32[2,16]{1,0:T(2,128)S(1)} %select_reduce_fusion.slots_ref, bf16[4,512,384]{2,1,0:T(8,128)(2,1)S(1)} %copy-done.14, bf16[4,512,384]{2,1,0:T(8,128)(2,1)S(1)} %copy-done.17, bf16[3,512,384]{2,1,0:T(8,128)(2,1)S(1)} %copy-done.33, ...), custom_call_target="tpu_custom_call" | custom-call | flops 5175000064 | bytes 4500000 | tf_op jit(solution)/shard_map/weight_terms/pallas_call | solution.py:666
  328.3 1.7 collective-permute-start.54
  330.7 1.7 gather_fusion.1
  332.5 6.4 %collective-permute-done.54 = bf16[1,192,384]{2,1,0:T(8,128)(2,1)} collective-permute-done((bf16[1,192,384]{2,1,0:T(8,128)(2,1)}, bf16[1,192,384]{2,1,0:T(8,128)(2,1)}, u32[]{:S(2)}, u32[]{:S(2)}) %collective-permute-start.54) | collective-permute-done | bytes 147488 | tf_op jit(solution)/shard_map/ppermute | solution.py:54
  340.3 1.8 add_convert_fusion
  346.1 2.6 collective-permute-start.60
  352.1 5.3 %collective-permute-done.60 = bf16[2,192,384]{2,1,0:T(8,128)(2,1)S(1)} collective-permute-done((bf16[2,192,384]{2,1,0:T(8,128)(2,1)S(1)}, bf16[2,192,384]{2,1,0:T(8,128)(2,1)S(1)}, u32[]{:S(2)}, u32[]{:S(2)}) %collective-permute-start.60) | collective-permute-done | bytes 294944 | tf_op jit(solution)/shard_map/ppermute | solution.py:54
  357.4 4.2 %collective-permute-done.62 = bf16[4,240,384]{2,1,0:T(8,128)(2,1)S(1)} collective-permute-done((bf16[4,240,384]{2,1,0:T(8,128)(2,1)S(1)}, bf16[4,240,384]{2,1,0:T(8,128)(2,1)S(1)}, u32[]{:S(2)}, u32[]{:S(2)}) %collective-permute-start.62) | collective-permute-done | bytes 737312 | tf_op jit(solution)/shard_map/ppermute | solution.py:54
  363.3 2.7 collective-permute-start.65
  367.0 3.7 collective-permute-done.64
  370.7 3.2 collective-permute-done.65
  373.9 2.2 collective-permute-done.67
  379.8 8.7 %collective-permute-done.68 = f32[2,2,576]{2,1,0:T(2,128)S(1)} collective-permute-done((f32[2,2,576]{2,1,0:T(2,128)S(1)}, f32[2,2,576]{2,1,0:T(2,128)S(1)}, u32[]{:S(2)}, u32[]{:S(2)}) %collective-permute-start.68) | collective-permute-done | bytes 9248 | tf_op jit(solution)/shard_map/ppermute | solution.py:54
  392.8 7.2 %collective-permute-done.73 = f32[1,2,576]{2,1,0:T(2,128)S(1)} collective-permute-done((f32[1,2,576]{2,1,0:T(2,128)S(1)}, f32[1,2,576]{2,1,0:T(2,128)S(1)}, u32[]{:S(2)}, u32[]{:S(2)}) %collective-permute-start.73) | collective-permute-done | bytes 4640 | tf_op jit(solution)/shard_map/ppermute | solution.py:54
  (436 shorter events, 96.0 us)
Async XLA Ops:
  2.1 9.8 %collective-permute-start = (bf16[1,144,384]{2,1,0:T(8,128)(2,1)S(1)}, bf16[1,144,384]{2,1,0:T(8,128)(2,1)S(1)}, u32[]{:S(2)}, u32[]{:S(2)}) collective-permute-start(bf16[1,144,384]{2,1,0:T(8,128)(2,1)S(1)} %bitcast.82), channel_id=1, source_target_pairs={{0,8},{1,9},{2,10},{3,11},{4,12},{5,13},{6,14},{7,15},{8,0},{9,1},... | collective-permute-start | bytes 331784 | tf_op jit(solution)/shard_map/ppermute | solution.py:54
  11.9 11.7 %collective-permute-start.2 = (bf16[2,144,384]{2,1,0:T(8,128)(2,1)S(1)}, bf16[2,144,384]{2,1,0:T(8,128)(2,1)S(1)}, u32[]{:S(2)}, u32[]{:S(2)}) collective-permute-start(bf16[2,144,384]{2,1,0:T(8,128)(2,1)S(1)} %constant_dynamic-update-slice_fusion), channel_id=1, source_target_pairs={{0,2},{1,3},{2,0},{3,1},{4,6},{5,7},{6,4},{7,5},{8,10},{9,11},{10,... | collective-permute-start | bytes 663560 | tf_op jit(solution)/shard_map/ppermute | solution.py:54
  13.5 10.1 %collective-permute-start.3 = (bf16[1,240,384]{2,1,0:T(8,128)(2,1)S(1)}, bf16[1,240,384]{2,1,0:T(8,128)(2,1)S(1)}, u32[]{:S(2)}, u32[]{:S(2)}) collective-permute-start(bf16[1,240,384]{2,1,0:T(8,128)(2,1)S(1)} %maximum_bitcast_fusion), channel_id=1, source_target_pairs={{0,8},{1,9},{2,10},{3,11},{4,12},{5,13},{6,14},{7,15},{8,0},{9,1},... | collective-permute-start | bytes 552968 | tf_op jit(solution)/shard_map/ppermute | solution.py:54
  23.7 13.0 %collective-permute-start.5 = (bf16[4,144,384]{2,1,0:T(8,128)(2,1)S(1)}, bf16[4,144,384]{2,1,0:T(8,128)(2,1)S(1)}, u32[]{:S(2)}, u32[]{:S(2)}) collective-permute-start(bf16[4,144,384]{2,1,0:T(8,128)(2,1)S(1)} %constant_dynamic-update-slice_fusion.2), channel_id=1, source_target_pairs={{0,4},{1,5},{2,6},{3,7},{4,0},{5,1},{6,2},{7,3},{8,12},{9,13},{10,... | collective-permute-start | bytes 1327112 | tf_op jit(solution)/shard_map/ppermute | solution.py:54
  23.8 12.8 %collective-permute-start.6 = (bf16[2,240,384]{2,1,0:T(8,128)(2,1)S(1)}, bf16[2,240,384]{2,1,0:T(8,128)(2,1)S(1)}, u32[]{:S(2)}, u32[]{:S(2)}) collective-permute-start(bf16[2,240,384]{2,1,0:T(8,128)(2,1)S(1)} %constant_dynamic-update-slice_fusion.4), channel_id=1, source_target_pairs={{0,2},{1,3},{2,0},{3,1},{4,6},{5,7},{6,4},{7,5},{8,10},{9,11},{10,... | collective-permute-start | bytes 1105928 | tf_op jit(solution)/shard_map/ppermute | solution.py:54
  25.4 11.3 %collective-permute-start.7 = (bf16[1,192,384]{2,1,0:T(8,128)(2,1)S(1)}, bf16[1,192,384]{2,1,0:T(8,128)(2,1)S(1)}, u32[]{:S(2)}, u32[]{:S(2)}) collective-permute-start(bf16[1,192,384]{2,1,0:T(8,128)(2,1)S(1)} %constant_dynamic-slice_fusion.8), channel_id=1, source_target_pairs={{0,8},{1,9},{2,10},{3,11},{4,12},{5,13},{6,14},{7,15},{8,0},{9,1},... | collective-permute-start | bytes 442376 | tf_op jit(solution)/shard_map/ppermute | solution.py:54
  27.4 9.2 %collective-permute-start.8 = (f32[4,2,576]{2,1,0:T(2,128)S(1)}, f32[4,2,576]{2,1,0:T(2,128)S(1)}, u32[]{:S(2)}, u32[]{:S(2)}) collective-permute-start(f32[4,2,576]{2,1,0:T(2,128)S(1)} %pad_maximum_fusion.9), channel_id=1, source_target_pairs={{0,4},{1,5},{2,6},{3,7},{4,0},{5,1},{6,2},{7,3},{8,12},{9,13},{10,... | collective-permute-start | bytes 55304 | tf_op jit(solution)/shard_map/ppermute | solution.py:54
  36.8 24.4 %collective-permute-start.9 = (bf16[8,144,384]{2,1,0:T(8,128)(2,1)S(1)}, bf16[8,144,384]{2,1,0:T(8,128)(2,1)}, u32[]{:S(2)}, u32[]{:S(2)}) collective-permute-start(bf16[8,144,384]{2,1,0:T(8,128)(2,1)S(1)} %constant_dynamic-update-slice_fusion.6), channel_id=1, source_target_pairs={{0,1},{1,0},{2,3},{3,2},{4,5},{5,4},{6,7},{7,6},{8,9},{9,8},{10,11... | collective-permute-start | bytes 2654216 | tf_op jit(solution)/shard_map/ppermute | solution.py:54
  38.8 21.6 %collective-permute-start.10 = (bf16[4,240,384]{2,1,0:T(8,128)(2,1)S(1)}, bf16[4,240,384]{2,1,0:T(8,128)(2,1)S(1)}, u32[]{:S(2)}, u32[]{:S(2)}) collective-permute-start(bf16[4,240,384]{2,1,0:T(8,128)(2,1)S(1)} %constant_dynamic-update-slice_fusion.8), channel_id=1, source_target_pairs={{0,4},{1,5},{2,6},{3,7},{4,0},{5,1},{6,2},{7,3},{8,12},{9,13},{10,... | collective-permute-start | bytes 2211848 | tf_op jit(solution)/shard_map/ppermute | solution.py:54
  41.1 18.5 %collective-permute-start.11 = (bf16[2,192,384]{2,1,0:T(8,128)(2,1)S(1)}, bf16[2,192,384]{2,1,0:T(8,128)(2,1)}, u32[]{:S(2)}, u32[]{:S(2)}) collective-permute-start(bf16[2,192,384]{2,1,0:T(8,128)(2,1)S(1)} %constant_dynamic-update-slice_fusion.10), channel_id=1, source_target_pairs={{0,2},{1,3},{2,0},{3,1},{4,6},{5,7},{6,4},{7,5},{8,10},{9,11},{10,... | collective-permute-start | bytes 884744 | tf_op jit(solution)/shard_map/ppermute | solution.py:54
  41.8 11.7 %collective-permute-start.13 = (f32[8,2,576]{2,1,0:T(2,128)S(1)}, f32[8,2,576]{2,1,0:T(2,128)S(1)}, u32[]{:S(2)}, u32[]{:S(2)}) collective-permute-start(f32[8,2,576]{2,1,0:T(2,128)S(1)} %pad_maximum_fusion.8), channel_id=1, source_target_pairs={{0,1},{1,0},{2,3},{3,2},{4,5},{5,4},{6,7},{7,6},{8,9},{9,8},{10,11... | collective-permute-start | bytes 110600 | tf_op jit(solution)/shard_map/ppermute | solution.py:54
  43.6 16.0 %collective-permute-start.12 = (bf16[1,192,384]{2,1,0:T(8,128)(2,1)S(1)}, bf16[1,192,384]{2,1,0:T(8,128)(2,1)S(1)}, u32[]{:S(2)}, u32[]{:S(2)}) collective-permute-start(bf16[1,192,384]{2,1,0:T(8,128)(2,1)S(1)} %maximum_bitcast_fusion.1), channel_id=1, source_target_pairs={{0,8},{1,9},{2,10},{3,11},{4,12},{5,13},{6,14},{7,15},{8,0},{9,1},... | collective-permute-start | bytes 442376 | tf_op jit(solution)/shard_map/ppermute | solution.py:54
  64.2 20.4 %collective-permute-start.16 = (bf16[2,192,384]{2,1,0:T(8,128)(2,1)S(1)}, bf16[2,192,384]{2,1,0:T(8,128)(2,1)S(1)}, u32[]{:S(2)}, u32[]{:S(2)}) collective-permute-start(bf16[2,192,384]{2,1,0:T(8,128)(2,1)S(1)} %constant_dynamic-update-slice_fusion.16), channel_id=1, source_target_pairs={{0,2},{1,3},{2,0},{3,1},{4,6},{5,7},{6,4},{7,5},{8,10},{9,11},{10,... | collective-permute-start | bytes 884744 | tf_op jit(solution)/shard_map/ppermute | solution.py:54
  65.7 19.7 %collective-permute-start.15 = (bf16[4,192,384]{2,1,0:T(8,128)(2,1)S(1)}, bf16[4,192,384]{2,1,0:T(8,128)(2,1)S(1)}, u32[]{:S(2)}, u32[]{:S(2)}) collective-permute-start(bf16[4,192,384]{2,1,0:T(8,128)(2,1)S(1)} %constant_dynamic-update-slice_fusion.14), channel_id=1, source_target_pairs={{0,4},{1,5},{2,6},{3,7},{4,0},{5,1},{6,2},{7,3},{8,12},{9,13},{10,... | collective-permute-start | bytes 1769480 | tf_op jit(solution)/shard_map/ppermute | solution.py:54
  68.7 19.4 %collective-permute-start.14 = (bf16[8,240,384]{2,1,0:T(8,128)(2,1)S(1)}, bf16[8,240,384]{2,1,0:T(8,128)(2,1)S(1)}, u32[]{:S(2)}, u32[]{:S(2)}) collective-permute-start(bf16[8,240,384]{2,1,0:T(8,128)(2,1)S(1)} %constant_dynamic-update-slice_fusion.12), channel_id=1, source_target_pairs={{0,1},{1,0},{2,3},{3,2},{4,5},{5,4},{6,7},{7,6},{8,9},{9,8},{10,11... | collective-permute-start | bytes 4423688 | tf_op jit(solution)/shard_map/ppermute | solution.py:54
  69.8 14.9 %collective-permute-start.17 = (bf16[1,192,384]{2,1,0:T(8,128)(2,1)S(1)}, bf16[1,192,384]{2,1,0:T(8,128)(2,1)S(1)}, u32[]{:S(2)}, u32[]{:S(2)}) collective-permute-start(bf16[1,192,384]{2,1,0:T(8,128)(2,1)S(1)} %bitcast.74), channel_id=1, source_target_pairs={{0,8},{1,9},{2,10},{3,11},{4,12},{5,13},{6,14},{7,15},{8,0},{9,1},... | collective-permute-start | bytes 442376 | tf_op jit(solution)/shard_map/ppermute | solution.py:54
  88.8 18.3 %collective-permute-start.21 = (bf16[2,192,384]{2,1,0:T(8,128)(2,1)S(1)}, bf16[2,192,384]{2,1,0:T(8,128)(2,1)S(1)}, u32[]{:S(2)}, u32[]{:S(2)}) collective-permute-start(bf16[2,192,384]{2,1,0:T(8,128)(2,1)S(1)} %constant_dynamic-update-slice_fusion.24), channel_id=1, source_target_pairs={{0,2},{1,3},{2,0},{3,1},{4,6},{5,7},{6,4},{7,5},{8,10},{9,11},{10,... | collective-permute-start | bytes 884744 | tf_op jit(solution)/shard_map/ppermute | solution.py:54
  90.6 17.9 %collective-permute-start.20 = (bf16[4,192,384]{2,1,0:T(8,128)(2,1)S(1)}, bf16[4,192,384]{2,1,0:T(8,128)(2,1)S(1)}, u32[]{:S(2)}, u32[]{:S(2)}) collective-permute-start(bf16[4,192,384]{2,1,0:T(8,128)(2,1)S(1)} %constant_dynamic-update-slice_fusion.22), channel_id=1, source_target_pairs={{0,4},{1,5},{2,6},{3,7},{4,0},{5,1},{6,2},{7,3},{8,12},{9,13},{10,... | collective-permute-start | bytes 1769480 | tf_op jit(solution)/shard_map/ppermute | solution.py:54
  90.8 17.8 %collective-permute-start.24 = (bf16[4,512,384]{2,1,0:T(8,128)(2,1)S(1)}, bf16[4,512,384]{2,1,0:T(8,128)(2,1)S(1)}, u32[]{:S(2)}, u32[]{:S(2)}) collective-permute-start(bf16[4,512,384]{2,1,0:T(8,128)(2,1)S(1)} %get-tuple-element.270.context_ref.refs_4_.refs_0_), channel_id=1, source_target_pairs={{0,16},{16,0},{1,17},{17,1},{2,18},{18,2},{3,19},{19,3},{4,20},{20... | collective-permute-start | bytes 4718600 | tf_op jit(solution)/shard_map/ppermute | solution.py:65
  91.0 17.6 %collective-permute-start.19 = (bf16[8,192,384]{2,1,0:T(8,128)(2,1)S(1)}, bf16[8,192,384]{2,1,0:T(8,128)(2,1)S(1)}, u32[]{:S(2)}, u32[]{:S(2)}) collective-permute-start(bf16[8,192,384]{2,1,0:T(8,128)(2,1)S(1)} %constant_dynamic-update-slice_fusion.20), channel_id=1, source_target_pairs={{0,1},{1,0},{2,3},{3,2},{4,5},{5,4},{6,7},{7,6},{8,9},{9,8},{10,11... | collective-permute-start | bytes 3538952 | tf_op jit(solution)/shard_map/ppermute | solution.py:54
  94.1 13.0 %collective-permute-start.22 = (bf16[1,192,384]{2,1,0:T(8,128)(2,1)S(1)}, bf16[1,192,384]{2,1,0:T(8,128)(2,1)S(1)}, u32[]{:S(2)}, u32[]{:S(2)}) collective-permute-start(bf16[1,192,384]{2,1,0:T(8,128)(2,1)S(1)} %copy-done.62), channel_id=1, source_target_pairs={{0,8},{1,9},{2,10},{3,11},{4,12},{5,13},{6,14},{7,15},{8,0},{9,1},... | collective-permute-start | bytes 442376 | tf_op jit(solution)/shard_map/ppermute | solution.py:54
  110.3 11.9 %collective-permute-start.27 = (bf16[2,192,384]{2,1,0:T(8,128)(2,1)S(1)}, bf16[2,192,384]{2,1,0:T(8,128)(2,1)}, u32[]{:S(2)}, u32[]{:S(2)}) collective-permute-start(bf16[2,192,384]{2,1,0:T(8,128)(2,1)S(1)} %constant_dynamic-update-slice_fusion.32), channel_id=1, source_target_pairs={{0,2},{1,3},{2,0},{3,1},{4,6},{5,7},{6,4},{7,5},{8,10},{9,11},{10,... | collective-permute-start | bytes 884744 | tf_op jit(solution)/shard_map/ppermute | solution.py:54
  111.7 17.6 %collective-permute-start.25 = (bf16[8,192,384]{2,1,0:T(8,128)(2,1)S(1)}, bf16[8,192,384]{2,1,0:T(8,128)(2,1)S(1)}, u32[]{:S(2)}, u32[]{:S(2)}) collective-permute-start(bf16[8,192,384]{2,1,0:T(8,128)(2,1)S(1)} %constant_dynamic-update-slice_fusion.28), channel_id=1, source_target_pairs={{0,1},{1,0},{2,3},{3,2},{4,5},{5,4},{6,7},{7,6},{8,9},{9,8},{10,11... | collective-permute-start | bytes 3538952 | tf_op jit(solution)/shard_map/ppermute | solution.py:54
  113.6 15.2 %collective-permute-start.26 = (bf16[4,192,384]{2,1,0:T(8,128)(2,1)S(1)}, bf16[4,192,384]{2,1,0:T(8,128)(2,1)S(1)}, u32[]{:S(2)}, u32[]{:S(2)}) collective-permute-start(bf16[4,192,384]{2,1,0:T(8,128)(2,1)S(1)} %constant_dynamic-update-slice_fusion.30), channel_id=1, source_target_pairs={{0,4},{1,5},{2,6},{3,7},{4,0},{5,1},{6,2},{7,3},{8,12},{9,13},{10,... | collective-permute-start | bytes 1769480 | tf_op jit(solution)/shard_map/ppermute | solution.py:54
  114.5 34.5 %collective-permute-start.32 = (bf16[10,512,384]{2,1,0:T(8,128)(2,1)}, bf16[10,512,384]{2,1,0:T(8,128)(2,1)}, u32[]{:S(2)}, u32[]{:S(2)}) collective-permute-start(bf16[10,512,384]{2,1,0:T(8,128)(2,1)} %get-tuple-element.282.active_ref.refs_0_), channel_id=1, source_target_pairs={{0,16},{16,0},{1,17},{17,1},{2,18},{18,2},{3,19},{19,3},{4,20},{20... | collective-permute-start | bytes 11796488 | tf_op jit(solution)/shard_map/ppermute | solution.py:65
  131.7 15.5 %collective-permute-start.30 = (bf16[4,192,384]{2,1,0:T(8,128)(2,1)S(1)}, bf16[4,192,384]{2,1,0:T(8,128)(2,1)S(1)}, u32[]{:S(2)}, u32[]{:S(2)}) collective-permute-start(bf16[4,192,384]{2,1,0:T(8,128)(2,1)S(1)} %constant_dynamic-update-slice_fusion.38), channel_id=1, source_target_pairs={{0,4},{1,5},{2,6},{3,7},{4,0},{5,1},{6,2},{7,3},{8,12},{9,13},{10,... | collective-permute-start | bytes 1769480 | tf_op jit(solution)/shard_map/ppermute | solution.py:54
  132.8 16.3 %collective-permute-start.29 = (bf16[8,192,384]{2,1,0:T(8,128)(2,1)S(1)}, bf16[8,192,384]{2,1,0:T(8,128)(2,1)S(1)}, u32[]{:S(2)}, u32[]{:S(2)}) collective-permute-start(bf16[8,192,384]{2,1,0:T(8,128)(2,1)S(1)} %constant_dynamic-update-slice_fusion.36), channel_id=1, source_target_pairs={{0,1},{1,0},{2,3},{3,2},{4,5},{5,4},{6,7},{7,6},{8,9},{9,8},{10,11... | collective-permute-start | bytes 3538952 | tf_op jit(solution)/shard_map/ppermute | solution.py:54
  149.6 16.9 %collective-permute-start.35 = (bf16[4,512,384]{2,1,0:T(8,128)(2,1)S(1)}, bf16[4,512,384]{2,1,0:T(8,128)(2,1)S(1)}, u32[]{:S(2)}, u32[]{:S(2)}) collective-permute-start(bf16[4,512,384]{2,1,0:T(8,128)(2,1)S(1)} %get-tuple-element.297.context_ref.refs_4_.refs_0_), channel_id=1, source_target_pairs={{0,16},{16,0},{1,17},{17,1},{2,18},{18,2},{3,19},{19,3},{4,20},{20... | collective-permute-start | bytes 4718600 | tf_op jit(solution)/shard_map/ppermute | solution.py:65
  150.2 16.3 %collective-permute-start.33 = (bf16[8,192,384]{2,1,0:T(8,128)(2,1)S(1)}, bf16[8,192,384]{2,1,0:T(8,128)(2,1)S(1)}, u32[]{:S(2)}, u32[]{:S(2)}) collective-permute-start(bf16[8,192,384]{2,1,0:T(8,128)(2,1)S(1)} %constant_dynamic-update-slice_fusion.42), channel_id=1, source_target_pairs={{0,1},{1,0},{2,3},{3,2},{4,5},{5,4},{6,7},{7,6},{8,9},{9,8},{10,11... | collective-permute-start | bytes 3538952 | tf_op jit(solution)/shard_map/ppermute | solution.py:54
  166.9 26.0 %collective-permute-start.37 = (bf16[10,512,384]{2,1,0:T(8,128)(2,1)S(1)}, bf16[10,512,384]{2,1,0:T(8,128)(2,1)S(1)}, u32[]{:S(2)}, u32[]{:S(2)}) collective-permute-start(bf16[10,512,384]{2,1,0:T(8,128)(2,1)S(1)} %get-tuple-element.304.active_ref.refs_0_), channel_id=1, source_target_pairs={{0,16},{16,0},{1,17},{17,1},{2,18},{18,2},{3,19},{19,3},{4,20},{20... | collective-permute-start | bytes 11796488 | tf_op jit(solution)/shard_map/ppermute | solution.py:65
  184.8 8.2 %collective-permute-start.38 = (bf16[5,512,384]{2,1,0:T(8,128)(2,1)S(1)}, bf16[5,512,384]{2,1,0:T(8,128)(2,1)S(1)}, u32[]{:S(2)}, u32[]{:S(2)}) collective-permute-start(bf16[5,512,384]{2,1,0:T(8,128)(2,1)S(1)} %get-tuple-element.312.sent_ref), channel_id=1, source_target_pairs={{0,16},{16,0},{1,17},{17,1},{2,18},{18,2},{3,19},{19,3},{4,20},{20... | collective-permute-start | bytes 5898248 | tf_op jit(solution)/shard_map/ppermute | solution.py:65
  218.2 18.0 %collective-permute-start.42 = (bf16[3,512,384]{2,1,0:T(8,128)(2,1)}, bf16[3,512,384]{2,1,0:T(8,128)(2,1)}, u32[]{:S(2)}, u32[]{:S(2)}) collective-permute-start(bf16[3,512,384]{2,1,0:T(8,128)(2,1)} %get-tuple-element.331.sent_ref), channel_id=1, source_target_pairs={{0,16},{16,0},{1,17},{17,1},{2,18},{18,2},{3,19},{19,3},{4,20},{20... | collective-permute-start | bytes 3538952 | tf_op jit(solution)/shard_map/ppermute | solution.py:65
  218.3 32.3 %collective-permute-start.41 = (bf16[8,240,384]{2,1,0:T(8,128)(2,1)}, bf16[8,240,384]{2,1,0:T(8,128)(2,1)}, u32[]{:S(2)}, u32[]{:S(2)}) collective-permute-start(bf16[8,240,384]{2,1,0:T(8,128)(2,1)} %get-tuple-element.326), channel_id=1, source_target_pairs={{0,1},{1,0},{2,3},{3,2},{4,5},{5,4},{6,7},{7,6},{8,9},{9,8},{10,11... | collective-permute-start | bytes 4423688 | tf_op jit(solution)/shard_map/ppermute | solution.py:54
  219.8 30.9 %collective-permute-start.40 = (bf16[8,192,384]{2,1,0:T(8,128)(2,1)}, bf16[8,192,384]{2,1,0:T(8,128)(2,1)}, u32[]{:S(2)}, u32[]{:S(2)}) collective-permute-start(bf16[8,192,384]{2,1,0:T(8,128)(2,1)} %get-tuple-element.325), channel_id=1, source_target_pairs={{0,1},{1,0},{2,3},{3,2},{4,5},{5,4},{6,7},{7,6},{8,9},{9,8},{10,11... | collective-permute-start | bytes 3538952 | tf_op jit(solution)/shard_map/ppermute | solution.py:54
  236.0 28.5 %collective-permute-start.46 = (bf16[5,512,384]{2,1,0:T(8,128)(2,1)}, bf16[5,512,384]{2,1,0:T(8,128)(2,1)}, u32[]{:S(2)}, u32[]{:S(2)}) collective-permute-start(bf16[5,512,384]{2,1,0:T(8,128)(2,1)} %get-tuple-element.352.sent_ref), channel_id=1, source_target_pairs={{0,16},{16,0},{1,17},{17,1},{2,18},{18,2},{3,19},{19,3},{4,20},{20... | collective-permute-start | bytes 5898248 | tf_op jit(solution)/shard_map/ppermute | solution.py:65
  252.5 27.3 %collective-permute-start.45 = (bf16[4,240,384]{2,1,0:T(8,128)(2,1)S(1)}, bf16[4,240,384]{2,1,0:T(8,128)(2,1)S(1)}, u32[]{:S(2)}, u32[]{:S(2)}) collective-permute-start(bf16[4,240,384]{2,1,0:T(8,128)(2,1)S(1)} %get-tuple-element.454), channel_id=1, source_target_pairs={{0,2},{1,3},{2,0},{3,1},{4,6},{5,7},{6,4},{7,5},{8,10},{9,11},{10,... | collective-permute-start | bytes 2211848 | tf_op jit(solution)/shard_map/ppermute | solution.py:54
  255.2 24.6 %collective-permute-start.43 = (bf16[4,192,384]{2,1,0:T(8,128)(2,1)S(1)}, bf16[4,192,384]{2,1,0:T(8,128)(2,1)S(1)}, u32[]{:S(2)}, u32[]{:S(2)}) collective-permute-start(bf16[4,192,384]{2,1,0:T(8,128)(2,1)S(1)} %get-tuple-element.458), channel_id=1, source_target_pairs={{0,2},{1,3},{2,0},{3,1},{4,6},{5,7},{6,4},{7,5},{8,10},{9,11},{10,... | collective-permute-start | bytes 1769480 | tf_op jit(solution)/shard_map/ppermute | solution.py:54
  256.3 23.6 %collective-permute-start.44 = (bf16[8,144,384]{2,1,0:T(8,128)(2,1)S(1)}, bf16[8,144,384]{2,1,0:T(8,128)(2,1)S(1)}, u32[]{:S(2)}, u32[]{:S(2)}) collective-permute-start(bf16[8,144,384]{2,1,0:T(8,128)(2,1)S(1)} %get-tuple-element.346), channel_id=1, source_target_pairs={{0,1},{1,0},{2,3},{3,2},{4,5},{5,4},{6,7},{7,6},{8,9},{9,8},{10,11... | collective-permute-start | bytes 2654216 | tf_op jit(solution)/shard_map/ppermute | solution.py:54
  264.5 34.9 %collective-permute-start.51 = (bf16[1,512,384]{2,1,0:T(8,128)(2,1)S(1)}, bf16[1,512,384]{2,1,0:T(8,128)(2,1)S(1)}, u32[]{:S(2)}, u32[]{:S(2)}) collective-permute-start(bf16[1,512,384]{2,1,0:T(8,128)(2,1)S(1)} %get-tuple-element.369.sent_ref), channel_id=1, source_target_pairs={{0,16},{16,0},{1,17},{17,1},{2,18},{18,2},{3,19},{19,3},{4,20},{20... | collective-permute-start | bytes 1179656 | tf_op jit(solution)/shard_map/ppermute | solution.py:65
  280.1 27.4 %collective-permute-start.50 = (bf16[2,240,384]{2,1,0:T(8,128)(2,1)S(1)}, bf16[2,240,384]{2,1,0:T(8,128)(2,1)S(1)}, u32[]{:S(2)}, u32[]{:S(2)}) collective-permute-start(bf16[2,240,384]{2,1,0:T(8,128)(2,1)S(1)} %get-tuple-element.466), channel_id=1, source_target_pairs={{0,4},{1,5},{2,6},{3,7},{4,0},{5,1},{6,2},{7,3},{8,12},{9,13},{10,... | collective-permute-start | bytes 1105928 | tf_op jit(solution)/shard_map/ppermute | solution.py:54
  281.5 25.9 %collective-permute-start.49 = (bf16[4,144,384]{2,1,0:T(8,128)(2,1)S(1)}, bf16[4,144,384]{2,1,0:T(8,128)(2,1)S(1)}, u32[]{:S(2)}, u32[]{:S(2)}) collective-permute-start(bf16[4,144,384]{2,1,0:T(8,128)(2,1)S(1)} %get-tuple-element.462), channel_id=1, source_target_pairs={{0,2},{1,3},{2,0},{3,1},{4,6},{5,7},{6,4},{7,5},{8,10},{9,11},{10,... | collective-permute-start | bytes 1327112 | tf_op jit(solution)/shard_map/ppermute | solution.py:54
  282.5 24.9 %collective-permute-start.47 = (bf16[8,192,384]{2,1,0:T(8,128)(2,1)S(1)}, bf16[8,192,384]{2,1,0:T(8,128)(2,1)S(1)}, u32[]{:S(2)}, u32[]{:S(2)}) collective-permute-start(bf16[8,192,384]{2,1,0:T(8,128)(2,1)S(1)} %get-tuple-element.364), channel_id=1, source_target_pairs={{0,1},{1,0},{2,3},{3,2},{4,5},{5,4},{6,7},{7,6},{8,9},{9,8},{10,11... | collective-permute-start | bytes 3538952 | tf_op jit(solution)/shard_map/ppermute | solution.py:54
  285.0 22.4 %collective-permute-start.48 = (bf16[2,192,384]{2,1,0:T(8,128)(2,1)S(1)}, bf16[2,192,384]{2,1,0:T(8,128)(2,1)S(1)}, u32[]{:S(2)}, u32[]{:S(2)}) collective-permute-start(bf16[2,192,384]{2,1,0:T(8,128)(2,1)S(1)} %get-tuple-element.470), channel_id=1, source_target_pairs={{0,4},{1,5},{2,6},{3,7},{4,0},{5,1},{6,2},{7,3},{8,12},{9,13},{10,... | collective-permute-start | bytes 884744 | tf_op jit(solution)/shard_map/ppermute | solution.py:54
  299.3 23.8 %collective-permute-start.57 = (bf16[3,512,384]{2,1,0:T(8,128)(2,1)}, bf16[3,512,384]{2,1,0:T(8,128)(2,1)}, u32[]{:S(2)}, u32[]{:S(2)}) collective-permute-start(bf16[3,512,384]{2,1,0:T(8,128)(2,1)} %get-tuple-element.387.sent_ref), channel_id=1, source_target_pairs={{0,16},{16,0},{1,17},{17,1},{2,18},{18,2},{3,19},{19,3},{4,20},{20... | collective-permute-start | bytes 3538952 | tf_op jit(solution)/shard_map/ppermute | solution.py:65
  308.3 32.0 %collective-permute-start.56 = (bf16[1,240,384]{2,1,0:T(8,128)(2,1)}, bf16[1,240,384]{2,1,0:T(8,128)(2,1)}, u32[]{:S(2)}, u32[]{:S(2)}) collective-permute-start(bf16[1,240,384]{2,1,0:T(8,128)(2,1)} %get-tuple-element.492), channel_id=1, source_target_pairs={{0,8},{1,9},{2,10},{3,11},{4,12},{5,13},{6,14},{7,15},{8,0},{9,1},... | collective-permute-start | bytes 552968 | tf_op jit(solution)/shard_map/ppermute | solution.py:54
  310.8 29.6 %collective-permute-start.55 = (bf16[2,144,384]{2,1,0:T(8,128)(2,1)}, bf16[2,144,384]{2,1,0:T(8,128)(2,1)}, u32[]{:S(2)}, u32[]{:S(2)}) collective-permute-start(bf16[2,144,384]{2,1,0:T(8,128)(2,1)} %get-tuple-element.482), channel_id=1, source_target_pairs={{0,4},{1,5},{2,6},{3,7},{4,0},{5,1},{6,2},{7,3},{8,12},{9,13},{10,... | collective-permute-start | bytes 663560 | tf_op jit(solution)/shard_map/ppermute | solution.py:54
  312.9 27.5 %collective-permute-start.52 = (bf16[4,192,384]{2,1,0:T(8,128)(2,1)}, bf16[4,192,384]{2,1,0:T(8,128)(2,1)}, u32[]{:S(2)}, u32[]{:S(2)}) collective-permute-start(bf16[4,192,384]{2,1,0:T(8,128)(2,1)} %get-tuple-element.456), channel_id=1, source_target_pairs={{0,2},{1,3},{2,0},{3,1},{4,6},{5,7},{6,4},{7,5},{8,10},{9,11},{10,... | collective-permute-start | bytes 1769480 | tf_op jit(solution)/shard_map/ppermute | solution.py:54
  313.8 26.5 %collective-permute-start.53 = (bf16[8,240,384]{2,1,0:T(8,128)(2,1)}, bf16[8,240,384]{2,1,0:T(8,128)(2,1)}, u32[]{:S(2)}, u32[]{:S(2)}) collective-permute-start(bf16[8,240,384]{2,1,0:T(8,128)(2,1)} %get-tuple-element.383), channel_id=1, source_target_pairs={{0,1},{1,0},{2,3},{3,2},{4,5},{5,4},{6,7},{7,6},{8,9},{9,8},{10,11... | collective-permute-start | bytes 4423688 | tf_op jit(solution)/shard_map/ppermute | solution.py:54
  328.3 10.6 %collective-permute-start.54 = (bf16[1,192,384]{2,1,0:T(8,128)(2,1)}, bf16[1,192,384]{2,1,0:T(8,128)(2,1)}, u32[]{:S(2)}, u32[]{:S(2)}) collective-permute-start(bf16[1,192,384]{2,1,0:T(8,128)(2,1)} %get-tuple-element.496), channel_id=1, source_target_pairs={{0,8},{1,9},{2,10},{3,11},{4,12},{5,13},{6,14},{7,15},{8,0},{9,1},... | collective-permute-start | bytes 442376 | tf_op jit(solution)/shard_map/ppermute | solution.py:54
  338.8 11.9 %collective-permute-start.59 = (f32[8,2,576]{2,1,0:T(2,128)S(1)}, f32[8,2,576]{2,1,0:T(2,128)S(1)}, u32[]{:S(2)}, u32[]{:S(2)}) collective-permute-start(f32[8,2,576]{2,1,0:T(2,128)S(1)} %get-tuple-element.534), channel_id=1, source_target_pairs={{0,1},{1,0},{2,3},{3,2},{4,5},{5,4},{6,7},{7,6},{8,9},{9,8},{10,11... | collective-permute-start | bytes 110600 | tf_op jit(solution)/shard_map/ppermute | solution.py:54
  342.2 19.4 %collective-permute-start.62 = (bf16[4,240,384]{2,1,0:T(8,128)(2,1)S(1)}, bf16[4,240,384]{2,1,0:T(8,128)(2,1)S(1)}, u32[]{:S(2)}, u32[]{:S(2)}) collective-permute-start(bf16[4,240,384]{2,1,0:T(8,128)(2,1)S(1)} %get-tuple-element.452), channel_id=1, source_target_pairs={{0,2},{1,3},{2,0},{3,1},{4,6},{5,7},{6,4},{7,5},{8,10},{9,11},{10,... | collective-permute-start | bytes 2211848 | tf_op jit(solution)/shard_map/ppermute | solution.py:54
  343.3 18.3 %collective-permute-start.61 = (bf16[8,144,384]{2,1,0:T(8,128)(2,1)S(1)}, bf16[8,144,384]{2,1,0:T(8,128)(2,1)S(1)}, u32[]{:S(2)}, u32[]{:S(2)}) collective-permute-start(bf16[8,144,384]{2,1,0:T(8,128)(2,1)S(1)} %get-tuple-element.405), channel_id=1, source_target_pairs={{0,1},{1,0},{2,3},{3,2},{4,5},{5,4},{6,7},{7,6},{8,9},{9,8},{10,11... | collective-permute-start | bytes 2654216 | tf_op jit(solution)/shard_map/ppermute | solution.py:54
  346.1 11.2 %collective-permute-start.60 = (bf16[2,192,384]{2,1,0:T(8,128)(2,1)S(1)}, bf16[2,192,384]{2,1,0:T(8,128)(2,1)S(1)}, u32[]{:S(2)}, u32[]{:S(2)}) collective-permute-start(bf16[2,192,384]{2,1,0:T(8,128)(2,1)S(1)} %get-tuple-element.468), channel_id=1, source_target_pairs={{0,4},{1,5},{2,6},{3,7},{4,0},{5,1},{6,2},{7,3},{8,12},{9,13},{10,... | collective-permute-start | bytes 884744 | tf_op jit(solution)/shard_map/ppermute | solution.py:54
  361.8 14.3 %collective-permute-start.67 = (bf16[2,240,384]{2,1,0:T(8,128)(2,1)S(1)}, bf16[2,240,384]{2,1,0:T(8,128)(2,1)S(1)}, u32[]{:S(2)}, u32[]{:S(2)}) collective-permute-start(bf16[2,240,384]{2,1,0:T(8,128)(2,1)S(1)} %get-tuple-element.464), channel_id=1, source_target_pairs={{0,4},{1,5},{2,6},{3,7},{4,0},{5,1},{6,2},{7,3},{8,12},{9,13},{10,... | collective-permute-start | bytes 1105928 | tf_op jit(solution)/shard_map/ppermute | solution.py:54
  362.1 14.0 %collective-permute-start.66 = (bf16[4,144,384]{2,1,0:T(8,128)(2,1)S(1)}, bf16[4,144,384]{2,1,0:T(8,128)(2,1)S(1)}, u32[]{:S(2)}, u32[]{:S(2)}) collective-permute-start(bf16[4,144,384]{2,1,0:T(8,128)(2,1)S(1)} %get-tuple-element.460), channel_id=1, source_target_pairs={{0,2},{1,3},{2,0},{3,1},{4,6},{5,7},{6,4},{7,5},{8,10},{9,11},{10,... | collective-permute-start | bytes 1327112 | tf_op jit(solution)/shard_map/ppermute | solution.py:54
  363.3 10.6 %collective-permute-start.65 = (bf16[1,192,384]{2,1,0:T(8,128)(2,1)S(1)}, bf16[1,192,384]{2,1,0:T(8,128)(2,1)S(1)}, u32[]{:S(2)}, u32[]{:S(2)}) collective-permute-start(bf16[1,192,384]{2,1,0:T(8,128)(2,1)S(1)} %get-tuple-element.494), channel_id=1, source_target_pairs={{0,8},{1,9},{2,10},{3,11},{4,12},{5,13},{6,14},{7,15},{8,0},{9,1},... | collective-permute-start | bytes 442376 | tf_op jit(solution)/shard_map/ppermute | solution.py:54
  376.2 12.3 %collective-permute-start.70 = (bf16[1,240,384]{2,1,0:T(8,128)(2,1)S(1)}, bf16[1,240,384]{2,1,0:T(8,128)(2,1)S(1)}, u32[]{:S(2)}, u32[]{:S(2)}) collective-permute-start(bf16[1,240,384]{2,1,0:T(8,128)(2,1)S(1)} %get-tuple-element.490), channel_id=1, source_target_pairs={{0,8},{1,9},{2,10},{3,11},{4,12},{5,13},{6,14},{7,15},{8,0},{9,1},... | collective-permute-start | bytes 552968 | tf_op jit(solution)/shard_map/ppermute | solution.py:54
  377.5 10.9 %collective-permute-start.69 = (bf16[2,144,384]{2,1,0:T(8,128)(2,1)S(1)}, bf16[2,144,384]{2,1,0:T(8,128)(2,1)S(1)}, u32[]{:S(2)}, u32[]{:S(2)}) collective-permute-start(bf16[2,144,384]{2,1,0:T(8,128)(2,1)S(1)} %get-tuple-element.480), channel_id=1, source_target_pairs={{0,4},{1,5},{2,6},{3,7},{4,0},{5,1},{6,2},{7,3},{8,12},{9,13},{10,... | collective-permute-start | bytes 663560 | tf_op jit(solution)/shard_map/ppermute | solution.py:54
  379.0 9.4 %collective-permute-start.68 = (f32[2,2,576]{2,1,0:T(2,128)S(1)}, f32[2,2,576]{2,1,0:T(2,128)S(1)}, u32[]{:S(2)}, u32[]{:S(2)}) collective-permute-start(f32[2,2,576]{2,1,0:T(2,128)S(1)} %get-tuple-element.536), channel_id=1, source_target_pairs={{0,4},{1,5},{2,6},{3,7},{4,0},{5,1},{6,2},{7,3},{8,12},{9,13},{10,... | collective-permute-start | bytes 27656 | tf_op jit(solution)/shard_map/ppermute | solution.py:54
  388.5 11.4 %collective-permute-start.72 = (bf16[1,144,384]{2,1,0:T(8,128)(2,1)S(1)}, bf16[1,144,384]{2,1,0:T(8,128)(2,1)S(1)}, u32[]{:S(2)}, u32[]{:S(2)}) collective-permute-start(bf16[1,144,384]{2,1,0:T(8,128)(2,1)S(1)} %get-tuple-element.504), channel_id=1, source_target_pairs={{0,24},{1,25},{2,26},{3,27},{4,28},{5,29},{6,30},{7,31},{8,16},{9,... | collective-permute-start | bytes 331784 | tf_op jit(solution)/shard_map/ppermute | solution.py:62
  388.7 11.3 %collective-permute-start.74 = (bf16[1,144,384]{2,1,0:T(8,128)(2,1)S(1)}, bf16[1,144,384]{2,1,0:T(8,128)(2,1)S(1)}, u32[]{:S(2)}, u32[]{:S(2)}) collective-permute-start(bf16[1,144,384]{2,1,0:T(8,128)(2,1)S(1)} %get-tuple-element.504), channel_id=1, source_target_pairs={{0,8},{1,9},{2,10},{3,11},{4,12},{5,13},{6,14},{7,15},{8,0},{9,1},... | collective-permute-start | bytes 331784 | tf_op jit(solution)/shard_map/ppermute | solution.py:54
  389.9 10.1 %collective-permute-start.71 = (bf16[1,144,384]{2,1,0:T(8,128)(2,1)S(1)}, bf16[1,144,384]{2,1,0:T(8,128)(2,1)S(1)}, u32[]{:S(2)}, u32[]{:S(2)}) collective-permute-start(bf16[1,144,384]{2,1,0:T(8,128)(2,1)S(1)} %get-tuple-element.424), channel_id=1, source_target_pairs={{0,16},{16,0},{1,17},{17,1},{2,18},{18,2},{3,19},{19,3},{4,20},{20... | collective-permute-start | bytes 331784 | tf_op jit(solution)/shard_map/ppermute | solution.py:65
  391.4 8.6 %collective-permute-start.73 = (f32[1,2,576]{2,1,0:T(2,128)S(1)}, f32[1,2,576]{2,1,0:T(2,128)S(1)}, u32[]{:S(2)}, u32[]{:S(2)}) collective-permute-start(f32[1,2,576]{2,1,0:T(2,128)S(1)} %get-tuple-element.538), channel_id=1, source_target_pairs={{0,8},{1,9},{2,10},{3,11},{4,12},{5,13},{6,14},{7,15},{8,0},{9,1},... | collective-permute-start | bytes 13832 | tf_op jit(solution)/shard_map/ppermute | solution.py:54
  392.6 8.1 %collective-permute-start.75 = (bf16[1008,384]{1,0:T(8,128)(2,1)S(1)}, bf16[1008,384]{1,0:T(8,128)(2,1)S(1)}, u32[]{:S(2)}, u32[]{:S(2)}) collective-permute-start(bf16[1008,384]{1,0:T(8,128)(2,1)S(1)} %get-tuple-element.442), channel_id=1, source_target_pairs={{0,16},{16,0},{1,17},{17,1},{2,18},{18,2},{3,19},{19,3},{4,20},{20... | collective-permute-start | bytes 2322440 | tf_op jit(solution)/shard_map/ppermute | solution.py:65
  (89 other events, 624.1 us)

commit v8 on v7

--- a/solution.py
+++ b/solution.py
@@ -792,24 +792,42 @@
     vector_all = jnp.take(vector_blocks, mixed_slots[0], axis=0).transpose(1, 0, 2).reshape(LAYERS, -1, width)
 
     hidden, h_low = tokens, tokens
-    kept, twins = [], []
+    kept, twins = [], [None] * (2 * LAYERS)
+    started = []
+
+    def close(*values):
+        values = gather.end((*values, *(twins[place] for place in started)))
+        for place, value in zip(reversed(started), reversed(values)):
+            twins[place] = value
+        values = values[: len(values) - len(started)]
+        started.clear()
+        return values
+
+    def trade(place, value, behind):
+        value, behind = lax.optimization_barrier((value, behind))
+        twins[place] = net.twin(value)
+        return behind
+
     for level in range(LAYERS):
         rows = vector_all[level]
         last = level == LAYERS - 1
         qkv, left_a = project(tables, h_low, rows, *weight(level, 0))
-        if level:
-            left_a, twins[1] = gather.end((left_a, twins[1]))
-        else:
-            (left_a,) = gather.end((left_a,))
-        twins.append(net.twin(left_a))
+        (left_a,) = close(left_a)
         first_sum, first_low = mix(tables, left_a, hidden, rows, *weight(level, 1))
         left_b, slope = expand(tables, first_low, rows, *weight(level, 2), parts)
-        left_b, twins[2 * level], slope = gather.end((left_b, twins[2 * level], slope))
-        twins.append(net.twin(left_b))
+        left_b = trade(2 * level, left_a, left_b)
+        left_b, slope = close(left_b, slope)
+        started.append(2 * level)
+        if last:
+            twins[2 * level + 1] = net.twin(left_b)
         second_sum, hidden, h_low = contract(
             tables, left_b, first_sum, rows, *weight(level, 3), inner_width, last
         )
-        (h_low,) = gather.end((h_low,))
+        if not last:
+            h_low = trade(2 * level + 1, left_b, h_low)
+        (h_low,) = close(h_low)
+        if not last:
+            started.append(2 * level + 1)
         kept.append((qkv, left_a, first_sum, left_b, slope, second_sum))
     layer_out = h_low
 
@@ -833,25 +851,19 @@
         )
         a_received = net.twin(a_sent)
         term = weight_terms(slots, count, (left_b, twin_b, 0, 2 * parts, f_kept, received, parts))
-        if level == 0:
-            *term, d_first_sum, a_kept, a_sent = reduce.turn((*term, d_first_sum, a_kept, a_sent))
-            reduce.push((level, "down"), *term)
+        *term, d_first_sum, a_kept, a_sent = reduce.turn((*term, d_first_sum, a_kept, a_sent))
+        reduce.push((level, "down"), *term)
         up_term = weight_terms(
             slots,
             count,
             (left_b, twin_b, 2 * parts, 2, u_kept, received, 0),
             (left_a, twin_a, 2, 2, a_kept, a_received, 0),
         )
-        if level:
-            *both, d_first_sum, a_kept, a_sent = reduce.turn((*term, *up_term, d_first_sum, a_kept, a_sent))
-            reduce.push((level, "down"), *both[:2])
-            reduce.push((level, "up"), *both[2:])
 
         q_kept, q_sent, sums_qv = attend_back(tables, a_kept, a_sent, qkv, *weight(level, 1))
         q_received = net.twin(q_sent)
-        if level == 0:
-            *up_term, q_kept, q_sent, sums_qv = reduce.turn((*up_term, q_kept, q_sent, sums_qv))
-            reduce.push((level, "up"), *up_term)
+        *up_term, q_kept, q_sent, sums_qv = reduce.turn((*up_term, q_kept, q_sent, sums_qv))
+        reduce.push((level, "up"), *up_term)
         d_vectors[level] = jnp.concatenate(
             [sums_qv.reshape(2, width), sums_a, sums_b, sums_u.reshape(-1, width)]
         ).reshape(count, -1)

time: 412 us -> 401 us (0.973)
  waiting for transfers between devices: 127 us -> 119 us
    ppermute x56, waiting for transfers between devices: 121 us -> 111 us  [trade(): return lax.ppermute(value, ('rep', 'fsdp'), pairs)]
    unnamed x206 -> x208, local copies, waits for them, and re-layouts: 19.3 us -> 20.4 us
  transfers between devices with their start and end apart: 76 -> 76, of which waited for: 31 -> 31; matrix products, arithmetic and copies ran while one was open for 7% -> 6% of each run, Pallas kernels for 32% -> 37%
where the time goes in v8:
time: 401 us; the launch traced here: 393 us
  Pallas kernels  147 us (37%)
  waiting for transfers between devices  119 us (30%)
  starting transfers between devices  72.1 us (18%)
  local copies, waits for them, and re-layouts  30 us (7%)
  other arithmetic  23 us (6%)
    ppermute x56, waiting for transfers between devices, trade(): return lax.ppermute(value, ('rep', 'fsdp'), pairs)  111 us
    ppermute x56, starting transfers between devices, trade(): return lax.ppermute(value, ('rep', 'fsdp'), pairs)  68 us
    pallas_call x6, Pallas kernels, weight_terms(): pl.pallas_call(body, grid=(chunks // 2,), out_shape=[shaped(half, sum(par...  35.2 us
    pallas_call x2, Pallas kernels, attend_back(): pl.pallas_call(body, grid=(1,), out_shape=[shaped(3, tokens, CHUNK), shap...  25.3 us
    unnamed x208, local copies, waits for them, and re-layouts  20.4 us
    pallas_call x2, Pallas kernels, project(): pl.pallas_call(body, grid=(3,), out_shape=[shaped(2, 3, tokens, CHUNK), s...  16.3 us
    pallas_call x2, Pallas kernels, contract(): pl.pallas_call(body, grid_spec=pltpu.PrefetchScalarGridSpec(num_scalar_pr...  14.5 us
    pallas_call x2, Pallas kernels, expand(): pl.pallas_call(body, grid=(parts + 1,), out_shape=[shaped(2 * parts + 2,...  14.4 us
  transfers between devices with their start and end apart: 76, of which 31 were waited for; matrix products, arithmetic and copies ran while one was open for 6% of the time, Pallas kernels for 37%

profile of v8, /device:TPU:0, one launch (start us, length us, event | category | flops | bytes accessed | tf_op | source)
XLA Modules:
  0.0 393.0 jit_solution(17357229263268655502)
XLA Ops:
  2.1 4.1 %collective-permute-start = (bf16[1,144,384]{2,1,0:T(8,128)(2,1)S(1)}, bf16[1,144,384]{2,1,0:T(8,128)(2,1)S(1)}, u32[]{:S(2)}, u32[]{:S(2)}) collective-permute-start(bf16[1,144,384]{2,1,0:T(8,128)(2,1)S(1)} %bitcast.82), channel_id=1, source_target_pairs={{0,8},{1,9},{2,10},{3,11},{4,12},{5,13},{6,14},{7,15},{8,0},{9,1},... | collective-permute-start | bytes 331784 | tf_op jit(solution)/shard_map/ppermute | solution.py:54
  9.3 2.5 collective-permute-done.1
  14.3 3.7 collective-permute-done.4
  18.0 5.6 %collective-permute-done.3 = bf16[1,240,384]{2,1,0:T(8,128)(2,1)S(1)} collective-permute-done((bf16[1,240,384]{2,1,0:T(8,128)(2,1)S(1)}, bf16[1,240,384]{2,1,0:T(8,128)(2,1)S(1)}, u32[]{:S(2)}, u32[]{:S(2)}) %collective-permute-start.3) | collective-permute-done | bytes 184352 | tf_op jit(solution)/shard_map/ppermute | solution.py:54
  25.4 2.0 collective-permute-start.7
  27.4 9.2 %collective-permute-done.8 = f32[4,2,576]{2,1,0:T(2,128)S(1)} collective-permute-done((f32[4,2,576]{2,1,0:T(2,128)S(1)}, f32[4,2,576]{2,1,0:T(2,128)S(1)}, u32[]{:S(2)}, u32[]{:S(2)}) %collective-permute-start.8) | collective-permute-done | bytes 18464 | tf_op jit(solution)/shard_map/ppermute | solution.py:54
  36.8 1.9 collective-permute-start.9
  38.8 2.3 collective-permute-start.10
  41.8 1.8 collective-permute-start.13
  43.6 2.0 collective-permute-start.12
  45.7 7.9 %collective-permute-done.13 = f32[8,2,576]{2,1,0:T(2,128)S(1)} collective-permute-done((f32[8,2,576]{2,1,0:T(2,128)S(1)}, f32[8,2,576]{2,1,0:T(2,128)S(1)}, u32[]{:S(2)}, u32[]{:S(2)}) %collective-permute-start.13) | collective-permute-done | bytes 36896 | tf_op jit(solution)/shard_map/ppermute | solution.py:54
  53.6 6.0 %collective-permute-done.12 = bf16[1,192,384]{2,1,0:T(8,128)(2,1)S(1)} collective-permute-done((bf16[1,192,384]{2,1,0:T(8,128)(2,1)S(1)}, bf16[1,192,384]{2,1,0:T(8,128)(2,1)S(1)}, u32[]{:S(2)}, u32[]{:S(2)}) %collective-permute-start.12) | collective-permute-done | bytes 147488 | tf_op jit(solution)/shard_map/ppermute | solution.py:54
  65.7 2.9 collective-permute-start.15
  70.6 8.3 %project.2 = (bf16[2,3,512,384]{3,2,1,0:T(8,128)(2,1)S(1)}, bf16[4,512,384]{2,1,0:T(8,128)(2,1)S(1)}) custom-call(s32[2,16]{1,0:T(2,128)S(1)} %select_reduce_fusion.1.slots_ref, s32[1]{0:T(128)} %bitcast.core_ref, s32[4]{0:T(128)S(1)} %copy-done.24, bf16[512,768]{1,0:T(8,128)(2,1)S(1)} %copy-done.22, f32[12,768]{1,0:T(8,128)S(1)} %squeeze.21.rows_ref, ...), custom_call_target="tpu_custom_call" | custom-call | flops 16675000320 | bytes 14500000 | tf_op jit(solution)/shard_map/project/pallas_call | solution.py:253
  80.3 4.4 %collective-permute-done.17 = bf16[1,192,384]{2,1,0:T(8,128)(2,1)S(1)} collective-permute-done((bf16[1,192,384]{2,1,0:T(8,128)(2,1)S(1)}, bf16[1,192,384]{2,1,0:T(8,128)(2,1)S(1)}, u32[]{:S(2)}, u32[]{:S(2)}) %collective-permute-start.17) | collective-permute-done | bytes 147488 | tf_op jit(solution)/shard_map/ppermute | solution.py:54
  85.5 2.8 collective-permute-done.14
  88.9 1.8 collective-permute-start.21
  94.2 1.9 mix.2
  96.2 7.7 %expand.2 = (bf16[10,512,384]{2,1,0:T(8,128)(2,1)}, bf16[8,512,384]{2,1,0:T(8,128)(2,1)S(1)}) custom-call(s32[2,16]{1,0:T(2,128)S(1)} %select_reduce_fusion.1.slots_ref, s32[1]{0:T(128)} %bitcast.core_ref, bf16[512,768]{1,0:T(8,128)(2,1)S(1)} %get-tuple-element.283.x_ref, f32[12,768]{1,0:T(8,128)S(1)} %squeeze.21.rows_ref, ...), custom_call_target="tpu_custom_call" | custom-call | flops 10350000128 | bytes 9000000 | tf_op jit(solution)/shard_map/expand/pallas_call | solution.py:319
  103.9 1.7 copy-done.29
  105.7 1.7 collective-permute-done.22
  113.8 7.6 %contract.2 = (f32[512,768]{1,0:T(8,128)S(1)}, f32[512,768]{1,0:T(8,128)S(1)}, bf16[512,768]{1,0:T(8,128)(2,1)S(1)}) custom-call(s32[2,16]{1,0:T(2,128)S(1)} %select_reduce_fusion.1.slots_ref, s32[1]{0:T(128)} %bitcast.core_ref, s32[4]{0:T(128)S(1)} %copy-done.24, bf16[10,512,384]{2,1,0:T(8,128)(2,1)} %get-tuple-element.308.active_ref.refs_0_, ...), custom_call_target="tpu_custom_call" | custom-call | flops 12419999744 | bytes 10800000 | tf_op jit(solution)/shard_map/contract/pallas_call | solution.py:380
  121.4 6.3 %collective-permute-done.25 = bf16[4,192,384]{2,1,0:T(8,128)(2,1)S(1)} collective-permute-done((bf16[4,192,384]{2,1,0:T(8,128)(2,1)S(1)}, bf16[4,192,384]{2,1,0:T(8,128)(2,1)S(1)}, u32[]{:S(2)}, u32[]{:S(2)}) %collective-permute-start.25) | collective-permute-done | bytes 589856 | tf_op jit(solution)/shard_map/ppermute | solution.py:54
  132.1 1.9 collective-permute-start.30
  134.2 1.7 collective-permute-start.29
  135.9 2.8 collective-permute-done.31.refs_1_
  138.7 8.0 %project.3 = (bf16[2,3,512,384]{3,2,1,0:T(8,128)(2,1)S(1)}, bf16[4,512,384]{2,1,0:T(8,128)(2,1)S(1)}) custom-call(s32[2,16]{1,0:T(2,128)S(1)} %select_reduce_fusion.1.slots_ref, s32[1]{0:T(128)} %bitcast.core_ref, s32[4]{0:T(128)S(1)} %copy-done.24, bf16[512,768]{1,0:T(8,128)(2,1)S(1)} %get-tuple-element.304.x_ref, f32[12,768]{1,0:T(8,128)S(1)} %squeeze.22.rows_ref, ...), custom_call_target="tpu_custom_call" | custom-call | flops 16675000320 | bytes 14500000 | tf_op jit(solution)/shard_map/project/pallas_call | solution.py:253
  147.7 2.8 collective-permute-done.29
  151.1 1.7 collective-permute-start.33
  152.8 2.5 mix.3
  155.5 6.7 %expand.3 = (bf16[10,512,384]{2,1,0:T(8,128)(2,1)S(1)}, bf16[8,512,384]{2,1,0:T(8,128)(2,1)S(1)}) custom-call(s32[2,16]{1,0:T(2,128)S(1)} %select_reduce_fusion.1.slots_ref, s32[1]{0:T(128)} %bitcast.core_ref, bf16[512,768]{1,0:T(8,128)(2,1)S(1)} %get-tuple-element.313.x_ref, f32[12,768]{1,0:T(8,128)S(1)} %squeeze.22.rows_ref, ...), custom_call_target="tpu_custom_call" | custom-call | flops 10350000128 | bytes 9000000 | tf_op jit(solution)/shard_map/expand/pallas_call | solution.py:319
  162.1 5.3 %collective-permute-done.33 = bf16[8,192,384]{2,1,0:T(8,128)(2,1)S(1)} collective-permute-done((bf16[8,192,384]{2,1,0:T(8,128)(2,1)S(1)}, bf16[8,192,384]{2,1,0:T(8,128)(2,1)S(1)}, u32[]{:S(2)}, u32[]{:S(2)}) %collective-permute-start.33) | collective-permute-done | bytes 1179680 | tf_op jit(solution)/shard_map/ppermute | solution.py:54
  168.3 4.0 %collective-permute-done.35.refs_4_.refs_5_.refs_6_.refs_7_ = bf16[16,192,384]{2,1,0:T(8,128)(2,1)S(1)} collective-permute-done((bf16[16,192,384]{2,1,0:T(8,128)(2,1)S(1)}, bf16[16,192,384]{2,1,0:T(8,128)(2,1)S(1)}, u32[]{:S(2)}, u32[]{:S(2)}) %collective-permute-start.35) | collective-permute-done | bytes 2359328 | tf_op jit(solution)/shard_map/ppermute | solution.py:65
  172.4 6.9 %contract.3 = (f32[512,768]{1,0:T(8,128)S(1)}, f32[512,768]{1,0:T(8,128)}, bf16[512,768]{1,0:T(8,128)(2,1)}) custom-call(s32[2,16]{1,0:T(2,128)S(1)} %select_reduce_fusion.1.slots_ref, s32[1]{0:T(128)} %bitcast.core_ref, s32[4]{0:T(128)S(1)} %copy-done.24, bf16[10,512,384]{2,1,0:T(8,128)(2,1)S(1)} %get-tuple-element.319.active_ref.refs_0_, ...), custom_call_target="tpu_custom_call" | custom-call | flops 12419999744 | bytes 10800000 | tf_op jit(solution)/shard_map/contract/pallas_call | solution.py:380
  179.3 5.9 %contract_back.2 = (f32[512,768]{1,0:T(8,128)S(1)}, bf16[1,512,384]{2,1,0:T(8,128)(2,1)S(1)}, bf16[4,512,384]{2,1,0:T(8,128)(2,1)S(1)}, bf16[5,512,384]{2,1,0:T(...) custom-call(s32[2,16]{1,0:T(2,128)S(1)} %select_reduce_fusion.1.slots_ref, s32[1]{0:T(128)} %bitcast.core_ref, ...), custom_call_target="tpu_custom_call" | custom-call | flops 12650000384 | bytes 11000000 | tf_op jit(solution)/shard_map/contract_back/pallas_call | solution.py:443
  187.1 6.3 %expand_back.2 = (f32[512,768]{1,0:T(8,128)S(1)}, bf16[1,512,384]{2,1,0:T(8,128)(2,1)S(1)}, bf16[1,512,384]{2,1,0:T(8,128)(2,1)S(1)}, f32[3,768]{1,0:T(4,128)S(1)}) custom-call(s32[2,16]{1,0:T(2,128)S(1)} %select_reduce_fusion.1.slots_ref, s32[1]{0:T(128)} %bitcast.core_ref, bf16[4,512,384]{2,1,0:T(8,128)(2,1)S(1)} %get-tuple-element.332.kept_ref.refs_2_, ...), custom_call_target="tpu_custom_call" | custom-call | flops 11269999616 | bytes 9800000 | tf_op jit(solution)/shard_map/expand_back/pallas_call | solution.py:514
  193.6 4.7 %weight_terms.6 = (bf16[8,192,384]{2,1,0:T(8,128)(2,1)S(1)}, bf16[8,192,384]{2,1,0:T(8,128)(2,1)S(1)}) custom-call(s32[2,16]{1,0:T(2,128)S(1)} %select_reduce_fusion.slots_ref, bf16[10,512,384]{2,1,0:T(8,128)(2,1)S(1)} %get-tuple-element.319.active_ref.refs_0_, bf16[10,512,384]{2,1,0:T(8,128)(2,1)S(1)} %collective-permute-done.37.refs_1_, ...), custom_call_target="tpu_custom_call" | custom-call | flops 6899999744 | bytes 6000000 | tf_op jit(solution)/shard_map/weight_terms/pallas_call | solution.py:666
  198.3 1.7 collective-permute-start.39
  200.1 13.0 %attend_back.2 = (bf16[3,512,384]{2,1,0:T(8,128)(2,1)S(1)}, bf16[3,512,384]{2,1,0:T(8,128)(2,1)}, f32[2,2,1,384]{3,2,1,0:T(1,128)S(1)}) custom-call(s32[2,16]{1,0:T(2,128)S(1)} %select_reduce_fusion.1.slots_ref, s32[1]{0:T(128)} %bitcast.core_ref, s32[4]{0:T(128)S(1)} %copy-done.24, bf16[1,512,384]{2,1,0:T(8,128)(2,1)S(1)} %get-tuple-element.340.refs_6_.kept_ref, ...), custom_call_target="tpu_custom_call" | custom-call | flops 23690000384 | bytes 20600000 | tf_op jit(solution)/shard_map/attend_back/pallas_call | solution.py:569
  213.0 6.8 %weight_terms.7 = (bf16[8,240,384]{2,1,0:T(8,128)(2,1)S(1)}, bf16[8,240,384]{2,1,0:T(8,128)(2,1)}) custom-call(s32[2,16]{1,0:T(2,128)S(1)} %select_reduce_fusion.slots_ref, bf16[10,512,384]{2,1,0:T(8,128)(2,1)S(1)} %get-tuple-element.319.active_ref.refs_0_, bf16[10,512,384]{2,1,0:T(8,128)(2,1)S(1)} %collective-permute-done.37.refs_1_, ...), custom_call_target="tpu_custom_call" | custom-call | flops 8625000448 | bytes 7500000 | tf_op jit(solution)/shard_map/weight_terms/pallas_call | solution.py:666
  221.4 1.7 collective-permute-start.42
  223.1 5.0 %project_back.2.d_out_ref = f32[512,768]{1,0:T(8,128)S(1)} custom-call(s32[2,16]{1,0:T(2,128)S(1)} %select_reduce_fusion.1.slots_ref, s32[1]{0:T(128)} %bitcast.core_ref, bf16[3,512,384]{2,1,0:T(8,128)(2,1)S(1)} %get-tuple-element.352.refs_2_.kept_ref, bf16[3,512,384]{2,1,0:T(8,128)(2,1)} %get-tuple-element.355.sent_ref, ...), custom_call_target="tpu_custom_call" | custom-call | flops 7590000128 | bytes 6600000 | tf_op jit(solution)/shard_map/project_back/pallas_call | solution.py:604
  228.1 7.0 %contract_back.3 = (f32[512,768]{1,0:T(8,128)S(1)}, bf16[1,512,384]{2,1,0:T(8,128)(2,1)S(1)}, bf16[4,512,384]{2,1,0:T(8,128)(2,1)S(1)}, bf16[5,512,384]{2,1,0:T(...) custom-call(s32[2,16]{1,0:T(2,128)S(1)} %select_reduce_fusion.1.slots_ref, s32[1]{0:T(128)} %bitcast.core_ref, ...), custom_call_target="tpu_custom_call" | custom-call | flops 12650000384 | bytes 11000000 | tf_op jit(solution)/shard_map/contract_back/pallas_call | solution.py:443
  241.7 4.4 %weight_terms.8 = (bf16[8,144,384]{2,1,0:T(8,128)(2,1)S(1)}, bf16[8,144,384]{2,1,0:T(8,128)(2,1)S(1)}) custom-call(s32[2,16]{1,0:T(2,128)S(1)} %select_reduce_fusion.slots_ref, bf16[4,512,384]{2,1,0:T(8,128)(2,1)S(1)} %copy-done.19, bf16[4,512,384]{2,1,0:T(8,128)(2,1)S(1)} %copy-done.21, bf16[3,512,384]{2,1,0:T(8,128)(2,1)S(1)} %copy-done.35, ...), custom_call_target="tpu_custom_call" | custom-call | flops 5175000064 | bytes 4500000 | tf_op jit(solution)/shard_map/weight_terms/pallas_call | solution.py:666
  246.5 1.9 add_convert_fusion.2
  250.6 6.7 %expand_back.3 = (f32[512,768]{1,0:T(8,128)S(1)}, bf16[1,512,384]{2,1,0:T(8,128)(2,1)S(1)}, bf16[1,512,384]{2,1,0:T(8,128)(2,1)S(1)}, f32[3,768]{1,0:T(4,128)S(1)}) custom-call(s32[2,16]{1,0:T(2,128)S(1)} %select_reduce_fusion.1.slots_ref, s32[1]{0:T(128)} %bitcast.core_ref, bf16[4,512,384]{2,1,0:T(8,128)(2,1)S(1)} %copy-done.37, ...), custom_call_target="tpu_custom_call" | custom-call | flops 11269999616 | bytes 9800000 | tf_op jit(solution)/shard_map/expand_back/pallas_call | solution.py:514
  257.3 6.8 %weight_terms.9 = (bf16[8,192,384]{2,1,0:T(8,128)(2,1)S(1)}, bf16[8,192,384]{2,1,0:T(8,128)(2,1)S(1)}) custom-call(s32[2,16]{1,0:T(2,128)S(1)} %select_reduce_fusion.slots_ref, bf16[10,512,384]{2,1,0:T(8,128)(2,1)} %get-tuple-element.308.active_ref.refs_0_, bf16[10,512,384]{2,1,0:T(8,128)(2,1)} %collective-permute-done.32.refs_1_, ...), custom_call_target="tpu_custom_call" | custom-call | flops 6899999744 | bytes 6000000 | tf_op jit(solution)/shard_map/weight_terms/pallas_call | solution.py:666
  264.2 3.3 collective-permute-done.46
  271.5 2.3 collective-permute-start.49
  273.8 12.4 %attend_back.3 = (bf16[3,512,384]{2,1,0:T(8,128)(2,1)S(1)}, bf16[3,512,384]{2,1,0:T(8,128)(2,1)}, f32[2,2,1,384]{3,2,1,0:T(1,128)S(1)}) custom-call(s32[2,16]{1,0:T(2,128)S(1)} %select_reduce_fusion.1.slots_ref, s32[1]{0:T(128)} %bitcast.core_ref, s32[4]{0:T(128)S(1)} %copy-done.24, bf16[1,512,384]{2,1,0:T(8,128)(2,1)S(1)} %get-tuple-element.388.refs_6_.kept_ref, ...), custom_call_target="tpu_custom_call" | custom-call | flops 23690000384 | bytes 20600000 | tf_op jit(solution)/shard_map/attend_back/pallas_call | solution.py:569
  287.2 8.1 %weight_terms.10 = (bf16[8,240,384]{2,1,0:T(8,128)(2,1)S(1)}, bf16[8,240,384]{2,1,0:T(8,128)(2,1)}) custom-call(s32[2,16]{1,0:T(2,128)S(1)} %select_reduce_fusion.slots_ref, bf16[10,512,384]{2,1,0:T(8,128)(2,1)} %get-tuple-element.308.active_ref.refs_0_, bf16[10,512,384]{2,1,0:T(8,128)(2,1)} %collective-permute-done.32.refs_1_, ...), custom_call_target="tpu_custom_call" | custom-call | flops 8625000448 | bytes 7500000 | tf_op jit(solution)/shard_map/weight_terms/pallas_call | solution.py:666
  297.7 1.9 collective-permute-start.55
  307.4 4.4 %weight_terms.11 = (bf16[8,144,384]{2,1,0:T(8,128)(2,1)S(1)}, bf16[8,144,384]{2,1,0:T(8,128)(2,1)S(1)}) custom-call(s32[2,16]{1,0:T(2,128)S(1)} %select_reduce_fusion.slots_ref, bf16[4,512,384]{2,1,0:T(8,128)(2,1)S(1)} %copy-done.14, bf16[4,512,384]{2,1,0:T(8,128)(2,1)S(1)} %copy-done.17, bf16[3,512,384]{2,1,0:T(8,128)(2,1)S(1)} %copy-done.32, ...), custom_call_target="tpu_custom_call" | custom-call | flops 5175000064 | bytes 4500000 | tf_op jit(solution)/shard_map/weight_terms/pallas_call | solution.py:666
  311.9 5.6 %project_back.3 = f32[512,768]{1,0:T(8,128)} custom-call(s32[2,16]{1,0:T(2,128)S(1)} %select_reduce_fusion.1.slots_ref, s32[1]{0:T(128)} %bitcast.core_ref, bf16[3,512,384]{2,1,0:T(8,128)(2,1)S(1)} %copy-done.33, bf16[3,512,384]{2,1,0:T(8,128)(2,1)} %get-tuple-element.407.sent_ref, f32[512,768]{1,0:T(8,128)S(1)} %copy-done.39, ...), custom_call_target="tpu_custom_call" | custom-call | flops 7590000128 | bytes 6600000 | tf_op jit(solution)/shard_map/project_back/pallas_call | solution.py:604
  319.0 1.7 gather_fusion.1
  320.8 5.1 %collective-permute-done.54 = bf16[8,240,384]{2,1,0:T(8,128)(2,1)} collective-permute-done((bf16[8,240,384]{2,1,0:T(8,128)(2,1)}, bf16[8,240,384]{2,1,0:T(8,128)(2,1)}, u32[]{:S(2)}, u32[]{:S(2)}) %collective-permute-start.54) | collective-permute-done | bytes 1474592 | tf_op jit(solution)/shard_map/ppermute | solution.py:54
  325.9 1.8 add_convert_fusion
  336.1 12.2 %collective-permute-done.59 = f32[8,2,576]{2,1,0:T(2,128)S(1)} collective-permute-done((f32[8,2,576]{2,1,0:T(2,128)S(1)}, f32[8,2,576]{2,1,0:T(2,128)S(1)}, u32[]{:S(2)}, u32[]{:S(2)}) %collective-permute-start.59) | collective-permute-done | bytes 36896 | tf_op jit(solution)/shard_map/ppermute | solution.py:54
  350.7 2.0 collective-permute-start.65
  353.6 4.6 %collective-permute-done.64 = f32[4,2,576]{2,1,0:T(2,128)S(1)} collective-permute-done((f32[4,2,576]{2,1,0:T(2,128)S(1)}, f32[4,2,576]{2,1,0:T(2,128)S(1)}, u32[]{:S(2)}, u32[]{:S(2)}) %collective-permute-start.64) | collective-permute-done | bytes 18464 | tf_op jit(solution)/shard_map/ppermute | solution.py:54
  358.2 2.5 collective-permute-done.65
  360.7 2.2 collective-permute-done.67
  366.6 8.4 %collective-permute-done.68 = f32[2,2,576]{2,1,0:T(2,128)S(1)} collective-permute-done((f32[2,2,576]{2,1,0:T(2,128)S(1)}, f32[2,2,576]{2,1,0:T(2,128)S(1)}, u32[]{:S(2)}, u32[]{:S(2)}) %collective-permute-start.68) | collective-permute-done | bytes 9248 | tf_op jit(solution)/shard_map/ppermute | solution.py:54
  378.6 8.7 %collective-permute-done.73 = f32[1,2,576]{2,1,0:T(2,128)S(1)} collective-permute-done((f32[1,2,576]{2,1,0:T(2,128)S(1)}, f32[1,2,576]{2,1,0:T(2,128)S(1)}, u32[]{:S(2)}, u32[]{:S(2)}) %collective-permute-start.73) | collective-permute-done | bytes 4640 | tf_op jit(solution)/shard_map/ppermute | solution.py:54
  (438 shorter events, 90.9 us)
Async XLA Ops:
  2.1 9.8 %collective-permute-start = (bf16[1,144,384]{2,1,0:T(8,128)(2,1)S(1)}, bf16[1,144,384]{2,1,0:T(8,128)(2,1)S(1)}, u32[]{:S(2)}, u32[]{:S(2)}) collective-permute-start(bf16[1,144,384]{2,1,0:T(8,128)(2,1)S(1)} %bitcast.82), channel_id=1, source_target_pairs={{0,8},{1,9},{2,10},{3,11},{4,12},{5,13},{6,14},{7,15},{8,0},{9,1},... | collective-permute-start | bytes 331784 | tf_op jit(solution)/shard_map/ppermute | solution.py:54
  11.9 11.7 %collective-permute-start.2 = (bf16[2,144,384]{2,1,0:T(8,128)(2,1)S(1)}, bf16[2,144,384]{2,1,0:T(8,128)(2,1)S(1)}, u32[]{:S(2)}, u32[]{:S(2)}) collective-permute-start(bf16[2,144,384]{2,1,0:T(8,128)(2,1)S(1)} %constant_dynamic-update-slice_fusion), channel_id=1, source_target_pairs={{0,2},{1,3},{2,0},{3,1},{4,6},{5,7},{6,4},{7,5},{8,10},{9,11},{10,... | collective-permute-start | bytes 663560 | tf_op jit(solution)/shard_map/ppermute | solution.py:54
  13.5 10.1 %collective-permute-start.3 = (bf16[1,240,384]{2,1,0:T(8,128)(2,1)S(1)}, bf16[1,240,384]{2,1,0:T(8,128)(2,1)S(1)}, u32[]{:S(2)}, u32[]{:S(2)}) collective-permute-start(bf16[1,240,384]{2,1,0:T(8,128)(2,1)S(1)} %maximum_bitcast_fusion), channel_id=1, source_target_pairs={{0,8},{1,9},{2,10},{3,11},{4,12},{5,13},{6,14},{7,15},{8,0},{9,1},... | collective-permute-start | bytes 552968 | tf_op jit(solution)/shard_map/ppermute | solution.py:54
  23.7 13.0 %collective-permute-start.5 = (bf16[4,144,384]{2,1,0:T(8,128)(2,1)S(1)}, bf16[4,144,384]{2,1,0:T(8,128)(2,1)S(1)}, u32[]{:S(2)}, u32[]{:S(2)}) collective-permute-start(bf16[4,144,384]{2,1,0:T(8,128)(2,1)S(1)} %constant_dynamic-update-slice_fusion.2), channel_id=1, source_target_pairs={{0,4},{1,5},{2,6},{3,7},{4,0},{5,1},{6,2},{7,3},{8,12},{9,13},{10,... | collective-permute-start | bytes 1327112 | tf_op jit(solution)/shard_map/ppermute | solution.py:54
  23.8 12.8 %collective-permute-start.6 = (bf16[2,240,384]{2,1,0:T(8,128)(2,1)S(1)}, bf16[2,240,384]{2,1,0:T(8,128)(2,1)S(1)}, u32[]{:S(2)}, u32[]{:S(2)}) collective-permute-start(bf16[2,240,384]{2,1,0:T(8,128)(2,1)S(1)} %constant_dynamic-update-slice_fusion.4), channel_id=1, source_target_pairs={{0,2},{1,3},{2,0},{3,1},{4,6},{5,7},{6,4},{7,5},{8,10},{9,11},{10,... | collective-permute-start | bytes 1105928 | tf_op jit(solution)/shard_map/ppermute | solution.py:54
  25.4 11.3 %collective-permute-start.7 = (bf16[1,192,384]{2,1,0:T(8,128)(2,1)S(1)}, bf16[1,192,384]{2,1,0:T(8,128)(2,1)S(1)}, u32[]{:S(2)}, u32[]{:S(2)}) collective-permute-start(bf16[1,192,384]{2,1,0:T(8,128)(2,1)S(1)} %constant_dynamic-slice_fusion.8), channel_id=1, source_target_pairs={{0,8},{1,9},{2,10},{3,11},{4,12},{5,13},{6,14},{7,15},{8,0},{9,1},... | collective-permute-start | bytes 442376 | tf_op jit(solution)/shard_map/ppermute | solution.py:54
  36.8 24.4 %collective-permute-start.9 = (bf16[8,144,384]{2,1,0:T(8,128)(2,1)S(1)}, bf16[8,144,384]{2,1,0:T(8,128)(2,1)}, u32[]{:S(2)}, u32[]{:S(2)}) collective-permute-start(bf16[8,144,384]{2,1,0:T(8,128)(2,1)S(1)} %constant_dynamic-update-slice_fusion.6), channel_id=1, source_target_pairs={{0,1},{1,0},{2,3},{3,2},{4,5},{5,4},{6,7},{7,6},{8,9},{9,8},{10,11... | collective-permute-start | bytes 2654216 | tf_op jit(solution)/shard_map/ppermute | solution.py:54
  38.8 21.6 %collective-permute-start.10 = (bf16[4,240,384]{2,1,0:T(8,128)(2,1)S(1)}, bf16[4,240,384]{2,1,0:T(8,128)(2,1)S(1)}, u32[]{:S(2)}, u32[]{:S(2)}) collective-permute-start(bf16[4,240,384]{2,1,0:T(8,128)(2,1)S(1)} %constant_dynamic-update-slice_fusion.8), channel_id=1, source_target_pairs={{0,4},{1,5},{2,6},{3,7},{4,0},{5,1},{6,2},{7,3},{8,12},{9,13},{10,... | collective-permute-start | bytes 2211848 | tf_op jit(solution)/shard_map/ppermute | solution.py:54
  41.1 18.5 %collective-permute-start.11 = (bf16[2,192,384]{2,1,0:T(8,128)(2,1)S(1)}, bf16[2,192,384]{2,1,0:T(8,128)(2,1)S(1)}, u32[]{:S(2)}, u32[]{:S(2)}) collective-permute-start(bf16[2,192,384]{2,1,0:T(8,128)(2,1)S(1)} %constant_dynamic-update-slice_fusion.10), channel_id=1, source_target_pairs={{0,2},{1,3},{2,0},{3,1},{4,6},{5,7},{6,4},{7,5},{8,10},{9,11},{10,... | collective-permute-start | bytes 884744 | tf_op jit(solution)/shard_map/ppermute | solution.py:54
  41.8 11.7 %collective-permute-start.13 = (f32[8,2,576]{2,1,0:T(2,128)S(1)}, f32[8,2,576]{2,1,0:T(2,128)S(1)}, u32[]{:S(2)}, u32[]{:S(2)}) collective-permute-start(f32[8,2,576]{2,1,0:T(2,128)S(1)} %pad_maximum_fusion.8), channel_id=1, source_target_pairs={{0,1},{1,0},{2,3},{3,2},{4,5},{5,4},{6,7},{7,6},{8,9},{9,8},{10,11... | collective-permute-start | bytes 110600 | tf_op jit(solution)/shard_map/ppermute | solution.py:54
  43.6 16.0 %collective-permute-start.12 = (bf16[1,192,384]{2,1,0:T(8,128)(2,1)S(1)}, bf16[1,192,384]{2,1,0:T(8,128)(2,1)S(1)}, u32[]{:S(2)}, u32[]{:S(2)}) collective-permute-start(bf16[1,192,384]{2,1,0:T(8,128)(2,1)S(1)} %maximum_bitcast_fusion.1), channel_id=1, source_target_pairs={{0,8},{1,9},{2,10},{3,11},{4,12},{5,13},{6,14},{7,15},{8,0},{9,1},... | collective-permute-start | bytes 442376 | tf_op jit(solution)/shard_map/ppermute | solution.py:54
  65.2 19.5 %collective-permute-start.16 = (bf16[2,192,384]{2,1,0:T(8,128)(2,1)S(1)}, bf16[2,192,384]{2,1,0:T(8,128)(2,1)S(1)}, u32[]{:S(2)}, u32[]{:S(2)}) collective-permute-start(bf16[2,192,384]{2,1,0:T(8,128)(2,1)S(1)} %constant_dynamic-update-slice_fusion.16), channel_id=1, source_target_pairs={{0,2},{1,3},{2,0},{3,1},{4,6},{5,7},{6,4},{7,5},{8,10},{9,11},{10,... | collective-permute-start | bytes 884744 | tf_op jit(solution)/shard_map/ppermute | solution.py:54
  65.7 19.8 %collective-permute-start.15 = (bf16[4,192,384]{2,1,0:T(8,128)(2,1)S(1)}, bf16[4,192,384]{2,1,0:T(8,128)(2,1)S(1)}, u32[]{:S(2)}, u32[]{:S(2)}) collective-permute-start(bf16[4,192,384]{2,1,0:T(8,128)(2,1)S(1)} %constant_dynamic-update-slice_fusion.14), channel_id=1, source_target_pairs={{0,4},{1,5},{2,6},{3,7},{4,0},{5,1},{6,2},{7,3},{8,12},{9,13},{10,... | collective-permute-start | bytes 1769480 | tf_op jit(solution)/shard_map/ppermute | solution.py:54
  68.8 19.4 %collective-permute-start.14 = (bf16[8,240,384]{2,1,0:T(8,128)(2,1)S(1)}, bf16[8,240,384]{2,1,0:T(8,128)(2,1)S(1)}, u32[]{:S(2)}, u32[]{:S(2)}) collective-permute-start(bf16[8,240,384]{2,1,0:T(8,128)(2,1)S(1)} %constant_dynamic-update-slice_fusion.12), channel_id=1, source_target_pairs={{0,1},{1,0},{2,3},{3,2},{4,5},{5,4},{6,7},{7,6},{8,9},{9,8},{10,11... | collective-permute-start | bytes 4423688 | tf_op jit(solution)/shard_map/ppermute | solution.py:54
  69.9 14.8 %collective-permute-start.17 = (bf16[1,192,384]{2,1,0:T(8,128)(2,1)S(1)}, bf16[1,192,384]{2,1,0:T(8,128)(2,1)S(1)}, u32[]{:S(2)}, u32[]{:S(2)}) collective-permute-start(bf16[1,192,384]{2,1,0:T(8,128)(2,1)S(1)} %bitcast.74), channel_id=1, source_target_pairs={{0,8},{1,9},{2,10},{3,11},{4,12},{5,13},{6,14},{7,15},{8,0},{9,1},... | collective-permute-start | bytes 442376 | tf_op jit(solution)/shard_map/ppermute | solution.py:54
  88.9 18.5 %collective-permute-start.21 = (bf16[2,192,384]{2,1,0:T(8,128)(2,1)S(1)}, bf16[2,192,384]{2,1,0:T(8,128)(2,1)S(1)}, u32[]{:S(2)}, u32[]{:S(2)}) collective-permute-start(bf16[2,192,384]{2,1,0:T(8,128)(2,1)S(1)} %constant_dynamic-update-slice_fusion.24), channel_id=1, source_target_pairs={{0,2},{1,3},{2,0},{3,1},{4,6},{5,7},{6,4},{7,5},{8,10},{9,11},{10,... | collective-permute-start | bytes 884744 | tf_op jit(solution)/shard_map/ppermute | solution.py:54
  90.8 17.9 %collective-permute-start.20 = (bf16[4,192,384]{2,1,0:T(8,128)(2,1)S(1)}, bf16[4,192,384]{2,1,0:T(8,128)(2,1)S(1)}, u32[]{:S(2)}, u32[]{:S(2)}) collective-permute-start(bf16[4,192,384]{2,1,0:T(8,128)(2,1)S(1)} %constant_dynamic-update-slice_fusion.22), channel_id=1, source_target_pairs={{0,4},{1,5},{2,6},{3,7},{4,0},{5,1},{6,2},{7,3},{8,12},{9,13},{10,... | collective-permute-start | bytes 1769480 | tf_op jit(solution)/shard_map/ppermute | solution.py:54
  91.7 17.0 %collective-permute-start.19 = (bf16[8,192,384]{2,1,0:T(8,128)(2,1)S(1)}, bf16[8,192,384]{2,1,0:T(8,128)(2,1)S(1)}, u32[]{:S(2)}, u32[]{:S(2)}) collective-permute-start(bf16[8,192,384]{2,1,0:T(8,128)(2,1)S(1)} %constant_dynamic-update-slice_fusion.20), channel_id=1, source_target_pairs={{0,1},{1,0},{2,3},{3,2},{4,5},{5,4},{6,7},{7,6},{8,9},{9,8},{10,11... | collective-permute-start | bytes 3538952 | tf_op jit(solution)/shard_map/ppermute | solution.py:54
  92.8 14.6 %collective-permute-start.22 = (bf16[1,192,384]{2,1,0:T(8,128)(2,1)S(1)}, bf16[1,192,384]{2,1,0:T(8,128)(2,1)S(1)}, u32[]{:S(2)}, u32[]{:S(2)}) collective-permute-start(bf16[1,192,384]{2,1,0:T(8,128)(2,1)S(1)} %copy-done.63), channel_id=1, source_target_pairs={{0,8},{1,9},{2,10},{3,11},{4,12},{5,13},{6,14},{7,15},{8,0},{9,1},... | collective-permute-start | bytes 442376 | tf_op jit(solution)/shard_map/ppermute | solution.py:54
  109.2 12.2 %collective-permute-start.26 = (bf16[2,192,384]{2,1,0:T(8,128)(2,1)S(1)}, bf16[2,192,384]{2,1,0:T(8,128)(2,1)}, u32[]{:S(2)}, u32[]{:S(2)}) collective-permute-start(bf16[2,192,384]{2,1,0:T(8,128)(2,1)S(1)} %constant_dynamic-update-slice_fusion.32), channel_id=1, source_target_pairs={{0,2},{1,3},{2,0},{3,1},{4,6},{5,7},{6,4},{7,5},{8,10},{9,11},{10,... | collective-permute-start | bytes 884744 | tf_op jit(solution)/shard_map/ppermute | solution.py:54
  110.4 17.7 %collective-permute-start.28 = (bf16[4,512,384]{2,1,0:T(8,128)(2,1)S(1)}, bf16[4,512,384]{2,1,0:T(8,128)(2,1)S(1)}, u32[]{:S(2)}, u32[]{:S(2)}) collective-permute-start(bf16[4,512,384]{2,1,0:T(8,128)(2,1)S(1)} %get-tuple-element.299.context_ref.refs_4_.refs_0_), channel_id=1, source_target_pairs={{0,16},{16,0},{1,17},{17,1},{2,18},{18,2},{3,19},{19,3},{4,20},{20... | collective-permute-start | bytes 4718600 | tf_op jit(solution)/shard_map/ppermute | solution.py:65
  110.9 17.3 %collective-permute-start.24 = (bf16[8,192,384]{2,1,0:T(8,128)(2,1)S(1)}, bf16[8,192,384]{2,1,0:T(8,128)(2,1)S(1)}, u32[]{:S(2)}, u32[]{:S(2)}) collective-permute-start(bf16[8,192,384]{2,1,0:T(8,128)(2,1)S(1)} %constant_dynamic-update-slice_fusion.28), channel_id=1, source_target_pairs={{0,1},{1,0},{2,3},{3,2},{4,5},{5,4},{6,7},{7,6},{8,9},{9,8},{10,11... | collective-permute-start | bytes 3538952 | tf_op jit(solution)/shard_map/ppermute | solution.py:54
  112.5 15.1 %collective-permute-start.25 = (bf16[4,192,384]{2,1,0:T(8,128)(2,1)S(1)}, bf16[4,192,384]{2,1,0:T(8,128)(2,1)S(1)}, u32[]{:S(2)}, u32[]{:S(2)}) collective-permute-start(bf16[4,192,384]{2,1,0:T(8,128)(2,1)S(1)} %constant_dynamic-update-slice_fusion.30), channel_id=1, source_target_pairs={{0,4},{1,5},{2,6},{3,7},{4,0},{5,1},{6,2},{7,3},{8,12},{9,13},{10,... | collective-permute-start | bytes 1769480 | tf_op jit(solution)/shard_map/ppermute | solution.py:54
  128.3 22.2 %collective-permute-start.32 = (bf16[10,512,384]{2,1,0:T(8,128)(2,1)}, bf16[10,512,384]{2,1,0:T(8,128)(2,1)}, u32[]{:S(2)}, u32[]{:S(2)}) collective-permute-start(bf16[10,512,384]{2,1,0:T(8,128)(2,1)} %get-tuple-element.308.active_ref.refs_0_), channel_id=1, source_target_pairs={{0,16},{16,0},{1,17},{17,1},{2,18},{18,2},{3,19},{19,3},{4,20},{20... | collective-permute-start | bytes 11796488 | tf_op jit(solution)/shard_map/ppermute | solution.py:65
  132.1 15.5 %collective-permute-start.30 = (bf16[4,192,384]{2,1,0:T(8,128)(2,1)S(1)}, bf16[4,192,384]{2,1,0:T(8,128)(2,1)S(1)}, u32[]{:S(2)}, u32[]{:S(2)}) collective-permute-start(bf16[4,192,384]{2,1,0:T(8,128)(2,1)S(1)} %constant_dynamic-update-slice_fusion.38), channel_id=1, source_target_pairs={{0,4},{1,5},{2,6},{3,7},{4,0},{5,1},{6,2},{7,3},{8,12},{9,13},{10,... | collective-permute-start | bytes 1769480 | tf_op jit(solution)/shard_map/ppermute | solution.py:54
  134.2 16.3 %collective-permute-start.29 = (bf16[8,192,384]{2,1,0:T(8,128)(2,1)S(1)}, bf16[8,192,384]{2,1,0:T(8,128)(2,1)S(1)}, u32[]{:S(2)}, u32[]{:S(2)}) collective-permute-start(bf16[8,192,384]{2,1,0:T(8,128)(2,1)S(1)} %constant_dynamic-update-slice_fusion.36), channel_id=1, source_target_pairs={{0,1},{1,0},{2,3},{3,2},{4,5},{5,4},{6,7},{7,6},{8,9},{9,8},{10,11... | collective-permute-start | bytes 3538952 | tf_op jit(solution)/shard_map/ppermute | solution.py:54
  151.1 16.3 %collective-permute-start.33 = (bf16[8,192,384]{2,1,0:T(8,128)(2,1)S(1)}, bf16[8,192,384]{2,1,0:T(8,128)(2,1)S(1)}, u32[]{:S(2)}, u32[]{:S(2)}) collective-permute-start(bf16[8,192,384]{2,1,0:T(8,128)(2,1)S(1)} %constant_dynamic-update-slice_fusion.42), channel_id=1, source_target_pairs={{0,1},{1,0},{2,3},{3,2},{4,5},{5,4},{6,7},{7,6},{8,9},{9,8},{10,11... | collective-permute-start | bytes 3538952 | tf_op jit(solution)/shard_map/ppermute | solution.py:54
  167.8 25.8 %collective-permute-start.37 = (bf16[10,512,384]{2,1,0:T(8,128)(2,1)S(1)}, bf16[10,512,384]{2,1,0:T(8,128)(2,1)S(1)}, u32[]{:S(2)}, u32[]{:S(2)}) collective-permute-start(bf16[10,512,384]{2,1,0:T(8,128)(2,1)S(1)} %get-tuple-element.319.active_ref.refs_0_), channel_id=1, source_target_pairs={{0,16},{16,0},{1,17},{17,1},{2,18},{18,2},{3,19},{19,3},{4,20},{20... | collective-permute-start | bytes 11796488 | tf_op jit(solution)/shard_map/ppermute | solution.py:65
  193.4 19.6 %collective-permute-start.40 = (bf16[1,512,384]{2,1,0:T(8,128)(2,1)S(1)}, bf16[1,512,384]{2,1,0:T(8,128)(2,1)S(1)}, u32[]{:S(2)}, u32[]{:S(2)}) collective-permute-start(bf16[1,512,384]{2,1,0:T(8,128)(2,1)S(1)} %get-tuple-element.343.sent_ref), channel_id=1, source_target_pairs={{0,16},{16,0},{1,17},{17,1},{2,18},{18,2},{3,19},{19,3},{4,20},{20... | collective-permute-start | bytes 1179656 | tf_op jit(solution)/shard_map/ppermute | solution.py:65
  198.3 21.5 %collective-permute-start.39 = (bf16[8,192,384]{2,1,0:T(8,128)(2,1)S(1)}, bf16[8,192,384]{2,1,0:T(8,128)(2,1)S(1)}, u32[]{:S(2)}, u32[]{:S(2)}) collective-permute-start(bf16[8,192,384]{2,1,0:T(8,128)(2,1)S(1)} %get-tuple-element.338), channel_id=1, source_target_pairs={{0,1},{1,0},{2,3},{3,2},{4,5},{5,4},{6,7},{7,6},{8,9},{9,8},{10,11... | collective-permute-start | bytes 3538952 | tf_op jit(solution)/shard_map/ppermute | solution.py:54
  213.0 24.6 %collective-permute-start.43 = (bf16[3,512,384]{2,1,0:T(8,128)(2,1)}, bf16[3,512,384]{2,1,0:T(8,128)(2,1)}, u32[]{:S(2)}, u32[]{:S(2)}) collective-permute-start(bf16[3,512,384]{2,1,0:T(8,128)(2,1)} %get-tuple-element.355.sent_ref), channel_id=1, source_target_pairs={{0,16},{16,0},{1,17},{17,1},{2,18},{18,2},{3,19},{19,3},{4,20},{20... | collective-permute-start | bytes 3538952 | tf_op jit(solution)/shard_map/ppermute | solution.py:65
  220.9 25.2 %collective-permute-start.41 = (bf16[4,192,384]{2,1,0:T(8,128)(2,1)}, bf16[4,192,384]{2,1,0:T(8,128)(2,1)S(1)}, u32[]{:S(2)}, u32[]{:S(2)}) collective-permute-start(bf16[4,192,384]{2,1,0:T(8,128)(2,1)} %get-tuple-element.478), channel_id=1, source_target_pairs={{0,2},{1,3},{2,0},{3,1},{4,6},{5,7},{6,4},{7,5},{8,10},{9,11},{10,... | collective-permute-start | bytes 1769480 | tf_op jit(solution)/shard_map/ppermute | solution.py:54
  221.4 25.1 %collective-permute-start.42 = (bf16[8,240,384]{2,1,0:T(8,128)(2,1)}, bf16[8,240,384]{2,1,0:T(8,128)(2,1)}, u32[]{:S(2)}, u32[]{:S(2)}) collective-permute-start(bf16[8,240,384]{2,1,0:T(8,128)(2,1)} %get-tuple-element.351), channel_id=1, source_target_pairs={{0,1},{1,0},{2,3},{3,2},{4,5},{5,4},{6,7},{7,6},{8,9},{9,8},{10,11... | collective-permute-start | bytes 4423688 | tf_op jit(solution)/shard_map/ppermute | solution.py:54
  237.4 19.9 %collective-permute-start.47 = (bf16[5,512,384]{2,1,0:T(8,128)(2,1)}, bf16[5,512,384]{2,1,0:T(8,128)(2,1)}, u32[]{:S(2)}, u32[]{:S(2)}) collective-permute-start(bf16[5,512,384]{2,1,0:T(8,128)(2,1)} %get-tuple-element.374.sent_ref), channel_id=1, source_target_pairs={{0,16},{16,0},{1,17},{17,1},{2,18},{18,2},{3,19},{19,3},{4,20},{20... | collective-permute-start | bytes 5898248 | tf_op jit(solution)/shard_map/ppermute | solution.py:65
  248.4 19.1 %collective-permute-start.46 = (bf16[4,240,384]{2,1,0:T(8,128)(2,1)S(1)}, bf16[4,240,384]{2,1,0:T(8,128)(2,1)S(1)}, u32[]{:S(2)}, u32[]{:S(2)}) collective-permute-start(bf16[4,240,384]{2,1,0:T(8,128)(2,1)S(1)} %get-tuple-element.474), channel_id=1, source_target_pairs={{0,2},{1,3},{2,0},{3,1},{4,6},{5,7},{6,4},{7,5},{8,10},{9,11},{10,... | collective-permute-start | bytes 2211848 | tf_op jit(solution)/shard_map/ppermute | solution.py:54
  248.9 15.3 %collective-permute-start.44 = (bf16[2,192,384]{2,1,0:T(8,128)(2,1)S(1)}, bf16[2,192,384]{2,1,0:T(8,128)(2,1)S(1)}, u32[]{:S(2)}, u32[]{:S(2)}) collective-permute-start(bf16[2,192,384]{2,1,0:T(8,128)(2,1)S(1)} %get-tuple-element.490), channel_id=1, source_target_pairs={{0,4},{1,5},{2,6},{3,7},{4,0},{5,1},{6,2},{7,3},{8,12},{9,13},{10,... | collective-permute-start | bytes 884744 | tf_op jit(solution)/shard_map/ppermute | solution.py:54
  250.1 18.5 %collective-permute-start.45 = (bf16[8,144,384]{2,1,0:T(8,128)(2,1)S(1)}, bf16[8,144,384]{2,1,0:T(8,128)(2,1)S(1)}, u32[]{:S(2)}, u32[]{:S(2)}) collective-permute-start(bf16[8,144,384]{2,1,0:T(8,128)(2,1)S(1)} %get-tuple-element.368), channel_id=1, source_target_pairs={{0,1},{1,0},{2,3},{3,2},{4,5},{5,4},{6,7},{7,6},{8,9},{9,8},{10,11... | collective-permute-start | bytes 2654216 | tf_op jit(solution)/shard_map/ppermute | solution.py:54
  257.2 30.0 %collective-permute-start.52 = (bf16[1,512,384]{2,1,0:T(8,128)(2,1)S(1)}, bf16[1,512,384]{2,1,0:T(8,128)(2,1)S(1)}, u32[]{:S(2)}, u32[]{:S(2)}) collective-permute-start(bf16[1,512,384]{2,1,0:T(8,128)(2,1)S(1)} %get-tuple-element.391.sent_ref), channel_id=1, source_target_pairs={{0,16},{16,0},{1,17},{17,1},{2,18},{18,2},{3,19},{19,3},{4,20},{20... | collective-permute-start | bytes 1179656 | tf_op jit(solution)/shard_map/ppermute | solution.py:65
  268.8 26.5 %collective-permute-start.51 = (bf16[2,240,384]{2,1,0:T(8,128)(2,1)S(1)}, bf16[2,240,384]{2,1,0:T(8,128)(2,1)S(1)}, u32[]{:S(2)}, u32[]{:S(2)}) collective-permute-start(bf16[2,240,384]{2,1,0:T(8,128)(2,1)S(1)} %get-tuple-element.486), channel_id=1, source_target_pairs={{0,4},{1,5},{2,6},{3,7},{4,0},{5,1},{6,2},{7,3},{8,12},{9,13},{10,... | collective-permute-start | bytes 1105928 | tf_op jit(solution)/shard_map/ppermute | solution.py:54
  269.3 26.0 %collective-permute-start.50 = (bf16[4,144,384]{2,1,0:T(8,128)(2,1)S(1)}, bf16[4,144,384]{2,1,0:T(8,128)(2,1)S(1)}, u32[]{:S(2)}, u32[]{:S(2)}) collective-permute-start(bf16[4,144,384]{2,1,0:T(8,128)(2,1)S(1)} %get-tuple-element.482), channel_id=1, source_target_pairs={{0,2},{1,3},{2,0},{3,1},{4,6},{5,7},{6,4},{7,5},{8,10},{9,11},{10,... | collective-permute-start | bytes 1327112 | tf_op jit(solution)/shard_map/ppermute | solution.py:54
  270.6 24.7 %collective-permute-start.48 = (bf16[8,192,384]{2,1,0:T(8,128)(2,1)S(1)}, bf16[8,192,384]{2,1,0:T(8,128)(2,1)S(1)}, u32[]{:S(2)}, u32[]{:S(2)}) collective-permute-start(bf16[8,192,384]{2,1,0:T(8,128)(2,1)S(1)} %get-tuple-element.386), channel_id=1, source_target_pairs={{0,1},{1,0},{2,3},{3,2},{4,5},{5,4},{6,7},{7,6},{8,9},{9,8},{10,11... | collective-permute-start | bytes 3538952 | tf_op jit(solution)/shard_map/ppermute | solution.py:54
  271.5 23.8 %collective-permute-start.49 = (bf16[1,192,384]{2,1,0:T(8,128)(2,1)S(1)}, bf16[1,192,384]{2,1,0:T(8,128)(2,1)S(1)}, u32[]{:S(2)}, u32[]{:S(2)}) collective-permute-start(bf16[1,192,384]{2,1,0:T(8,128)(2,1)S(1)} %get-tuple-element.516), channel_id=1, source_target_pairs={{0,8},{1,9},{2,10},{3,11},{4,12},{5,13},{6,14},{7,15},{8,0},{9,1},... | collective-permute-start | bytes 442376 | tf_op jit(solution)/shard_map/ppermute | solution.py:54
  287.2 16.0 %collective-permute-start.57 = (bf16[3,512,384]{2,1,0:T(8,128)(2,1)}, bf16[3,512,384]{2,1,0:T(8,128)(2,1)}, u32[]{:S(2)}, u32[]{:S(2)}) collective-permute-start(bf16[3,512,384]{2,1,0:T(8,128)(2,1)} %get-tuple-element.407.sent_ref), channel_id=1, source_target_pairs={{0,16},{16,0},{1,17},{17,1},{2,18},{18,2},{3,19},{19,3},{4,20},{20... | collective-permute-start | bytes 3538952 | tf_op jit(solution)/shard_map/ppermute | solution.py:65
  296.2 24.6 %collective-permute-start.56 = (bf16[1,240,384]{2,1,0:T(8,128)(2,1)}, bf16[1,240,384]{2,1,0:T(8,128)(2,1)}, u32[]{:S(2)}, u32[]{:S(2)}) collective-permute-start(bf16[1,240,384]{2,1,0:T(8,128)(2,1)} %get-tuple-element.512), channel_id=1, source_target_pairs={{0,8},{1,9},{2,10},{3,11},{4,12},{5,13},{6,14},{7,15},{8,0},{9,1},... | collective-permute-start | bytes 552968 | tf_op jit(solution)/shard_map/ppermute | solution.py:54
  297.7 23.0 %collective-permute-start.55 = (bf16[2,144,384]{2,1,0:T(8,128)(2,1)}, bf16[2,144,384]{2,1,0:T(8,128)(2,1)}, u32[]{:S(2)}, u32[]{:S(2)}) collective-permute-start(bf16[2,144,384]{2,1,0:T(8,128)(2,1)} %get-tuple-element.502), channel_id=1, source_target_pairs={{0,4},{1,5},{2,6},{3,7},{4,0},{5,1},{6,2},{7,3},{8,12},{9,13},{10,... | collective-permute-start | bytes 663560 | tf_op jit(solution)/shard_map/ppermute | solution.py:54
  300.9 19.8 %collective-permute-start.53 = (bf16[4,192,384]{2,1,0:T(8,128)(2,1)}, bf16[4,192,384]{2,1,0:T(8,128)(2,1)}, u32[]{:S(2)}, u32[]{:S(2)}) collective-permute-start(bf16[4,192,384]{2,1,0:T(8,128)(2,1)} %get-tuple-element.476), channel_id=1, source_target_pairs={{0,2},{1,3},{2,0},{3,1},{4,6},{5,7},{6,4},{7,5},{8,10},{9,11},{10,... | collective-permute-start | bytes 1769480 | tf_op jit(solution)/shard_map/ppermute | solution.py:54
  301.4 24.5 %collective-permute-start.54 = (bf16[8,240,384]{2,1,0:T(8,128)(2,1)}, bf16[8,240,384]{2,1,0:T(8,128)(2,1)}, u32[]{:S(2)}, u32[]{:S(2)}) collective-permute-start(bf16[8,240,384]{2,1,0:T(8,128)(2,1)} %get-tuple-element.403), channel_id=1, source_target_pairs={{0,1},{1,0},{2,3},{3,2},{4,5},{5,4},{6,7},{7,6},{8,9},{9,8},{10,11... | collective-permute-start | bytes 4423688 | tf_op jit(solution)/shard_map/ppermute | solution.py:54
  303.2 15.1 %collective-permute-start.58 = (f32[16,2,576]{2,1,0:T(2,128)S(1)}, f32[16,2,576]{2,1,0:T(2,128)S(1)}, u32[]{:S(2)}, u32[]{:S(2)}) collective-permute-start(f32[16,2,576]{2,1,0:T(2,128)S(1)} %pad_maximum_fusion.5), channel_id=1, source_target_pairs={{0,16},{16,0},{1,17},{17,1},{2,18},{18,2},{3,19},{19,3},{4,20},{20... | collective-permute-start | bytes 221192 | tf_op jit(solution)/shard_map/ppermute | solution.py:65
  327.7 20.6 %collective-permute-start.62 = (bf16[4,240,384]{2,1,0:T(8,128)(2,1)S(1)}, bf16[4,240,384]{2,1,0:T(8,128)(2,1)S(1)}, u32[]{:S(2)}, u32[]{:S(2)}) collective-permute-start(bf16[4,240,384]{2,1,0:T(8,128)(2,1)S(1)} %get-tuple-element.472), channel_id=1, source_target_pairs={{0,2},{1,3},{2,0},{3,1},{4,6},{5,7},{6,4},{7,5},{8,10},{9,11},{10,... | collective-permute-start | bytes 2211848 | tf_op jit(solution)/shard_map/ppermute | solution.py:54
  328.2 20.1 %collective-permute-start.61 = (bf16[8,144,384]{2,1,0:T(8,128)(2,1)S(1)}, bf16[8,144,384]{2,1,0:T(8,128)(2,1)S(1)}, u32[]{:S(2)}, u32[]{:S(2)}) collective-permute-start(bf16[8,144,384]{2,1,0:T(8,128)(2,1)S(1)} %get-tuple-element.425), channel_id=1, source_target_pairs={{0,1},{1,0},{2,3},{3,2},{4,5},{5,4},{6,7},{7,6},{8,9},{9,8},{10,11... | collective-permute-start | bytes 2654216 | tf_op jit(solution)/shard_map/ppermute | solution.py:54
  329.7 18.6 %collective-permute-start.59 = (f32[8,2,576]{2,1,0:T(2,128)S(1)}, f32[8,2,576]{2,1,0:T(2,128)S(1)}, u32[]{:S(2)}, u32[]{:S(2)}) collective-permute-start(f32[8,2,576]{2,1,0:T(2,128)S(1)} %get-tuple-element.554), channel_id=1, source_target_pairs={{0,1},{1,0},{2,3},{3,2},{4,5},{5,4},{6,7},{7,6},{8,9},{9,8},{10,11... | collective-permute-start | bytes 110600 | tf_op jit(solution)/shard_map/ppermute | solution.py:54
  331.5 16.8 %collective-permute-start.60 = (bf16[2,192,384]{2,1,0:T(8,128)(2,1)S(1)}, bf16[2,192,384]{2,1,0:T(8,128)(2,1)S(1)}, u32[]{:S(2)}, u32[]{:S(2)}) collective-permute-start(bf16[2,192,384]{2,1,0:T(8,128)(2,1)S(1)} %get-tuple-element.488), channel_id=1, source_target_pairs={{0,4},{1,5},{2,6},{3,7},{4,0},{5,1},{6,2},{7,3},{8,12},{9,13},{10,... | collective-permute-start | bytes 884744 | tf_op jit(solution)/shard_map/ppermute | solution.py:54
  333.6 14.8 %collective-permute-start.63 = (bf16[1,144,384]{2,1,0:T(8,128)(2,1)S(1)}, bf16[1,144,384]{2,1,0:T(8,128)(2,1)S(1)}, u32[]{:S(2)}, u32[]{:S(2)}) collective-permute-start(bf16[1,144,384]{2,1,0:T(8,128)(2,1)S(1)} %get-tuple-element.526), channel_id=1, source_target_pairs={{0,8},{1,9},{2,10},{3,11},{4,12},{5,13},{6,14},{7,15},{8,0},{9,1},... | collective-permute-start | bytes 331784 | tf_op jit(solution)/shard_map/ppermute | solution.py:54
  348.5 14.4 %collective-permute-start.67 = (bf16[2,240,384]{2,1,0:T(8,128)(2,1)S(1)}, bf16[2,240,384]{2,1,0:T(8,128)(2,1)S(1)}, u32[]{:S(2)}, u32[]{:S(2)}) collective-permute-start(bf16[2,240,384]{2,1,0:T(8,128)(2,1)S(1)} %get-tuple-element.484), channel_id=1, source_target_pairs={{0,4},{1,5},{2,6},{3,7},{4,0},{5,1},{6,2},{7,3},{8,12},{9,13},{10,... | collective-permute-start | bytes 1105928 | tf_op jit(solution)/shard_map/ppermute | solution.py:54
  349.6 13.3 %collective-permute-start.66 = (bf16[4,144,384]{2,1,0:T(8,128)(2,1)S(1)}, bf16[4,144,384]{2,1,0:T(8,128)(2,1)S(1)}, u32[]{:S(2)}, u32[]{:S(2)}) collective-permute-start(bf16[4,144,384]{2,1,0:T(8,128)(2,1)S(1)} %get-tuple-element.480), channel_id=1, source_target_pairs={{0,2},{1,3},{2,0},{3,1},{4,6},{5,7},{6,4},{7,5},{8,10},{9,11},{10,... | collective-permute-start | bytes 1327112 | tf_op jit(solution)/shard_map/ppermute | solution.py:54
  350.7 10.1 %collective-permute-start.65 = (bf16[1,192,384]{2,1,0:T(8,128)(2,1)S(1)}, bf16[1,192,384]{2,1,0:T(8,128)(2,1)S(1)}, u32[]{:S(2)}, u32[]{:S(2)}) collective-permute-start(bf16[1,192,384]{2,1,0:T(8,128)(2,1)S(1)} %get-tuple-element.514), channel_id=1, source_target_pairs={{0,8},{1,9},{2,10},{3,11},{4,12},{5,13},{6,14},{7,15},{8,0},{9,1},... | collective-permute-start | bytes 442376 | tf_op jit(solution)/shard_map/ppermute | solution.py:54
  363.0 12.0 %collective-permute-start.70 = (bf16[1,240,384]{2,1,0:T(8,128)(2,1)S(1)}, bf16[1,240,384]{2,1,0:T(8,128)(2,1)S(1)}, u32[]{:S(2)}, u32[]{:S(2)}) collective-permute-start(bf16[1,240,384]{2,1,0:T(8,128)(2,1)S(1)} %get-tuple-element.510), channel_id=1, source_target_pairs={{0,8},{1,9},{2,10},{3,11},{4,12},{5,13},{6,14},{7,15},{8,0},{9,1},... | collective-permute-start | bytes 552968 | tf_op jit(solution)/shard_map/ppermute | solution.py:54
  364.4 10.6 %collective-permute-start.69 = (bf16[2,144,384]{2,1,0:T(8,128)(2,1)S(1)}, bf16[2,144,384]{2,1,0:T(8,128)(2,1)S(1)}, u32[]{:S(2)}, u32[]{:S(2)}) collective-permute-start(bf16[2,144,384]{2,1,0:T(8,128)(2,1)S(1)} %get-tuple-element.500), channel_id=1, source_target_pairs={{0,4},{1,5},{2,6},{3,7},{4,0},{5,1},{6,2},{7,3},{8,12},{9,13},{10,... | collective-permute-start | bytes 663560 | tf_op jit(solution)/shard_map/ppermute | solution.py:54
  365.7 9.4 %collective-permute-start.68 = (f32[2,2,576]{2,1,0:T(2,128)S(1)}, f32[2,2,576]{2,1,0:T(2,128)S(1)}, u32[]{:S(2)}, u32[]{:S(2)}) collective-permute-start(f32[2,2,576]{2,1,0:T(2,128)S(1)} %get-tuple-element.556), channel_id=1, source_target_pairs={{0,4},{1,5},{2,6},{3,7},{4,0},{5,1},{6,2},{7,3},{8,12},{9,13},{10,... | collective-permute-start | bytes 27656 | tf_op jit(solution)/shard_map/ppermute | solution.py:54
  375.1 12.3 %collective-permute-start.72 = (bf16[1,144,384]{2,1,0:T(8,128)(2,1)S(1)}, bf16[1,144,384]{2,1,0:T(8,128)(2,1)S(1)}, u32[]{:S(2)}, u32[]{:S(2)}) collective-permute-start(bf16[1,144,384]{2,1,0:T(8,128)(2,1)S(1)} %get-tuple-element.524), channel_id=1, source_target_pairs={{0,24},{1,25},{2,26},{3,27},{4,28},{5,29},{6,30},{7,31},{8,16},{9,... | collective-permute-start | bytes 331784 | tf_op jit(solution)/shard_map/ppermute | solution.py:62
  375.2 12.2 %collective-permute-start.74 = (bf16[1,144,384]{2,1,0:T(8,128)(2,1)S(1)}, bf16[1,144,384]{2,1,0:T(8,128)(2,1)S(1)}, u32[]{:S(2)}, u32[]{:S(2)}) collective-permute-start(bf16[1,144,384]{2,1,0:T(8,128)(2,1)S(1)} %get-tuple-element.524), channel_id=1, source_target_pairs={{0,8},{1,9},{2,10},{3,11},{4,12},{5,13},{6,14},{7,15},{8,0},{9,1},... | collective-permute-start | bytes 331784 | tf_op jit(solution)/shard_map/ppermute | solution.py:54
  376.7 10.7 %collective-permute-start.71 = (bf16[1,144,384]{2,1,0:T(8,128)(2,1)S(1)}, bf16[1,144,384]{2,1,0:T(8,128)(2,1)S(1)}, u32[]{:S(2)}, u32[]{:S(2)}) collective-permute-start(bf16[1,144,384]{2,1,0:T(8,128)(2,1)S(1)} %get-tuple-element.444), channel_id=1, source_target_pairs={{0,16},{16,0},{1,17},{17,1},{2,18},{18,2},{3,19},{19,3},{4,20},{20... | collective-permute-start | bytes 331784 | tf_op jit(solution)/shard_map/ppermute | solution.py:65
  378.0 9.4 %collective-permute-start.73 = (f32[1,2,576]{2,1,0:T(2,128)S(1)}, f32[1,2,576]{2,1,0:T(2,128)S(1)}, u32[]{:S(2)}, u32[]{:S(2)}) collective-permute-start(f32[1,2,576]{2,1,0:T(2,128)S(1)} %get-tuple-element.558), channel_id=1, source_target_pairs={{0,8},{1,9},{2,10},{3,11},{4,12},{5,13},{6,14},{7,15},{8,0},{9,1},... | collective-permute-start | bytes 13832 | tf_op jit(solution)/shard_map/ppermute | solution.py:54
  378.5 9.6 %collective-permute-start.75 = (bf16[1008,384]{1,0:T(8,128)(2,1)S(1)}, bf16[1008,384]{1,0:T(8,128)(2,1)S(1)}, u32[]{:S(2)}, u32[]{:S(2)}) collective-permute-start(bf16[1008,384]{1,0:T(8,128)(2,1)S(1)} %get-tuple-element.462), channel_id=1, source_target_pairs={{0,16},{16,0},{1,17},{17,1},{2,18},{18,2},{3,19},{19,3},{4,20},{20... | collective-permute-start | bytes 2322440 | tf_op jit(solution)/shard_map/ppermute | solution.py:65
  (90 other events, 682.7 us)

commit v9 on v8

--- a/solution.py
+++ b/solution.py
@@ -815,19 +815,16 @@
         (left_a,) = close(left_a)
         first_sum, first_low = mix(tables, left_a, hidden, rows, *weight(level, 1))
         left_b, slope = expand(tables, first_low, rows, *weight(level, 2), parts)
-        left_b = trade(2 * level, left_a, left_b)
+        if last:
+            left_b = trade(2 * level, left_a, left_b)
         left_b, slope = close(left_b, slope)
-        started.append(2 * level)
         if last:
+            started.append(2 * level)
             twins[2 * level + 1] = net.twin(left_b)
         second_sum, hidden, h_low = contract(
             tables, left_b, first_sum, rows, *weight(level, 3), inner_width, last
         )
-        if not last:
-            h_low = trade(2 * level + 1, left_b, h_low)
         (h_low,) = close(h_low)
-        if not last:
-            started.append(2 * level + 1)
         kept.append((qkv, left_a, first_sum, left_b, slope, second_sum))
     layer_out = h_low
 
@@ -864,6 +861,11 @@
         q_received = net.twin(q_sent)
         *up_term, q_kept, q_sent, sums_qv = reduce.turn((*up_term, q_kept, q_sent, sums_qv))
         reduce.push((level, "up"), *up_term)
+        if level:
+            below = kept[level - 1]
+            lefts = (below[1], below[3])
+            lefts, q_kept = lax.optimization_barrier((lefts, q_kept))
+            twins[2 * level - 2 : 2 * level] = [net.twin(left) for left in lefts]
         d_vectors[level] = jnp.concatenate(
             [sums_qv.reshape(2, width), sums_a, sums_b, sums_u.reshape(-1, width)]
         ).reshape(count, -1)

time: 401 us -> 398 us (level)
    unnamed x208 -> x212, local copies, waits for them, and re-layouts: 20.4 us -> 19.9 us
where the time goes in v9:
time: 398 us; the launch traced here: 391 us
  Pallas kernels  145 us (36%)
  waiting for transfers between devices  118 us (30%)
  starting transfers between devices  72.7 us (18%)
  local copies, waits for them, and re-layouts  29.5 us (7%)
  other arithmetic  23 us (6%)
    ppermute x56, waiting for transfers between devices, trade(): return lax.ppermute(value, ('rep', 'fsdp'), pairs)  113 us
    ppermute x56, starting transfers between devices, trade(): return lax.ppermute(value, ('rep', 'fsdp'), pairs)  68.5 us
    pallas_call x6, Pallas kernels, weight_terms(): pl.pallas_call(body, grid=(chunks // 2,), out_shape=[shaped(half, sum(par...  35 us
    pallas_call x2, Pallas kernels, attend_back(): pl.pallas_call(body, grid=(1,), out_shape=[shaped(3, tokens, CHUNK), shap...  24.3 us
    unnamed x212, local copies, waits for them, and re-layouts  19.9 us
    pallas_call x2, Pallas kernels, project(): pl.pallas_call(body, grid=(3,), out_shape=[shaped(2, 3, tokens, CHUNK), s...  16.7 us
    pallas_call x2, Pallas kernels, expand(): pl.pallas_call(body, grid=(parts + 1,), out_shape=[shaped(2 * parts + 2,...  14.4 us
    pallas_call x2, Pallas kernels, contract(): pl.pallas_call(body, grid_spec=pltpu.PrefetchScalarGridSpec(num_scalar_pr...  14 us
  transfers between devices with their start and end apart: 76, of which 31 were waited for; matrix products, arithmetic and copies ran while one was open for 6% of the time, Pallas kernels for 37%

profile of v9, /device:TPU:0, one launch (start us, length us, event | category | flops | bytes accessed | tf_op | source)
XLA Modules:
  0.0 391.3 jit_solution(2578370229592514358)
XLA Ops:
  2.1 4.1 %collective-permute-start = (bf16[1,144,384]{2,1,0:T(8,128)(2,1)S(1)}, bf16[1,144,384]{2,1,0:T(8,128)(2,1)S(1)}, u32[]{:S(2)}, u32[]{:S(2)}) collective-permute-start(bf16[1,144,384]{2,1,0:T(8,128)(2,1)S(1)} %bitcast.82), channel_id=1, source_target_pairs={{0,8},{1,9},{2,10},{3,11},{4,12},{5,13},{6,14},{7,15},{8,0},{9,1},... | collective-permute-start | bytes 331784 | tf_op jit(solution)/shard_map/ppermute | solution.py:54
  9.3 2.5 collective-permute-done.1
  11.9 1.6 collective-permute-start.2
  14.3 3.7 collective-permute-done.4
  18.0 5.6 %collective-permute-done.3 = bf16[1,240,384]{2,1,0:T(8,128)(2,1)S(1)} collective-permute-done((bf16[1,240,384]{2,1,0:T(8,128)(2,1)S(1)}, bf16[1,240,384]{2,1,0:T(8,128)(2,1)S(1)}, u32[]{:S(2)}, u32[]{:S(2)}) %collective-permute-start.3) | collective-permute-done | bytes 184352 | tf_op jit(solution)/shard_map/ppermute | solution.py:54
  25.4 2.0 collective-permute-start.7
  27.4 9.2 %collective-permute-done.8 = f32[4,2,576]{2,1,0:T(2,128)S(1)} collective-permute-done((f32[4,2,576]{2,1,0:T(2,128)S(1)}, f32[4,2,576]{2,1,0:T(2,128)S(1)}, u32[]{:S(2)}, u32[]{:S(2)}) %collective-permute-start.8) | collective-permute-done | bytes 18464 | tf_op jit(solution)/shard_map/ppermute | solution.py:54
  36.8 1.9 collective-permute-start.9
  38.8 2.3 collective-permute-start.10
  41.8 1.8 collective-permute-start.13
  43.6 2.0 collective-permute-start.12
  45.7 7.9 %collective-permute-done.13 = f32[8,2,576]{2,1,0:T(2,128)S(1)} collective-permute-done((f32[8,2,576]{2,1,0:T(2,128)S(1)}, f32[8,2,576]{2,1,0:T(2,128)S(1)}, u32[]{:S(2)}, u32[]{:S(2)}) %collective-permute-start.13) | collective-permute-done | bytes 36896 | tf_op jit(solution)/shard_map/ppermute | solution.py:54
  53.6 6.0 %collective-permute-done.12 = bf16[1,192,384]{2,1,0:T(8,128)(2,1)S(1)} collective-permute-done((bf16[1,192,384]{2,1,0:T(8,128)(2,1)S(1)}, bf16[1,192,384]{2,1,0:T(8,128)(2,1)S(1)}, u32[]{:S(2)}, u32[]{:S(2)}) %collective-permute-start.12) | collective-permute-done | bytes 147488 | tf_op jit(solution)/shard_map/ppermute | solution.py:54
  65.7 2.9 collective-permute-start.15
  70.6 8.3 %project.2 = (bf16[2,3,512,384]{3,2,1,0:T(8,128)(2,1)S(1)}, bf16[4,512,384]{2,1,0:T(8,128)(2,1)S(1)}) custom-call(s32[2,16]{1,0:T(2,128)S(1)} %select_reduce_fusion.1.slots_ref, s32[1]{0:T(128)} %bitcast.core_ref, s32[4]{0:T(128)S(1)} %copy-done.25, bf16[512,768]{1,0:T(8,128)(2,1)S(1)} %copy-done.23, f32[12,768]{1,0:T(8,128)S(1)} %squeeze.21.rows_ref, ...), custom_call_target="tpu_custom_call" | custom-call | flops 16675000320 | bytes 14500000 | tf_op jit(solution)/shard_map/project/pallas_call | solution.py:253
  80.3 4.4 %collective-permute-done.17 = bf16[1,192,384]{2,1,0:T(8,128)(2,1)S(1)} collective-permute-done((bf16[1,192,384]{2,1,0:T(8,128)(2,1)S(1)}, bf16[1,192,384]{2,1,0:T(8,128)(2,1)S(1)}, u32[]{:S(2)}, u32[]{:S(2)}) %collective-permute-start.17) | collective-permute-done | bytes 147488 | tf_op jit(solution)/shard_map/ppermute | solution.py:54
  85.5 2.8 collective-permute-done.14
  88.9 1.8 collective-permute-start.21
  94.2 1.9 mix.2
  96.2 7.8 %expand.2 = (bf16[10,512,384]{2,1,0:T(8,128)(2,1)}, bf16[8,512,384]{2,1,0:T(8,128)(2,1)S(1)}) custom-call(s32[2,16]{1,0:T(2,128)S(1)} %select_reduce_fusion.1.slots_ref, s32[1]{0:T(128)} %bitcast.core_ref, bf16[512,768]{1,0:T(8,128)(2,1)S(1)} %get-tuple-element.280.x_ref, f32[12,768]{1,0:T(8,128)S(1)} %squeeze.21.rows_ref, ...), custom_call_target="tpu_custom_call" | custom-call | flops 10350000128 | bytes 9000000 | tf_op jit(solution)/shard_map/expand/pallas_call | solution.py:319
  103.9 1.7 copy-done.30
  105.7 1.7 collective-permute-done.22
  110.6 1.8 collective-permute-start.24
  113.7 7.1 %contract.2 = (f32[512,768]{1,0:T(8,128)S(1)}, f32[512,768]{1,0:T(8,128)S(1)}, bf16[512,768]{1,0:T(8,128)(2,1)S(1)}) custom-call(s32[2,16]{1,0:T(2,128)S(1)} %select_reduce_fusion.1.slots_ref, s32[1]{0:T(128)} %bitcast.core_ref, s32[4]{0:T(128)S(1)} %copy-done.25, bf16[10,512,384]{2,1,0:T(8,128)(2,1)} %get-tuple-element.363.active_ref.refs_0_, ...), custom_call_target="tpu_custom_call" | custom-call | flops 12419999744 | bytes 10800000 | tf_op jit(solution)/shard_map/contract/pallas_call | solution.py:380
  120.9 6.8 %collective-permute-done.25 = bf16[4,192,384]{2,1,0:T(8,128)(2,1)S(1)} collective-permute-done((bf16[4,192,384]{2,1,0:T(8,128)(2,1)S(1)}, bf16[4,192,384]{2,1,0:T(8,128)(2,1)S(1)}, u32[]{:S(2)}, u32[]{:S(2)}) %collective-permute-start.25) | collective-permute-done | bytes 589856 | tf_op jit(solution)/shard_map/ppermute | solution.py:54
  131.4 1.8 collective-permute-start.29
  135.0 8.5 %project.3 = (bf16[2,3,512,384]{3,2,1,0:T(8,128)(2,1)S(1)}, bf16[4,512,384]{2,1,0:T(8,128)(2,1)S(1)}) custom-call(s32[2,16]{1,0:T(2,128)S(1)} %select_reduce_fusion.1.slots_ref, s32[1]{0:T(128)} %bitcast.core_ref, s32[4]{0:T(128)S(1)} %copy-done.25, bf16[512,768]{1,0:T(8,128)(2,1)S(1)} %get-tuple-element.298.x_ref, f32[12,768]{1,0:T(8,128)S(1)} %squeeze.22.rows_ref, ...), custom_call_target="tpu_custom_call" | custom-call | flops 16675000320 | bytes 14500000 | tf_op jit(solution)/shard_map/project/pallas_call | solution.py:253
  143.5 3.4 collective-permute-done.29
  146.9 2.8 collective-permute-done.28
  151.9 2.5 mix.3
  154.7 6.7 %expand.3 = (bf16[10,512,384]{2,1,0:T(8,128)(2,1)S(1)}, bf16[8,512,384]{2,1,0:T(8,128)(2,1)S(1)}) custom-call(s32[2,16]{1,0:T(2,128)S(1)} %select_reduce_fusion.1.slots_ref, s32[1]{0:T(128)} %bitcast.core_ref, bf16[512,768]{1,0:T(8,128)(2,1)S(1)} %get-tuple-element.306.x_ref, f32[12,768]{1,0:T(8,128)S(1)} %squeeze.22.rows_ref, ...), custom_call_target="tpu_custom_call" | custom-call | flops 10350000128 | bytes 9000000 | tf_op jit(solution)/shard_map/expand/pallas_call | solution.py:319
  161.3 5.3 %collective-permute-done.31 = bf16[8,192,384]{2,1,0:T(8,128)(2,1)S(1)} collective-permute-done((bf16[8,192,384]{2,1,0:T(8,128)(2,1)S(1)}, bf16[8,192,384]{2,1,0:T(8,128)(2,1)S(1)}, u32[]{:S(2)}, u32[]{:S(2)}) %collective-permute-start.31) | collective-permute-done | bytes 1179680 | tf_op jit(solution)/shard_map/ppermute | solution.py:54
  167.5 4.0 %collective-permute-done.33.refs_4_.refs_5_.refs_6_.refs_7_ = bf16[16,192,384]{2,1,0:T(8,128)(2,1)S(1)} collective-permute-done((bf16[16,192,384]{2,1,0:T(8,128)(2,1)S(1)}, bf16[16,192,384]{2,1,0:T(8,128)(2,1)S(1)}, u32[]{:S(2)}, u32[]{:S(2)}) %collective-permute-start.33) | collective-permute-done | bytes 2359328 | tf_op jit(solution)/shard_map/ppermute | solution.py:65
  171.6 6.9 %contract.3 = (f32[512,768]{1,0:T(8,128)S(1)}, f32[512,768]{1,0:T(8,128)}, bf16[512,768]{1,0:T(8,128)(2,1)}) custom-call(s32[2,16]{1,0:T(2,128)S(1)} %select_reduce_fusion.1.slots_ref, s32[1]{0:T(128)} %bitcast.core_ref, s32[4]{0:T(128)S(1)} %copy-done.25, bf16[10,512,384]{2,1,0:T(8,128)(2,1)S(1)} %get-tuple-element.312.active_ref.refs_0_, ...), custom_call_target="tpu_custom_call" | custom-call | flops 12419999744 | bytes 10800000 | tf_op jit(solution)/shard_map/contract/pallas_call | solution.py:380
  178.5 5.9 %contract_back.2 = (f32[512,768]{1,0:T(8,128)S(1)}, bf16[1,512,384]{2,1,0:T(8,128)(2,1)S(1)}, bf16[4,512,384]{2,1,0:T(8,128)(2,1)S(1)}, bf16[5,512,384]{2,1,0:T(...) custom-call(s32[2,16]{1,0:T(2,128)S(1)} %select_reduce_fusion.1.slots_ref, s32[1]{0:T(128)} %bitcast.core_ref, ...), custom_call_target="tpu_custom_call" | custom-call | flops 12650000384 | bytes 11000000 | tf_op jit(solution)/shard_map/contract_back/pallas_call | solution.py:443
  186.3 6.3 %expand_back.2 = (f32[512,768]{1,0:T(8,128)S(1)}, bf16[1,512,384]{2,1,0:T(8,128)(2,1)S(1)}, bf16[1,512,384]{2,1,0:T(8,128)(2,1)S(1)}, f32[3,768]{1,0:T(4,128)S(1)}) custom-call(s32[2,16]{1,0:T(2,128)S(1)} %select_reduce_fusion.1.slots_ref, s32[1]{0:T(128)} %bitcast.core_ref, bf16[4,512,384]{2,1,0:T(8,128)(2,1)S(1)} %get-tuple-element.325.kept_ref.refs_2_, ...), custom_call_target="tpu_custom_call" | custom-call | flops 11269999616 | bytes 9800000 | tf_op jit(solution)/shard_map/expand_back/pallas_call | solution.py:514
  192.8 4.7 %weight_terms.6 = (bf16[8,192,384]{2,1,0:T(8,128)(2,1)S(1)}, bf16[8,192,384]{2,1,0:T(8,128)(2,1)S(1)}) custom-call(s32[2,16]{1,0:T(2,128)S(1)} %select_reduce_fusion.slots_ref, bf16[10,512,384]{2,1,0:T(8,128)(2,1)S(1)} %get-tuple-element.312.active_ref.refs_0_, bf16[10,512,384]{2,1,0:T(8,128)(2,1)S(1)} %collective-permute-done.35.refs_1_, ...), custom_call_target="tpu_custom_call" | custom-call | flops 6899999744 | bytes 6000000 | tf_op jit(solution)/shard_map/weight_terms/pallas_call | solution.py:666
  199.1 13.0 %attend_back.2 = (bf16[3,512,384]{2,1,0:T(8,128)(2,1)S(1)}, bf16[3,512,384]{2,1,0:T(8,128)(2,1)}, f32[2,2,1,384]{3,2,1,0:T(1,128)S(1)}) custom-call(s32[2,16]{1,0:T(2,128)S(1)} %select_reduce_fusion.1.slots_ref, s32[1]{0:T(128)} %bitcast.core_ref, s32[4]{0:T(128)S(1)} %copy-done.25, bf16[1,512,384]{2,1,0:T(8,128)(2,1)S(1)} %get-tuple-element.333.refs_6_.kept_ref, ...), custom_call_target="tpu_custom_call" | custom-call | flops 23690000384 | bytes 20600000 | tf_op jit(solution)/shard_map/attend_back/pallas_call | solution.py:569
  212.1 6.7 %weight_terms.7 = (bf16[8,240,384]{2,1,0:T(8,128)(2,1)S(1)}, bf16[8,240,384]{2,1,0:T(8,128)(2,1)}) custom-call(s32[2,16]{1,0:T(2,128)S(1)} %select_reduce_fusion.slots_ref, bf16[10,512,384]{2,1,0:T(8,128)(2,1)S(1)} %get-tuple-element.312.active_ref.refs_0_, bf16[10,512,384]{2,1,0:T(8,128)(2,1)S(1)} %collective-permute-done.35.refs_1_, ...), custom_call_target="tpu_custom_call" | custom-call | flops 8625000448 | bytes 7500000 | tf_op jit(solution)/shard_map/weight_terms/pallas_call | solution.py:666
  222.2 5.0 %project_back.2.d_out_ref = f32[512,768]{1,0:T(8,128)S(1)} custom-call(s32[2,16]{1,0:T(2,128)S(1)} %select_reduce_fusion.1.slots_ref, s32[1]{0:T(128)} %bitcast.core_ref, bf16[3,512,384]{2,1,0:T(8,128)(2,1)S(1)} %get-tuple-element.346.refs_2_.kept_ref, bf16[3,512,384]{2,1,0:T(8,128)(2,1)} %get-tuple-element.349.sent_ref, ...), custom_call_target="tpu_custom_call" | custom-call | flops 7590000128 | bytes 6600000 | tf_op jit(solution)/shard_map/project_back/pallas_call | solution.py:604
  227.2 7.1 %contract_back.3 = (f32[512,768]{1,0:T(8,128)S(1)}, bf16[1,512,384]{2,1,0:T(8,128)(2,1)S(1)}, bf16[4,512,384]{2,1,0:T(8,128)(2,1)S(1)}, bf16[5,512,384]{2,1,0:T(...) custom-call(s32[2,16]{1,0:T(2,128)S(1)} %select_reduce_fusion.1.slots_ref, s32[1]{0:T(128)} %bitcast.core_ref, ...), custom_call_target="tpu_custom_call" | custom-call | flops 12650000384 | bytes 11000000 | tf_op jit(solution)/shard_map/contract_back/pallas_call | solution.py:443
  241.5 4.4 %weight_terms.8 = (bf16[8,144,384]{2,1,0:T(8,128)(2,1)S(1)}, bf16[8,144,384]{2,1,0:T(8,128)(2,1)S(1)}) custom-call(s32[2,16]{1,0:T(2,128)S(1)} %select_reduce_fusion.slots_ref, bf16[4,512,384]{2,1,0:T(8,128)(2,1)S(1)} %copy-done.16, bf16[4,512,384]{2,1,0:T(8,128)(2,1)S(1)} %copy-done.20, bf16[3,512,384]{2,1,0:T(8,128)(2,1)S(1)} %copy-done.35, ...), custom_call_target="tpu_custom_call" | custom-call | flops 5175000064 | bytes 4500000 | tf_op jit(solution)/shard_map/weight_terms/pallas_call | solution.py:666
  245.9 1.9 add_convert_fusion.2
  250.0 6.7 %expand_back.3 = (f32[512,768]{1,0:T(8,128)S(1)}, bf16[1,512,384]{2,1,0:T(8,128)(2,1)S(1)}, bf16[1,512,384]{2,1,0:T(8,128)(2,1)S(1)}, f32[3,768]{1,0:T(4,128)S(1)}) custom-call(s32[2,16]{1,0:T(2,128)S(1)} %select_reduce_fusion.1.slots_ref, s32[1]{0:T(128)} %bitcast.core_ref, bf16[4,512,384]{2,1,0:T(8,128)(2,1)S(1)} %copy-done.37, ...), custom_call_target="tpu_custom_call" | custom-call | flops 11269999616 | bytes 9800000 | tf_op jit(solution)/shard_map/expand_back/pallas_call | solution.py:514
  257.1 6.6 %weight_terms.9 = (bf16[8,192,384]{2,1,0:T(8,128)(2,1)S(1)}, bf16[8,192,384]{2,1,0:T(8,128)(2,1)S(1)}) custom-call(s32[2,16]{1,0:T(2,128)S(1)} %select_reduce_fusion.slots_ref, bf16[10,512,384]{2,1,0:T(8,128)(2,1)} %get-tuple-element.363.active_ref.refs_0_, bf16[10,512,384]{2,1,0:T(8,128)(2,1)} %collective-permute-done.45.refs_1_, ...), custom_call_target="tpu_custom_call" | custom-call | flops 6899999744 | bytes 6000000 | tf_op jit(solution)/shard_map/weight_terms/pallas_call | solution.py:666
  263.7 1.7 collective-permute-done.42
  265.3 1.9 collective-permute-done.44
  270.8 11.4 %attend_back.3 = (bf16[3,512,384]{2,1,0:T(8,128)(2,1)S(1)}, bf16[3,512,384]{2,1,0:T(8,128)(2,1)S(1)}, f32[2,2,1,384]{3,2,1,0:T(1,128)S(1)}) custom-call(s32[2,16]{1,0:T(2,128)S(1)} %select_reduce_fusion.1.slots_ref, s32[1]{0:T(128)} %bitcast.core_ref, s32[4]{0:T(128)S(1)} %copy-done.25, bf16[1,512,384]{2,1,0:T(8,128)(2,1)S(1)} %get-tuple-element.382.refs_6_.kept_ref, ...), custom_call_target="tpu_custom_call" | custom-call | flops 23690000384 | bytes 20600000 | tf_op jit(solution)/shard_map/attend_back/pallas_call | solution.py:569
  283.3 2.2 collective-permute-start.48
  285.5 8.1 %weight_terms.10 = (bf16[8,240,384]{2,1,0:T(8,128)(2,1)S(1)}, bf16[8,240,384]{2,1,0:T(8,128)(2,1)}) custom-call(s32[2,16]{1,0:T(2,128)S(1)} %select_reduce_fusion.slots_ref, bf16[10,512,384]{2,1,0:T(8,128)(2,1)} %get-tuple-element.363.active_ref.refs_0_, bf16[10,512,384]{2,1,0:T(8,128)(2,1)} %collective-permute-done.45.refs_1_, ...), custom_call_target="tpu_custom_call" | custom-call | flops 8625000448 | bytes 7500000 | tf_op jit(solution)/shard_map/weight_terms/pallas_call | solution.py:666
  296.1 1.8 collective-permute-start.55
  306.2 4.4 %weight_terms.11 = (bf16[8,144,384]{2,1,0:T(8,128)(2,1)S(1)}, bf16[8,144,384]{2,1,0:T(8,128)(2,1)S(1)}) custom-call(s32[2,16]{1,0:T(2,128)S(1)} %select_reduce_fusion.slots_ref, bf16[4,512,384]{2,1,0:T(8,128)(2,1)S(1)} %copy-done.14, bf16[4,512,384]{2,1,0:T(8,128)(2,1)S(1)} %copy-done.18, bf16[3,512,384]{2,1,0:T(8,128)(2,1)S(1)} %copy-done.33, ...), custom_call_target="tpu_custom_call" | custom-call | flops 5175000064 | bytes 4500000 | tf_op jit(solution)/shard_map/weight_terms/pallas_call | solution.py:666
  310.7 5.5 %project_back.3 = f32[512,768]{1,0:T(8,128)} custom-call(s32[2,16]{1,0:T(2,128)S(1)} %select_reduce_fusion.1.slots_ref, s32[1]{0:T(128)} %bitcast.core_ref, bf16[3,512,384]{2,1,0:T(8,128)(2,1)S(1)} %copy-done.33, bf16[3,512,384]{2,1,0:T(8,128)(2,1)S(1)} %copy-done.22, f32[512,768]{1,0:T(8,128)S(1)} %copy-done.39, bf16[16,144,384]{2,1,0:T(8,128)(2,1)S(1)} %copy-done.7, ...), custom_call_target="tpu_custom_call" | custom-call | flops 7590000128 | bytes 6600000 | tf_op jit(solution)/shard_map/project_back/pallas_call | solution.py:604
  317.6 1.7 gather_fusion.1
  319.4 4.8 %collective-permute-done.54 = bf16[8,240,384]{2,1,0:T(8,128)(2,1)} collective-permute-done((bf16[8,240,384]{2,1,0:T(8,128)(2,1)}, bf16[8,240,384]{2,1,0:T(8,128)(2,1)}, u32[]{:S(2)}, u32[]{:S(2)}) %collective-permute-start.54) | collective-permute-done | bytes 1474592 | tf_op jit(solution)/shard_map/ppermute | solution.py:54
  324.2 1.8 add_convert_fusion
  331.8 2.0 collective-permute-start.63
  334.9 12.1 %collective-permute-done.59 = f32[8,2,576]{2,1,0:T(2,128)S(1)} collective-permute-done((f32[8,2,576]{2,1,0:T(2,128)S(1)}, f32[8,2,576]{2,1,0:T(2,128)S(1)}, u32[]{:S(2)}, u32[]{:S(2)}) %collective-permute-start.59) | collective-permute-done | bytes 36896 | tf_op jit(solution)/shard_map/ppermute | solution.py:54
  349.4 2.0 collective-permute-start.65
  352.2 4.5 %collective-permute-done.64 = f32[4,2,576]{2,1,0:T(2,128)S(1)} collective-permute-done((f32[4,2,576]{2,1,0:T(2,128)S(1)}, f32[4,2,576]{2,1,0:T(2,128)S(1)}, u32[]{:S(2)}, u32[]{:S(2)}) %collective-permute-start.64) | collective-permute-done | bytes 18464 | tf_op jit(solution)/shard_map/ppermute | solution.py:54
  356.7 2.5 collective-permute-done.65
  359.2 2.1 collective-permute-done.67
  365.0 8.3 %collective-permute-done.68 = f32[2,2,576]{2,1,0:T(2,128)S(1)} collective-permute-done((f32[2,2,576]{2,1,0:T(2,128)S(1)}, f32[2,2,576]{2,1,0:T(2,128)S(1)}, u32[]{:S(2)}, u32[]{:S(2)}) %collective-permute-start.68) | collective-permute-done | bytes 9248 | tf_op jit(solution)/shard_map/ppermute | solution.py:54
  377.1 8.6 %collective-permute-done.73 = f32[1,2,576]{2,1,0:T(2,128)S(1)} collective-permute-done((f32[1,2,576]{2,1,0:T(2,128)S(1)}, f32[1,2,576]{2,1,0:T(2,128)S(1)}, u32[]{:S(2)}, u32[]{:S(2)}) %collective-permute-start.73) | collective-permute-done | bytes 4640 | tf_op jit(solution)/shard_map/ppermute | solution.py:54
  (442 shorter events, 91.6 us)
Async XLA Ops:
  2.1 9.8 %collective-permute-start = (bf16[1,144,384]{2,1,0:T(8,128)(2,1)S(1)}, bf16[1,144,384]{2,1,0:T(8,128)(2,1)S(1)}, u32[]{:S(2)}, u32[]{:S(2)}) collective-permute-start(bf16[1,144,384]{2,1,0:T(8,128)(2,1)S(1)} %bitcast.82), channel_id=1, source_target_pairs={{0,8},{1,9},{2,10},{3,11},{4,12},{5,13},{6,14},{7,15},{8,0},{9,1},... | collective-permute-start | bytes 331784 | tf_op jit(solution)/shard_map/ppermute | solution.py:54
  11.9 11.7 %collective-permute-start.2 = (bf16[2,144,384]{2,1,0:T(8,128)(2,1)S(1)}, bf16[2,144,384]{2,1,0:T(8,128)(2,1)S(1)}, u32[]{:S(2)}, u32[]{:S(2)}) collective-permute-start(bf16[2,144,384]{2,1,0:T(8,128)(2,1)S(1)} %constant_dynamic-update-slice_fusion), channel_id=1, source_target_pairs={{0,2},{1,3},{2,0},{3,1},{4,6},{5,7},{6,4},{7,5},{8,10},{9,11},{10,... | collective-permute-start | bytes 663560 | tf_op jit(solution)/shard_map/ppermute | solution.py:54
  13.5 10.1 %collective-permute-start.3 = (bf16[1,240,384]{2,1,0:T(8,128)(2,1)S(1)}, bf16[1,240,384]{2,1,0:T(8,128)(2,1)S(1)}, u32[]{:S(2)}, u32[]{:S(2)}) collective-permute-start(bf16[1,240,384]{2,1,0:T(8,128)(2,1)S(1)} %maximum_bitcast_fusion), channel_id=1, source_target_pairs={{0,8},{1,9},{2,10},{3,11},{4,12},{5,13},{6,14},{7,15},{8,0},{9,1},... | collective-permute-start | bytes 552968 | tf_op jit(solution)/shard_map/ppermute | solution.py:54
  23.7 13.0 %collective-permute-start.5 = (bf16[4,144,384]{2,1,0:T(8,128)(2,1)S(1)}, bf16[4,144,384]{2,1,0:T(8,128)(2,1)S(1)}, u32[]{:S(2)}, u32[]{:S(2)}) collective-permute-start(bf16[4,144,384]{2,1,0:T(8,128)(2,1)S(1)} %constant_dynamic-update-slice_fusion.2), channel_id=1, source_target_pairs={{0,4},{1,5},{2,6},{3,7},{4,0},{5,1},{6,2},{7,3},{8,12},{9,13},{10,... | collective-permute-start | bytes 1327112 | tf_op jit(solution)/shard_map/ppermute | solution.py:54
  23.8 12.8 %collective-permute-start.6 = (bf16[2,240,384]{2,1,0:T(8,128)(2,1)S(1)}, bf16[2,240,384]{2,1,0:T(8,128)(2,1)S(1)}, u32[]{:S(2)}, u32[]{:S(2)}) collective-permute-start(bf16[2,240,384]{2,1,0:T(8,128)(2,1)S(1)} %constant_dynamic-update-slice_fusion.4), channel_id=1, source_target_pairs={{0,2},{1,3},{2,0},{3,1},{4,6},{5,7},{6,4},{7,5},{8,10},{9,11},{10,... | collective-permute-start | bytes 1105928 | tf_op jit(solution)/shard_map/ppermute | solution.py:54
  25.4 11.3 %collective-permute-start.7 = (bf16[1,192,384]{2,1,0:T(8,128)(2,1)S(1)}, bf16[1,192,384]{2,1,0:T(8,128)(2,1)S(1)}, u32[]{:S(2)}, u32[]{:S(2)}) collective-permute-start(bf16[1,192,384]{2,1,0:T(8,128)(2,1)S(1)} %constant_dynamic-slice_fusion.8), channel_id=1, source_target_pairs={{0,8},{1,9},{2,10},{3,11},{4,12},{5,13},{6,14},{7,15},{8,0},{9,1},... | collective-permute-start | bytes 442376 | tf_op jit(solution)/shard_map/ppermute | solution.py:54
  27.4 9.2 %collective-permute-start.8 = (f32[4,2,576]{2,1,0:T(2,128)S(1)}, f32[4,2,576]{2,1,0:T(2,128)S(1)}, u32[]{:S(2)}, u32[]{:S(2)}) collective-permute-start(f32[4,2,576]{2,1,0:T(2,128)S(1)} %pad_maximum_fusion.9), channel_id=1, source_target_pairs={{0,4},{1,5},{2,6},{3,7},{4,0},{5,1},{6,2},{7,3},{8,12},{9,13},{10,... | collective-permute-start | bytes 55304 | tf_op jit(solution)/shard_map/ppermute | solution.py:54
  36.8 24.4 %collective-permute-start.9 = (bf16[8,144,384]{2,1,0:T(8,128)(2,1)S(1)}, bf16[8,144,384]{2,1,0:T(8,128)(2,1)}, u32[]{:S(2)}, u32[]{:S(2)}) collective-permute-start(bf16[8,144,384]{2,1,0:T(8,128)(2,1)S(1)} %constant_dynamic-update-slice_fusion.6), channel_id=1, source_target_pairs={{0,1},{1,0},{2,3},{3,2},{4,5},{5,4},{6,7},{7,6},{8,9},{9,8},{10,11... | collective-permute-start | bytes 2654216 | tf_op jit(solution)/shard_map/ppermute | solution.py:54
  38.8 21.6 %collective-permute-start.10 = (bf16[4,240,384]{2,1,0:T(8,128)(2,1)S(1)}, bf16[4,240,384]{2,1,0:T(8,128)(2,1)S(1)}, u32[]{:S(2)}, u32[]{:S(2)}) collective-permute-start(bf16[4,240,384]{2,1,0:T(8,128)(2,1)S(1)} %constant_dynamic-update-slice_fusion.8), channel_id=1, source_target_pairs={{0,4},{1,5},{2,6},{3,7},{4,0},{5,1},{6,2},{7,3},{8,12},{9,13},{10,... | collective-permute-start | bytes 2211848 | tf_op jit(solution)/shard_map/ppermute | solution.py:54
  41.1 18.5 %collective-permute-start.11 = (bf16[2,192,384]{2,1,0:T(8,128)(2,1)S(1)}, bf16[2,192,384]{2,1,0:T(8,128)(2,1)S(1)}, u32[]{:S(2)}, u32[]{:S(2)}) collective-permute-start(bf16[2,192,384]{2,1,0:T(8,128)(2,1)S(1)} %constant_dynamic-update-slice_fusion.10), channel_id=1, source_target_pairs={{0,2},{1,3},{2,0},{3,1},{4,6},{5,7},{6,4},{7,5},{8,10},{9,11},{10,... | collective-permute-start | bytes 884744 | tf_op jit(solution)/shard_map/ppermute | solution.py:54
  41.8 11.7 %collective-permute-start.13 = (f32[8,2,576]{2,1,0:T(2,128)S(1)}, f32[8,2,576]{2,1,0:T(2,128)S(1)}, u32[]{:S(2)}, u32[]{:S(2)}) collective-permute-start(f32[8,2,576]{2,1,0:T(2,128)S(1)} %pad_maximum_fusion.8), channel_id=1, source_target_pairs={{0,1},{1,0},{2,3},{3,2},{4,5},{5,4},{6,7},{7,6},{8,9},{9,8},{10,11... | collective-permute-start | bytes 110600 | tf_op jit(solution)/shard_map/ppermute | solution.py:54
  43.6 16.0 %collective-permute-start.12 = (bf16[1,192,384]{2,1,0:T(8,128)(2,1)S(1)}, bf16[1,192,384]{2,1,0:T(8,128)(2,1)S(1)}, u32[]{:S(2)}, u32[]{:S(2)}) collective-permute-start(bf16[1,192,384]{2,1,0:T(8,128)(2,1)S(1)} %maximum_bitcast_fusion.1), channel_id=1, source_target_pairs={{0,8},{1,9},{2,10},{3,11},{4,12},{5,13},{6,14},{7,15},{8,0},{9,1},... | collective-permute-start | bytes 442376 | tf_op jit(solution)/shard_map/ppermute | solution.py:54
  65.2 19.5 %collective-permute-start.16 = (bf16[2,192,384]{2,1,0:T(8,128)(2,1)S(1)}, bf16[2,192,384]{2,1,0:T(8,128)(2,1)S(1)}, u32[]{:S(2)}, u32[]{:S(2)}) collective-permute-start(bf16[2,192,384]{2,1,0:T(8,128)(2,1)S(1)} %constant_dynamic-update-slice_fusion.16), channel_id=1, source_target_pairs={{0,2},{1,3},{2,0},{3,1},{4,6},{5,7},{6,4},{7,5},{8,10},{9,11},{10,... | collective-permute-start | bytes 884744 | tf_op jit(solution)/shard_map/ppermute | solution.py:54
  65.7 19.8 %collective-permute-start.15 = (bf16[4,192,384]{2,1,0:T(8,128)(2,1)S(1)}, bf16[4,192,384]{2,1,0:T(8,128)(2,1)S(1)}, u32[]{:S(2)}, u32[]{:S(2)}) collective-permute-start(bf16[4,192,384]{2,1,0:T(8,128)(2,1)S(1)} %constant_dynamic-update-slice_fusion.14), channel_id=1, source_target_pairs={{0,4},{1,5},{2,6},{3,7},{4,0},{5,1},{6,2},{7,3},{8,12},{9,13},{10,... | collective-permute-start | bytes 1769480 | tf_op jit(solution)/shard_map/ppermute | solution.py:54
  68.8 19.4 %collective-permute-start.14 = (bf16[8,240,384]{2,1,0:T(8,128)(2,1)S(1)}, bf16[8,240,384]{2,1,0:T(8,128)(2,1)S(1)}, u32[]{:S(2)}, u32[]{:S(2)}) collective-permute-start(bf16[8,240,384]{2,1,0:T(8,128)(2,1)S(1)} %constant_dynamic-update-slice_fusion.12), channel_id=1, source_target_pairs={{0,1},{1,0},{2,3},{3,2},{4,5},{5,4},{6,7},{7,6},{8,9},{9,8},{10,11... | collective-permute-start | bytes 4423688 | tf_op jit(solution)/shard_map/ppermute | solution.py:54
  69.9 14.8 %collective-permute-start.17 = (bf16[1,192,384]{2,1,0:T(8,128)(2,1)S(1)}, bf16[1,192,384]{2,1,0:T(8,128)(2,1)S(1)}, u32[]{:S(2)}, u32[]{:S(2)}) collective-permute-start(bf16[1,192,384]{2,1,0:T(8,128)(2,1)S(1)} %bitcast.74), channel_id=1, source_target_pairs={{0,8},{1,9},{2,10},{3,11},{4,12},{5,13},{6,14},{7,15},{8,0},{9,1},... | collective-permute-start | bytes 442376 | tf_op jit(solution)/shard_map/ppermute | solution.py:54
  88.9 18.5 %collective-permute-start.21 = (bf16[2,192,384]{2,1,0:T(8,128)(2,1)S(1)}, bf16[2,192,384]{2,1,0:T(8,128)(2,1)S(1)}, u32[]{:S(2)}, u32[]{:S(2)}) collective-permute-start(bf16[2,192,384]{2,1,0:T(8,128)(2,1)S(1)} %constant_dynamic-update-slice_fusion.24), channel_id=1, source_target_pairs={{0,2},{1,3},{2,0},{3,1},{4,6},{5,7},{6,4},{7,5},{8,10},{9,11},{10,... | collective-permute-start | bytes 884744 | tf_op jit(solution)/shard_map/ppermute | solution.py:54
  90.8 17.9 %collective-permute-start.20 = (bf16[4,192,384]{2,1,0:T(8,128)(2,1)S(1)}, bf16[4,192,384]{2,1,0:T(8,128)(2,1)S(1)}, u32[]{:S(2)}, u32[]{:S(2)}) collective-permute-start(bf16[4,192,384]{2,1,0:T(8,128)(2,1)S(1)} %constant_dynamic-update-slice_fusion.22), channel_id=1, source_target_pairs={{0,4},{1,5},{2,6},{3,7},{4,0},{5,1},{6,2},{7,3},{8,12},{9,13},{10,... | collective-permute-start | bytes 1769480 | tf_op jit(solution)/shard_map/ppermute | solution.py:54
  91.7 17.0 %collective-permute-start.19 = (bf16[8,192,384]{2,1,0:T(8,128)(2,1)S(1)}, bf16[8,192,384]{2,1,0:T(8,128)(2,1)S(1)}, u32[]{:S(2)}, u32[]{:S(2)}) collective-permute-start(bf16[8,192,384]{2,1,0:T(8,128)(2,1)S(1)} %constant_dynamic-update-slice_fusion.20), channel_id=1, source_target_pairs={{0,1},{1,0},{2,3},{3,2},{4,5},{5,4},{6,7},{7,6},{8,9},{9,8},{10,11... | collective-permute-start | bytes 3538952 | tf_op jit(solution)/shard_map/ppermute | solution.py:54
  92.8 14.6 %collective-permute-start.22 = (bf16[1,192,384]{2,1,0:T(8,128)(2,1)S(1)}, bf16[1,192,384]{2,1,0:T(8,128)(2,1)S(1)}, u32[]{:S(2)}, u32[]{:S(2)}) collective-permute-start(bf16[1,192,384]{2,1,0:T(8,128)(2,1)S(1)} %copy-done.64), channel_id=1, source_target_pairs={{0,8},{1,9},{2,10},{3,11},{4,12},{5,13},{6,14},{7,15},{8,0},{9,1},... | collective-permute-start | bytes 442376 | tf_op jit(solution)/shard_map/ppermute | solution.py:54
  109.2 11.6 %collective-permute-start.26 = (bf16[2,192,384]{2,1,0:T(8,128)(2,1)S(1)}, bf16[2,192,384]{2,1,0:T(8,128)(2,1)S(1)}, u32[]{:S(2)}, u32[]{:S(2)}) collective-permute-start(bf16[2,192,384]{2,1,0:T(8,128)(2,1)S(1)} %constant_dynamic-update-slice_fusion.32), channel_id=1, source_target_pairs={{0,2},{1,3},{2,0},{3,1},{4,6},{5,7},{6,4},{7,5},{8,10},{9,11},{10,... | collective-permute-start | bytes 884744 | tf_op jit(solution)/shard_map/ppermute | solution.py:54
  110.6 17.6 %collective-permute-start.24 = (bf16[8,192,384]{2,1,0:T(8,128)(2,1)S(1)}, bf16[8,192,384]{2,1,0:T(8,128)(2,1)S(1)}, u32[]{:S(2)}, u32[]{:S(2)}) collective-permute-start(bf16[8,192,384]{2,1,0:T(8,128)(2,1)S(1)} %constant_dynamic-update-slice_fusion.28), channel_id=1, source_target_pairs={{0,1},{1,0},{2,3},{3,2},{4,5},{5,4},{6,7},{7,6},{8,9},{9,8},{10,11... | collective-permute-start | bytes 3538952 | tf_op jit(solution)/shard_map/ppermute | solution.py:54
  112.5 15.1 %collective-permute-start.25 = (bf16[4,192,384]{2,1,0:T(8,128)(2,1)S(1)}, bf16[4,192,384]{2,1,0:T(8,128)(2,1)S(1)}, u32[]{:S(2)}, u32[]{:S(2)}) collective-permute-start(bf16[4,192,384]{2,1,0:T(8,128)(2,1)S(1)} %constant_dynamic-update-slice_fusion.30), channel_id=1, source_target_pairs={{0,4},{1,5},{2,6},{3,7},{4,0},{5,1},{6,2},{7,3},{8,12},{9,13},{10,... | collective-permute-start | bytes 1769480 | tf_op jit(solution)/shard_map/ppermute | solution.py:54
  131.4 15.5 %collective-permute-start.29 = (bf16[4,192,384]{2,1,0:T(8,128)(2,1)S(1)}, bf16[4,192,384]{2,1,0:T(8,128)(2,1)S(1)}, u32[]{:S(2)}, u32[]{:S(2)}) collective-permute-start(bf16[4,192,384]{2,1,0:T(8,128)(2,1)S(1)} %constant_dynamic-update-slice_fusion.38), channel_id=1, source_target_pairs={{0,4},{1,5},{2,6},{3,7},{4,0},{5,1},{6,2},{7,3},{8,12},{9,13},{10,... | collective-permute-start | bytes 1769480 | tf_op jit(solution)/shard_map/ppermute | solution.py:54
  133.4 16.3 %collective-permute-start.28 = (bf16[8,192,384]{2,1,0:T(8,128)(2,1)S(1)}, bf16[8,192,384]{2,1,0:T(8,128)(2,1)S(1)}, u32[]{:S(2)}, u32[]{:S(2)}) collective-permute-start(bf16[8,192,384]{2,1,0:T(8,128)(2,1)S(1)} %constant_dynamic-update-slice_fusion.36), channel_id=1, source_target_pairs={{0,1},{1,0},{2,3},{3,2},{4,5},{5,4},{6,7},{7,6},{8,9},{9,8},{10,11... | collective-permute-start | bytes 3538952 | tf_op jit(solution)/shard_map/ppermute | solution.py:54
  150.3 16.3 %collective-permute-start.31 = (bf16[8,192,384]{2,1,0:T(8,128)(2,1)S(1)}, bf16[8,192,384]{2,1,0:T(8,128)(2,1)S(1)}, u32[]{:S(2)}, u32[]{:S(2)}) collective-permute-start(bf16[8,192,384]{2,1,0:T(8,128)(2,1)S(1)} %constant_dynamic-update-slice_fusion.42), channel_id=1, source_target_pairs={{0,1},{1,0},{2,3},{3,2},{4,5},{5,4},{6,7},{7,6},{8,9},{9,8},{10,11... | collective-permute-start | bytes 3538952 | tf_op jit(solution)/shard_map/ppermute | solution.py:54
  167.0 25.7 %collective-permute-start.35 = (bf16[10,512,384]{2,1,0:T(8,128)(2,1)S(1)}, bf16[10,512,384]{2,1,0:T(8,128)(2,1)S(1)}, u32[]{:S(2)}, u32[]{:S(2)}) collective-permute-start(bf16[10,512,384]{2,1,0:T(8,128)(2,1)S(1)} %get-tuple-element.312.active_ref.refs_0_), channel_id=1, source_target_pairs={{0,16},{16,0},{1,17},{17,1},{2,18},{18,2},{3,19},{19,3},{4,20},{20... | collective-permute-start | bytes 11796488 | tf_op jit(solution)/shard_map/ppermute | solution.py:65
  192.6 19.5 %collective-permute-start.38 = (bf16[1,512,384]{2,1,0:T(8,128)(2,1)S(1)}, bf16[1,512,384]{2,1,0:T(8,128)(2,1)S(1)}, u32[]{:S(2)}, u32[]{:S(2)}) collective-permute-start(bf16[1,512,384]{2,1,0:T(8,128)(2,1)S(1)} %get-tuple-element.336.sent_ref), channel_id=1, source_target_pairs={{0,16},{16,0},{1,17},{17,1},{2,18},{18,2},{3,19},{19,3},{4,20},{20... | collective-permute-start | bytes 1179656 | tf_op jit(solution)/shard_map/ppermute | solution.py:65
  197.5 21.3 %collective-permute-start.37 = (bf16[8,192,384]{2,1,0:T(8,128)(2,1)S(1)}, bf16[8,192,384]{2,1,0:T(8,128)(2,1)S(1)}, u32[]{:S(2)}, u32[]{:S(2)}) collective-permute-start(bf16[8,192,384]{2,1,0:T(8,128)(2,1)S(1)} %get-tuple-element.331), channel_id=1, source_target_pairs={{0,1},{1,0},{2,3},{3,2},{4,5},{5,4},{6,7},{7,6},{8,9},{9,8},{10,11... | collective-permute-start | bytes 3538952 | tf_op jit(solution)/shard_map/ppermute | solution.py:54
  212.1 25.2 %collective-permute-start.41 = (bf16[3,512,384]{2,1,0:T(8,128)(2,1)}, bf16[3,512,384]{2,1,0:T(8,128)(2,1)}, u32[]{:S(2)}, u32[]{:S(2)}) collective-permute-start(bf16[3,512,384]{2,1,0:T(8,128)(2,1)} %get-tuple-element.349.sent_ref), channel_id=1, source_target_pairs={{0,16},{16,0},{1,17},{17,1},{2,18},{18,2},{3,19},{19,3},{4,20},{20... | collective-permute-start | bytes 3538952 | tf_op jit(solution)/shard_map/ppermute | solution.py:65
  220.0 25.9 %collective-permute-start.39 = (bf16[4,192,384]{2,1,0:T(8,128)(2,1)S(1)}, bf16[4,192,384]{2,1,0:T(8,128)(2,1)S(1)}, u32[]{:S(2)}, u32[]{:S(2)}) collective-permute-start(bf16[4,192,384]{2,1,0:T(8,128)(2,1)S(1)} %get-tuple-element.472), channel_id=1, source_target_pairs={{0,2},{1,3},{2,0},{3,1},{4,6},{5,7},{6,4},{7,5},{8,10},{9,11},{10,... | collective-permute-start | bytes 1769480 | tf_op jit(solution)/shard_map/ppermute | solution.py:54
  220.6 25.3 %collective-permute-start.40 = (bf16[8,240,384]{2,1,0:T(8,128)(2,1)}, bf16[8,240,384]{2,1,0:T(8,128)(2,1)}, u32[]{:S(2)}, u32[]{:S(2)}) collective-permute-start(bf16[8,240,384]{2,1,0:T(8,128)(2,1)} %get-tuple-element.344), channel_id=1, source_target_pairs={{0,1},{1,0},{2,3},{3,2},{4,5},{5,4},{6,7},{7,6},{8,9},{9,8},{10,11... | collective-permute-start | bytes 4423688 | tf_op jit(solution)/shard_map/ppermute | solution.py:54
  222.1 34.9 %collective-permute-start.45 = (bf16[10,512,384]{2,1,0:T(8,128)(2,1)}, bf16[10,512,384]{2,1,0:T(8,128)(2,1)}, u32[]{:S(2)}, u32[]{:S(2)}) collective-permute-start(bf16[10,512,384]{2,1,0:T(8,128)(2,1)} %get-tuple-element.363.active_ref.refs_0_), channel_id=1, source_target_pairs={{0,16},{16,0},{1,17},{17,1},{2,18},{18,2},{3,19},{19,3},{4,20},{20... | collective-permute-start | bytes 11796488 | tf_op jit(solution)/shard_map/ppermute | solution.py:65
  236.6 20.3 %collective-permute-start.46 = (bf16[5,512,384]{2,1,0:T(8,128)(2,1)}, bf16[5,512,384]{2,1,0:T(8,128)(2,1)}, u32[]{:S(2)}, u32[]{:S(2)}) collective-permute-start(bf16[5,512,384]{2,1,0:T(8,128)(2,1)} %get-tuple-element.368.sent_ref), channel_id=1, source_target_pairs={{0,16},{16,0},{1,17},{17,1},{2,18},{18,2},{3,19},{19,3},{4,20},{20... | collective-permute-start | bytes 5898248 | tf_op jit(solution)/shard_map/ppermute | solution.py:65
  237.3 46.0 %collective-permute-start.51 = (bf16[4,512,384]{2,1,0:T(8,128)(2,1)}, bf16[4,512,384]{2,1,0:T(8,128)(2,1)S(1)}, u32[]{:S(2)}, u32[]{:S(2)}) collective-permute-start(bf16[4,512,384]{2,1,0:T(8,128)(2,1)} %copy-done.12), channel_id=1, source_target_pairs={{0,16},{16,0},{1,17},{17,1},{2,18},{18,2},{3,19},{19,3},{4,20},{20... | collective-permute-start | bytes 4718600 | tf_op jit(solution)/shard_map/ppermute | solution.py:65
  247.8 19.4 %collective-permute-start.44 = (bf16[4,240,384]{2,1,0:T(8,128)(2,1)S(1)}, bf16[4,240,384]{2,1,0:T(8,128)(2,1)S(1)}, u32[]{:S(2)}, u32[]{:S(2)}) collective-permute-start(bf16[4,240,384]{2,1,0:T(8,128)(2,1)S(1)} %get-tuple-element.468), channel_id=1, source_target_pairs={{0,2},{1,3},{2,0},{3,1},{4,6},{5,7},{6,4},{7,5},{8,10},{9,11},{10,... | collective-permute-start | bytes 2211848 | tf_op jit(solution)/shard_map/ppermute | solution.py:54
  248.5 19.9 %collective-permute-start.43 = (bf16[8,144,384]{2,1,0:T(8,128)(2,1)S(1)}, bf16[8,144,384]{2,1,0:T(8,128)(2,1)S(1)}, u32[]{:S(2)}, u32[]{:S(2)}) collective-permute-start(bf16[8,144,384]{2,1,0:T(8,128)(2,1)S(1)} %get-tuple-element.362), channel_id=1, source_target_pairs={{0,1},{1,0},{2,3},{3,2},{4,5},{5,4},{6,7},{7,6},{8,9},{9,8},{10,11... | collective-permute-start | bytes 2654216 | tf_op jit(solution)/shard_map/ppermute | solution.py:54
  257.0 28.5 %collective-permute-start.52 = (bf16[1,512,384]{2,1,0:T(8,128)(2,1)S(1)}, bf16[1,512,384]{2,1,0:T(8,128)(2,1)S(1)}, u32[]{:S(2)}, u32[]{:S(2)}) collective-permute-start(bf16[1,512,384]{2,1,0:T(8,128)(2,1)S(1)} %get-tuple-element.385.sent_ref), channel_id=1, source_target_pairs={{0,16},{16,0},{1,17},{17,1},{2,18},{18,2},{3,19},{19,3},{4,20},{20... | collective-permute-start | bytes 1179656 | tf_op jit(solution)/shard_map/ppermute | solution.py:65
  268.5 25.1 %collective-permute-start.50 = (bf16[2,240,384]{2,1,0:T(8,128)(2,1)S(1)}, bf16[2,240,384]{2,1,0:T(8,128)(2,1)S(1)}, u32[]{:S(2)}, u32[]{:S(2)}) collective-permute-start(bf16[2,240,384]{2,1,0:T(8,128)(2,1)S(1)} %get-tuple-element.480), channel_id=1, source_target_pairs={{0,4},{1,5},{2,6},{3,7},{4,0},{5,1},{6,2},{7,3},{8,12},{9,13},{10,... | collective-permute-start | bytes 1105928 | tf_op jit(solution)/shard_map/ppermute | solution.py:54
  268.9 24.8 %collective-permute-start.49 = (bf16[4,144,384]{2,1,0:T(8,128)(2,1)S(1)}, bf16[4,144,384]{2,1,0:T(8,128)(2,1)S(1)}, u32[]{:S(2)}, u32[]{:S(2)}) collective-permute-start(bf16[4,144,384]{2,1,0:T(8,128)(2,1)S(1)} %get-tuple-element.476), channel_id=1, source_target_pairs={{0,2},{1,3},{2,0},{3,1},{4,6},{5,7},{6,4},{7,5},{8,10},{9,11},{10,... | collective-permute-start | bytes 1327112 | tf_op jit(solution)/shard_map/ppermute | solution.py:54
  270.3 23.4 %collective-permute-start.47 = (bf16[8,192,384]{2,1,0:T(8,128)(2,1)S(1)}, bf16[8,192,384]{2,1,0:T(8,128)(2,1)S(1)}, u32[]{:S(2)}, u32[]{:S(2)}) collective-permute-start(bf16[8,192,384]{2,1,0:T(8,128)(2,1)S(1)} %get-tuple-element.380), channel_id=1, source_target_pairs={{0,1},{1,0},{2,3},{3,2},{4,5},{5,4},{6,7},{7,6},{8,9},{9,8},{10,11... | collective-permute-start | bytes 3538952 | tf_op jit(solution)/shard_map/ppermute | solution.py:54
  283.3 10.4 %collective-permute-start.48 = (bf16[1,192,384]{2,1,0:T(8,128)(2,1)S(1)}, bf16[1,192,384]{2,1,0:T(8,128)(2,1)S(1)}, u32[]{:S(2)}, u32[]{:S(2)}) collective-permute-start(bf16[1,192,384]{2,1,0:T(8,128)(2,1)S(1)} %get-tuple-element.510), channel_id=1, source_target_pairs={{0,8},{1,9},{2,10},{3,11},{4,12},{5,13},{6,14},{7,15},{8,0},{9,1},... | collective-permute-start | bytes 442376 | tf_op jit(solution)/shard_map/ppermute | solution.py:54
  285.5 16.4 %collective-permute-start.57 = (bf16[3,512,384]{2,1,0:T(8,128)(2,1)S(1)}, bf16[3,512,384]{2,1,0:T(8,128)(2,1)}, u32[]{:S(2)}, u32[]{:S(2)}) collective-permute-start(bf16[3,512,384]{2,1,0:T(8,128)(2,1)S(1)} %get-tuple-element.401.sent_ref), channel_id=1, source_target_pairs={{0,16},{16,0},{1,17},{17,1},{2,18},{18,2},{3,19},{19,3},{4,20},{20... | collective-permute-start | bytes 3538952 | tf_op jit(solution)/shard_map/ppermute | solution.py:65
  294.5 24.9 %collective-permute-start.56 = (bf16[1,240,384]{2,1,0:T(8,128)(2,1)}, bf16[1,240,384]{2,1,0:T(8,128)(2,1)}, u32[]{:S(2)}, u32[]{:S(2)}) collective-permute-start(bf16[1,240,384]{2,1,0:T(8,128)(2,1)} %get-tuple-element.506), channel_id=1, source_target_pairs={{0,8},{1,9},{2,10},{3,11},{4,12},{5,13},{6,14},{7,15},{8,0},{9,1},... | collective-permute-start | bytes 552968 | tf_op jit(solution)/shard_map/ppermute | solution.py:54
  296.1 23.2 %collective-permute-start.55 = (bf16[2,144,384]{2,1,0:T(8,128)(2,1)}, bf16[2,144,384]{2,1,0:T(8,128)(2,1)}, u32[]{:S(2)}, u32[]{:S(2)}) collective-permute-start(bf16[2,144,384]{2,1,0:T(8,128)(2,1)} %get-tuple-element.496), channel_id=1, source_target_pairs={{0,4},{1,5},{2,6},{3,7},{4,0},{5,1},{6,2},{7,3},{8,12},{9,13},{10,... | collective-permute-start | bytes 663560 | tf_op jit(solution)/shard_map/ppermute | solution.py:54
  299.3 20.1 %collective-permute-start.53 = (bf16[4,192,384]{2,1,0:T(8,128)(2,1)}, bf16[4,192,384]{2,1,0:T(8,128)(2,1)}, u32[]{:S(2)}, u32[]{:S(2)}) collective-permute-start(bf16[4,192,384]{2,1,0:T(8,128)(2,1)} %get-tuple-element.470), channel_id=1, source_target_pairs={{0,2},{1,3},{2,0},{3,1},{4,6},{5,7},{6,4},{7,5},{8,10},{9,11},{10,... | collective-permute-start | bytes 1769480 | tf_op jit(solution)/shard_map/ppermute | solution.py:54
  300.2 24.1 %collective-permute-start.54 = (bf16[8,240,384]{2,1,0:T(8,128)(2,1)}, bf16[8,240,384]{2,1,0:T(8,128)(2,1)}, u32[]{:S(2)}, u32[]{:S(2)}) collective-permute-start(bf16[8,240,384]{2,1,0:T(8,128)(2,1)} %get-tuple-element.397), channel_id=1, source_target_pairs={{0,1},{1,0},{2,3},{3,2},{4,5},{5,4},{6,7},{7,6},{8,9},{9,8},{10,11... | collective-permute-start | bytes 4423688 | tf_op jit(solution)/shard_map/ppermute | solution.py:54
  302.0 14.9 %collective-permute-start.58 = (f32[16,2,576]{2,1,0:T(2,128)S(1)}, f32[16,2,576]{2,1,0:T(2,128)S(1)}, u32[]{:S(2)}, u32[]{:S(2)}) collective-permute-start(f32[16,2,576]{2,1,0:T(2,128)S(1)} %pad_maximum_fusion.5), channel_id=1, source_target_pairs={{0,16},{16,0},{1,17},{17,1},{2,18},{18,2},{3,19},{19,3},{4,20},{20... | collective-permute-start | bytes 221192 | tf_op jit(solution)/shard_map/ppermute | solution.py:65
  326.0 20.9 %collective-permute-start.62 = (bf16[4,240,384]{2,1,0:T(8,128)(2,1)S(1)}, bf16[4,240,384]{2,1,0:T(8,128)(2,1)S(1)}, u32[]{:S(2)}, u32[]{:S(2)}) collective-permute-start(bf16[4,240,384]{2,1,0:T(8,128)(2,1)S(1)} %get-tuple-element.466), channel_id=1, source_target_pairs={{0,2},{1,3},{2,0},{3,1},{4,6},{5,7},{6,4},{7,5},{8,10},{9,11},{10,... | collective-permute-start | bytes 2211848 | tf_op jit(solution)/shard_map/ppermute | solution.py:54
  327.0 20.0 %collective-permute-start.61 = (bf16[8,144,384]{2,1,0:T(8,128)(2,1)S(1)}, bf16[8,144,384]{2,1,0:T(8,128)(2,1)S(1)}, u32[]{:S(2)}, u32[]{:S(2)}) collective-permute-start(bf16[8,144,384]{2,1,0:T(8,128)(2,1)S(1)} %get-tuple-element.419), channel_id=1, source_target_pairs={{0,1},{1,0},{2,3},{3,2},{4,5},{5,4},{6,7},{7,6},{8,9},{9,8},{10,11... | collective-permute-start | bytes 2654216 | tf_op jit(solution)/shard_map/ppermute | solution.py:54
  328.5 18.4 %collective-permute-start.59 = (f32[8,2,576]{2,1,0:T(2,128)S(1)}, f32[8,2,576]{2,1,0:T(2,128)S(1)}, u32[]{:S(2)}, u32[]{:S(2)}) collective-permute-start(f32[8,2,576]{2,1,0:T(2,128)S(1)} %get-tuple-element.548), channel_id=1, source_target_pairs={{0,1},{1,0},{2,3},{3,2},{4,5},{5,4},{6,7},{7,6},{8,9},{9,8},{10,11... | collective-permute-start | bytes 110600 | tf_op jit(solution)/shard_map/ppermute | solution.py:54
  330.3 16.7 %collective-permute-start.60 = (bf16[2,192,384]{2,1,0:T(8,128)(2,1)S(1)}, bf16[2,192,384]{2,1,0:T(8,128)(2,1)S(1)}, u32[]{:S(2)}, u32[]{:S(2)}) collective-permute-start(bf16[2,192,384]{2,1,0:T(8,128)(2,1)S(1)} %get-tuple-element.482), channel_id=1, source_target_pairs={{0,4},{1,5},{2,6},{3,7},{4,0},{5,1},{6,2},{7,3},{8,12},{9,13},{10,... | collective-permute-start | bytes 884744 | tf_op jit(solution)/shard_map/ppermute | solution.py:54
  331.8 15.1 %collective-permute-start.63 = (bf16[1,144,384]{2,1,0:T(8,128)(2,1)S(1)}, bf16[1,144,384]{2,1,0:T(8,128)(2,1)S(1)}, u32[]{:S(2)}, u32[]{:S(2)}) collective-permute-start(bf16[1,144,384]{2,1,0:T(8,128)(2,1)S(1)} %get-tuple-element.520), channel_id=1, source_target_pairs={{0,8},{1,9},{2,10},{3,11},{4,12},{5,13},{6,14},{7,15},{8,0},{9,1},... | collective-permute-start | bytes 331784 | tf_op jit(solution)/shard_map/ppermute | solution.py:54
  347.2 14.1 %collective-permute-start.67 = (bf16[2,240,384]{2,1,0:T(8,128)(2,1)S(1)}, bf16[2,240,384]{2,1,0:T(8,128)(2,1)S(1)}, u32[]{:S(2)}, u32[]{:S(2)}) collective-permute-start(bf16[2,240,384]{2,1,0:T(8,128)(2,1)S(1)} %get-tuple-element.478), channel_id=1, source_target_pairs={{0,4},{1,5},{2,6},{3,7},{4,0},{5,1},{6,2},{7,3},{8,12},{9,13},{10,... | collective-permute-start | bytes 1105928 | tf_op jit(solution)/shard_map/ppermute | solution.py:54
  348.1 13.1 %collective-permute-start.66 = (bf16[4,144,384]{2,1,0:T(8,128)(2,1)S(1)}, bf16[4,144,384]{2,1,0:T(8,128)(2,1)S(1)}, u32[]{:S(2)}, u32[]{:S(2)}) collective-permute-start(bf16[4,144,384]{2,1,0:T(8,128)(2,1)S(1)} %get-tuple-element.474), channel_id=1, source_target_pairs={{0,2},{1,3},{2,0},{3,1},{4,6},{5,7},{6,4},{7,5},{8,10},{9,11},{10,... | collective-permute-start | bytes 1327112 | tf_op jit(solution)/shard_map/ppermute | solution.py:54
  349.4 9.8 %collective-permute-start.65 = (bf16[1,192,384]{2,1,0:T(8,128)(2,1)S(1)}, bf16[1,192,384]{2,1,0:T(8,128)(2,1)S(1)}, u32[]{:S(2)}, u32[]{:S(2)}) collective-permute-start(bf16[1,192,384]{2,1,0:T(8,128)(2,1)S(1)} %get-tuple-element.508), channel_id=1, source_target_pairs={{0,8},{1,9},{2,10},{3,11},{4,12},{5,13},{6,14},{7,15},{8,0},{9,1},... | collective-permute-start | bytes 442376 | tf_op jit(solution)/shard_map/ppermute | solution.py:54
  361.3 12.0 %collective-permute-start.70 = (bf16[1,240,384]{2,1,0:T(8,128)(2,1)S(1)}, bf16[1,240,384]{2,1,0:T(8,128)(2,1)S(1)}, u32[]{:S(2)}, u32[]{:S(2)}) collective-permute-start(bf16[1,240,384]{2,1,0:T(8,128)(2,1)S(1)} %get-tuple-element.504), channel_id=1, source_target_pairs={{0,8},{1,9},{2,10},{3,11},{4,12},{5,13},{6,14},{7,15},{8,0},{9,1},... | collective-permute-start | bytes 552968 | tf_op jit(solution)/shard_map/ppermute | solution.py:54
  362.8 10.5 %collective-permute-start.69 = (bf16[2,144,384]{2,1,0:T(8,128)(2,1)S(1)}, bf16[2,144,384]{2,1,0:T(8,128)(2,1)S(1)}, u32[]{:S(2)}, u32[]{:S(2)}) collective-permute-start(bf16[2,144,384]{2,1,0:T(8,128)(2,1)S(1)} %get-tuple-element.494), channel_id=1, source_target_pairs={{0,4},{1,5},{2,6},{3,7},{4,0},{5,1},{6,2},{7,3},{8,12},{9,13},{10,... | collective-permute-start | bytes 663560 | tf_op jit(solution)/shard_map/ppermute | solution.py:54
  364.0 9.4 %collective-permute-start.68 = (f32[2,2,576]{2,1,0:T(2,128)S(1)}, f32[2,2,576]{2,1,0:T(2,128)S(1)}, u32[]{:S(2)}, u32[]{:S(2)}) collective-permute-start(f32[2,2,576]{2,1,0:T(2,128)S(1)} %get-tuple-element.550), channel_id=1, source_target_pairs={{0,4},{1,5},{2,6},{3,7},{4,0},{5,1},{6,2},{7,3},{8,12},{9,13},{10,... | collective-permute-start | bytes 27656 | tf_op jit(solution)/shard_map/ppermute | solution.py:54
  373.4 12.3 %collective-permute-start.72 = (bf16[1,144,384]{2,1,0:T(8,128)(2,1)S(1)}, bf16[1,144,384]{2,1,0:T(8,128)(2,1)S(1)}, u32[]{:S(2)}, u32[]{:S(2)}) collective-permute-start(bf16[1,144,384]{2,1,0:T(8,128)(2,1)S(1)} %get-tuple-element.518), channel_id=1, source_target_pairs={{0,24},{1,25},{2,26},{3,27},{4,28},{5,29},{6,30},{7,31},{8,16},{9,... | collective-permute-start | bytes 331784 | tf_op jit(solution)/shard_map/ppermute | solution.py:62
  373.5 12.2 %collective-permute-start.74 = (bf16[1,144,384]{2,1,0:T(8,128)(2,1)S(1)}, bf16[1,144,384]{2,1,0:T(8,128)(2,1)S(1)}, u32[]{:S(2)}, u32[]{:S(2)}) collective-permute-start(bf16[1,144,384]{2,1,0:T(8,128)(2,1)S(1)} %get-tuple-element.518), channel_id=1, source_target_pairs={{0,8},{1,9},{2,10},{3,11},{4,12},{5,13},{6,14},{7,15},{8,0},{9,1},... | collective-permute-start | bytes 331784 | tf_op jit(solution)/shard_map/ppermute | solution.py:54
  375.0 10.8 %collective-permute-start.71 = (bf16[1,144,384]{2,1,0:T(8,128)(2,1)S(1)}, bf16[1,144,384]{2,1,0:T(8,128)(2,1)S(1)}, u32[]{:S(2)}, u32[]{:S(2)}) collective-permute-start(bf16[1,144,384]{2,1,0:T(8,128)(2,1)S(1)} %get-tuple-element.438), channel_id=1, source_target_pairs={{0,16},{16,0},{1,17},{17,1},{2,18},{18,2},{3,19},{19,3},{4,20},{20... | collective-permute-start | bytes 331784 | tf_op jit(solution)/shard_map/ppermute | solution.py:65
  376.3 9.5 %collective-permute-start.73 = (f32[1,2,576]{2,1,0:T(2,128)S(1)}, f32[1,2,576]{2,1,0:T(2,128)S(1)}, u32[]{:S(2)}, u32[]{:S(2)}) collective-permute-start(f32[1,2,576]{2,1,0:T(2,128)S(1)} %get-tuple-element.552), channel_id=1, source_target_pairs={{0,8},{1,9},{2,10},{3,11},{4,12},{5,13},{6,14},{7,15},{8,0},{9,1},... | collective-permute-start | bytes 13832 | tf_op jit(solution)/shard_map/ppermute | solution.py:54
  377.0 9.5 %collective-permute-start.75 = (bf16[1008,384]{1,0:T(8,128)(2,1)S(1)}, bf16[1008,384]{1,0:T(8,128)(2,1)S(1)}, u32[]{:S(2)}, u32[]{:S(2)}) collective-permute-start(bf16[1008,384]{1,0:T(8,128)(2,1)S(1)} %get-tuple-element.456), channel_id=1, source_target_pairs={{0,16},{16,0},{1,17},{17,1},{2,18},{18,2},{3,19},{19,3},{4,20},{20... | collective-permute-start | bytes 2322440 | tf_op jit(solution)/shard_map/ppermute | solution.py:65
  (92 other events, 688.8 us)
